TPU v7x, 512 devices: a whole 4x8x8 slice. The times are simulated.
512 devices in a mesh: wide: 64 (over z, y), rows: 8 (over x, core).
Axes of the slice: x: 4, y: 8, z: 8, core: 2. Of those that a mesh axis runs over, the one named last changes fastest.
Arguments:
- slabs: bfloat16 [64, 8, 10, 32, 128], P('wide', 'rows'), may hold values from -6 to 6
- dest: int32 [64, 8, 10], P('wide', 'rows'), may hold values from 0 to 63, as said below
- pos: int32 [64, 8, 10], P('wide', 'rows'), may hold values from 0 to 9, as said below
- lengths: int32 [64], P('wide'), may hold values from 1 to 5
- cot: bfloat16 [64, 5, 16, 32, 128], P('wide', None, 'rows'), may hold values from -6 to 6
- w_first: bfloat16 [3456, 128], P('wide'), may hold values from -0.109375 to 0.109375
- w_second: bfloat16 [3456, 128], P('wide'), may hold values from -0.109375 to 0.109375
Outputs:
- block_out: bfloat16 [64, 5, 16, 32, 128], P('wide', None, 'rows')
- grad_input: bfloat16 [64, 5, 16, 32, 128], P('wide', None, 'rows')
- grad_w_first: float32 [3456, 128], P('wide')
- grad_w_second: float32 [3456, 128], P('wide')
Inputs may be any that keep to these rules, and one draw needn't show every extreme that they name: `dest`: within a band no loader sends more than one slab to any clip; every clip receives exactly 10 slabs in each band. `pos`: for every clip and band the 10 slabs it receives carry the places 0 to 9, each once.
All inputs are finite; a program needn't handle non-finite values.
Results may differ from a plain program's by a relative error of at most 0.018.
Values may be sent and summed in bfloat16 or wider, within the bound.
A program may use at most 64 MiB of HBM per device.

v0:
```python
import math

import jax
import jax.numpy as jnp
from jax import lax
from jax.sharding import PartitionSpec as P


def with_halo(block, sides, width):
    for axis, dim in sides:
        count = lax.axis_size(axis)
        forward = [(i, i + 1) for i in range(count - 1)]
        backward = [(target, source) for source, target in forward]
        low = lax.ppermute(
            lax.slice_in_dim(block, block.shape[dim] - width, None, axis=dim), axis, forward
        )
        high = lax.ppermute(lax.slice_in_dim(block, 0, width, axis=dim), axis, backward)
        block = jnp.concatenate([low, block, high], axis=dim)
    return block


def silu_slope(values):
    sig = jax.nn.sigmoid(values)
    return sig * (1.0 + values * (1.0 - sig))


def conv_forward(extended, kernel):
    padded = jnp.concatenate([extended[:1], extended[:1], extended], axis=0)
    result = lax.conv_general_dilated(
        padded[None],
        kernel,
        (1, 1, 1),
        ((0, 0), (0, 0), (1, 1)),
        dimension_numbers=("NDHWC", "DHWIO", "NDHWC"),
        preferred_element_type=jnp.float32,
    )
    return result[0]


def conv_weight_grad(extended, upstream):
    padded = jnp.concatenate([extended[:1], extended[:1], extended], axis=0)
    result = lax.conv_general_dilated(
        padded[None],
        upstream[None],
        (1, 1, 1),
        ((0, 0), (0, 0), (1, 1)),
        dimension_numbers=("CDHWN", "IDHWO", "NDHWC"),
        preferred_element_type=jnp.float32,
    )
    channels = extended.shape[-1]
    return jnp.transpose(result, (1, 2, 3, 0, 4)).reshape(27 * channels, upstream.shape[-1])


def conv_data_grad(upstream_ext, kernel):
    padded = jnp.pad(upstream_ext, ((2, 2), (0, 0), (0, 0), (0, 0)))
    flipped = kernel[::-1, ::-1, ::-1]
    result = lax.conv_general_dilated(
        padded[None],
        flipped,
        (1, 1, 1),
        ((0, 0), (0, 0), (1, 1)),
        dimension_numbers=("NDHWC", "DHWOI", "NDHWC"),
        preferred_element_type=jnp.float32,
    )[0]
    head = (result[0] + result[1] + result[2])[None]
    return jnp.concatenate([head, result[3:]], axis=0)


def body(slabs, dest, pos, lengths, cot, w_first, w_second):
    wide_size = lax.axis_size("wide")
    band_count = lax.axis_size("rows")
    slab_count = slabs.shape[2]
    columns = slabs.shape[3]
    channels = slabs.shape[4]
    frames = cot.shape[1]
    band_rows = cot.shape[2]
    capacity = -(-slab_count // wide_size)
    slot_count = wide_size * capacity
    targets = dest[0, 0]
    places = pos[0, 0]
    ranking = jnp.arange(slab_count, dtype=jnp.int32)
    earlier = (targets[None, :] == targets[:, None]) & (ranking[None, :] < ranking[:, None])
    slab_rank = jnp.sum(earlier.astype(jnp.int32), axis=1)
    slot_of = targets * capacity + slab_rank
    placing = slot_of[None, :] == jnp.arange(slot_count, dtype=jnp.int32)[:, None]
    flat_slabs = slabs[0, 0].reshape(slab_count, columns * channels)
    outgoing = jnp.dot(placing.astype(jnp.bfloat16), flat_slabs, preferred_element_type=jnp.float32)
    outgoing = outgoing.astype(jnp.bfloat16).reshape(wide_size, capacity, columns * channels)
    labels = jnp.sum(jnp.where(placing, places[None, :] + 1, 0), axis=1) - 1
    labels = labels.reshape(wide_size, capacity)
    arrived, arrived_places = (
        lax.all_to_all(outgoing, "wide", split_axis=0, concat_axis=0, tiled=True),
        lax.all_to_all(labels, "wide", split_axis=0, concat_axis=0, tiled=True),
    )
    settle = (
        arrived_places.reshape(slot_count)[None, :]
        == jnp.arange(slab_count, dtype=jnp.int32)[:, None]
    )
    tile = jnp.dot(
        settle.astype(jnp.bfloat16),
        arrived.reshape(slot_count, columns * channels),
        preferred_element_type=jnp.float32,
    )
    tile = tile.astype(jnp.bfloat16).reshape(frames, band_rows, columns, channels)
    full_first, full_second = (
        lax.all_gather(w_first, "wide", axis=0, tiled=True),
        lax.all_gather(w_second, "wide", axis=0, tiled=True),
    )
    kernel_first = full_first.reshape(3, 3, 3, channels, channels)
    kernel_second = full_second.reshape(3, 3, 3, channels, channels)
    tile_wide = tile.astype(jnp.float32)
    first = jax.nn.silu(tile_wide).astype(jnp.bfloat16)
    first_ext = with_halo(first, (("rows", 1),), 1)
    act = conv_forward(first_ext, kernel_first).astype(jnp.bfloat16)
    second = jax.nn.silu(act.astype(jnp.float32)).astype(jnp.bfloat16)
    second_ext = with_halo(second, (("rows", 1),), 1)
    block_out = (tile_wide + conv_forward(second_ext, kernel_second)).astype(jnp.bfloat16)
    live = (jnp.arange(frames, dtype=jnp.int32) < lengths[0])[:, None, None, None]
    out_grad = jnp.where(live, cot[0], jnp.zeros_like(cot[0]))
    out_grad_ext = with_halo(out_grad, (("rows", 1),), 1)
    weight_second = conv_weight_grad(second_ext, out_grad)
    hidden_grad = conv_data_grad(out_grad_ext, kernel_second)
    act_grad = (hidden_grad * silu_slope(act.astype(jnp.float32))).astype(jnp.bfloat16)
    act_grad_ext = with_halo(act_grad, (("rows", 1),), 1)
    weight_first = conv_weight_grad(first_ext, act_grad)
    first_grad = conv_data_grad(act_grad_ext, kernel_first)
    grad_input = (out_grad.astype(jnp.float32) + first_grad * silu_slope(tile_wide)).astype(
        jnp.bfloat16
    )
    scale = 1.0 / math.sqrt(frames * band_rows * columns * band_count * wide_size)
    weight_first = weight_first * scale
    weight_second = weight_second * scale
    total_first, total_second = (
        lax.psum(weight_first.astype(jnp.bfloat16), "rows").astype(jnp.float32),
        lax.psum(weight_second.astype(jnp.bfloat16), "rows").astype(jnp.float32),
    )
    share_first, share_second = (
        lax.psum_scatter(total_first, "wide", scatter_dimension=0, tiled=True),
        lax.psum_scatter(total_second, "wide", scatter_dimension=0, tiled=True),
    )
    return (block_out[None], grad_input[None], share_first, share_second)


def solution(mesh):
    return jax.shard_map(
        body,
        mesh=mesh,
        in_specs=(
            P("wide", "rows", None, None, None),
            P("wide", "rows", None),
            P("wide", "rows", None),
            P("wide"),
            P("wide", None, "rows", None, None),
            P("wide", None),
            P("wide", None),
        ),
        out_specs=(
            P("wide", None, "rows", None, None),
            P("wide", None, "rows", None, None),
            P("wide", None),
            P("wide", None),
        ),
        check_vma=False,
    )
```

profile of v0, /device:TPU:24, one launch (start us, length us, event | category | flops | bytes accessed | tf_op | source)
XLA Modules:
  0.0 527.8 jit_solution(5221411180850742156)
XLA Ops:
  7.2 0.9 convert_reduce_fusion
  8.1 0.7 bitcast_add_fusion
  8.7 0.7 add_bitcast_fusion.1
  9.5 0.7 copy.172
  10.2 16.4 %all-to-all-start = ((s32[64,1,1]{2,1,0:T(1,128)}), s32[64,1,1]{2,1,0:T(1,128)S(1)}, u32[]{:S(2)}, u32[]{:S(2)}) async-start(s32[64,1,1]{2,1,0:T(1,128)} %copy.172), calls=%async_computation | async-start | bytes 65536 | tf_op jit(solution)/shard_map/all_to_all | solution.py:93
  27.2 0.9 pad.71
  28.2 1.0 bitcast_select_fusion
  30.1 1.0 reduce.1
  31.1 1.2 reshape.276
  32.3 3.5 all-to-all-done
  35.8 9.2 %all-to-all-start.1 = ((bf16[64,2,2048]{2,1,0:T(2,128)(2,1)}), bf16[64,2,2048]{2,1,0:T(2,128)(2,1)S(1)}, u32[]{:S(2)}, u32[]{:S(2)}) async-start(bf16[64,2,2048]{2,1,0:T(2,128)(2,1)} %reshape.276), calls=%async_computation.1 | async-start | bytes 1048576 | tf_op jit(solution)/shard_map/all_to_all | solution.py:92
  45.1 1.3 collective-permute-start.5
  46.4 3.0 collective-permute-start.4
  49.4 52.7 %all-gather = bf16[64,54,128]{2,1,0:T(8,128)(2,1)S(1)} all-gather(bf16[1,54,128]{2,1,0:T(8,128)(2,1)S(1)} %bitcast.138), channel_id=1, replica_groups=mesh['wide'=64,'rows'=8] {'wide'}, dimensions={0}, use_global_device_ids=true | all-gather | bytes 898560 | tf_op jit(solution)/shard_map/all_gather | solution.py:106
  102.1 48.3 %all-gather.1 = bf16[64,54,128]{2,1,0:T(8,128)(2,1)S(1)} all-gather(bf16[1,54,128]{2,1,0:T(8,128)(2,1)S(1)} %bitcast.139), channel_id=1, replica_groups=mesh['wide'=64,'rows'=8] {'wide'}, dimensions={0}, use_global_device_ids=true | all-gather | bytes 898560 | tf_op jit(solution)/shard_map/all_gather | solution.py:107
  150.4 1.2 reshape.194
  151.8 1.2 reduce
  153.5 1.2 convolution_select_fusion.1
  155.2 0.7 fusion.3
  156.0 1.3 collective-permute-start.1
  157.3 3.0 collective-permute-start
  160.6 0.6 collective-permute-done
  161.7 0.9 fusion.47
  162.8 1.3 collective-permute-start.7
  164.1 3.8 collective-permute-start.6
  168.0 1.3 collective-permute-start.3
  169.3 5.0 collective-permute-start.2
  174.5 3.5 multiply_convert_fusion.1
  178.4 1.2 convolution_select_fusion
  180.2 0.9 convolution_select_fusion.2
  181.3 0.7 fusion.59
  182.0 3.5 multiply_convert_fusion
  185.6 74.2 %all-reduce.10.cloned.1.call-done = (bf16[3456,128]{1,0:T(8,128)(2,1)}, bf16[3456,128]{1,0:T(8,128)(2,1)}) async-done(((bf16[3456,128]{1,0:T(8,128)(2,1)}, bf16[3456,128]{1,0:T(8,128)(2,1)}), (bf16[3456,128]{1,0:T(8,128)(2,1)}, bf16[3456,128]{1,0:T(8,128)(2,1)})) %all-reduce.10.cloned.1.call-update) | async-done | bytes 1769488 | tf_op jit(solution)/shard_map/psum | solution.py:134
  259.7 1.4 convert_element_type.113
  261.3 162.5 %fusion.84 = (f32[64,128]{1,0:T(8,128)}, f32[64,128]{1,0:T(8,128)}) fusion(f32[3456,128]{1,0:T(8,128)S(1)} %convert_element_type.113, f32[3456,128]{1,0:T(8,128)S(1)} %convert_element_type.116), kind=kCustom, calls=%all-reduce-scatter.2 | all-reduce-scatter fusion | flops 1048577 | bytes 3606528
  423.8 1.3 collective-permute-start.16
  425.1 1.3 collective-permute-start.15
  426.4 4.0 collective-permute-start.14
  430.4 0.8 slice.135
  431.2 11.2 %collective-permute-start.13 = (f32[64,128]{1,0:T(8,128)}, f32[64,128]{1,0:T(8,128)S(1)}, u32[]{:S(2)}, u32[]{:S(2)}) collective-permute-start(f32[64,128]{1,0:T(8,128)} %get-tuple-element.28), channel_id=1, source_target_pairs={{0,48},{8,56},{16,64},{24,72},{32,80},{40,88},{48,96},{56,104},{64... | collective-permute-start | bytes 98312
  442.4 2.7 collective-permute-start.17
  445.1 1.5 collective-permute-done.17
  446.6 4.9 collective-permute-start.12
  451.6 9.5 %collective-permute-start.11 = (f32[64,128]{1,0:T(8,128)}, f32[64,128]{1,0:T(8,128)S(1)}, u32[]{:S(2)}, u32[]{:S(2)}) collective-permute-start(f32[64,128]{1,0:T(8,128)} %get-tuple-element.28), channel_id=1, source_target_pairs={{0,32},{8,40},{16,48},{24,56},{32,64},{40,72},{48,80},{56,88},{64,... | collective-permute-start | bytes 98312
  461.1 3.2 collective-permute-start.10
  464.3 7.9 %collective-permute-start.9 = (f32[64,128]{1,0:T(8,128)}, f32[64,128]{1,0:T(8,128)S(1)}, u32[]{:S(2)}, u32[]{:S(2)}) collective-permute-start(f32[64,128]{1,0:T(8,128)} %get-tuple-element.28), channel_id=1, source_target_pairs={{0,16},{8,24},{16,32},{24,40},{32,48},{40,56},{48,64},{56,72},{64,... | collective-permute-start | bytes 98312
  472.2 1.9 collective-permute-start.8
  474.2 1.3 collective-permute-start.26
  475.5 3.5 collective-permute-start.25
  479.0 3.4 collective-permute-start.24
  482.4 3.1 collective-permute-start.23
  485.6 0.8 slice.136
  486.3 4.0 collective-permute-start.27
  490.4 1.3 dynamic-slice.6
  492.3 2.3 concatenate.49
  494.6 1.3 collective-permute-start.22
  495.9 7.8 %collective-permute-start.21 = (f32[64,128]{1,0:T(8,128)}, f32[64,128]{1,0:T(8,128)S(1)}, u32[]{:S(2)}, u32[]{:S(2)}) collective-permute-start(f32[64,128]{1,0:T(8,128)} %get-tuple-element.29), channel_id=1, source_target_pairs={{0,32},{8,40},{16,48},{24,56},{32,64},{40,72},{48,80},{56,88},{64,... | collective-permute-start | bytes 98312
  503.7 2.5 collective-permute-start.20
  506.2 5.9 %collective-permute-start.19 = (f32[64,128]{1,0:T(8,128)}, f32[64,128]{1,0:T(8,128)S(1)}, u32[]{:S(2)}, u32[]{:S(2)}) collective-permute-start(f32[64,128]{1,0:T(8,128)} %get-tuple-element.29), channel_id=1, source_target_pairs={{0,16},{8,24},{16,32},{24,40},{32,48},{40,56},{48,64},{56,72},{64,... | collective-permute-start | bytes 98312
  512.1 1.9 collective-permute-start.18
  514.0 0.6 constant_dynamic-slice_fusion.1
  514.6 3.4 collective-permute-done.18
  518.1 2.2 concatenate.50
  520.3 0.6 constant_dynamic-slice_fusion
  (102 shorter events, 4.7 us)
Async XLA Ops:
  10.2 25.6 %all-to-all-start = ((s32[64,1,1]{2,1,0:T(1,128)}), s32[64,1,1]{2,1,0:T(1,128)S(1)}, u32[]{:S(2)}, u32[]{:S(2)}) async-start(s32[64,1,1]{2,1,0:T(1,128)} %copy.172), calls=%async_computation | async-start | bytes 65536 | tf_op jit(solution)/shard_map/all_to_all | solution.py:93
  29.6 19.8 %copy-start.3 = (bf16[54,128]{1,0:T(8,128)(2,1)S(1)}, bf16[54,128]{1,0:T(8,128)(2,1)}, u32[]{:S(2)}) copy-start(bf16[54,128]{1,0:T(8,128)(2,1)} %param.12) | copy-start | bytes 41476
  31.1 71.0 %copy-start.4 = (bf16[54,128]{1,0:T(8,128)(2,1)S(1)}, bf16[54,128]{1,0:T(8,128)(2,1)}, u32[]{:S(2)}) copy-start(bf16[54,128]{1,0:T(8,128)(2,1)} %param.13) | copy-start | bytes 41476
  35.8 118.8 %all-to-all-start.1 = ((bf16[64,2,2048]{2,1,0:T(2,128)(2,1)}), bf16[64,2,2048]{2,1,0:T(2,128)(2,1)S(1)}, u32[]{:S(2)}, u32[]{:S(2)}) async-start(bf16[64,2,2048]{2,1,0:T(2,128)(2,1)} %reshape.276), calls=%async_computation.1 | async-start | bytes 1048576 | tf_op jit(solution)/shard_map/all_to_all | solution.py:92
  45.0 214.7 %all-reduce.10.cloned.1.call-start = ((), (), s32[]{:S(2)}) async-start(), calls=%async_computation.2 | async-start | bytes 3538944 | tf_op jit(solution)/shard_map/psum | solution.py:134
  45.1 107.9 %collective-permute-start.5 = (bf16[5,1,32,128]{3,2,1,0:T(8,128)(2,1)S(1)}, bf16[5,1,32,128]{3,2,1,0:T(8,128)(2,1)S(1)}, u32[]{:S(2)}, u32[]{:S(2)}) collective-permute-start(bf16[5,1,32,128]{3,2,1,0:T(8,128)(2,1)S(1)} %get-tuple-element.44), channel_id=1, source_target_pairs={{1,0},{2,1},{3,2},{4,3},{5,4},{6,5},{7,6},{9,8},{10,9},{11,10},{12... | collective-permute-start | bytes 122888 | tf_op jit(solution)/shard_map/ppermute | solution.py:17
  46.4 106.6 %collective-permute-start.4 = (bf16[5,1,32,128]{3,2,1,0:T(8,128)(2,1)S(1)}, bf16[5,1,32,128]{3,2,1,0:T(8,128)(2,1)S(1)}, u32[]{:S(2)}, u32[]{:S(2)}) collective-permute-start(bf16[5,1,32,128]{3,2,1,0:T(8,128)(2,1)S(1)} %get-tuple-element.43), channel_id=1, source_target_pairs={{0,1},{1,2},{2,3},{3,4},{4,5},{5,6},{6,7},{8,9},{9,10},{10,11},{11... | collective-permute-start | bytes 122888 | tf_op jit(solution)/shard_map/ppermute | solution.py:14
  151.7 1.7 copy-start.5
  156.0 4.6 collective-permute-start.1
  157.3 3.9 collective-permute-start
  160.5 1.2 copy-start
  162.8 15.1 %collective-permute-start.7 = (bf16[5,1,32,128]{3,2,1,0:T(8,128)(2,1)S(1)}, bf16[5,1,32,128]{3,2,1,0:T(8,128)(2,1)S(1)}, u32[]{:S(2)}, u32[]{:S(2)}) collective-permute-start(bf16[5,1,32,128]{3,2,1,0:T(8,128)(2,1)S(1)} %get-tuple-element.40), channel_id=1, source_target_pairs={{1,0},{2,1},{3,2},{4,3},{5,4},{6,5},{7,6},{9,8},{10,9},{11,10},{12... | collective-permute-start | bytes 122888 | tf_op jit(solution)/shard_map/ppermute | solution.py:17
  164.1 13.8 %collective-permute-start.6 = (bf16[5,1,32,128]{3,2,1,0:T(8,128)(2,1)S(1)}, bf16[5,1,32,128]{3,2,1,0:T(8,128)(2,1)S(1)}, u32[]{:S(2)}, u32[]{:S(2)}) collective-permute-start(bf16[5,1,32,128]{3,2,1,0:T(8,128)(2,1)S(1)} %get-tuple-element.39), channel_id=1, source_target_pairs={{0,1},{1,2},{2,3},{3,4},{4,5},{5,6},{6,7},{8,9},{9,10},{10,11},{11... | collective-permute-start | bytes 122888 | tf_op jit(solution)/shard_map/ppermute | solution.py:14
  168.0 11.9 %collective-permute-start.3 = (bf16[5,1,32,128]{3,2,1,0:T(8,128)(2,1)S(1)}, bf16[5,1,32,128]{3,2,1,0:T(8,128)(2,1)S(1)}, u32[]{:S(2)}, u32[]{:S(2)}) collective-permute-start(bf16[5,1,32,128]{3,2,1,0:T(8,128)(2,1)S(1)} %get-tuple-element.46), channel_id=1, source_target_pairs={{1,0},{2,1},{3,2},{4,3},{5,4},{6,5},{7,6},{9,8},{10,9},{11,10},{12... | collective-permute-start | bytes 122888 | tf_op jit(solution)/shard_map/ppermute | solution.py:17
  169.3 10.6 %collective-permute-start.2 = (bf16[5,1,32,128]{3,2,1,0:T(8,128)(2,1)S(1)}, bf16[5,1,32,128]{3,2,1,0:T(8,128)(2,1)S(1)}, u32[]{:S(2)}, u32[]{:S(2)}) collective-permute-start(bf16[5,1,32,128]{3,2,1,0:T(8,128)(2,1)S(1)} %get-tuple-element.45), channel_id=1, source_target_pairs={{0,1},{1,2},{2,3},{3,4},{4,5},{5,6},{6,7},{8,9},{9,10},{10,11},{11... | collective-permute-start | bytes 122888 | tf_op jit(solution)/shard_map/ppermute | solution.py:14
  180.2 1.0 copy-start.2
  259.7 1.4 copy-start.1
  423.8 27.8 %collective-permute-start.16 = (f32[64,128]{1,0:T(8,128)}, f32[64,128]{1,0:T(8,128)S(1)}, u32[]{:S(2)}, u32[]{:S(2)}) collective-permute-start(f32[64,128]{1,0:T(8,128)} %get-tuple-element.28), channel_id=1, source_target_pairs={{0,72},{8,80},{16,88},{24,96},{32,104},{40,112},{48,120},{56,128},... | collective-permute-start | bytes 98312
  425.1 36.0 %collective-permute-start.15 = (f32[64,128]{1,0:T(8,128)}, f32[64,128]{1,0:T(8,128)S(1)}, u32[]{:S(2)}, u32[]{:S(2)}) collective-permute-start(f32[64,128]{1,0:T(8,128)} %get-tuple-element.28), channel_id=1, source_target_pairs={{0,64},{8,72},{16,80},{24,88},{32,96},{40,104},{48,112},{56,120},{... | collective-permute-start | bytes 98312
  426.4 37.9 %collective-permute-start.14 = (f32[64,128]{1,0:T(8,128)}, f32[64,128]{1,0:T(8,128)S(1)}, u32[]{:S(2)}, u32[]{:S(2)}) collective-permute-start(f32[64,128]{1,0:T(8,128)} %get-tuple-element.28), channel_id=1, source_target_pairs={{0,56},{8,64},{16,72},{24,80},{32,88},{40,96},{48,104},{56,112},{6... | collective-permute-start | bytes 98312
  431.2 41.1 %collective-permute-start.13 = (f32[64,128]{1,0:T(8,128)}, f32[64,128]{1,0:T(8,128)S(1)}, u32[]{:S(2)}, u32[]{:S(2)}) collective-permute-start(f32[64,128]{1,0:T(8,128)} %get-tuple-element.28), channel_id=1, source_target_pairs={{0,48},{8,56},{16,64},{24,72},{32,80},{40,88},{48,96},{56,104},{64... | collective-permute-start | bytes 98312
  442.4 4.2 collective-permute-start.17
  446.6 27.5 %collective-permute-start.12 = (f32[64,128]{1,0:T(8,128)}, f32[64,128]{1,0:T(8,128)S(1)}, u32[]{:S(2)}, u32[]{:S(2)}) collective-permute-start(f32[64,128]{1,0:T(8,128)} %get-tuple-element.28), channel_id=1, source_target_pairs={{0,40},{8,48},{16,56},{24,64},{32,72},{40,80},{48,88},{56,96},{64,... | collective-permute-start | bytes 98312
  451.6 23.9 %collective-permute-start.11 = (f32[64,128]{1,0:T(8,128)}, f32[64,128]{1,0:T(8,128)S(1)}, u32[]{:S(2)}, u32[]{:S(2)}) collective-permute-start(f32[64,128]{1,0:T(8,128)} %get-tuple-element.28), channel_id=1, source_target_pairs={{0,32},{8,40},{16,48},{24,56},{32,64},{40,72},{48,80},{56,88},{64,... | collective-permute-start | bytes 98312
  461.1 17.9 %collective-permute-start.10 = (f32[64,128]{1,0:T(8,128)}, f32[64,128]{1,0:T(8,128)S(1)}, u32[]{:S(2)}, u32[]{:S(2)}) collective-permute-start(f32[64,128]{1,0:T(8,128)} %get-tuple-element.28), channel_id=1, source_target_pairs={{0,24},{8,32},{16,40},{24,48},{32,56},{40,64},{48,72},{56,80},{64,... | collective-permute-start | bytes 98312
  464.3 18.1 %collective-permute-start.9 = (f32[64,128]{1,0:T(8,128)}, f32[64,128]{1,0:T(8,128)S(1)}, u32[]{:S(2)}, u32[]{:S(2)}) collective-permute-start(f32[64,128]{1,0:T(8,128)} %get-tuple-element.28), channel_id=1, source_target_pairs={{0,16},{8,24},{16,32},{24,40},{32,48},{40,56},{48,64},{56,72},{64,... | collective-permute-start | bytes 98312
  472.2 14.1 %collective-permute-start.8 = (f32[64,128]{1,0:T(8,128)}, f32[64,128]{1,0:T(8,128)S(1)}, u32[]{:S(2)}, u32[]{:S(2)}) collective-permute-start(f32[64,128]{1,0:T(8,128)} %get-tuple-element.28), channel_id=1, source_target_pairs={{0,8},{8,16},{16,24},{24,32},{32,40},{40,48},{48,56},{56,64},{64,7... | collective-permute-start | bytes 98312
  474.2 21.7 %collective-permute-start.26 = (f32[64,128]{1,0:T(8,128)}, f32[64,128]{1,0:T(8,128)S(1)}, u32[]{:S(2)}, u32[]{:S(2)}) collective-permute-start(f32[64,128]{1,0:T(8,128)} %get-tuple-element.29), channel_id=1, source_target_pairs={{0,72},{8,80},{16,88},{24,96},{32,104},{40,112},{48,120},{56,128},... | collective-permute-start | bytes 98312
  475.5 28.2 %collective-permute-start.25 = (f32[64,128]{1,0:T(8,128)}, f32[64,128]{1,0:T(8,128)S(1)}, u32[]{:S(2)}, u32[]{:S(2)}) collective-permute-start(f32[64,128]{1,0:T(8,128)} %get-tuple-element.29), channel_id=1, source_target_pairs={{0,64},{8,72},{16,80},{24,88},{32,96},{40,104},{48,112},{56,120},{... | collective-permute-start | bytes 98312
  479.0 27.1 %collective-permute-start.24 = (f32[64,128]{1,0:T(8,128)}, f32[64,128]{1,0:T(8,128)S(1)}, u32[]{:S(2)}, u32[]{:S(2)}) collective-permute-start(f32[64,128]{1,0:T(8,128)} %get-tuple-element.29), channel_id=1, source_target_pairs={{0,56},{8,64},{16,72},{24,80},{32,88},{40,96},{48,104},{56,112},{6... | collective-permute-start | bytes 98312
  482.4 29.6 %collective-permute-start.23 = (f32[64,128]{1,0:T(8,128)}, f32[64,128]{1,0:T(8,128)S(1)}, u32[]{:S(2)}, u32[]{:S(2)}) collective-permute-start(f32[64,128]{1,0:T(8,128)} %get-tuple-element.29), channel_id=1, source_target_pairs={{0,48},{8,56},{16,64},{24,72},{32,80},{40,88},{48,96},{56,104},{64... | collective-permute-start | bytes 98312
  486.3 8.3 %collective-permute-start.27 = (f32[54,128]{1,0:T(8,128)S(1)}, f32[54,128]{1,0:T(8,128)S(1)}, u32[]{:S(2)}, u32[]{:S(2)}) collective-permute-start(f32[54,128]{1,0:T(8,128)S(1)} %slice.136), channel_id=1, source_target_pairs={{0,80},{8,88},{16,96},{24,104},{32,112},{40,120},{48,128},{56,136}... | collective-permute-start | bytes 82952
  494.6 20.0 %collective-permute-start.22 = (f32[64,128]{1,0:T(8,128)}, f32[64,128]{1,0:T(8,128)S(1)}, u32[]{:S(2)}, u32[]{:S(2)}) collective-permute-start(f32[64,128]{1,0:T(8,128)} %get-tuple-element.29), channel_id=1, source_target_pairs={{0,40},{8,48},{16,56},{24,64},{32,72},{40,80},{48,88},{56,96},{64,... | collective-permute-start | bytes 98312
  495.9 18.7 %collective-permute-start.21 = (f32[64,128]{1,0:T(8,128)}, f32[64,128]{1,0:T(8,128)S(1)}, u32[]{:S(2)}, u32[]{:S(2)}) collective-permute-start(f32[64,128]{1,0:T(8,128)} %get-tuple-element.29), channel_id=1, source_target_pairs={{0,32},{8,40},{16,48},{24,56},{32,64},{40,72},{48,80},{56,88},{64,... | collective-permute-start | bytes 98312
  503.7 10.9 %collective-permute-start.20 = (f32[64,128]{1,0:T(8,128)}, f32[64,128]{1,0:T(8,128)S(1)}, u32[]{:S(2)}, u32[]{:S(2)}) collective-permute-start(f32[64,128]{1,0:T(8,128)} %get-tuple-element.29), channel_id=1, source_target_pairs={{0,24},{8,32},{16,40},{24,48},{32,56},{40,64},{48,72},{56,80},{64,... | collective-permute-start | bytes 98312
  506.2 8.4 %collective-permute-start.19 = (f32[64,128]{1,0:T(8,128)}, f32[64,128]{1,0:T(8,128)S(1)}, u32[]{:S(2)}, u32[]{:S(2)}) collective-permute-start(f32[64,128]{1,0:T(8,128)} %get-tuple-element.29), channel_id=1, source_target_pairs={{0,16},{8,24},{16,32},{24,40},{32,48},{40,56},{48,64},{56,72},{64,... | collective-permute-start | bytes 98312
  512.1 6.0 %collective-permute-start.18 = (f32[64,128]{1,0:T(8,128)}, f32[64,128]{1,0:T(8,128)S(1)}, u32[]{:S(2)}, u32[]{:S(2)}) collective-permute-start(f32[64,128]{1,0:T(8,128)} %get-tuple-element.29), channel_id=1, source_target_pairs={{0,8},{8,16},{16,24},{24,32},{32,40},{40,48},{48,56},{56,64},{64,7... | collective-permute-start | bytes 98312
Sparse Core Ops, SparseCore 0:
  185.7 74.0 all-reduce.9
where the time goes:
time: 529 us; the launch traced here: 528 us
  blocking collectives  263 us (50%)
  starting transfers between devices  128 us (24%)
  waiting for transfers between devices  83.3 us (16%)
  between operations  16.3 us (3%)
  local copies, waits for them, and re-layouts  16.2 us (3%)
  matrix products  12.2 us (2%)
  other arithmetic  8.08 us (2%)
    unnamed x1, blocking collectives  163 us
    unnamed x20, starting transfers between devices  82.6 us
    psum x1, waiting for transfers between devices, body(): lax.psum(weight_first.astype(jnp.bfloat16), 'rows').astype(jnp.float32)  74.2 us
    all_gather x1, blocking collectives, body(): lax.all_gather(w_first, 'wide', axis=0, tiled=True)  52.7 us
    all_gather x1, blocking collectives, body(): lax.all_gather(w_second, 'wide', axis=0, tiled=True)  48.3 us
    all_to_all x1, starting transfers between devices, body(): lax.all_to_all(labels, 'wide', split_axis=0, concat_axis=0, tiled=True)  16.4 us
    ppermute x4, starting transfers between devices, with_halo(): lax.ppermute(lax.slice_in_dim(block, block.shape[dim] - width, None, axis...  14.9 us
    unnamed x33, local copies, waits for them, and re-layouts  12.1 us
  transfers between devices with their start and end apart: 31, of which 5 were waited for; matrix products, arithmetic and copies ran while one was open for 4% of the time, Pallas kernels for 0%

commit v1 on v0

--- a/solution.py
+++ b/solution.py
@@ -66,6 +66,39 @@
     return jnp.concatenate([head, result[3:]], axis=0)
 
 
+def gather_weights(w_first, w_second, band_count):
+    rows_local, channels = w_first.shape
+    part = channels // band_count
+    me = lax.axis_index("rows")
+    both = jnp.stack([w_first, w_second]).reshape(2, rows_local, band_count, part)
+    mine = lax.dynamic_index_in_dim(both, me, axis=2, keepdims=False)
+    mine = mine.reshape(1, 2, rows_local * part)
+    wide_all = lax.all_gather(mine, "wide", axis=0, tiled=True)
+    full = lax.all_gather(wide_all[None], "rows", axis=0, tiled=True)
+    count = wide_all.shape[0]
+    full = full.reshape(band_count, count, 2, rows_local, part)
+    full = jnp.transpose(full, (2, 1, 3, 0, 4)).reshape(2, count * rows_local, channels)
+    shape = (3, 3, 3, channels, channels)
+    return full[0].reshape(shape), full[1].reshape(shape)
+
+
+def reduce_weight_grads(weight_first, weight_second, band_count, wide_size):
+    total_rows, channels = weight_first.shape
+    part = channels // band_count
+    chunk = total_rows // wide_size
+    both = jnp.stack([weight_first, weight_second]).astype(jnp.bfloat16)
+    both = both.reshape(2, total_rows, band_count, part)
+    both = jnp.transpose(both, (2, 0, 1, 3)).reshape(band_count, 2, total_rows * part)
+    band_sum = lax.psum_scatter(both, "rows", scatter_dimension=0, tiled=True)
+    band_sum = band_sum.astype(jnp.float32).reshape(2, wide_size, chunk * part)
+    band_sum = jnp.transpose(band_sum, (1, 0, 2))
+    share = lax.psum_scatter(band_sum, "wide", scatter_dimension=0, tiled=True)
+    joined = lax.all_gather(share, "rows", axis=0, tiled=True)
+    joined = joined.reshape(band_count, 2, chunk, part)
+    joined = jnp.transpose(joined, (1, 2, 0, 3)).reshape(2, chunk, channels)
+    return joined[0], joined[1]
+
+
 def body(slabs, dest, pos, lengths, cot, w_first, w_second):
     wide_size = lax.axis_size("wide")
     band_count = lax.axis_size("rows")
@@ -102,12 +135,7 @@
         preferred_element_type=jnp.float32,
     )
     tile = tile.astype(jnp.bfloat16).reshape(frames, band_rows, columns, channels)
-    full_first, full_second = (
-        lax.all_gather(w_first, "wide", axis=0, tiled=True),
-        lax.all_gather(w_second, "wide", axis=0, tiled=True),
-    )
-    kernel_first = full_first.reshape(3, 3, 3, channels, channels)
-    kernel_second = full_second.reshape(3, 3, 3, channels, channels)
+    kernel_first, kernel_second = gather_weights(w_first, w_second, band_count)
     tile_wide = tile.astype(jnp.float32)
     first = jax.nn.silu(tile_wide).astype(jnp.bfloat16)
     first_ext = with_halo(first, (("rows", 1),), 1)
@@ -130,14 +158,7 @@
     scale = 1.0 / math.sqrt(frames * band_rows * columns * band_count * wide_size)
     weight_first = weight_first * scale
     weight_second = weight_second * scale
-    total_first, total_second = (
-        lax.psum(weight_first.astype(jnp.bfloat16), "rows").astype(jnp.float32),
-        lax.psum(weight_second.astype(jnp.bfloat16), "rows").astype(jnp.float32),
-    )
-    share_first, share_second = (
-        lax.psum_scatter(total_first, "wide", scatter_dimension=0, tiled=True),
-        lax.psum_scatter(total_second, "wide", scatter_dimension=0, tiled=True),
-    )
+    share_first, share_second = reduce_weight_grads(weight_first, weight_second, band_count, wide_size)
     return (block_out[None], grad_input[None], share_first, share_second)
 
 

time: 529 us -> 460 us (0.87)
  the two profiles are of different devices: /device:TPU:24 before, /device:TPU:1 now
where the time goes in v1:
time: 460 us; the launch traced here: 459 us
  waiting for transfers between devices  224 us (49%)
  local copies, waits for them, and re-layouts  77.6 us (17%)
  blocking collectives  66.1 us (14%)
  starting transfers between devices  57.1 us (12%)
  between operations  15.3 us (3%)
  matrix products  10.3 us (2%)
  other arithmetic  8.36 us (2%)
    unnamed x5, waiting for transfers between devices  217 us
    all_gather x1, blocking collectives, gather_weights(): wide_all = lax.all_gather(mine, 'wide', axis=0, tiled=True)  48.7 us
    ppermute x4, starting transfers between devices, with_halo(): lax.ppermute(lax.slice_in_dim(block, 0, width, axis=dim), axis, backward)  29.5 us
    reshape x2, local copies, waits for them, and re-layouts, reduce_weight_grads(): jnp.transpose(both, (2, 0, 1, 3)).reshape(band_count, 2, total_rows * part)  25.6 us
    all_gather x1, blocking collectives, reduce_weight_grads(): joined = lax.all_gather(share, 'rows', axis=0, tiled=True)  17.4 us
    ppermute x4, starting transfers between devices, with_halo(): lax.ppermute(lax.slice_in_dim(block, block.shape[dim] - width, None, axis...  14 us
    unnamed x55, local copies, waits for them, and re-layouts  13.8 us
    slice x3, local copies, waits for them, and re-layouts, gather_weights(): return (full[0].reshape(shape), full[1].reshape(shape))  9.42 us
  transfers between devices with their start and end apart: 13, of which 3 were waited for; matrix products, arithmetic and copies ran while one was open for 5% of the time, Pallas kernels for 0%

profile of v1, /device:TPU:1, one launch (start us, length us, event | category | flops | bytes accessed | tf_op | source)
XLA Modules:
  0.0 458.6 jit_solution(10041641804432245874)
XLA Ops:
  7.2 0.8 copy.271
  8.0 0.8 copy.272
  9.1 48.7 %all_gather.9 = bf16[64,2,864]{2,1,0:T(2,128)(2,1)} all-gather(bf16[1,2,864]{2,1,0:T(2,128)(2,1)S(1)} %reshape.245), channel_id=1, replica_groups=mesh['wide'=64,'rows'=8] {'wide'}, dimensions={0}, use_global_device_ids=true | all-gather | bytes 224640 | tf_op jit(solution)/shard_map/all_gather | solution.py:76
  57.9 0.9 convert_reduce_fusion
  58.8 0.7 add_bitcast_fusion.1
  59.4 0.7 bitcast_add_fusion
  60.2 0.7 copy.266
  60.9 8.0 %all-to-all-start = ((s32[64,1,1]{2,1,0:T(1,128)}), s32[64,1,1]{2,1,0:T(1,128)S(1)}, u32[]{:S(2)}, u32[]{:S(2)}) async-start(s32[64,1,1]{2,1,0:T(1,128)} %copy.266), calls=%async_computation | async-start | bytes 65536 | tf_op jit(solution)/shard_map/all_to_all | solution.py:126
  68.9 0.9 pad.73
  70.8 1.0 reduce.1
  71.8 1.2 reshape.328
  73.0 6.7 %all-to-all-done = s32[64,1,1]{2,1,0:T(1,128)S(1)} async-done(((s32[64,1,1]{2,1,0:T(1,128)}), s32[64,1,1]{2,1,0:T(1,128)S(1)}, u32[]{:S(2)}, u32[]{:S(2)}) %all-to-all-start) | async-done | bytes 288 | tf_op jit(solution)/shard_map/all_to_all | solution.py:126
  79.7 5.5 %all-to-all-start.1 = ((bf16[64,2,2048]{2,1,0:T(2,128)(2,1)}), bf16[64,2,2048]{2,1,0:T(2,128)(2,1)S(1)}, u32[]{:S(2)}, u32[]{:S(2)}) async-start(bf16[64,2,2048]{2,1,0:T(2,128)(2,1)} %reshape.328), calls=%async_computation.1 | async-start | bytes 1048576 | tf_op jit(solution)/shard_map/all_to_all | solution.py:125
  86.0 15.3 %collective-permute-start.5 = (bf16[5,1,32,128]{3,2,1,0:T(8,128)(2,1)S(1)}, bf16[5,1,32,128]{3,2,1,0:T(8,128)(2,1)S(1)}, u32[]{:S(2)}, u32[]{:S(2)}) collective-permute-start(bf16[5,1,32,128]{3,2,1,0:T(8,128)(2,1)S(1)} %get-tuple-element.46), channel_id=1, source_target_pairs={{1,0},{2,1},{3,2},{4,3},{5,4},{6,5},{7,6},{9,8},{10,9},{11,10},{12... | collective-permute-start | bytes 122888 | tf_op jit(solution)/shard_map/ppermute | solution.py:17
  101.3 3.0 collective-permute-start.4
  104.3 1.2 reduce
  105.5 0.5 reshape.329
  106.1 0.7 fusion.1
  106.8 0.7 copy-done
  107.6 10.4 %collective-permute-start.1 = (bf16[5,1,32,128]{3,2,1,0:T(8,128)(2,1)S(1)}, bf16[5,1,32,128]{3,2,1,0:T(8,128)(2,1)S(1)}, u32[]{:S(2)}, u32[]{:S(2)}) collective-permute-start(bf16[5,1,32,128]{3,2,1,0:T(8,128)(2,1)S(1)} %get-tuple-element.50), channel_id=1, source_target_pairs={{1,0},{2,1},{3,2},{4,3},{5,4},{6,5},{7,6},{9,8},{10,9},{11,10},{12... | collective-permute-start | bytes 122888 | tf_op jit(solution)/shard_map/ppermute | solution.py:17
  118.0 3.2 collective-permute-start
  121.6 0.8 slice.140
  122.4 0.7 fusion.70
  123.4 0.7 copy-done.9
  124.1 0.7 slice.130
  124.8 5.5 %copy.274 = bf16[512,2,864]{0,2,1:T(8,128)(2,1)} copy(bf16[512,2,864]{2,1,0:T(2,128)(2,1)} %all-gather.3.cloned.1.call-done) | data formatting | bytes 3538944 | tf_op jit(solution)/shard_map/all_gather | solution.py:77
  130.3 4.3 reshape.246
  134.6 2.0 fusion.83
  136.6 3.7 copy.282
  140.3 3.6 reshape_squeeze.11
  143.9 1.0 copy.283
  145.0 1.2 convolution_select_fusion.1
  146.2 0.7 copy-done.8
  146.9 3.7 copy.275
  150.6 3.6 reshape_squeeze.10
  154.2 1.0 copy.276
  155.5 0.9 fusion.45
  156.7 1.9 collective-permute-start.7
  158.7 3.9 collective-permute-start.6
  162.6 1.9 collective-permute-start.3
  164.5 3.9 collective-permute-start.2
  168.6 2.5 multiply_convert_fusion.1
  171.1 1.0 copy.306
  172.1 0.8 mul.95
  173.3 0.7 copy-done.5
  174.0 1.2 convolution_select_fusion
  175.8 0.7 copy-done.3
  176.5 0.9 convolution_select_fusion.2
  177.5 0.7 fusion.57
  178.3 2.6 multiply_convert_fusion
  180.9 1.0 copy.309
  181.8 0.8 mul.97
  182.8 9.0 %copy.318 = bf16[8,2,3456,16]{3,2,1,0:T(8,128)(2,1)} copy(bf16[8,2,3456,16]{2,3,0,1:T(8,128)(2,1)S(1)} %maximum_bitcast_fusion) | data formatting | bytes 3538944 | tf_op jit(solution)/shard_map/reshape | solution.py:91
  191.8 16.6 %reshape.324 = bf16[8,2,55296]{2,1,0:T(2,128)(2,1)} reshape(bf16[8,2,3456,16]{3,2,1,0:T(8,128)(2,1)} %copy.318) | data formatting | bytes 3538944 | tf_op jit(solution)/shard_map/reshape | solution.py:91
  208.5 1.3 dynamic-slice
  209.8 64.9 %all-reduce.7.cloned.1.call-done = bf16[8,2,55296]{2,1,0:T(2,128)(2,1)} async-done(((bf16[8,2,55296]{2,1,0:T(2,128)(2,1)}), bf16[8,2,55296]{2,1,0:T(2,128)(2,1)}) %all-reduce.7.cloned.1.call-update) | async-done | bytes 1769488
  274.6 1.7 dynamic-slice_convert_fusion
  276.8 1.1 copy.367
  278.0 1.3 dynamic-slice.2
  279.3 152.1 %all-reduce.9.cloned.1.call-done = f32[64,2,864]{2,1,0:T(2,128)} async-done(((f32[64,2,864]{2,1,0:T(2,128)}), f32[64,2,864]{2,1,0:T(2,128)}) %all-reduce.9.cloned.1.call-update) | async-done | bytes 442384
  431.4 1.3 constant_dynamic-slice_fusion
  432.8 17.4 %all_gather.11 = f32[8,2,864]{2,1,0:T(2,128)S(1)} all-gather(f32[1,2,864]{2,1,0:T(2,128)S(1)} %constant_dynamic-slice_fusion), channel_id=1, replica_groups=mesh['wide'=64,'rows'=8] {'rows'}, dimensions={0}, use_global_device_ids=true | all-gather | bytes 62208 | tf_op jit(solution)/shard_map/all_gather | solution.py:96
  450.5 0.7 copy.316
  451.4 0.7 copy.317
  (113 shorter events, 5.1 us)
Async XLA Ops:
  7.2 117.7 %all-gather.3.cloned.1.call-start = ((), (), s32[]{:S(2)}) async-start(), calls=%async_computation.2 | async-start | bytes 2064384 | tf_op jit(solution)/shard_map/all_gather | solution.py:77
  60.9 18.8 %all-to-all-start = ((s32[64,1,1]{2,1,0:T(1,128)}), s32[64,1,1]{2,1,0:T(1,128)S(1)}, u32[]{:S(2)}, u32[]{:S(2)}) async-start(s32[64,1,1]{2,1,0:T(1,128)} %copy.266), calls=%async_computation | async-start | bytes 65536 | tf_op jit(solution)/shard_map/all_to_all | solution.py:126
  69.9 16.0 %copy-start.11 = (bf16[1,5,2,32,128]{4,3,2,1,0:T(8,128)(2,1)S(1)}, bf16[1,5,2,32,128]{4,3,2,1,0:T(8,128)(2,1)}, u32[]{:S(2)}) copy-start(bf16[1,5,2,32,128]{4,3,2,1,0:T(8,128)(2,1)} %param.11) | copy-start | bytes 245764
  79.7 25.9 %all-to-all-start.1 = ((bf16[64,2,2048]{2,1,0:T(2,128)(2,1)}), bf16[64,2,2048]{2,1,0:T(2,128)(2,1)S(1)}, u32[]{:S(2)}, u32[]{:S(2)}) async-start(bf16[64,2,2048]{2,1,0:T(2,128)(2,1)} %reshape.328), calls=%async_computation.1 | async-start | bytes 1048576 | tf_op jit(solution)/shard_map/all_to_all | solution.py:125
  85.2 189.5 %all-reduce.7.cloned.1.call-start = ((), (), s32[]{:S(2)}) async-start(), calls=%async_computation.3 | async-start | bytes 3538944
  86.0 35.2 %collective-permute-start.5 = (bf16[5,1,32,128]{3,2,1,0:T(8,128)(2,1)S(1)}, bf16[5,1,32,128]{3,2,1,0:T(8,128)(2,1)S(1)}, u32[]{:S(2)}, u32[]{:S(2)}) collective-permute-start(bf16[5,1,32,128]{3,2,1,0:T(8,128)(2,1)S(1)} %get-tuple-element.46), channel_id=1, source_target_pairs={{1,0},{2,1},{3,2},{4,3},{5,4},{6,5},{7,6},{9,8},{10,9},{11,10},{12... | collective-permute-start | bytes 122888 | tf_op jit(solution)/shard_map/ppermute | solution.py:17
  101.3 19.9 %collective-permute-start.4 = (bf16[5,1,32,128]{3,2,1,0:T(8,128)(2,1)S(1)}, bf16[5,1,32,128]{3,2,1,0:T(8,128)(2,1)S(1)}, u32[]{:S(2)}, u32[]{:S(2)}) collective-permute-start(bf16[5,1,32,128]{3,2,1,0:T(8,128)(2,1)S(1)} %get-tuple-element.45), channel_id=1, source_target_pairs={{0,1},{1,2},{2,3},{3,4},{4,5},{5,6},{6,7},{8,9},{9,10},{10,11},{11... | collective-permute-start | bytes 122888 | tf_op jit(solution)/shard_map/ppermute | solution.py:14
  106.8 0.7 copy-start
  107.6 14.8 %collective-permute-start.1 = (bf16[5,1,32,128]{3,2,1,0:T(8,128)(2,1)S(1)}, bf16[5,1,32,128]{3,2,1,0:T(8,128)(2,1)S(1)}, u32[]{:S(2)}, u32[]{:S(2)}) collective-permute-start(bf16[5,1,32,128]{3,2,1,0:T(8,128)(2,1)S(1)} %get-tuple-element.50), channel_id=1, source_target_pairs={{1,0},{2,1},{3,2},{4,3},{5,4},{6,5},{7,6},{9,8},{10,9},{11,10},{12... | collective-permute-start | bytes 122888 | tf_op jit(solution)/shard_map/ppermute | solution.py:17
  118.0 4.4 collective-permute-start
  121.6 1.5 copy-start.6
  123.4 0.7 copy-start.9
  143.9 1.1 copy-start.7
  143.9 1.1 copy-start.14
  143.9 1.1 copy-start.16
  145.0 1.2 copy-start.2
  146.2 0.7 copy-start.8
  154.2 1.1 slice-start
  154.2 1.3 copy-start.10
  154.2 1.3 copy-start.15
  155.3 1.1 copy-start.4
  156.4 12.1 %copy-start.13 = (bf16[1,7,4,32,128]{4,3,2,1,0:T(8,128)(2,1)S(1)}, bf16[1,7,4,32,128]{4,3,2,1,0:T(8,128)(2,1)}, u32[]{:S(2)}) copy-start(bf16[1,7,4,32,128]{4,3,2,1,0:T(8,128)(2,1)} %get-tuple-element.34) | copy-start | bytes 688132
  156.7 16.1 %collective-permute-start.7 = (bf16[5,1,32,128]{3,2,1,0:T(8,128)(2,1)S(1)}, bf16[5,1,32,128]{3,2,1,0:T(8,128)(2,1)S(1)}, u32[]{:S(2)}, u32[]{:S(2)}) collective-permute-start(bf16[5,1,32,128]{3,2,1,0:T(8,128)(2,1)S(1)} %get-tuple-element.42), channel_id=1, source_target_pairs={{1,0},{2,1},{3,2},{4,3},{5,4},{6,5},{7,6},{9,8},{10,9},{11,10},{12... | collective-permute-start | bytes 122888 | tf_op jit(solution)/shard_map/ppermute | solution.py:17
  158.7 14.2 %collective-permute-start.6 = (bf16[5,1,32,128]{3,2,1,0:T(8,128)(2,1)S(1)}, bf16[5,1,32,128]{3,2,1,0:T(8,128)(2,1)S(1)}, u32[]{:S(2)}, u32[]{:S(2)}) collective-permute-start(bf16[5,1,32,128]{3,2,1,0:T(8,128)(2,1)S(1)} %get-tuple-element.41), channel_id=1, source_target_pairs={{0,1},{1,2},{2,3},{3,4},{4,5},{5,6},{6,7},{8,9},{9,10},{10,11},{11... | collective-permute-start | bytes 122888 | tf_op jit(solution)/shard_map/ppermute | solution.py:14
  162.6 12.8 %collective-permute-start.3 = (bf16[5,1,32,128]{3,2,1,0:T(8,128)(2,1)S(1)}, bf16[5,1,32,128]{3,2,1,0:T(8,128)(2,1)S(1)}, u32[]{:S(2)}, u32[]{:S(2)}) collective-permute-start(bf16[5,1,32,128]{3,2,1,0:T(8,128)(2,1)S(1)} %get-tuple-element.48), channel_id=1, source_target_pairs={{1,0},{2,1},{3,2},{4,3},{5,4},{6,5},{7,6},{9,8},{10,9},{11,10},{12... | collective-permute-start | bytes 122888 | tf_op jit(solution)/shard_map/ppermute | solution.py:17
  164.5 10.9 %collective-permute-start.2 = (bf16[5,1,32,128]{3,2,1,0:T(8,128)(2,1)S(1)}, bf16[5,1,32,128]{3,2,1,0:T(8,128)(2,1)S(1)}, u32[]{:S(2)}, u32[]{:S(2)}) collective-permute-start(bf16[5,1,32,128]{3,2,1,0:T(8,128)(2,1)S(1)} %get-tuple-element.47), channel_id=1, source_target_pairs={{0,1},{1,2},{2,3},{3,4},{4,5},{5,6},{6,7},{8,9},{9,10},{10,11},{11... | collective-permute-start | bytes 122888 | tf_op jit(solution)/shard_map/ppermute | solution.py:14
  172.9 1.2 copy-start.5
  175.3 1.2 copy-start.3
  176.5 1.0 copy-start.1
  176.5 1.0 copy-start.12
  208.4 223.0 %all-reduce.9.cloned.1.call-start = ((), (), s32[]{:S(2)}) async-start(), calls=%async_computation.4 | async-start | bytes 917504
Sparse Core Ops, SparseCore 0:
  58.0 38.9 all-gather.2
  208.6 66.0 all-reduce.6
  278.1 153.2 all-reduce.8

commit v2 on v1

--- a/solution.py
+++ b/solution.py
@@ -73,9 +73,11 @@
     both = jnp.stack([w_first, w_second]).reshape(2, rows_local, band_count, part)
     mine = lax.dynamic_index_in_dim(both, me, axis=2, keepdims=False)
     mine = mine.reshape(1, 2, rows_local * part)
-    wide_all = lax.all_gather(mine, "wide", axis=0, tiled=True)
+    count = lax.axis_size("wide")
+    wide_all = lax.all_to_all(
+        jnp.broadcast_to(mine, (count,) + mine.shape[1:]), "wide", 0, 0, tiled=True
+    )
     full = lax.all_gather(wide_all[None], "rows", axis=0, tiled=True)
-    count = wide_all.shape[0]
     full = full.reshape(band_count, count, 2, rows_local, part)
     full = jnp.transpose(full, (2, 1, 3, 0, 4)).reshape(2, count * rows_local, channels)
     shape = (3, 3, 3, channels, channels)
@@ -89,11 +91,14 @@
     both = jnp.stack([weight_first, weight_second]).astype(jnp.bfloat16)
     both = both.reshape(2, total_rows, band_count, part)
     both = jnp.transpose(both, (2, 0, 1, 3)).reshape(band_count, 2, total_rows * part)
-    band_sum = lax.psum_scatter(both, "rows", scatter_dimension=0, tiled=True)
-    band_sum = band_sum.astype(jnp.float32).reshape(2, wide_size, chunk * part)
-    band_sum = jnp.transpose(band_sum, (1, 0, 2))
-    share = lax.psum_scatter(band_sum, "wide", scatter_dimension=0, tiled=True)
-    joined = lax.all_gather(share, "rows", axis=0, tiled=True)
+    band_parts = lax.all_to_all(both, "rows", 0, 0, tiled=True)
+    band_sum = jnp.sum(band_parts.astype(jnp.float32), axis=0)
+    band_sum = jnp.transpose(band_sum.reshape(2, wide_size, chunk * part), (1, 0, 2))
+    wide_parts = lax.all_to_all(band_sum, "wide", 0, 0, tiled=True)
+    share = jnp.sum(wide_parts, axis=0, keepdims=True)
+    joined = lax.all_to_all(
+        jnp.broadcast_to(share, (band_count,) + share.shape[1:]), "rows", 0, 0, tiled=True
+    )
     joined = joined.reshape(band_count, 2, chunk, part)
     joined = jnp.transpose(joined, (1, 2, 0, 3)).reshape(2, chunk, channels)
     return joined[0], joined[1]
@@ -121,10 +126,14 @@
     outgoing = outgoing.astype(jnp.bfloat16).reshape(wide_size, capacity, columns * channels)
     labels = jnp.sum(jnp.where(placing, places[None, :] + 1, 0), axis=1) - 1
     labels = labels.reshape(wide_size, capacity)
-    arrived, arrived_places = (
-        lax.all_to_all(outgoing, "wide", split_axis=0, concat_axis=0, tiled=True),
-        lax.all_to_all(labels, "wide", split_axis=0, concat_axis=0, tiled=True),
+    lane_block = 128
+    tagged = jnp.concatenate(
+        [outgoing, jnp.broadcast_to(labels.astype(jnp.bfloat16)[:, :, None], (wide_size, capacity, lane_block))],
+        axis=2,
     )
+    tagged = lax.all_to_all(tagged, "wide", split_axis=0, concat_axis=0, tiled=True)
+    arrived = tagged[:, :, : columns * channels]
+    arrived_places = tagged[:, :, columns * channels].astype(jnp.int32)
     settle = (
         arrived_places.reshape(slot_count)[None, :]
         == jnp.arange(slab_count, dtype=jnp.int32)[:, None]

time: 460 us -> 237 us (0.52)
  waiting for transfers between devices: 224 us -> 19.2 us
  starting transfers between devices: 57.1 us -> 50 us
  blocking collectives: 66.1 us -> 59 us
    unnamed x5 -> x1, waiting for transfers between devices: 217 us -> 0.02 us
    all_gather x2 -> x0, blocking collectives: 66.1 us -> none  [the longest x1 48.7 us: gather_weights(): wide_all = lax.all_gather(mine, 'wide', axis=0, tiled=True)]
    all_to_all x0 -> x3, blocking collectives: none -> 59 us  [the longest x1 27.7 us: reduce_weight_grads(): band_parts = lax.all_to_all(both, 'rows', 0, 0, tiled=True)]
    ppermute x4, starting transfers between devices: 29.5 us -> 8.57 us  [with_halo(): lax.ppermute(lax.slice_in_dim(block, 0, width, axis=dim), axis, backward)]
    all_to_all x2, waiting for transfers between devices: 6.66 us -> 17.2 us  [the longest x1 9.27 us: gather_weights(): lax.all_to_all(jnp.broadcast_to(mine, (count,) + mine.shape[1:]), 'wide',...]
    all_to_all x2, starting transfers between devices: 13.5 us -> 22.6 us  [the longest x1 17.1 us: gather_weights(): lax.all_to_all(jnp.broadcast_to(mine, (count,) + mine.shape[1:]), 'wide',...]
    ppermute x4, starting transfers between devices: 14 us -> 18.8 us  [with_halo(): lax.ppermute(lax.slice_in_dim(block, block.shape[dim] - width, None, axis...]
    unnamed x55 -> x56, local copies, waits for them, and re-layouts: 13.8 us -> 10.7 us
  transfers between devices with their start and end apart: 13 -> 11, of which waited for: 3 -> 3; matrix products, arithmetic and copies ran while one was open for 5% -> 8% of each run, Pallas kernels for 0% -> 0%
where the time goes in v2:
time: 237 us; the launch traced here: 236 us
  local copies, waits for them, and re-layouts  74.3 us (31%)
  blocking collectives  59 us (25%)
  starting transfers between devices  50 us (21%)
  waiting for transfers between devices  19.2 us (8%)
  between operations  15.7 us (7%)
  matrix products  10.3 us (4%)
  other arithmetic  7.75 us (3%)
    all_to_all x1, blocking collectives, reduce_weight_grads(): band_parts = lax.all_to_all(both, 'rows', 0, 0, tiled=True)  27.7 us
    reshape x2, local copies, waits for them, and re-layouts, reduce_weight_grads(): jnp.transpose(both, (2, 0, 1, 3)).reshape(band_count, 2, total_rows * part)  24.9 us
    all_to_all x1, blocking collectives, reduce_weight_grads(): wide_parts = lax.all_to_all(band_sum, 'wide', 0, 0, tiled=True)  20.2 us
    ppermute x4, starting transfers between devices, with_halo(): lax.ppermute(lax.slice_in_dim(block, block.shape[dim] - width, None, axis...  18.8 us
    all_to_all x1, starting transfers between devices, gather_weights(): lax.all_to_all(jnp.broadcast_to(mine, (count,) + mine.shape[1:]), 'wide',...  17.1 us
    all_to_all x1, blocking collectives, reduce_weight_grads(): lax.all_to_all(jnp.broadcast_to(share, (band_count,) + share.shape[1:]),...  11 us
    unnamed x56, local copies, waits for them, and re-layouts  10.7 us
    slice x3, local copies, waits for them, and re-layouts, gather_weights(): return (full[0].reshape(shape), full[1].reshape(shape))  9.42 us
  transfers between devices with their start and end apart: 11, of which 3 were waited for; matrix products, arithmetic and copies ran while one was open for 8% of the time, Pallas kernels for 0%

profile of v2, /device:TPU:1, one launch (start us, length us, event | category | flops | bytes accessed | tf_op | source)
XLA Modules:
  0.0 236.2 jit_solution(258477224977766668)
XLA Ops:
  7.2 0.8 copy.267
  8.0 0.8 copy.268
  9.1 0.8 broadcast_in_dim.80
  9.9 17.1 %all-to-all-start.1 = ((bf16[64,2,864]{2,1,0:T(2,128)(2,1)}), bf16[64,2,864]{2,1,0:T(2,128)(2,1)S(1)}, u32[]{:S(2)}, u32[]{:S(2)}) async-start(bf16[64,2,864]{2,1,0:T(2,128)(2,1)} %broadcast_in_dim.80), calls=%async_computation.1 | async-start | bytes 458752 | tf_op jit(solution)/shard_map/all_to_all | solution.py:77
  27.1 0.9 convert_reduce_fusion.1
  28.0 0.7 bitcast_add_fusion
  28.7 0.9 pad.75
  30.1 9.3 %all-to-all-done.1 = bf16[64,2,864]{2,1,0:T(2,128)(2,1)S(1)} async-done(((bf16[64,2,864]{2,1,0:T(2,128)(2,1)}), bf16[64,2,864]{2,1,0:T(2,128)(2,1)S(1)}, u32[]{:S(2)}, u32[]{:S(2)}) %all-to-all-start.1) | async-done | bytes 221216 | tf_op jit(solution)/shard_map/all_to_all | solution.py:77
  39.3 0.7 copy-done.2
  40.3 0.5 broadcast.184
  40.8 1.0 reduce.2
  41.8 1.2 reshape.328
  43.0 5.5 %all-to-all-start = ((bf16[64,2,2112]{2,1,0:T(2,128)(2,1)}), bf16[64,2,2112]{2,1,0:T(2,128)(2,1)S(1)}, u32[]{:S(2)}, u32[]{:S(2)}) async-start(bf16[64,2,2112]{2,1,0:T(2,128)(2,1)} %reshape.328), calls=%async_computation | async-start | bytes 1114112 | tf_op jit(solution)/shard_map/all_to_all | solution.py:134
  49.3 5.1 %collective-permute-start.4 = (bf16[5,1,32,128]{3,2,1,0:T(8,128)(2,1)S(1)}, bf16[5,1,32,128]{3,2,1,0:T(8,128)(2,1)S(1)}, u32[]{:S(2)}, u32[]{:S(2)}) collective-permute-start(bf16[5,1,32,128]{3,2,1,0:T(8,128)(2,1)S(1)} %get-tuple-element.45), channel_id=1, source_target_pairs={{0,1},{1,2},{2,3},{3,4},{4,5},{5,6},{6,7},{8,9},{9,10},{10,11},{11... | collective-permute-start | bytes 122888 | tf_op jit(solution)/shard_map/ppermute | solution.py:14
  54.4 1.9 collective-permute-start.5
  56.3 7.9 %all-to-all-done = bf16[64,2,2112]{2,1,0:T(2,128)(2,1)S(1)} async-done(((bf16[64,2,2112]{2,1,0:T(2,128)(2,1)}), bf16[64,2,2112]{2,1,0:T(2,128)(2,1)S(1)}, u32[]{:S(2)}, u32[]{:S(2)}) %all-to-all-start) | async-done | bytes 540704 | tf_op jit(solution)/shard_map/all_to_all | solution.py:134
  64.2 0.6 reshape.329
  64.9 1.1 slice.137
  65.9 1.2 fusion.61
  67.2 0.7 fusion.1
  67.9 0.7 copy-done
  68.7 8.6 %collective-permute-start = (bf16[5,1,32,128]{3,2,1,0:T(8,128)(2,1)S(1)}, bf16[5,1,32,128]{3,2,1,0:T(8,128)(2,1)S(1)}, u32[]{:S(2)}, u32[]{:S(2)}) collective-permute-start(bf16[5,1,32,128]{3,2,1,0:T(8,128)(2,1)S(1)} %get-tuple-element.49), channel_id=1, source_target_pairs={{0,1},{1,2},{2,3},{3,4},{4,5},{5,6},{6,7},{8,9},{9,10},{10,11},{11... | collective-permute-start | bytes 122888 | tf_op jit(solution)/shard_map/ppermute | solution.py:14
  77.2 2.1 collective-permute-start.1
  79.8 0.8 slice.150
  80.5 2.0 collective-permute-done.1
  82.6 0.7 fusion.69
  83.6 0.7 copy-done.10
  84.3 0.7 slice.140
  85.0 5.5 %copy.270 = bf16[512,2,864]{0,2,1:T(8,128)(2,1)} copy(bf16[512,2,864]{2,1,0:T(2,128)(2,1)} %all-gather.3.cloned.1.call-done) | data formatting | bytes 3538944 | tf_op jit(solution)/shard_map/all_gather | solution.py:80
  90.5 4.3 %reshape.248 = bf16[8,64,2,54,16]{1,0,4,3,2:T(8,128)(2,1)S(1)} reshape(bf16[512,2,864]{0,2,1:T(8,128)(2,1)} %copy.270) | data formatting | bytes 3538944 | tf_op jit(solution)/shard_map/reshape | solution.py:81
  94.7 2.0 fusion.82
  96.7 3.7 %copy.278 = bf16[1,64,54,8,16]{2,1,4,3,0:T(8,128)(2,1)S(1)} copy(bf16[1,64,54,8,16]{1,3,4,2,0:T(8,128)(2,1)} %get-tuple-element.31) | data formatting | bytes 1769472 | tf_op jit(solution)/shard_map/slice | solution.py:84
  100.5 3.6 %reshape_squeeze.11 = bf16[3,3,3,128,128]{3,2,1,0,4:T(4,128)(2,1)S(1)} reshape(bf16[1,64,54,8,16]{2,1,4,3,0:T(8,128)(2,1)S(1)} %copy.278) | data formatting | bytes 1769472 | tf_op jit(solution)/shard_map/reshape;squeeze | solution.py:84
  104.1 1.0 copy.279
  105.1 1.2 convolution_select_fusion.1
  106.4 0.7 copy-done.9
  107.1 3.7 %copy.271 = bf16[1,64,54,8,16]{2,1,4,3,0:T(8,128)(2,1)S(1)} copy(bf16[1,64,54,8,16]{1,3,4,2,0:T(8,128)(2,1)} %get-tuple-element.30) | data formatting | bytes 1769472 | tf_op jit(solution)/shard_map/slice | solution.py:84
  110.8 3.6 %reshape_squeeze.10 = bf16[3,3,3,128,128]{3,2,1,0,4:T(4,128)(2,1)S(1)} reshape(bf16[1,64,54,8,16]{2,1,4,3,0:T(8,128)(2,1)S(1)} %copy.271) | data formatting | bytes 1769472 | tf_op jit(solution)/shard_map/reshape;squeeze | solution.py:84
  114.4 1.0 copy.272
  115.5 0.9 fusion.43
  117.0 1.9 collective-permute-start.6
  118.9 2.4 %collective-permute-start.7 = (bf16[5,1,32,128]{3,2,1,0:T(8,128)(2,1)S(1)}, bf16[5,1,32,128]{3,2,1,0:T(8,128)(2,1)S(1)}, u32[]{:S(2)}, u32[]{:S(2)}) collective-permute-start(bf16[5,1,32,128]{3,2,1,0:T(8,128)(2,1)S(1)} %get-tuple-element.42), channel_id=1, source_target_pairs={{1,0},{2,1},{3,2},{4,3},{5,4},{6,5},{7,6},{9,8},{10,9},{11,10},{12... | collective-permute-start | bytes 122888 | tf_op jit(solution)/shard_map/ppermute | solution.py:17
  121.4 3.2 %collective-permute-start.2 = (bf16[5,1,32,128]{3,2,1,0:T(8,128)(2,1)S(1)}, bf16[5,1,32,128]{3,2,1,0:T(8,128)(2,1)S(1)}, u32[]{:S(2)}, u32[]{:S(2)}) collective-permute-start(bf16[5,1,32,128]{3,2,1,0:T(8,128)(2,1)S(1)} %get-tuple-element.47), channel_id=1, source_target_pairs={{0,1},{1,2},{2,3},{3,4},{4,5},{5,6},{6,7},{8,9},{9,10},{10,11},{11... | collective-permute-start | bytes 122888 | tf_op jit(solution)/shard_map/ppermute | solution.py:14
  124.5 2.1 collective-permute-start.3
  126.7 2.5 %multiply_convert_fusion.1 = bf16[3,3,3,128,128]{4,3,2,1,0:T(8,128)(2,1)S(1)} fusion(bf16[1,7,4,32,128]{4,3,2,1,0:T(8,128)(2,1)S(1)} %copy-done.14, bf16[1,5,2,32,128]{4,3,2,1,0:T(8,128)(2,1)S(1)} %fusion.56), kind=kOutput, calls=%fused_computation.7 | convolution fusion | flops 278102016 | bytes 1196032 | tf_op jit(solution)/shard_map/transpose | solution.py:51
  129.2 1.0 copy.302
  130.2 0.8 mul.95
  131.5 0.7 copy-done.6
  132.2 1.2 convolution_select_fusion
  134.0 0.7 copy-done.4
  134.6 0.9 convolution_select_fusion.2
  135.7 0.7 fusion.55
  136.4 2.6 %multiply_convert_fusion = bf16[3,3,3,128,128]{4,3,2,1,0:T(8,128)(2,1)S(1)} fusion(bf16[1,7,4,32,128]{4,3,2,1,0:T(8,128)(2,1)S(1)} %get-tuple-element.36, bf16[1,5,2,32,128]{4,3,2,1,0:T(8,128)(2,1)S(1)} %get-tuple-element.29), kind=kOutput, calls=%fused_computation.6 | convolution fusion | flops 278102016 | bytes 1196032 | tf_op jit(solution)/shard_map/transpose | solution.py:51
  139.0 1.0 copy.305
  140.0 0.8 mul.97
  140.9 9.1 %copy.314 = bf16[8,2,3456,16]{3,2,1,0:T(8,128)(2,1)} copy(bf16[8,2,3456,16]{2,3,0,1:T(8,128)(2,1)S(1)} %maximum_bitcast_fusion) | data formatting | bytes 3538944 | tf_op jit(solution)/shard_map/reshape | solution.py:93
  150.0 15.8 %reshape.326 = bf16[8,2,55296]{2,1,0:T(2,128)(2,1)S(1)} reshape(bf16[8,2,3456,16]{3,2,1,0:T(8,128)(2,1)} %copy.314) | data formatting | bytes 3538944 | tf_op jit(solution)/shard_map/reshape | solution.py:93
  165.9 27.7 %all_to_all.25 = bf16[8,2,55296]{2,1,0:T(2,128)(2,1)S(1)} all-to-all(bf16[8,2,55296]{2,1,0:T(2,128)(2,1)S(1)} %reshape.326), channel_id=1, replica_groups=mesh['wide'=64,'rows'=8] {'rows'}, dimensions={0} | all-to-all | bytes 3538944 | tf_op jit(solution)/shard_map/all_to_all | solution.py:94
  193.6 1.6 convert_reduce_fusion
  195.2 0.5 reshape.250
  196.0 20.2 %all_to_all.26 = f32[64,2,864]{2,1,0:T(2,128)S(1)} all-to-all(f32[64,2,864]{2,1,0:T(2,128)S(1)} %copy.308), channel_id=1, replica_groups=mesh['wide'=64,'rows'=8] {'wide'}, dimensions={0} | all-to-all | bytes 884736 | tf_op jit(solution)/shard_map/all_to_all | solution.py:97
  216.5 11.0 %all_to_all.27 = f32[8,2,864]{2,1,0:T(2,128)S(1)} all-to-all(f32[8,2,864]{2,1,0:T(2,128)S(1)} %broadcast_in_dim.89), channel_id=1, replica_groups=mesh['wide'=64,'rows'=8] {'rows'}, dimensions={0} | all-to-all | bytes 110592 | tf_op jit(solution)/shard_map/all_to_all | solution.py:99
  227.9 0.7 copy.313
  228.7 0.7 copy.312
  (114 shorter events, 4.7 us)
Async XLA Ops:
  7.2 22.9 %copy-start.17 = (s32[1,1,10]{2,1,0:T(1,128)S(1)}, s32[1,1,10]{2,1,0:T(1,128)}, u32[]{:S(2)}) copy-start(s32[1,1,10]{2,1,0:T(1,128)} %param.9) | copy-start | bytes 124
  9.9 29.4 %all-to-all-start.1 = ((bf16[64,2,864]{2,1,0:T(2,128)(2,1)}), bf16[64,2,864]{2,1,0:T(2,128)(2,1)S(1)}, u32[]{:S(2)}, u32[]{:S(2)}) async-start(bf16[64,2,864]{2,1,0:T(2,128)(2,1)} %broadcast_in_dim.80), calls=%async_computation.1 | async-start | bytes 458752 | tf_op jit(solution)/shard_map/all_to_all | solution.py:77
  27.0 57.9 %all-gather.3.cloned.1.call-start = ((), (), s32[]{:S(2)}) async-start(), calls=%async_computation.5 | async-start | bytes 2064384 | tf_op jit(solution)/shard_map/all_gather | solution.py:80
  39.3 0.7 copy-start.2
  40.3 8.9 %copy-start.12 = (bf16[1,5,2,32,128]{4,3,2,1,0:T(8,128)(2,1)S(1)}, bf16[1,5,2,32,128]{4,3,2,1,0:T(8,128)(2,1)}, u32[]{:S(2)}) copy-start(bf16[1,5,2,32,128]{4,3,2,1,0:T(8,128)(2,1)} %param.11) | copy-start | bytes 245764
  43.0 21.3 %all-to-all-start = ((bf16[64,2,2112]{2,1,0:T(2,128)(2,1)}), bf16[64,2,2112]{2,1,0:T(2,128)(2,1)S(1)}, u32[]{:S(2)}, u32[]{:S(2)}) async-start(bf16[64,2,2112]{2,1,0:T(2,128)(2,1)} %reshape.328), calls=%async_computation | async-start | bytes 1114112 | tf_op jit(solution)/shard_map/all_to_all | solution.py:134
  49.3 30.1 %collective-permute-start.4 = (bf16[5,1,32,128]{3,2,1,0:T(8,128)(2,1)S(1)}, bf16[5,1,32,128]{3,2,1,0:T(8,128)(2,1)S(1)}, u32[]{:S(2)}, u32[]{:S(2)}) collective-permute-start(bf16[5,1,32,128]{3,2,1,0:T(8,128)(2,1)S(1)} %get-tuple-element.45), channel_id=1, source_target_pairs={{0,1},{1,2},{2,3},{3,4},{4,5},{5,6},{6,7},{8,9},{9,10},{10,11},{11... | collective-permute-start | bytes 122888 | tf_op jit(solution)/shard_map/ppermute | solution.py:14
  54.4 24.9 %collective-permute-start.5 = (bf16[5,1,32,128]{3,2,1,0:T(8,128)(2,1)S(1)}, bf16[5,1,32,128]{3,2,1,0:T(8,128)(2,1)S(1)}, u32[]{:S(2)}, u32[]{:S(2)}) collective-permute-start(bf16[5,1,32,128]{3,2,1,0:T(8,128)(2,1)S(1)} %get-tuple-element.46), channel_id=1, source_target_pairs={{1,0},{2,1},{3,2},{4,3},{5,4},{6,5},{7,6},{9,8},{10,9},{11,10},{12... | collective-permute-start | bytes 122888 | tf_op jit(solution)/shard_map/ppermute | solution.py:17
  67.9 0.7 copy-start
  68.7 11.9 %collective-permute-start = (bf16[5,1,32,128]{3,2,1,0:T(8,128)(2,1)S(1)}, bf16[5,1,32,128]{3,2,1,0:T(8,128)(2,1)S(1)}, u32[]{:S(2)}, u32[]{:S(2)}) collective-permute-start(bf16[5,1,32,128]{3,2,1,0:T(8,128)(2,1)S(1)} %get-tuple-element.49), channel_id=1, source_target_pairs={{0,1},{1,2},{2,3},{3,4},{4,5},{5,6},{6,7},{8,9},{9,10},{10,11},{11... | collective-permute-start | bytes 122888 | tf_op jit(solution)/shard_map/ppermute | solution.py:14
  77.2 5.3 %collective-permute-start.1 = (bf16[5,1,32,128]{3,2,1,0:T(8,128)(2,1)S(1)}, bf16[5,1,32,128]{3,2,1,0:T(8,128)(2,1)S(1)}, u32[]{:S(2)}, u32[]{:S(2)}) collective-permute-start(bf16[5,1,32,128]{3,2,1,0:T(8,128)(2,1)S(1)} %get-tuple-element.50), channel_id=1, source_target_pairs={{1,0},{2,1},{3,2},{4,3},{5,4},{6,5},{7,6},{9,8},{10,9},{11,10},{12... | collective-permute-start | bytes 122888 | tf_op jit(solution)/shard_map/ppermute | solution.py:17
  79.8 3.5 %copy-start.7 = (bf16[9,4,1,8,5,128]{5,3,4,1,0,2:T(8,128)(2,1)}, bf16[9,4,1,8,5,128]{5,3,4,1,0,2:T(8,128)(2,1)S(1)}, u32[]{:S(2)}) copy-start(bf16[9,4,1,8,5,128]{5,3,4,1,0,2:T(8,128)(2,1)S(1)} %copy.284) | copy-start | bytes 1105924
  83.6 0.7 copy-start.10
  104.0 1.1 copy-start.8
  104.0 1.1 copy-start.15
  104.1 1.1 copy-start.18
  105.1 1.2 copy-start.3
  106.3 0.7 copy-start.9
  114.4 1.1 copy-start.11
  114.4 1.1 copy-start.16
  115.4 0.9 copy-start.5
  115.4 1.2 slice-start
  116.4 10.3 %copy-start.14 = (bf16[1,7,4,32,128]{4,3,2,1,0:T(8,128)(2,1)S(1)}, bf16[1,7,4,32,128]{4,3,2,1,0:T(8,128)(2,1)}, u32[]{:S(2)}) copy-start(bf16[1,7,4,32,128]{4,3,2,1,0:T(8,128)(2,1)} %get-tuple-element.34) | copy-start | bytes 688132
  117.0 14.0 %collective-permute-start.6 = (bf16[5,1,32,128]{3,2,1,0:T(8,128)(2,1)S(1)}, bf16[5,1,32,128]{3,2,1,0:T(8,128)(2,1)S(1)}, u32[]{:S(2)}, u32[]{:S(2)}) collective-permute-start(bf16[5,1,32,128]{3,2,1,0:T(8,128)(2,1)S(1)} %get-tuple-element.41), channel_id=1, source_target_pairs={{0,1},{1,2},{2,3},{3,4},{4,5},{5,6},{6,7},{8,9},{9,10},{10,11},{11... | collective-permute-start | bytes 122888 | tf_op jit(solution)/shard_map/ppermute | solution.py:14
  118.9 12.1 %collective-permute-start.7 = (bf16[5,1,32,128]{3,2,1,0:T(8,128)(2,1)S(1)}, bf16[5,1,32,128]{3,2,1,0:T(8,128)(2,1)S(1)}, u32[]{:S(2)}, u32[]{:S(2)}) collective-permute-start(bf16[5,1,32,128]{3,2,1,0:T(8,128)(2,1)S(1)} %get-tuple-element.42), channel_id=1, source_target_pairs={{1,0},{2,1},{3,2},{4,3},{5,4},{6,5},{7,6},{9,8},{10,9},{11,10},{12... | collective-permute-start | bytes 122888 | tf_op jit(solution)/shard_map/ppermute | solution.py:17
  121.4 12.2 %collective-permute-start.2 = (bf16[5,1,32,128]{3,2,1,0:T(8,128)(2,1)S(1)}, bf16[5,1,32,128]{3,2,1,0:T(8,128)(2,1)S(1)}, u32[]{:S(2)}, u32[]{:S(2)}) collective-permute-start(bf16[5,1,32,128]{3,2,1,0:T(8,128)(2,1)S(1)} %get-tuple-element.47), channel_id=1, source_target_pairs={{0,1},{1,2},{2,3},{3,4},{4,5},{5,6},{6,7},{8,9},{9,10},{10,11},{11... | collective-permute-start | bytes 122888 | tf_op jit(solution)/shard_map/ppermute | solution.py:14
  124.5 9.1 %collective-permute-start.3 = (bf16[5,1,32,128]{3,2,1,0:T(8,128)(2,1)S(1)}, bf16[5,1,32,128]{3,2,1,0:T(8,128)(2,1)S(1)}, u32[]{:S(2)}, u32[]{:S(2)}) collective-permute-start(bf16[5,1,32,128]{3,2,1,0:T(8,128)(2,1)S(1)} %get-tuple-element.48), channel_id=1, source_target_pairs={{1,0},{2,1},{3,2},{4,3},{5,4},{6,5},{7,6},{9,8},{10,9},{11,10},{12... | collective-permute-start | bytes 122888 | tf_op jit(solution)/shard_map/ppermute | solution.py:17
  131.0 1.2 copy-start.6
  133.5 1.2 copy-start.4
  134.6 1.0 copy-start.1
  134.6 1.0 copy-start.13
Sparse Core Ops, SparseCore 0:
  40.2 25.0 all-gather.2

commit v3 on v0

v3 whole, which is shorter than its diff:
```python
import math

import jax
import jax.numpy as jnp
from jax import lax
from jax.sharding import PartitionSpec as P


def with_halo(block, sides, width):
    for axis, dim in sides:
        count = lax.axis_size(axis)
        forward = [(i, i + 1) for i in range(count - 1)]
        backward = [(target, source) for source, target in forward]
        low = lax.ppermute(
            lax.slice_in_dim(block, block.shape[dim] - width, None, axis=dim), axis, forward
        )
        high = lax.ppermute(lax.slice_in_dim(block, 0, width, axis=dim), axis, backward)
        block = jnp.concatenate([low, block, high], axis=dim)
    return block


def silu_slope(values):
    sig = jax.nn.sigmoid(values)
    return sig * (1.0 + values * (1.0 - sig))


def weight_pieces(w_first, w_second, band_count):
    rows_local, channels = w_first.shape
    part = channels // band_count
    me = lax.axis_index("rows")
    both = jnp.stack([w_first, w_second])
    mine = lax.dynamic_slice_in_dim(both, me * part, part, axis=2)
    return jnp.transpose(mine, (0, 2, 1)).reshape(2 * part * rows_local)


def assemble_weights(pieces, band_count, rows_local, channels):
    count = pieces.shape[0]
    part = channels // band_count
    block = pieces.reshape(count, 2, part, rows_local)
    block = jnp.transpose(block, (1, 2, 0, 3)).reshape(2, part, count * rows_local)
    full = lax.all_gather(block, "rows", axis=1, tiled=True)
    return full[0], full[1]


def reduce_weight_grads(grad_t, band_count, wide_size):
    _, channels, total_rows = grad_t.shape
    part = channels // band_count
    chunk = total_rows // wide_size
    blocks = grad_t.astype(jnp.bfloat16).reshape(2, band_count, part, total_rows)
    blocks = jnp.transpose(blocks, (1, 0, 2, 3))
    band_parts = lax.all_to_all(blocks, "rows", 0, 0, tiled=True)
    band_sum = jnp.sum(band_parts.astype(jnp.float32), axis=0)
    band_sum = band_sum.reshape(2, part, wide_size, chunk)
    band_sum = jnp.transpose(band_sum, (2, 0, 1, 3)).reshape(wide_size, 2 * part * chunk)
    wide_parts = lax.all_to_all(band_sum, "wide", 0, 0, tiled=True)
    share = jnp.sum(wide_parts, axis=0, keepdims=True)
    joined = lax.all_to_all(
        jnp.broadcast_to(share, (band_count,) + share.shape[1:]), "rows", 0, 0, tiled=True
    )
    joined = joined.reshape(band_count, 2, part, chunk)
    joined = jnp.transpose(joined, (1, 3, 0, 2)).reshape(2, chunk, channels)
    return joined[0], joined[1]


def tap_patches(padded, frames, rows, cols):
    taps = [
        padded[a : a + frames, b : b + rows, e : e + cols]
        for a in range(3)
        for b in range(3)
        for e in range(3)
    ]
    stacked = jnp.stack(taps, axis=3)
    return stacked.reshape(frames * rows * cols, 27 * padded.shape[-1])


def forward_patches(extended):
    frames, rows_ext, cols, _ = extended.shape
    padded = jnp.concatenate([extended[:1], extended[:1], extended], axis=0)
    padded = jnp.pad(padded, ((0, 0), (0, 0), (1, 1), (0, 0)))
    return tap_patches(padded, frames, rows_ext - 2, cols)


def conv_out(patches, kernel_t, shape):
    result = lax.dot_general(
        patches, kernel_t, (((1,), (1,)), ((), ())), preferred_element_type=jnp.float32
    )
    return result.reshape(shape)


def weight_grad_t(patches, upstream):
    flat = upstream.reshape(-1, upstream.shape[-1])
    return lax.dot_general(
        flat, patches, (((0,), (0,)), ((), ())), preferred_element_type=jnp.float32
    )


def data_grad(upstream_ext, kernel_t):
    frames, rows_ext, cols, _ = upstream_ext.shape
    rows = rows_ext - 2
    padded = jnp.pad(upstream_ext, ((2, 2), (0, 0), (1, 1), (0, 0)))
    padded = padded[::-1, ::-1, ::-1]
    patches = tap_patches(padded, frames + 2, rows, cols)
    cout = kernel_t.shape[0]
    regrouped = kernel_t.reshape(cout, 27, -1).transpose(1, 0, 2).reshape(27 * cout, -1)
    result = jnp.dot(patches, regrouped, preferred_element_type=jnp.float32)
    result = result.reshape(frames + 2, rows, cols, -1)[::-1, ::-1, ::-1]
    head = (result[0] + result[1] + result[2])[None]
    return jnp.concatenate([head, result[3:]], axis=0)


def body(slabs, dest, pos, lengths, cot, w_first, w_second):
    wide_size = lax.axis_size("wide")
    band_count = lax.axis_size("rows")
    slab_count = slabs.shape[2]
    columns = slabs.shape[3]
    channels = slabs.shape[4]
    frames = cot.shape[1]
    band_rows = cot.shape[2]
    rows_local = w_first.shape[0]
    capacity = -(-slab_count // wide_size)
    slot_count = wide_size * capacity
    targets = dest[0, 0]
    places = pos[0, 0]
    ranking = jnp.arange(slab_count, dtype=jnp.int32)
    earlier = (targets[None, :] == targets[:, None]) & (ranking[None, :] < ranking[:, None])
    slab_rank = jnp.sum(earlier.astype(jnp.int32), axis=1)
    slot_of = targets * capacity + slab_rank
    placing = slot_of[None, :] == jnp.arange(slot_count, dtype=jnp.int32)[:, None]
    flat_slabs = slabs[0, 0].reshape(slab_count, columns * channels)
    outgoing = jnp.dot(placing.astype(jnp.bfloat16), flat_slabs, preferred_element_type=jnp.float32)
    outgoing = outgoing.astype(jnp.bfloat16).reshape(wide_size, capacity * columns * channels)
    labels = jnp.sum(jnp.where(placing, places[None, :] + 1, 0), axis=1) - 1
    labels = labels.reshape(wide_size, capacity).astype(jnp.bfloat16)
    label_block = 64
    pieces = weight_pieces(w_first, w_second, band_count)
    tagged = jnp.concatenate(
        [
            outgoing,
            jnp.repeat(labels, label_block // capacity, axis=1),
            jnp.broadcast_to(pieces[None], (wide_size, pieces.shape[0])),
        ],
        axis=1,
    )
    tagged = lax.all_to_all(tagged, "wide", split_axis=0, concat_axis=0, tiled=True)
    payload = capacity * columns * channels
    arrived = tagged[:, :payload].reshape(slot_count, columns * channels)
    arrived_places = tagged[:, payload : payload + label_block : label_block // capacity]
    arrived_places = arrived_places.astype(jnp.int32).reshape(slot_count)
    kernel_first, kernel_second = assemble_weights(
        tagged[:, payload + label_block :], band_count, rows_local, channels
    )
    settle = arrived_places[None, :] == jnp.arange(slab_count, dtype=jnp.int32)[:, None]
    tile = jnp.dot(settle.astype(jnp.bfloat16), arrived, preferred_element_type=jnp.float32)
    tile = tile.astype(jnp.bfloat16).reshape(frames, band_rows, columns, channels)
    field = (frames, band_rows, columns, channels)
    tile_wide = tile.astype(jnp.float32)
    first = jax.nn.silu(tile_wide).astype(jnp.bfloat16)
    first_ext = with_halo(first, (("rows", 1),), 1)
    first_patches = forward_patches(first_ext)
    act = conv_out(first_patches, kernel_first, field).astype(jnp.bfloat16)
    second = jax.nn.silu(act.astype(jnp.float32)).astype(jnp.bfloat16)
    second_ext = with_halo(second, (("rows", 1),), 1)
    second_patches = forward_patches(second_ext)
    block_out = (tile_wide + conv_out(second_patches, kernel_second, field)).astype(jnp.bfloat16)
    live = (jnp.arange(frames, dtype=jnp.int32) < lengths[0])[:, None, None, None]
    out_grad = jnp.where(live, cot[0], jnp.zeros_like(cot[0]))
    out_grad_ext = with_halo(out_grad, (("rows", 1),), 1)
    weight_second = weight_grad_t(second_patches, out_grad)
    hidden_grad = data_grad(out_grad_ext, kernel_second)
    act_grad = (hidden_grad * silu_slope(act.astype(jnp.float32))).astype(jnp.bfloat16)
    act_grad_ext = with_halo(act_grad, (("rows", 1),), 1)
    weight_first = weight_grad_t(first_patches, act_grad)
    first_grad = data_grad(act_grad_ext, kernel_first)
    grad_input = (out_grad.astype(jnp.float32) + first_grad * silu_slope(tile_wide)).astype(
        jnp.bfloat16
    )
    scale = 1.0 / math.sqrt(frames * band_rows * columns * band_count * wide_size)
    grads = jnp.stack([weight_first, weight_second]) * scale
    share_first, share_second = reduce_weight_grads(grads, band_count, wide_size)
    return (block_out[None], grad_input[None], share_first, share_second)


def solution(mesh):

    return jax.shard_map(
        body,
        mesh=mesh,
        in_specs=(
            P("wide", "rows", None, None, None),
            P("wide", "rows", None),
            P("wide", "rows", None),
            P("wide"),
            P("wide", None, "rows", None, None),
            P("wide", None),
            P("wide", None),
        ),
        out_specs=(
            P("wide", None, "rows", None, None),
            P("wide", None, "rows", None, None),
            P("wide", None),
            P("wide", None),
        ),
        check_vma=False,
    )
```

time: 529 us -> 265 us (0.50)
  the two profiles are of different devices: /device:TPU:24 before, /device:TPU:1 now
where the time goes in v3:
time: 265 us; the launch traced here: 263 us
  local copies, waits for them, and re-layouts  93.3 us (35%)
  blocking collectives  56.3 us (21%)
  starting transfers between devices  46.3 us (17%)
  waiting for transfers between devices  25.9 us (10%)
  matrix products  17.4 us (7%)
  between operations  15.8 us (6%)
  other arithmetic  8.38 us (3%)
    unnamed x146, local copies, waits for them, and re-layouts  48.5 us
    all_to_all x1, blocking collectives, reduce_weight_grads(): wide_parts = lax.all_to_all(band_sum, 'wide', 0, 0, tiled=True)  28.2 us
    all_to_all x1, blocking collectives, reduce_weight_grads(): band_parts = lax.all_to_all(blocks, 'rows', 0, 0, tiled=True)  28 us
    all_gather x1, waiting for transfers between devices, assemble_weights(): full = lax.all_gather(block, 'rows', axis=1, tiled=True)  24.2 us
    slice x58, local copies, waits for them, and re-layouts, tap_patches(): padded[a:a + frames, b:b + rows, e:e + cols]  17.9 us
    ppermute x4, starting transfers between devices, with_halo(): lax.ppermute(lax.slice_in_dim(block, block.shape[dim] - width, None, axis...  14.3 us
    all_to_all x1, starting transfers between devices, body(): lax.all_to_all(tagged, 'wide', split_axis=0, concat_axis=0, tiled=True)  12.7 us
    ppermute x4, starting transfers between devices, with_halo(): lax.ppermute(lax.slice_in_dim(block, 0, width, axis=dim), axis, backward)  12.2 us
  transfers between devices with their start and end apart: 11, of which 2 were waited for; matrix products, arithmetic and copies ran while one was open for 34% of the time, Pallas kernels for 0%

profile of v3, /device:TPU:1, one launch (start us, length us, event | category | flops | bytes accessed | tf_op | source)
XLA Modules:
  0.0 263.4 jit_solution(7550578809233111152)
XLA Ops:
  7.8 1.0 bitcast_select_fusion
  8.8 4.5 %collective-permute-start.4 = (bf16[5,1,32,128]{3,2,1,0:T(8,128)(2,1)S(1)}, bf16[5,1,32,128]{3,2,1,0:T(8,128)(2,1)S(1)}, u32[]{:S(2)}, u32[]{:S(2)}) collective-permute-start(bf16[5,1,32,128]{3,2,1,0:T(8,128)(2,1)S(1)} %get-tuple-element.94), channel_id=1, source_target_pairs={{0,1},{1,2},{2,3},{3,4},{4,5},{5,6},{6,7},{8,9},{9,10},{10,11},{11... | collective-permute-start | bytes 122888 | tf_op jit(solution)/shard_map/ppermute | solution.py:14
  13.3 5.6 %collective-permute-start.5 = (bf16[5,1,32,128]{3,2,1,0:T(8,128)(2,1)S(1)}, bf16[5,1,32,128]{3,2,1,0:T(8,128)(2,1)S(1)}, u32[]{:S(2)}, u32[]{:S(2)}) collective-permute-start(bf16[5,1,32,128]{3,2,1,0:T(8,128)(2,1)S(1)} %get-tuple-element.95), channel_id=1, source_target_pairs={{1,0},{2,1},{3,2},{4,3},{5,4},{6,5},{7,6},{9,8},{10,9},{11,10},{12... | collective-permute-start | bytes 122888 | tf_op jit(solution)/shard_map/ppermute | solution.py:17
  18.9 0.9 convert_reduce_fusion.2
  20.5 0.9 pad.84
  22.6 0.8 fusion.85
  24.7 1.2 reduce.4
  25.8 1.1 reshape.235
  26.9 12.7 %all-to-all-start = ((bf16[64,2,2944]{2,1,0:T(2,128)(2,1)}), bf16[64,2,2944]{2,1,0:T(2,128)(2,1)S(1)}, u32[]{:S(2)}, u32[]{:S(2)}) async-start(bf16[64,2,2944]{2,1,0:T(2,128)(2,1)} %reshape.235), calls=%async_computation | async-start | bytes 1507328 | tf_op jit(solution)/shard_map/all_to_all | solution.py:144
  39.9 1.2 fusion.94
  42.4 0.9 slice.706
  43.8 0.9 slice.724
  51.6 0.7 constant_dynamic-update-slice_fusion.69
  53.6 0.7 constant_dynamic-update-slice_fusion.66
  63.3 4.7 %collective-permute-start = (bf16[5,1,32,128]{3,2,1,0:T(8,128)(2,1)S(1)}, bf16[5,1,32,128]{3,2,1,0:T(8,128)(2,1)S(1)}, u32[]{:S(2)}, u32[]{:S(2)}) collective-permute-start(bf16[5,1,32,128]{3,2,1,0:T(8,128)(2,1)S(1)} %get-tuple-element.98), channel_id=1, source_target_pairs={{0,1},{1,2},{2,3},{3,4},{4,5},{5,6},{6,7},{8,9},{9,10},{10,11},{11... | collective-permute-start | bytes 122888 | tf_op jit(solution)/shard_map/ppermute | solution.py:14
  68.1 2.1 collective-permute-start.1
  71.0 1.6 reshape.210
  72.8 1.3 reshape.211
  75.2 1.3 copy-done.2
  76.6 1.5 copy.236
  78.0 2.5 reshape.229
  80.6 24.2 %all-gather.2.cloned.1.call-done = bf16[2,128,3456]{2,1,0:T(8,128)(2,1)} async-done(((bf16[2,16,3456]{2,1,0:T(8,128)(2,1)}), bf16[2,128,3456]{2,1,0:T(8,128)(2,1)}) %all-gather.2.cloned.1.call-update) | async-done | bytes 1769488 | tf_op jit(solution)/shard_map/all_gather | solution.py:41
  104.8 1.6 fusion.91
  106.4 1.0 copy.265
  107.4 1.3 copy.266
  108.7 2.8 %convolution_bitcast_fusion.2 = f32[7,2,32,128]{3,2,1,0:T(8,128)S(1)} fusion(bf16[7,2,32,27,128]{4,2,3,1,0:T(8,128)(2,1)} %constant_dynamic-update-slice_fusion.54, bf16[128,27,128]{2,0,1:T(8,128)(2,1)S(1)} %copy.266), kind=kOutput, calls=%fused_computation.17 | convolution fusion | flops 396361728 | bytes 4210688 | tf_op jit(solution)/shard_map/dot_general | solution.py:105
  111.7 2.8 %fusion.42 = (bf16[5,2,32,128]{3,2,1,0:T(8,128)(2,1)S(1)}, bf16[5,2,32,128]{3,2,1,0:T(8,128)(2,1)S(1)}) fusion(f32[4,2,32,128]{3,2,1,0:T(8,128)S(1)} %slice.746, f32[1,2,32,128]{3,2,1,0:T(8,128)S(1)} %add_add_fusion, bf16[2,128,3456]{2,1,0:T(8,128)(2,1)} %all-gather.2.cloned.1.call-done, bf16[5,2,32,27,128]{4,2,1,0,3:T(8,128)(2,1)} %copy-done.2), kind=kOutput, calls=%fused_computation.196 | convolution fusion | flops 283688960 | bytes 3424256 | tf_op jit(solution)/shard_map/dot_general | solution.py:84
  115.1 0.8 copy.269
  115.8 1.9 collective-permute-start.6
  117.7 2.4 collective-permute-start.7
  120.8 3.1 %collective-permute-start.2 = (bf16[5,1,32,128]{3,2,1,0:T(8,128)(2,1)}, bf16[5,1,32,128]{3,2,1,0:T(8,128)(2,1)S(1)}, u32[]{:S(2)}, u32[]{:S(2)}) collective-permute-start(bf16[5,1,32,128]{3,2,1,0:T(8,128)(2,1)} %get-tuple-element.96), channel_id=1, source_target_pairs={{0,1},{1,2},{2,3},{3,4},{4,5},{5,6},{6,7},{8,9},{9,10},{10,11},{11... | collective-permute-start | bytes 122888 | tf_op jit(solution)/shard_map/ppermute | solution.py:14
  123.9 2.1 collective-permute-start.3
  126.1 2.8 %convolution_bitcast_fusion.1 = f32[1,8,16,3456]{3,2,1,0:T(8,128)} fusion(bf16[8,16,320]{2,1,0:T(8,128)(2,1)} %bitcast.523, bf16[320,3456,1]{1,0,2:T(8,128)(2,1)S(1)} %copy-done), kind=kOutput, calls=%fused_computation.1 | convolution fusion | flops 283115520 | bytes 4063232 | tf_op jit(solution)/shard_map/dot_general | solution.py:92
  128.9 1.0 copy.267
  129.8 1.3 copy.268
  131.2 0.9 select_maximum_fusion
  132.2 1.2 fusion.92
  138.8 0.9 slice.788
  139.8 0.9 slice.790
  140.7 0.9 slice.792
  141.6 0.9 slice.794
  142.6 0.9 slice.796
  143.5 0.9 slice.798
  144.4 0.9 slice.800
  145.4 0.9 slice.802
  146.3 1.5 constant_dynamic-update-slice_fusion.106
  147.9 1.5 constant_dynamic-update-slice_fusion.105
  149.4 1.6 constant_dynamic-update-slice_fusion.104
  151.0 1.6 constant_dynamic-update-slice_fusion.103
  152.5 1.6 constant_dynamic-update-slice_fusion.102
  154.7 1.5 constant_dynamic-update-slice_fusion.100
  168.7 2.9 %fusion.2 = f32[7,2,32,128,1]{3,2,0,1,4:T(8,128)S(1)} fusion(bf16[7,2,32,27,128]{4,2,1,0,3:T(8,128)(2,1)} %constant_dynamic-update-slice_fusion.81, bf16[128,27,128]{2,0,1:T(8,128)(2,1)S(1)} %copy.268), kind=kOutput, calls=%fused_computation.8 | convolution fusion | flops 396361728 | bytes 4210688 | tf_op jit(solution)/shard_map/dot_general | solution.py:105
  171.7 0.7 fusion.44
  173.6 1.4 copy-done.3
  175.0 1.5 copy.238
  176.4 2.5 reshape.230
  179.0 2.4 convolution_bitcast_fusion
  181.8 28.0 %all_to_all.33 = bf16[8,2,16,3456]{3,2,1,0:T(8,128)(2,1)S(1)} all-to-all(bf16[8,2,16,3456]{3,2,1,0:T(8,128)(2,1)S(1)} %copy.273), channel_id=1, replica_groups=mesh['wide'=64,'rows'=8] {'rows'}, dimensions={0} | all-to-all | bytes 3538944 | tf_op jit(solution)/shard_map/all_to_all | solution.py:51
  210.1 1.4 reshape.217
  212.2 1.5 all_to_all.28
  213.7 28.2 %all_to_all.34 = f32[64,1,1728]{2,1,0:T(1,128)S(1)} all-to-all(f32[64,1,1728]{2,1,0:T(1,128)S(1)} %all_to_all.28), channel_id=1, replica_groups=mesh['wide'=64,'rows'=8] {'wide'}, dimensions={0} | all-to-all | bytes 884736 | tf_op jit(solution)/shard_map/all_to_all | solution.py:55
  242.9 7.1 %all-to-all-start.3 = ((f32[8,1,1728]{2,1,0:T(1,128)}), f32[8,1,1728]{2,1,0:T(1,128)S(1)}, u32[]{:S(2)}, u32[]{:S(2)}) async-start(f32[8,1,1728]{2,1,0:T(1,128)} %broadcast_in_dim.62), calls=%async_computation.3 | async-start | bytes 114688 | tf_op jit(solution)/shard_map/all_to_all | solution.py:57
  250.0 3.2 %fusion.23 = bf16[1,5,2,32,128]{4,3,2,1,0:T(8,128)(2,1)} fusion(f32[5,2,32,128]{3,2,1,0:T(8,128)S(1)} %bitcast.511, bf16[2,128,3456]{2,1,0:T(8,128)(2,1)} %all-gather.2.cloned.1.call-done, bf16[5,2,32,27,128]{4,2,1,0,3:T(8,128)(2,1)} %copy-done.3), kind=kOutput, calls=%fused_computation.22 | convolution fusion | flops 283197440 | bytes 3342336 | tf_op jit(solution)/shard_map/dot_general | solution.py:84
  253.2 1.6 all-to-all-done.3
  (253 shorter events, 48.9 us)
Async XLA Ops:
  7.8 14.8 %copy-start.17 = (pred[5]{0:T(512)(128)(4,1)}, pred[5]{0:T(512)(128)(4,1)S(1)}, u32[]{:S(2)}) copy-start(pred[5]{0:T(512)(128)(4,1)S(1)} %iota_compare_fusion.9) | copy-start | bytes 19
  8.8 30.8 %collective-permute-start.4 = (bf16[5,1,32,128]{3,2,1,0:T(8,128)(2,1)S(1)}, bf16[5,1,32,128]{3,2,1,0:T(8,128)(2,1)S(1)}, u32[]{:S(2)}, u32[]{:S(2)}) collective-permute-start(bf16[5,1,32,128]{3,2,1,0:T(8,128)(2,1)S(1)} %get-tuple-element.94), channel_id=1, source_target_pairs={{0,1},{1,2},{2,3},{3,4},{4,5},{5,6},{6,7},{8,9},{9,10},{10,11},{11... | collective-permute-start | bytes 122888 | tf_op jit(solution)/shard_map/ppermute | solution.py:14
  13.3 26.3 %collective-permute-start.5 = (bf16[5,1,32,128]{3,2,1,0:T(8,128)(2,1)S(1)}, bf16[5,1,32,128]{3,2,1,0:T(8,128)(2,1)S(1)}, u32[]{:S(2)}, u32[]{:S(2)}) collective-permute-start(bf16[5,1,32,128]{3,2,1,0:T(8,128)(2,1)S(1)} %get-tuple-element.95), channel_id=1, source_target_pairs={{1,0},{2,1},{3,2},{4,3},{5,4},{6,5},{7,6},{9,8},{10,9},{11,10},{12... | collective-permute-start | bytes 122888 | tf_op jit(solution)/shard_map/ppermute | solution.py:17
  26.9 35.3 %all-to-all-start = ((bf16[64,2,2944]{2,1,0:T(2,128)(2,1)}), bf16[64,2,2944]{2,1,0:T(2,128)(2,1)S(1)}, u32[]{:S(2)}, u32[]{:S(2)}) async-start(bf16[64,2,2944]{2,1,0:T(2,128)(2,1)} %reshape.235), calls=%async_computation | async-start | bytes 1507328 | tf_op jit(solution)/shard_map/all_to_all | solution.py:144
  39.6 65.2 %all-gather.2.cloned.1.call-start = ((), (), s32[]{:S(2)}) async-start(), calls=%async_computation.4 | async-start | bytes 1990656 | tf_op jit(solution)/shard_map/all_gather | solution.py:41
  41.2 2.1 copy-start.15
  41.9 1.5 copy-start.14
  42.0 1.5 copy-start.13
  42.0 1.5 copy-start.12
  42.1 1.5 copy-start.11
  42.2 1.5 copy-start.10
  42.2 1.5 copy-start.8
  42.3 1.5 copy-start.6
  45.4 12.3 %copy-start.4 = (bf16[7,2,32,128]{3,2,1,0:T(8,128)(2,1)S(1)}, bf16[7,2,32,128]{3,2,1,0:T(8,128)(2,1)}, u32[]{:S(2)}) copy-start(bf16[7,2,32,128]{3,2,1,0:T(8,128)(2,1)} %get-tuple-element.60) | copy-start | bytes 344068
  46.1 11.6 %copy-start.5 = (bf16[7,2,32,128]{3,2,1,0:T(8,128)(2,1)S(1)}, bf16[7,2,32,128]{3,2,1,0:T(8,128)(2,1)}, u32[]{:S(2)}) copy-start(bf16[7,2,32,128]{3,2,1,0:T(8,128)(2,1)} %get-tuple-element.61) | copy-start | bytes 344068
  63.3 10.8 %collective-permute-start = (bf16[5,1,32,128]{3,2,1,0:T(8,128)(2,1)S(1)}, bf16[5,1,32,128]{3,2,1,0:T(8,128)(2,1)S(1)}, u32[]{:S(2)}, u32[]{:S(2)}) collective-permute-start(bf16[5,1,32,128]{3,2,1,0:T(8,128)(2,1)S(1)} %get-tuple-element.98), channel_id=1, source_target_pairs={{0,1},{1,2},{2,3},{3,4},{4,5},{5,6},{6,7},{8,9},{9,10},{10,11},{11... | collective-permute-start | bytes 122888 | tf_op jit(solution)/shard_map/ppermute | solution.py:14
  68.1 6.1 %collective-permute-start.1 = (bf16[5,1,32,128]{3,2,1,0:T(8,128)(2,1)S(1)}, bf16[5,1,32,128]{3,2,1,0:T(8,128)(2,1)S(1)}, u32[]{:S(2)}, u32[]{:S(2)}) collective-permute-start(bf16[5,1,32,128]{3,2,1,0:T(8,128)(2,1)S(1)} %get-tuple-element.99), channel_id=1, source_target_pairs={{1,0},{2,1},{3,2},{4,3},{5,4},{6,5},{7,6},{9,8},{10,9},{11,10},{12... | collective-permute-start | bytes 122888 | tf_op jit(solution)/shard_map/ppermute | solution.py:17
  75.2 1.4 copy-start.2
  111.7 14.4 %copy-start = (bf16[320,3456,1]{1,0,2:T(8,128)(2,1)S(1)}, bf16[320,3456,1]{1,0,2:T(8,128)(2,1)}, u32[]{:S(2)}) copy-start(bf16[320,3456,1]{1,0,2:T(8,128)(2,1)} %reshape.229) | copy-start | bytes 6635524
  115.8 15.3 %collective-permute-start.6 = (bf16[5,1,32,128]{3,2,1,0:T(8,128)(2,1)}, bf16[5,1,32,128]{3,2,1,0:T(8,128)(2,1)S(1)}, u32[]{:S(2)}, u32[]{:S(2)}) collective-permute-start(bf16[5,1,32,128]{3,2,1,0:T(8,128)(2,1)} %get-tuple-element.92), channel_id=1, source_target_pairs={{0,1},{1,2},{2,3},{3,4},{4,5},{5,6},{6,7},{8,9},{9,10},{10,11},{11... | collective-permute-start | bytes 122888 | tf_op jit(solution)/shard_map/ppermute | solution.py:14
  117.7 13.4 %collective-permute-start.7 = (bf16[5,1,32,128]{3,2,1,0:T(8,128)(2,1)}, bf16[5,1,32,128]{3,2,1,0:T(8,128)(2,1)}, u32[]{:S(2)}, u32[]{:S(2)}) collective-permute-start(bf16[5,1,32,128]{3,2,1,0:T(8,128)(2,1)} %get-tuple-element.93), channel_id=1, source_target_pairs={{1,0},{2,1},{3,2},{4,3},{5,4},{6,5},{7,6},{9,8},{10,9},{11,10},{12... | collective-permute-start | bytes 122888 | tf_op jit(solution)/shard_map/ppermute | solution.py:17
  120.8 51.8 %collective-permute-start.2 = (bf16[5,1,32,128]{3,2,1,0:T(8,128)(2,1)}, bf16[5,1,32,128]{3,2,1,0:T(8,128)(2,1)S(1)}, u32[]{:S(2)}, u32[]{:S(2)}) collective-permute-start(bf16[5,1,32,128]{3,2,1,0:T(8,128)(2,1)} %get-tuple-element.96), channel_id=1, source_target_pairs={{0,1},{1,2},{2,3},{3,4},{4,5},{5,6},{6,7},{8,9},{9,10},{10,11},{11... | collective-permute-start | bytes 122888 | tf_op jit(solution)/shard_map/ppermute | solution.py:14
  123.9 48.7 %collective-permute-start.3 = (bf16[5,1,32,128]{3,2,1,0:T(8,128)(2,1)}, bf16[5,1,32,128]{3,2,1,0:T(8,128)(2,1)S(1)}, u32[]{:S(2)}, u32[]{:S(2)}) collective-permute-start(bf16[5,1,32,128]{3,2,1,0:T(8,128)(2,1)} %get-tuple-element.97), channel_id=1, source_target_pairs={{1,0},{2,1},{3,2},{4,3},{5,4},{6,5},{7,6},{9,8},{10,9},{11,10},{12... | collective-permute-start | bytes 122888 | tf_op jit(solution)/shard_map/ppermute | solution.py:17
  133.5 5.3 %copy-start.7 = (bf16[7,2,32,128]{3,2,1,0:T(8,128)(2,1)S(1)}, bf16[7,2,32,128]{3,2,1,0:T(8,128)(2,1)}, u32[]{:S(2)}) copy-start(bf16[7,2,32,128]{3,2,1,0:T(8,128)(2,1)} %get-tuple-element.36) | copy-start | bytes 344068
  134.1 4.6 %copy-start.9 = (bf16[7,2,32,128]{3,2,1,0:T(8,128)(2,1)S(1)}, bf16[7,2,32,128]{3,2,1,0:T(8,128)(2,1)}, u32[]{:S(2)}) copy-start(bf16[7,2,32,128]{3,2,1,0:T(8,128)(2,1)} %get-tuple-element.37) | copy-start | bytes 344068
  168.7 3.0 %copy-start.16 = (bf16[1,5,2,32,128]{4,3,2,1,0:T(8,128)(2,1)S(1)}, bf16[1,5,2,32,128]{4,3,2,1,0:T(8,128)(2,1)}, u32[]{:S(2)}) copy-start(bf16[1,5,2,32,128]{4,3,2,1,0:T(8,128)(2,1)} %param.11) | copy-start | bytes 245764
  168.7 3.0 %copy-start.18 = (pred[5]{0:T(512)(128)(4,1)S(1)}, pred[5]{0:T(512)(128)(4,1)}, u32[]{:S(2)}) copy-start(pred[5]{0:T(512)(128)(4,1)} %copy-done.17) | copy-start | bytes 19
  173.6 1.4 copy-start.3
  179.0 2.4 copy-start.1
  242.9 11.9 %all-to-all-start.3 = ((f32[8,1,1728]{2,1,0:T(1,128)}), f32[8,1,1728]{2,1,0:T(1,128)S(1)}, u32[]{:S(2)}, u32[]{:S(2)}) async-start(f32[8,1,1728]{2,1,0:T(1,128)} %broadcast_in_dim.62), calls=%async_computation.3 | async-start | bytes 114688 | tf_op jit(solution)/shard_map/all_to_all | solution.py:57
Sparse Core Ops, SparseCore 0:
  74.3 30.4 all-gather.1

commit v4 on v3

--- a/solution.py
+++ b/solution.py
@@ -62,48 +62,34 @@
     return joined[0], joined[1]
 
 
-def tap_patches(padded, frames, rows, cols):
-    taps = [
-        padded[a : a + frames, b : b + rows, e : e + cols]
-        for a in range(3)
-        for b in range(3)
-        for e in range(3)
-    ]
-    stacked = jnp.stack(taps, axis=3)
-    return stacked.reshape(frames * rows * cols, 27 * padded.shape[-1])
+def conv_forward_t(extended, kernel_t):
+    cout = kernel_t.shape[0]
+    kernel = kernel_t.reshape(cout, 3, 3, 3, -1)
+    padded = jnp.concatenate([extended[:1], extended[:1], extended], axis=0)
+    result = lax.conv_general_dilated(
+        padded[None], kernel, (1, 1, 1), ((0, 0), (0, 0), (1, 1)),
+        dimension_numbers=("NDHWC", "ODHWI", "NDHWC"), preferred_element_type=jnp.float32,
+    )
+    return result[0]
 
 
-def forward_patches(extended):
-    frames, rows_ext, cols, _ = extended.shape
+def conv_weight_grad_t(extended, upstream):
     padded = jnp.concatenate([extended[:1], extended[:1], extended], axis=0)
-    padded = jnp.pad(padded, ((0, 0), (0, 0), (1, 1), (0, 0)))
-    return tap_patches(padded, frames, rows_ext - 2, cols)
+    result = lax.conv_general_dilated(
+        padded[None], upstream[None], (1, 1, 1), ((0, 0), (0, 0), (1, 1)),
+        dimension_numbers=("CDHWN", "IDHWO", "CDHWN"), preferred_element_type=jnp.float32,
+    )
+    return result.reshape(upstream.shape[-1], -1)
 
 
-def conv_out(patches, kernel_t, shape):
-    result = lax.dot_general(
-        patches, kernel_t, (((1,), (1,)), ((), ())), preferred_element_type=jnp.float32
-    )
-    return result.reshape(shape)
-
-
-def weight_grad_t(patches, upstream):
-    flat = upstream.reshape(-1, upstream.shape[-1])
-    return lax.dot_general(
-        flat, patches, (((0,), (0,)), ((), ())), preferred_element_type=jnp.float32
-    )
-
-
-def data_grad(upstream_ext, kernel_t):
-    frames, rows_ext, cols, _ = upstream_ext.shape
-    rows = rows_ext - 2
-    padded = jnp.pad(upstream_ext, ((2, 2), (0, 0), (1, 1), (0, 0)))
-    padded = padded[::-1, ::-1, ::-1]
-    patches = tap_patches(padded, frames + 2, rows, cols)
+def conv_data_grad_t(upstream_ext, kernel_t):
     cout = kernel_t.shape[0]
-    regrouped = kernel_t.reshape(cout, 27, -1).transpose(1, 0, 2).reshape(27 * cout, -1)
-    result = jnp.dot(patches, regrouped, preferred_element_type=jnp.float32)
-    result = result.reshape(frames + 2, rows, cols, -1)[::-1, ::-1, ::-1]
+    kernel = kernel_t.reshape(cout, 3, 3, 3, -1)[:, ::-1, ::-1, ::-1, :]
+    padded = jnp.pad(upstream_ext, ((2, 2), (0, 0), (0, 0), (0, 0)))
+    result = lax.conv_general_dilated(
+        padded[None], kernel, (1, 1, 1), ((0, 0), (0, 0), (1, 1)),
+        dimension_numbers=("NDHWC", "IDHWO", "NDHWC"), preferred_element_type=jnp.float32,
+    )[0]
     head = (result[0] + result[1] + result[2])[None]
     return jnp.concatenate([head, result[3:]], axis=0)
 
@@ -131,46 +117,39 @@
     outgoing = outgoing.astype(jnp.bfloat16).reshape(wide_size, capacity * columns * channels)
     labels = jnp.sum(jnp.where(placing, places[None, :] + 1, 0), axis=1) - 1
     labels = labels.reshape(wide_size, capacity).astype(jnp.bfloat16)
-    label_block = 64
+    label_block = 128
     pieces = weight_pieces(w_first, w_second, band_count)
+    pieces = lax.all_to_all(
+        jnp.broadcast_to(pieces[None], (wide_size, pieces.shape[0])), "wide", 0, 0, tiled=True
+    )
+    kernel_first, kernel_second = assemble_weights(pieces, band_count, rows_local, channels)
     tagged = jnp.concatenate(
-        [
-            outgoing,
-            jnp.repeat(labels, label_block // capacity, axis=1),
-            jnp.broadcast_to(pieces[None], (wide_size, pieces.shape[0])),
-        ],
-        axis=1,
+        [outgoing, jnp.repeat(labels, label_block // capacity, axis=1)], axis=1
     )
     tagged = lax.all_to_all(tagged, "wide", split_axis=0, concat_axis=0, tiled=True)
     payload = capacity * columns * channels
     arrived = tagged[:, :payload].reshape(slot_count, columns * channels)
     arrived_places = tagged[:, payload : payload + label_block : label_block // capacity]
     arrived_places = arrived_places.astype(jnp.int32).reshape(slot_count)
-    kernel_first, kernel_second = assemble_weights(
-        tagged[:, payload + label_block :], band_count, rows_local, channels
-    )
     settle = arrived_places[None, :] == jnp.arange(slab_count, dtype=jnp.int32)[:, None]
     tile = jnp.dot(settle.astype(jnp.bfloat16), arrived, preferred_element_type=jnp.float32)
     tile = tile.astype(jnp.bfloat16).reshape(frames, band_rows, columns, channels)
-    field = (frames, band_rows, columns, channels)
     tile_wide = tile.astype(jnp.float32)
     first = jax.nn.silu(tile_wide).astype(jnp.bfloat16)
     first_ext = with_halo(first, (("rows", 1),), 1)
-    first_patches = forward_patches(first_ext)
-    act = conv_out(first_patches, kernel_first, field).astype(jnp.bfloat16)
+    act = conv_forward_t(first_ext, kernel_first).astype(jnp.bfloat16)
     second = jax.nn.silu(act.astype(jnp.float32)).astype(jnp.bfloat16)
     second_ext = with_halo(second, (("rows", 1),), 1)
-    second_patches = forward_patches(second_ext)
-    block_out = (tile_wide + conv_out(second_patches, kernel_second, field)).astype(jnp.bfloat16)
+    block_out = (tile_wide + conv_forward_t(second_ext, kernel_second)).astype(jnp.bfloat16)
     live = (jnp.arange(frames, dtype=jnp.int32) < lengths[0])[:, None, None, None]
     out_grad = jnp.where(live, cot[0], jnp.zeros_like(cot[0]))
     out_grad_ext = with_halo(out_grad, (("rows", 1),), 1)
-    weight_second = weight_grad_t(second_patches, out_grad)
-    hidden_grad = data_grad(out_grad_ext, kernel_second)
+    weight_second = conv_weight_grad_t(second_ext, out_grad)
+    hidden_grad = conv_data_grad_t(out_grad_ext, kernel_second)
     act_grad = (hidden_grad * silu_slope(act.astype(jnp.float32))).astype(jnp.bfloat16)
     act_grad_ext = with_halo(act_grad, (("rows", 1),), 1)
-    weight_first = weight_grad_t(first_patches, act_grad)
-    first_grad = data_grad(act_grad_ext, kernel_first)
+    weight_first = conv_weight_grad_t(first_ext, act_grad)
+    first_grad = conv_data_grad_t(act_grad_ext, kernel_first)
     grad_input = (out_grad.astype(jnp.float32) + first_grad * silu_slope(tile_wide)).astype(
         jnp.bfloat16
     )

time: 265 us -> 205 us (0.77)
  local copies, waits for them, and re-layouts: 93.3 us -> 31.2 us
  other arithmetic: 8.38 us -> 13 us
  matrix products: 17.4 us -> 13.3 us
  starting transfers between devices: 46.3 us -> 49.8 us
  waiting for transfers between devices: 25.9 us -> 22.6 us
  blocking collectives: 56.3 us -> 59 us
    unnamed x146 -> x45, local copies, waits for them, and re-layouts: 48.5 us -> 6.64 us
    all_gather x1, waiting for transfers between devices: 24.2 us -> 0.01 us  [assemble_weights(): full = lax.all_gather(block, 'rows', axis=1, tiled=True)]
    slice x71 -> x0, local copies, waits for them, and re-layouts: 18.2 us -> none  [the longest x58 17.9 us: tap_patches(): padded[a:a + frames, b:b + rows, e:e + cols]]
    dot_general x6 -> x0, matrix products: 16.8 us -> none  [the longest x2 5.97 us: conv_out(): lax.dot_general(patches, kernel_t, (((1,), (1,)), ((), ())), preferred_el...]
    conv_general_dilated x0 -> x6, matrix products: none -> 12.7 us  [the longest x2 7.41 us: conv_weight_grad_t(): lax.conv_general_dilated(padded[None], upstream[None], (1, 1, 1), ((0, 0)...]
    all_to_all x0 -> x1, blocking collectives: none -> 11 us  [reduce_weight_grads(): lax.all_to_all(jnp.broadcast_to(share, (band_count,) + share.shape[1:]),...]
    all_to_all x1, waiting for transfers between devices: 1.62 us -> 11.9 us  [body(): lax.all_to_all(jnp.broadcast_to(pieces[None], (wide_size, pieces.shape[0]...]
    all_to_all x1, starting transfers between devices: 7.07 us -> 17.1 us  [body(): lax.all_to_all(jnp.broadcast_to(pieces[None], (wide_size, pieces.shape[0]...]
  transfers between devices with their start and end apart: 11 -> 11, of which waited for: 2 -> 3; matrix products, arithmetic and copies ran while one was open for 34% -> 9% of each run, Pallas kernels for 0% -> 0%
where the time goes in v4:
time: 205 us; the launch traced here: 204 us
  blocking collectives  59 us (29%)
  starting transfers between devices  49.8 us (24%)
  local copies, waits for them, and re-layouts  31.2 us (15%)
  waiting for transfers between devices  22.6 us (11%)
  between operations  15.6 us (8%)
  matrix products  13.3 us (6%)
  other arithmetic  13 us (6%)
    all_to_all x1, blocking collectives, reduce_weight_grads(): band_parts = lax.all_to_all(blocks, 'rows', 0, 0, tiled=True)  27.7 us
    all_to_all x1, blocking collectives, reduce_weight_grads(): wide_parts = lax.all_to_all(band_sum, 'wide', 0, 0, tiled=True)  20.2 us
    ppermute x4, starting transfers between devices, with_halo(): lax.ppermute(lax.slice_in_dim(block, block.shape[dim] - width, None, axis...  18.2 us
    all_to_all x1, starting transfers between devices, body(): lax.all_to_all(jnp.broadcast_to(pieces[None], (wide_size, pieces.shape[0]...  17.1 us
    all_to_all x1, waiting for transfers between devices, body(): lax.all_to_all(jnp.broadcast_to(pieces[None], (wide_size, pieces.shape[0]...  11.9 us
    all_to_all x1, blocking collectives, reduce_weight_grads(): lax.all_to_all(jnp.broadcast_to(share, (band_count,) + share.shape[1:]),...  11 us
    ppermute x4, starting transfers between devices, with_halo(): lax.ppermute(lax.slice_in_dim(block, 0, width, axis=dim), axis, backward)  8.94 us
    all_to_all x1, waiting for transfers between devices, body(): lax.all_to_all(tagged, 'wide', split_axis=0, concat_axis=0, tiled=True)  7.9 us
  transfers between devices with their start and end apart: 11, of which 3 were waited for; matrix products, arithmetic and copies ran while one was open for 9% of the time, Pallas kernels for 0%

profile of v4, /device:TPU:1, one launch (start us, length us, event | category | flops | bytes accessed | tf_op | source)
XLA Modules:
  0.0 204.5 jit_solution(7063115184698829981)
XLA Ops:
  7.2 0.8 fusion.65
  8.2 0.2 broadcast_in_dim.71
  8.5 0.5 broadcast.165
  9.0 2.0 %reduce.5 = bf16[64,1728]{1,0:T(8,128)(2,1)S(1)} reduce(bf16[64,1,1728]{2,1,0:T(2,128)(2,1)S(1)} %broadcast_in_dim.71, bf16[]{:T(256)} %broadcast.165), dimensions={1}, to_apply=%broadcast_in_dim.71.reduce_sub_computation | reduce | bytes 442370 | tf_op jit(solution)/shard_map/broadcast_in_dim | solution.py:123
  11.0 0.9 reshape.291
  12.0 17.1 %all-to-all-start.1 = ((bf16[64,2,864]{2,1,0:T(2,128)(2,1)}), bf16[64,2,864]{2,1,0:T(2,128)(2,1)S(1)}, u32[]{:S(2)}, u32[]{:S(2)}) async-start(bf16[64,2,864]{2,1,0:T(2,128)(2,1)} %reshape.291), calls=%async_computation.1 | async-start | bytes 458752 | tf_op jit(solution)/shard_map/all_to_all | solution.py:122
  29.2 0.2 convert_reduce_fusion.2
  29.5 11.9 %all-to-all-done.1 = bf16[64,2,864]{2,1,0:T(2,128)(2,1)S(1)} async-done(((bf16[64,2,864]{2,1,0:T(2,128)(2,1)}), bf16[64,2,864]{2,1,0:T(2,128)(2,1)S(1)}, u32[]{:S(2)}, u32[]{:S(2)}) %all-to-all-start.1) | async-done | bytes 221216 | tf_op jit(solution)/shard_map/all_to_all | solution.py:122
  41.4 0.3 reshape.292
  41.7 1.4 reduce.2
  43.2 1.6 reshape.210
  44.7 0.2 copy.225
  45.0 1.3 reshape.211
  46.4 0.4 convolution_convert_fusion
  47.0 1.0 reduce.6
  48.0 1.2 reshape.289
  49.2 5.5 %all-to-all-start = ((bf16[64,2,2112]{2,1,0:T(2,128)(2,1)}), bf16[64,2,2112]{2,1,0:T(2,128)(2,1)S(1)}, u32[]{:S(2)}, u32[]{:S(2)}) async-start(bf16[64,2,2112]{2,1,0:T(2,128)(2,1)} %reshape.289), calls=%async_computation | async-start | bytes 1114112 | tf_op jit(solution)/shard_map/all_to_all | solution.py:129
  55.4 5.1 %collective-permute-start.4 = (bf16[5,1,32,128]{3,2,1,0:T(8,128)(2,1)S(1)}, bf16[5,1,32,128]{3,2,1,0:T(8,128)(2,1)S(1)}, u32[]{:S(2)}, u32[]{:S(2)}) collective-permute-start(bf16[5,1,32,128]{3,2,1,0:T(8,128)(2,1)S(1)} %get-tuple-element.45), channel_id=1, source_target_pairs={{0,1},{1,2},{2,3},{3,4},{4,5},{5,6},{6,7},{8,9},{9,10},{10,11},{11... | collective-permute-start | bytes 122888 | tf_op jit(solution)/shard_map/ppermute | solution.py:14
  60.6 1.9 collective-permute-start.5
  62.5 7.9 %all-to-all-done = bf16[64,2,2112]{2,1,0:T(2,128)(2,1)S(1)} async-done(((bf16[64,2,2112]{2,1,0:T(2,128)(2,1)}), bf16[64,2,2112]{2,1,0:T(2,128)(2,1)S(1)}, u32[]{:S(2)}, u32[]{:S(2)}) %all-to-all-start) | async-done | bytes 540704 | tf_op jit(solution)/shard_map/all_to_all | solution.py:129
  70.4 0.6 reshape.290
  71.2 0.2 fusion
  71.6 8.6 %collective-permute-start = (bf16[5,1,32,128]{3,2,1,0:T(8,128)(2,1)S(1)}, bf16[5,1,32,128]{3,2,1,0:T(8,128)(2,1)S(1)}, u32[]{:S(2)}, u32[]{:S(2)}) collective-permute-start(bf16[5,1,32,128]{3,2,1,0:T(8,128)(2,1)S(1)} %get-tuple-element.49), channel_id=1, source_target_pairs={{0,1},{1,2},{2,3},{3,4},{4,5},{5,6},{6,7},{8,9},{9,10},{10,11},{11... | collective-permute-start | bytes 122888 | tf_op jit(solution)/shard_map/ppermute | solution.py:14
  80.1 2.1 %collective-permute-start.1 = (bf16[5,1,32,128]{3,2,1,0:T(8,128)(2,1)S(1)}, bf16[5,1,32,128]{3,2,1,0:T(8,128)(2,1)S(1)}, u32[]{:S(2)}, u32[]{:S(2)}) collective-permute-start(bf16[5,1,32,128]{3,2,1,0:T(8,128)(2,1)S(1)} %get-tuple-element.50), channel_id=1, source_target_pairs={{1,0},{2,1},{3,2},{4,3},{5,4},{6,5},{7,6},{9,8},{10,9},{11,10},{12... | collective-permute-start | bytes 122888 | tf_op jit(solution)/shard_map/ppermute | solution.py:17
  82.7 2.7 %collective-permute-done.1 = bf16[5,1,32,128]{3,2,1,0:T(8,128)(2,1)S(1)} collective-permute-done((bf16[5,1,32,128]{3,2,1,0:T(8,128)(2,1)S(1)}, bf16[5,1,32,128]{3,2,1,0:T(8,128)(2,1)S(1)}, u32[]{:S(2)}, u32[]{:S(2)}) %collective-permute-start.1) | collective-permute-done | bytes 40992 | tf_op jit(solution)/shard_map/ppermute | solution.py:17
  85.5 0.7 fusion.72
  86.5 0.7 copy-done.4
  87.2 0.7 slice.139
  87.9 1.6 fusion.85
  89.5 1.0 copy.232
  90.5 1.2 convolution_select_fusion.1
  91.7 0.7 copy-done.3
  92.4 1.0 copy.226
  93.4 2.1 %fusion.47 = (f32[5,2,8,5,128]{4,2,3,1,0:T(8,128)S(1)}, bf16[5,2,8,5,128]{4,2,3,1,0:T(8,128)(2,1)S(1)}) fusion(bf16[128,3,3,3,128]{0,4,3,2,1:T(8,128)(2,1)S(1)} %bitcast.132, bf16[7,4,1,7,2,128]{5,3,4,1,0,2:T(8,128)(2,1)} %slice.139, bf16[7,4,1,8,5,128]{5,3,4,1,0,2:T(8,128)(2,1)S(1)} %copy-done.5, pred[8,5]{0,1:T(8,128)(4,1)S(1)} %copy-done.12), kind=kOutput, calls=%fused_computation.68 | convolution fusion | flops 355610624 | bytes 1579048 | tf_op jit(solution)/shard_map/conv_general_dilated | solution.py:69
  96.1 0.7 fusion.87
  96.7 1.9 collective-permute-start.6
  98.6 3.0 %collective-permute-start.7 = (bf16[5,1,32,128]{3,2,1,0:T(8,128)(2,1)}, bf16[5,1,32,128]{3,2,1,0:T(8,128)(2,1)}, u32[]{:S(2)}, u32[]{:S(2)}) collective-permute-start(bf16[5,1,32,128]{3,2,1,0:T(8,128)(2,1)} %get-tuple-element.42), channel_id=1, source_target_pairs={{1,0},{2,1},{3,2},{4,3},{5,4},{6,5},{7,6},{9,8},{10,9},{11,10},{12... | collective-permute-start | bytes 122888 | tf_op jit(solution)/shard_map/ppermute | solution.py:17
  101.7 0.6 fusion.89
  102.3 2.6 %collective-permute-start.2 = (bf16[5,1,32,128]{3,2,1,0:T(8,128)(2,1)}, bf16[5,1,32,128]{3,2,1,0:T(8,128)(2,1)S(1)}, u32[]{:S(2)}, u32[]{:S(2)}) collective-permute-start(bf16[5,1,32,128]{3,2,1,0:T(8,128)(2,1)} %get-tuple-element.47), channel_id=1, source_target_pairs={{0,1},{1,2},{2,3},{3,4},{4,5},{5,6},{6,7},{8,9},{9,10},{10,11},{11... | collective-permute-start | bytes 122888 | tf_op jit(solution)/shard_map/ppermute | solution.py:14
  104.8 1.9 collective-permute-start.3
  106.8 3.7 %fusion.24 = f32[128,3,3,3,128]{0,4,3,2,1:T(8,128)} fusion(bf16[1,7,4,32,128]{4,3,2,1,0:T(8,128)(2,1)S(1)} %copy-done.8, bf16[1,5,2,32,128]{4,3,2,1,0:T(8,128)(2,1)S(1)} %fusion.60), kind=kOutput, calls=%fused_computation.36 | convolution fusion | flops 277217280 | bytes 2080768 | tf_op jit(solution)/shard_map/conv_general_dilated | solution.py:78
  110.5 2.8 %copy.253 = f32[128,3,3,3,128]{4,3,2,1,0:T(4,128)S(1)} copy(f32[128,3,3,3,128]{0,4,3,2,1:T(8,128)} %fusion.24) | data formatting | bytes 3538944 | tf_op jit(solution)/shard_map/conv_general_dilated | solution.py:78
  113.3 2.0 stack.19
  115.3 1.0 fusion.38
  116.7 1.2 convolution_select_fusion
  118.2 0.7 pad_maximum_fusion
  118.9 0.8 fusion.70
  120.0 0.9 convolution_select_fusion.2
  121.1 0.7 fusion.59
  121.8 3.7 %fusion.22 = f32[128,3,3,3,128]{0,4,3,2,1:T(8,128)} fusion(bf16[1,7,4,32,128]{4,3,2,1,0:T(8,128)(2,1)S(1)} %get-tuple-element.34, bf16[1,5,2,32,128]{4,3,2,1,0:T(8,128)(2,1)S(1)} %get-tuple-element.29), kind=kOutput, calls=%fused_computation.34 | convolution fusion | flops 277217280 | bytes 2080768 | tf_op jit(solution)/shard_map/conv_general_dilated | solution.py:78
  125.5 2.8 %copy.256 = f32[128,3,3,3,128]{4,3,2,1,0:T(4,128)S(1)} copy(f32[128,3,3,3,128]{0,4,3,2,1:T(8,128)} %fusion.22) | data formatting | bytes 3538944 | tf_op jit(solution)/shard_map/conv_general_dilated | solution.py:78
  128.4 1.9 stack.20
  130.3 2.3 %fusion.2 = bf16[8,2,16,3456]{3,2,0,1:T(8,128)(2,1)S(1)} fusion(f32[1,8,16,3456]{3,2,1,0:T(8,128)} %stack.20, f32[1,8,16,3456]{3,2,1,0:T(8,128)} %stack.19), kind=kLoop, calls=%fused_computation.6 | loop fusion | flops 2654208 | bytes 5308416 | tf_op jit(solution)/shard_map/transpose | solution.py:50
  132.7 27.7 %all_to_all.39 = bf16[8,2,16,3456]{3,2,1,0:T(8,128)(2,1)S(1)} all-to-all(bf16[8,2,16,3456]{3,2,1,0:T(8,128)(2,1)S(1)} %copy.257), channel_id=1, replica_groups=mesh['wide'=64,'rows'=8] {'rows'}, dimensions={0} | all-to-all | bytes 3538944 | tf_op jit(solution)/shard_map/all_to_all | solution.py:51
  160.4 0.2 convert_reduce_fusion
  160.7 1.4 reshape.212
  162.1 0.6 copy.258
  162.7 1.5 all_to_all.33
  164.3 20.2 %all_to_all.40 = f32[64,1,1728]{2,1,0:T(1,128)S(1)} all-to-all(f32[64,1,1728]{2,1,0:T(1,128)S(1)} %all_to_all.33), channel_id=1, replica_groups=mesh['wide'=64,'rows'=8] {'wide'}, dimensions={0} | all-to-all | bytes 884736 | tf_op jit(solution)/shard_map/all_to_all | solution.py:55
  184.5 0.3 reduce_sum.39
  184.9 11.0 %all_to_all.41 = f32[8,1,1728]{2,1,0:T(1,128)S(1)} all-to-all(f32[8,1,1728]{2,1,0:T(1,128)S(1)} %broadcast_in_dim.79), channel_id=1, replica_groups=mesh['wide'=64,'rows'=8] {'rows'}, dimensions={0} | all-to-all | bytes 110592 | tf_op jit(solution)/shard_map/all_to_all | solution.py:57
  196.0 0.2 reshape.213
  196.2 0.7 copy.261
  196.9 0.7 copy.260
  (99 shorter events, 3.5 us)
Async XLA Ops:
  7.2 22.0 %copy-start.10 = (s32[1,1,10]{2,1,0:T(1,128)S(1)}, s32[1,1,10]{2,1,0:T(1,128)}, u32[]{:S(2)}) copy-start(s32[1,1,10]{2,1,0:T(1,128)} %param.9) | copy-start | bytes 124
  7.2 22.0 %copy-start.11 = (s32[1,1,10]{2,1,0:T(1,128)S(1)}, s32[1,1,10]{2,1,0:T(1,128)}, u32[]{:S(2)}) copy-start(s32[1,1,10]{2,1,0:T(1,128)} %param.8) | copy-start | bytes 124
  12.0 29.4 %all-to-all-start.1 = ((bf16[64,2,864]{2,1,0:T(2,128)(2,1)}), bf16[64,2,864]{2,1,0:T(2,128)(2,1)S(1)}, u32[]{:S(2)}, u32[]{:S(2)}) async-start(bf16[64,2,864]{2,1,0:T(2,128)(2,1)} %reshape.291), calls=%async_computation.1 | async-start | bytes 458752 | tf_op jit(solution)/shard_map/all_to_all | solution.py:122
  29.1 58.8 %all-gather.2.cloned.1.call-start = ((), (), s32[]{:S(2)}) async-start(), calls=%async_computation.5 | async-start | bytes 1990656 | tf_op jit(solution)/shard_map/all_gather | solution.py:41
  41.7 4.6 %copy-start.9 = (bf16[1,1,10,32,128]{4,3,2,1,0:T(8,128)(2,1)S(1)}, bf16[1,1,10,32,128]{4,3,2,1,0:T(8,128)(2,1)}, u32[]{:S(2)}) copy-start(bf16[1,1,10,32,128]{4,3,2,1,0:T(8,128)(2,1)} %param.7) | copy-start | bytes 245764
  47.0 8.4 %copy-start.6 = (bf16[1,5,2,32,128]{4,3,2,1,0:T(8,128)(2,1)S(1)}, bf16[1,5,2,32,128]{4,3,2,1,0:T(8,128)(2,1)}, u32[]{:S(2)}) copy-start(bf16[1,5,2,32,128]{4,3,2,1,0:T(8,128)(2,1)} %param.11) | copy-start | bytes 245764
  49.2 21.3 %all-to-all-start = ((bf16[64,2,2112]{2,1,0:T(2,128)(2,1)}), bf16[64,2,2112]{2,1,0:T(2,128)(2,1)S(1)}, u32[]{:S(2)}, u32[]{:S(2)}) async-start(bf16[64,2,2112]{2,1,0:T(2,128)(2,1)} %reshape.289), calls=%async_computation | async-start | bytes 1114112 | tf_op jit(solution)/shard_map/all_to_all | solution.py:129
  55.4 26.8 %collective-permute-start.4 = (bf16[5,1,32,128]{3,2,1,0:T(8,128)(2,1)S(1)}, bf16[5,1,32,128]{3,2,1,0:T(8,128)(2,1)S(1)}, u32[]{:S(2)}, u32[]{:S(2)}) collective-permute-start(bf16[5,1,32,128]{3,2,1,0:T(8,128)(2,1)S(1)} %get-tuple-element.45), channel_id=1, source_target_pairs={{0,1},{1,2},{2,3},{3,4},{4,5},{5,6},{6,7},{8,9},{9,10},{10,11},{11... | collective-permute-start | bytes 122888 | tf_op jit(solution)/shard_map/ppermute | solution.py:14
  60.6 21.7 %collective-permute-start.5 = (bf16[5,1,32,128]{3,2,1,0:T(8,128)(2,1)S(1)}, bf16[5,1,32,128]{3,2,1,0:T(8,128)(2,1)S(1)}, u32[]{:S(2)}, u32[]{:S(2)}) collective-permute-start(bf16[5,1,32,128]{3,2,1,0:T(8,128)(2,1)S(1)} %get-tuple-element.46), channel_id=1, source_target_pairs={{1,0},{2,1},{3,2},{4,3},{5,4},{6,5},{7,6},{9,8},{10,9},{11,10},{12... | collective-permute-start | bytes 122888 | tf_op jit(solution)/shard_map/ppermute | solution.py:17
  71.6 11.1 %collective-permute-start = (bf16[5,1,32,128]{3,2,1,0:T(8,128)(2,1)S(1)}, bf16[5,1,32,128]{3,2,1,0:T(8,128)(2,1)S(1)}, u32[]{:S(2)}, u32[]{:S(2)}) collective-permute-start(bf16[5,1,32,128]{3,2,1,0:T(8,128)(2,1)S(1)} %get-tuple-element.49), channel_id=1, source_target_pairs={{0,1},{1,2},{2,3},{3,4},{4,5},{5,6},{6,7},{8,9},{9,10},{10,11},{11... | collective-permute-start | bytes 122888 | tf_op jit(solution)/shard_map/ppermute | solution.py:14
  80.1 5.3 %collective-permute-start.1 = (bf16[5,1,32,128]{3,2,1,0:T(8,128)(2,1)S(1)}, bf16[5,1,32,128]{3,2,1,0:T(8,128)(2,1)S(1)}, u32[]{:S(2)}, u32[]{:S(2)}) collective-permute-start(bf16[5,1,32,128]{3,2,1,0:T(8,128)(2,1)S(1)} %get-tuple-element.50), channel_id=1, source_target_pairs={{1,0},{2,1},{3,2},{4,3},{5,4},{6,5},{7,6},{9,8},{10,9},{11,10},{12... | collective-permute-start | bytes 122888 | tf_op jit(solution)/shard_map/ppermute | solution.py:17
  86.5 0.7 copy-start.4
  89.4 1.0 copy-start.12
  91.7 0.7 copy-start.3
  91.7 1.7 copy-start.5
  93.3 2.1 %copy-start = (bf16[1,128,3456]{1,2,0:T(8,128)(2,1)}, bf16[1,128,3456]{1,2,0:T(8,128)(2,1)S(1)}, u32[]{:S(2)}) copy-start(bf16[1,128,3456]{1,2,0:T(8,128)(2,1)S(1)} %copy.226) | copy-start | bytes 2654212
  93.4 2.4 %slice-start = ((f32[7,2,8,5,128]{4,2,3,1,0:T(8,128)}), f32[4,2,8,5,128]{4,2,3,1,0:T(8,128)S(1)}, s32[]{:S(2)}) async-start(f32[7,2,8,5,128]{4,2,3,1,0:T(8,128)} %copy-done.3), calls=%async_computation.6 | async-start | bytes 327680 | tf_op jit(solution)/shard_map/conv_general_dilated | solution.py:89
  95.5 11.3 %copy-start.8 = (bf16[1,7,4,32,128]{4,3,2,1,0:T(8,128)(2,1)S(1)}, bf16[1,7,4,32,128]{4,3,2,1,0:T(8,128)(2,1)}, u32[]{:S(2)}) copy-start(bf16[1,7,4,32,128]{4,3,2,1,0:T(8,128)(2,1)} %get-tuple-element.32) | copy-start | bytes 688132
  96.1 10.7 %copy-start.2 = (bf16[5,2,32,128]{3,2,1,0:T(8,128)(2,1)}, bf16[5,2,32,128]{3,2,1,0:T(8,128)(2,1)S(1)}, u32[]{:S(2)}) copy-start(bf16[5,2,32,128]{3,2,1,0:T(8,128)(2,1)S(1)} %get-tuple-element.43) | copy-start | bytes 245764
  96.7 18.6 %collective-permute-start.6 = (bf16[5,1,32,128]{3,2,1,0:T(8,128)(2,1)}, bf16[5,1,32,128]{3,2,1,0:T(8,128)(2,1)}, u32[]{:S(2)}, u32[]{:S(2)}) collective-permute-start(bf16[5,1,32,128]{3,2,1,0:T(8,128)(2,1)} %get-tuple-element.41), channel_id=1, source_target_pairs={{0,1},{1,2},{2,3},{3,4},{4,5},{5,6},{6,7},{8,9},{9,10},{10,11},{11... | collective-permute-start | bytes 122888 | tf_op jit(solution)/shard_map/ppermute | solution.py:14
  98.6 16.7 %collective-permute-start.7 = (bf16[5,1,32,128]{3,2,1,0:T(8,128)(2,1)}, bf16[5,1,32,128]{3,2,1,0:T(8,128)(2,1)}, u32[]{:S(2)}, u32[]{:S(2)}) collective-permute-start(bf16[5,1,32,128]{3,2,1,0:T(8,128)(2,1)} %get-tuple-element.42), channel_id=1, source_target_pairs={{1,0},{2,1},{3,2},{4,3},{5,4},{6,5},{7,6},{9,8},{10,9},{11,10},{12... | collective-permute-start | bytes 122888 | tf_op jit(solution)/shard_map/ppermute | solution.py:17
  102.3 15.9 %collective-permute-start.2 = (bf16[5,1,32,128]{3,2,1,0:T(8,128)(2,1)}, bf16[5,1,32,128]{3,2,1,0:T(8,128)(2,1)S(1)}, u32[]{:S(2)}, u32[]{:S(2)}) collective-permute-start(bf16[5,1,32,128]{3,2,1,0:T(8,128)(2,1)} %get-tuple-element.47), channel_id=1, source_target_pairs={{0,1},{1,2},{2,3},{3,4},{4,5},{5,6},{6,7},{8,9},{9,10},{10,11},{11... | collective-permute-start | bytes 122888 | tf_op jit(solution)/shard_map/ppermute | solution.py:14
  104.8 13.3 %collective-permute-start.3 = (bf16[5,1,32,128]{3,2,1,0:T(8,128)(2,1)}, bf16[5,1,32,128]{3,2,1,0:T(8,128)(2,1)}, u32[]{:S(2)}, u32[]{:S(2)}) collective-permute-start(bf16[5,1,32,128]{3,2,1,0:T(8,128)(2,1)} %get-tuple-element.48), channel_id=1, source_target_pairs={{1,0},{2,1},{3,2},{4,3},{5,4},{6,5},{7,6},{9,8},{10,9},{11,10},{12... | collective-permute-start | bytes 122888 | tf_op jit(solution)/shard_map/ppermute | solution.py:17
  115.3 1.4 copy-start.1
  120.0 1.0 copy-start.7
Sparse Core Ops, SparseCore 0:
  46.4 24.9 all-gather.1

commit v5 on v4

--- a/solution.py
+++ b/solution.py
@@ -24,24 +24,6 @@
     return sig * (1.0 + values * (1.0 - sig))
 
 
-def weight_pieces(w_first, w_second, band_count):
-    rows_local, channels = w_first.shape
-    part = channels // band_count
-    me = lax.axis_index("rows")
-    both = jnp.stack([w_first, w_second])
-    mine = lax.dynamic_slice_in_dim(both, me * part, part, axis=2)
-    return jnp.transpose(mine, (0, 2, 1)).reshape(2 * part * rows_local)
-
-
-def assemble_weights(pieces, band_count, rows_local, channels):
-    count = pieces.shape[0]
-    part = channels // band_count
-    block = pieces.reshape(count, 2, part, rows_local)
-    block = jnp.transpose(block, (1, 2, 0, 3)).reshape(2, part, count * rows_local)
-    full = lax.all_gather(block, "rows", axis=1, tiled=True)
-    return full[0], full[1]
-
-
 def reduce_weight_grads(grad_t, band_count, wide_size):
     _, channels, total_rows = grad_t.shape
     part = channels // band_count
@@ -62,15 +44,24 @@
     return joined[0], joined[1]
 
 
-def conv_forward_t(extended, kernel_t):
-    cout = kernel_t.shape[0]
-    kernel = kernel_t.reshape(cout, 3, 3, 3, -1)
+def conv_forward(extended, kernel):
     padded = jnp.concatenate([extended[:1], extended[:1], extended], axis=0)
     result = lax.conv_general_dilated(
         padded[None], kernel, (1, 1, 1), ((0, 0), (0, 0), (1, 1)),
-        dimension_numbers=("NDHWC", "ODHWI", "NDHWC"), preferred_element_type=jnp.float32,
+        dimension_numbers=("NDHWC", "DHWIO", "NDHWC"), preferred_element_type=jnp.float32,
     )
     return result[0]
+
+
+def conv_data_grad(upstream_ext, kernel):
+    padded = jnp.pad(upstream_ext, ((2, 2), (0, 0), (0, 0), (0, 0)))
+    flipped = kernel[::-1, ::-1, ::-1]
+    result = lax.conv_general_dilated(
+        padded[None], flipped, (1, 1, 1), ((0, 0), (0, 0), (1, 1)),
+        dimension_numbers=("NDHWC", "DHWOI", "NDHWC"), preferred_element_type=jnp.float32,
+    )[0]
+    head = (result[0] + result[1] + result[2])[None]
+    return jnp.concatenate([head, result[3:]], axis=0)
 
 
 def conv_weight_grad_t(extended, upstream):
@@ -80,18 +71,6 @@
         dimension_numbers=("CDHWN", "IDHWO", "CDHWN"), preferred_element_type=jnp.float32,
     )
     return result.reshape(upstream.shape[-1], -1)
-
-
-def conv_data_grad_t(upstream_ext, kernel_t):
-    cout = kernel_t.shape[0]
-    kernel = kernel_t.reshape(cout, 3, 3, 3, -1)[:, ::-1, ::-1, ::-1, :]
-    padded = jnp.pad(upstream_ext, ((2, 2), (0, 0), (0, 0), (0, 0)))
-    result = lax.conv_general_dilated(
-        padded[None], kernel, (1, 1, 1), ((0, 0), (0, 0), (1, 1)),
-        dimension_numbers=("NDHWC", "IDHWO", "NDHWC"), preferred_element_type=jnp.float32,
-    )[0]
-    head = (result[0] + result[1] + result[2])[None]
-    return jnp.concatenate([head, result[3:]], axis=0)
 
 
 def body(slabs, dest, pos, lengths, cot, w_first, w_second):
@@ -118,38 +97,42 @@
     labels = jnp.sum(jnp.where(placing, places[None, :] + 1, 0), axis=1) - 1
     labels = labels.reshape(wide_size, capacity).astype(jnp.bfloat16)
     label_block = 128
-    pieces = weight_pieces(w_first, w_second, band_count)
-    pieces = lax.all_to_all(
-        jnp.broadcast_to(pieces[None], (wide_size, pieces.shape[0])), "wide", 0, 0, tiled=True
-    )
-    kernel_first, kernel_second = assemble_weights(pieces, band_count, rows_local, channels)
+    chunk_both = jnp.stack([w_first, w_second]).reshape(1, 2 * rows_local * channels)
     tagged = jnp.concatenate(
-        [outgoing, jnp.repeat(labels, label_block // capacity, axis=1)], axis=1
+        [
+            outgoing,
+            jnp.repeat(labels, label_block // capacity, axis=1),
+            jnp.broadcast_to(chunk_both, (wide_size, chunk_both.shape[1])),
+        ],
+        axis=1,
     )
     tagged = lax.all_to_all(tagged, "wide", split_axis=0, concat_axis=0, tiled=True)
     payload = capacity * columns * channels
     arrived = tagged[:, :payload].reshape(slot_count, columns * channels)
     arrived_places = tagged[:, payload : payload + label_block : label_block // capacity]
     arrived_places = arrived_places.astype(jnp.int32).reshape(slot_count)
+    weights = tagged[:, payload + label_block :].reshape(wide_size, 2, rows_local, channels)
+    weights = jnp.transpose(weights, (1, 0, 2, 3)).reshape(2, 3, 3, 3, channels, channels)
+    kernel_first, kernel_second = weights[0], weights[1]
     settle = arrived_places[None, :] == jnp.arange(slab_count, dtype=jnp.int32)[:, None]
     tile = jnp.dot(settle.astype(jnp.bfloat16), arrived, preferred_element_type=jnp.float32)
     tile = tile.astype(jnp.bfloat16).reshape(frames, band_rows, columns, channels)
     tile_wide = tile.astype(jnp.float32)
     first = jax.nn.silu(tile_wide).astype(jnp.bfloat16)
     first_ext = with_halo(first, (("rows", 1),), 1)
-    act = conv_forward_t(first_ext, kernel_first).astype(jnp.bfloat16)
+    act = conv_forward(first_ext, kernel_first).astype(jnp.bfloat16)
     second = jax.nn.silu(act.astype(jnp.float32)).astype(jnp.bfloat16)
     second_ext = with_halo(second, (("rows", 1),), 1)
-    block_out = (tile_wide + conv_forward_t(second_ext, kernel_second)).astype(jnp.bfloat16)
+    block_out = (tile_wide + conv_forward(second_ext, kernel_second)).astype(jnp.bfloat16)
     live = (jnp.arange(frames, dtype=jnp.int32) < lengths[0])[:, None, None, None]
     out_grad = jnp.where(live, cot[0], jnp.zeros_like(cot[0]))
     out_grad_ext = with_halo(out_grad, (("rows", 1),), 1)
     weight_second = conv_weight_grad_t(second_ext, out_grad)
-    hidden_grad = conv_data_grad_t(out_grad_ext, kernel_second)
+    hidden_grad = conv_data_grad(out_grad_ext, kernel_second)
     act_grad = (hidden_grad * silu_slope(act.astype(jnp.float32))).astype(jnp.bfloat16)
     act_grad_ext = with_halo(act_grad, (("rows", 1),), 1)
     weight_first = conv_weight_grad_t(first_ext, act_grad)
-    first_grad = conv_data_grad_t(act_grad_ext, kernel_first)
+    first_grad = conv_data_grad(act_grad_ext, kernel_first)
     grad_input = (out_grad.astype(jnp.float32) + first_grad * silu_slope(tile_wide)).astype(
         jnp.bfloat16
     )

time: 205 us -> 225 us (1.098)
  waiting for transfers between devices: 22.6 us -> 47.5 us
  between operations: 15.6 us -> 2.02 us
  local copies, waits for them, and re-layouts: 31.2 us -> 42.2 us
  starting transfers between devices: 49.8 us -> 43.8 us
  blocking collectives: 59 us -> 63.4 us
    all_to_all x1, waiting for transfers between devices: 7.9 us -> 42.9 us  [body(): lax.all_to_all(tagged, 'wide', split_axis=0, concat_axis=0, tiled=True)]
    all_to_all x1 -> x0, starting transfers between devices: 17.1 us -> none  [body(): lax.all_to_all(jnp.broadcast_to(pieces[None], (wide_size, pieces.shape[0]...]
    all_to_all x1 -> x0, waiting for transfers between devices: 11.9 us -> none  [body(): lax.all_to_all(jnp.broadcast_to(pieces[None], (wide_size, pieces.shape[0]...]
    all_to_all x1, starting transfers between devices: 5.5 us -> 17.3 us  [body(): lax.all_to_all(tagged, 'wide', split_axis=0, concat_axis=0, tiled=True)]
    unnamed x45 -> x29, local copies, waits for them, and re-layouts: 6.64 us -> 18 us
    all_to_all x1, blocking collectives: 20.2 us -> 24.9 us  [reduce_weight_grads(): wide_parts = lax.all_to_all(band_sum, 'wide', 0, 0, tiled=True)]
    broadcast_in_dim x5 -> x4, other arithmetic: 4.64 us -> 0.91 us  [the longest x2 0.84 us: conv_data_grad(): padded[None]]
  transfers between devices with their start and end apart: 11 -> 9, of which waited for: 3 -> 3; matrix products, arithmetic and copies ran while one was open for 9% -> 9% of each run, Pallas kernels for 0% -> 0%
where the time goes in v5:
time: 225 us; the launch traced here: 223 us
  blocking collectives  63.4 us (28%)
  waiting for transfers between devices  47.5 us (21%)
  starting transfers between devices  43.8 us (19%)
  local copies, waits for them, and re-layouts  42.2 us (19%)
  matrix products  13.1 us (6%)
  other arithmetic  11.4 us (5%)
    all_to_all x1, waiting for transfers between devices, body(): lax.all_to_all(tagged, 'wide', split_axis=0, concat_axis=0, tiled=True)  42.9 us
    all_to_all x1, blocking collectives, reduce_weight_grads(): band_parts = lax.all_to_all(blocks, 'rows', 0, 0, tiled=True)  27.6 us
    all_to_all x1, blocking collectives, reduce_weight_grads(): wide_parts = lax.all_to_all(band_sum, 'wide', 0, 0, tiled=True)  24.9 us
    ppermute x4, starting transfers between devices, with_halo(): lax.ppermute(lax.slice_in_dim(block, block.shape[dim] - width, None, axis...  18.6 us
    unnamed x29, local copies, waits for them, and re-layouts  18 us
    all_to_all x1, starting transfers between devices, body(): lax.all_to_all(tagged, 'wide', split_axis=0, concat_axis=0, tiled=True)  17.3 us
    all_to_all x1, blocking collectives, reduce_weight_grads(): lax.all_to_all(jnp.broadcast_to(share, (band_count,) + share.shape[1:]),...  11 us
    ppermute x4, starting transfers between devices, with_halo(): lax.ppermute(lax.slice_in_dim(block, 0, width, axis=dim), axis, backward)  7.86 us
  transfers between devices with their start and end apart: 9, of which 3 were waited for; matrix products, arithmetic and copies ran while one was open for 9% of the time, Pallas kernels for 0%

profile of v5, /device:TPU:1, one launch (start us, length us, event | category | flops | bytes accessed | tf_op | source)
XLA Modules:
  0.0 223.4 jit_solution(957580499515858776)
XLA Ops:
  0.6 0.9 convert_reduce_fusion.2
  1.5 0.7 bitcast_add_fusion
  2.2 0.9 pad.76
  3.2 0.7 add_bitcast_fusion
  3.8 0.4 convolution_convert_fusion
  4.3 0.7 pad_maximum_fusion.4
  5.2 0.2 maximum_bitcast_fusion
  5.4 0.5 broadcast.163
  5.9 3.1 %reduce.4 = bf16[64,18048]{1,0:T(8,128)(2,1)} reduce(bf16[64,1,18048]{2,0,1:T(8,128)(2,1)S(1)} %maximum_bitcast_fusion, bf16[]{:T(256)} %broadcast.163), dimensions={1}, to_apply=%copy.237.reduce_sub_computation | reduce | bytes 4620290 | tf_op jit(solution)/shard_map/all_to_all | solution.py:109
  9.0 4.9 %reshape.283 = bf16[64,2,9024]{2,1,0:T(2,128)(2,1)} reshape(bf16[64,18048]{1,0:T(8,128)(2,1)} %reduce.4) | data formatting | bytes 4620288
  13.9 17.3 %all-to-all-start = ((bf16[64,2,9024]{2,1,0:T(2,128)(2,1)}), bf16[64,2,9024]{2,1,0:T(2,128)(2,1)S(1)}, u32[]{:S(2)}, u32[]{:S(2)}) async-start(bf16[64,2,9024]{2,1,0:T(2,128)(2,1)} %reshape.283), calls=%async_computation | async-start | bytes 4653056 | tf_op jit(solution)/shard_map/all_to_all | solution.py:109
  31.9 4.0 %collective-permute-start.4 = (bf16[5,1,32,128]{3,2,1,0:T(8,128)(2,1)S(1)}, bf16[5,1,32,128]{3,2,1,0:T(8,128)(2,1)S(1)}, u32[]{:S(2)}, u32[]{:S(2)}) collective-permute-start(bf16[5,1,32,128]{3,2,1,0:T(8,128)(2,1)S(1)} %get-tuple-element.49), channel_id=1, source_target_pairs={{0,1},{1,2},{2,3},{3,4},{4,5},{5,6},{6,7},{8,9},{9,10},{10,11},{11... | collective-permute-start | bytes 122888 | tf_op jit(solution)/shard_map/ppermute | solution.py:14
  35.9 1.9 collective-permute-start.5
  37.8 3.7 %collective-permute-done.5 = bf16[5,1,32,128]{3,2,1,0:T(8,128)(2,1)S(1)} collective-permute-done((bf16[5,1,32,128]{3,2,1,0:T(8,128)(2,1)S(1)}, bf16[5,1,32,128]{3,2,1,0:T(8,128)(2,1)S(1)}, u32[]{:S(2)}, u32[]{:S(2)}) %collective-permute-start.5) | collective-permute-done | bytes 40992 | tf_op jit(solution)/shard_map/ppermute | solution.py:17
  41.6 0.2 copy.285
  41.7 0.1 pad.13.clone
  41.9 0.7 slice.156
  42.6 42.9 %all-to-all-done = bf16[64,2,9024]{2,1,0:T(2,128)(2,1)S(1)} async-done(((bf16[64,2,9024]{2,1,0:T(2,128)(2,1)}), bf16[64,2,9024]{2,1,0:T(2,128)(2,1)S(1)}, u32[]{:S(2)}, u32[]{:S(2)}) %all-to-all-start) | async-done | bytes 2310176 | tf_op jit(solution)/shard_map/all_to_all | solution.py:109
  85.5 7.5 %reshape.284 = bf16[64,1,18048]{2,1,0:T(2,128)(2,1)} reshape(bf16[64,2,9024]{2,1,0:T(2,128)(2,1)S(1)} %all-to-all-done) | data formatting | bytes 4620288
  93.0 2.6 %copy.318 = bf16[64,1,18048]{2,0,1:T(8,128)(2,1)S(1)} copy(bf16[64,1,18048]{2,1,0:T(2,128)(2,1)} %reshape.284) | data formatting | bytes 4620288
  95.7 1.4 slice.146
  97.1 0.2 fusion
  97.4 0.6 fusion.89
  98.0 7.3 %collective-permute-start = (bf16[5,1,32,128]{3,2,1,0:T(8,128)(2,1)}, bf16[5,1,32,128]{3,2,1,0:T(8,128)(2,1)S(1)}, u32[]{:S(2)}, u32[]{:S(2)}) collective-permute-start(bf16[5,1,32,128]{3,2,1,0:T(8,128)(2,1)} %get-tuple-element.53), channel_id=1, source_target_pairs={{0,1},{1,2},{2,3},{3,4},{4,5},{5,6},{6,7},{8,9},{9,10},{10,11},{11... | collective-permute-start | bytes 122888 | tf_op jit(solution)/shard_map/ppermute | solution.py:14
  105.3 1.9 collective-permute-start.1
  107.2 2.8 %reshape.205 = bf16[64,2,54,128]{3,2,1,0:T(8,128)(2,1)S(1)} reshape(bf16[64,13824]{1,0:T(8,128)(2,1)} %slice.146) | data formatting | bytes 3538944 | tf_op jit(solution)/shard_map/reshape | solution.py:114
  110.0 1.1 fusion.84
  111.1 1.3 squeeze.16
  112.5 2.2 %convolution_select_fusion.1 = f32[7,2,8,5,128]{4,2,3,1,0:T(8,128)S(1)} fusion(bf16[3,3,3,128,128]{4,3,2,1,0:T(8,128)(2,1)S(1)} %squeeze.16, bf16[9,4,1,7,2,128]{5,3,4,1,0,2:T(8,128)(2,1)} %slice.156, bf16[9,4,1,8,5,128]{5,3,4,1,0,2:T(8,128)(2,1)S(1)} %copy.250, pred[8,5]{0,1:T(8,128)(4,1)S(1)} %copy-done.5), kind=kOutput, calls=%fused_computation.10 | convolution fusion | flops 497072128 | bytes 1669160 | tf_op jit(solution)/shard_map/conv_general_dilated | solution.py:59
  114.8 0.2 squeeze.15
  115.3 0.1 copy.283
  115.6 0.9 fusion.47
  117.0 0.6 fusion.86
  117.6 3.6 %collective-permute-start.6 = (bf16[5,1,32,128]{3,2,1,0:T(8,128)(2,1)}, bf16[5,1,32,128]{3,2,1,0:T(8,128)(2,1)S(1)}, u32[]{:S(2)}, u32[]{:S(2)}) collective-permute-start(bf16[5,1,32,128]{3,2,1,0:T(8,128)(2,1)} %get-tuple-element.45), channel_id=1, source_target_pairs={{0,1},{1,2},{2,3},{3,4},{4,5},{5,6},{6,7},{8,9},{9,10},{10,11},{11... | collective-permute-start | bytes 122888 | tf_op jit(solution)/shard_map/ppermute | solution.py:14
  121.2 2.1 collective-permute-start.7
  123.4 3.7 %fusion.24 = f32[128,3,3,3,128]{0,4,3,2,1:T(8,128)} fusion(bf16[1,7,4,32,128]{4,3,2,1,0:T(8,128)(2,1)S(1)} %get-tuple-element.36, bf16[1,5,2,32,128]{4,3,2,1,0:T(8,128)(2,1)S(1)} %fusion.60), kind=kOutput, calls=%fused_computation.36 | convolution fusion | flops 277217280 | bytes 2080768 | tf_op jit(solution)/shard_map/conv_general_dilated | solution.py:69
  127.1 2.8 %copy.266 = f32[128,3,3,3,128]{4,3,2,1,0:T(4,128)S(1)} copy(f32[128,3,3,3,128]{0,4,3,2,1:T(8,128)} %fusion.24) | data formatting | bytes 3538944 | tf_op jit(solution)/shard_map/conv_general_dilated | solution.py:69
  129.9 1.9 stack.19
  131.8 3.8 %collective-permute-start.2 = (bf16[5,1,32,128]{3,2,1,0:T(8,128)(2,1)S(1)}, bf16[5,1,32,128]{3,2,1,0:T(8,128)(2,1)S(1)}, u32[]{:S(2)}, u32[]{:S(2)}) collective-permute-start(bf16[5,1,32,128]{3,2,1,0:T(8,128)(2,1)S(1)} %get-tuple-element.51), channel_id=1, source_target_pairs={{0,1},{1,2},{2,3},{3,4},{4,5},{5,6},{6,7},{8,9},{9,10},{10,11},{11... | collective-permute-start | bytes 122888 | tf_op jit(solution)/shard_map/ppermute | solution.py:14
  135.6 1.9 collective-permute-start.3
  137.5 0.8 fusion.38
  138.4 0.2 copy.286
  138.5 0.1 pad.15.clone
  138.8 1.2 convolution_select_fusion
  140.0 0.9 collective-permute-done.3
  141.3 0.9 convolution_select_fusion.2
  142.5 0.7 fusion.59
  143.2 3.6 %fusion.22 = f32[128,3,3,3,128]{0,4,3,2,1:T(8,128)} fusion(bf16[1,7,4,32,128]{4,3,2,1,0:T(8,128)(2,1)S(1)} %get-tuple-element.38, bf16[1,5,2,32,128]{4,3,2,1,0:T(8,128)(2,1)S(1)} %get-tuple-element.33), kind=kOutput, calls=%fused_computation.34 | convolution fusion | flops 277217280 | bytes 2080768 | tf_op jit(solution)/shard_map/conv_general_dilated | solution.py:69
  146.9 2.8 %copy.269 = f32[128,3,3,3,128]{4,3,2,1,0:T(4,128)S(1)} copy(f32[128,3,3,3,128]{0,4,3,2,1:T(8,128)} %fusion.22) | data formatting | bytes 3538944 | tf_op jit(solution)/shard_map/conv_general_dilated | solution.py:69
  149.7 1.9 stack.20
  151.6 2.3 %fusion.2 = bf16[8,2,16,3456]{3,2,0,1:T(8,128)(2,1)S(1)} fusion(f32[1,8,16,3456]{3,2,1,0:T(8,128)} %stack.20, f32[1,8,16,3456]{3,2,1,0:T(8,128)} %stack.19), kind=kLoop, calls=%fused_computation.8 | loop fusion | flops 2654208 | bytes 5308416 | tf_op jit(solution)/shard_map/transpose | solution.py:32
  153.9 0.1 copy.270
  154.0 27.6 %all_to_all.33 = bf16[8,2,16,3456]{3,2,1,0:T(8,128)(2,1)S(1)} all-to-all(bf16[8,2,16,3456]{3,2,1,0:T(8,128)(2,1)S(1)} %copy.270), channel_id=1, replica_groups=mesh['wide'=64,'rows'=8] {'rows'}, dimensions={0} | all-to-all | bytes 3538944 | tf_op jit(solution)/shard_map/all_to_all | solution.py:33
  181.6 0.2 convert_reduce_fusion
  181.8 1.4 reshape.206
  183.3 0.6 copy.271
  183.9 1.5 all_to_all.28
  185.5 24.9 %all_to_all.34 = f32[64,1,1728]{2,1,0:T(1,128)S(1)} all-to-all(f32[64,1,1728]{2,1,0:T(1,128)S(1)} %all_to_all.28), channel_id=1, replica_groups=mesh['wide'=64,'rows'=8] {'wide'}, dimensions={0} | all-to-all | bytes 884736 | tf_op jit(solution)/shard_map/all_to_all | solution.py:37
  210.3 0.3 reduce_sum.39
  210.7 11.0 %all_to_all.35 = f32[8,1,1728]{2,1,0:T(1,128)S(1)} all-to-all(f32[8,1,1728]{2,1,0:T(1,128)S(1)} %broadcast_in_dim.79), channel_id=1, replica_groups=mesh['wide'=64,'rows'=8] {'rows'}, dimensions={0} | all-to-all | bytes 110592 | tf_op jit(solution)/shard_map/all_to_all | solution.py:39
  221.7 0.1 reduce.2
  221.8 0.2 reshape.207
  222.0 0.7 copy.273
  222.7 0.7 copy.274
  (73 shorter events, 2.2 us)
Async XLA Ops:
  13.9 17.9 %copy-start.4 = (bf16[1,5,2,32,128]{4,3,2,1,0:T(8,128)(2,1)S(1)}, bf16[1,5,2,32,128]{4,3,2,1,0:T(8,128)(2,1)}, u32[]{:S(2)}) copy-start(bf16[1,5,2,32,128]{4,3,2,1,0:T(8,128)(2,1)} %param.11) | copy-start | bytes 245764
  13.9 71.6 %all-to-all-start = ((bf16[64,2,9024]{2,1,0:T(2,128)(2,1)}), bf16[64,2,9024]{2,1,0:T(2,128)(2,1)S(1)}, u32[]{:S(2)}, u32[]{:S(2)}) async-start(bf16[64,2,9024]{2,1,0:T(2,128)(2,1)} %reshape.283), calls=%async_computation | async-start | bytes 4653056 | tf_op jit(solution)/shard_map/all_to_all | solution.py:109
  31.9 5.9 %collective-permute-start.4 = (bf16[5,1,32,128]{3,2,1,0:T(8,128)(2,1)S(1)}, bf16[5,1,32,128]{3,2,1,0:T(8,128)(2,1)S(1)}, u32[]{:S(2)}, u32[]{:S(2)}) collective-permute-start(bf16[5,1,32,128]{3,2,1,0:T(8,128)(2,1)S(1)} %get-tuple-element.49), channel_id=1, source_target_pairs={{0,1},{1,2},{2,3},{3,4},{4,5},{5,6},{6,7},{8,9},{9,10},{10,11},{11... | collective-permute-start | bytes 122888 | tf_op jit(solution)/shard_map/ppermute | solution.py:14
  35.9 5.6 %collective-permute-start.5 = (bf16[5,1,32,128]{3,2,1,0:T(8,128)(2,1)S(1)}, bf16[5,1,32,128]{3,2,1,0:T(8,128)(2,1)S(1)}, u32[]{:S(2)}, u32[]{:S(2)}) collective-permute-start(bf16[5,1,32,128]{3,2,1,0:T(8,128)(2,1)S(1)} %get-tuple-element.50), channel_id=1, source_target_pairs={{1,0},{2,1},{3,2},{4,3},{5,4},{6,5},{7,6},{9,8},{10,9},{11,10},{12... | collective-permute-start | bytes 122888 | tf_op jit(solution)/shard_map/ppermute | solution.py:17
  98.0 17.2 %collective-permute-start = (bf16[5,1,32,128]{3,2,1,0:T(8,128)(2,1)}, bf16[5,1,32,128]{3,2,1,0:T(8,128)(2,1)S(1)}, u32[]{:S(2)}, u32[]{:S(2)}) collective-permute-start(bf16[5,1,32,128]{3,2,1,0:T(8,128)(2,1)} %get-tuple-element.53), channel_id=1, source_target_pairs={{0,1},{1,2},{2,3},{3,4},{4,5},{5,6},{6,7},{8,9},{9,10},{10,11},{11... | collective-permute-start | bytes 122888 | tf_op jit(solution)/shard_map/ppermute | solution.py:14
  105.3 9.9 %collective-permute-start.1 = (bf16[5,1,32,128]{3,2,1,0:T(8,128)(2,1)}, bf16[5,1,32,128]{3,2,1,0:T(8,128)(2,1)S(1)}, u32[]{:S(2)}, u32[]{:S(2)}) collective-permute-start(bf16[5,1,32,128]{3,2,1,0:T(8,128)(2,1)} %get-tuple-element.54), channel_id=1, source_target_pairs={{1,0},{2,1},{3,2},{4,3},{5,4},{6,5},{7,6},{9,8},{10,9},{11,10},{12... | collective-permute-start | bytes 122888 | tf_op jit(solution)/shard_map/ppermute | solution.py:17
  110.0 2.5 %copy-start.5 = (pred[8,5]{0,1:T(8,128)(4,1)S(1)}, pred[8,5]{0,1:T(8,128)(4,1)}, u32[]{:S(2)}) copy-start(pred[8,5]{0,1:T(8,128)(4,1)} %constant.46) | copy-start | bytes 124
  112.5 2.3 %copy-start = (bf16[3,3,3,128,128]{4,3,2,1,0:T(8,128)(2,1)}, bf16[3,3,3,128,128]{4,3,2,1,0:T(8,128)(2,1)S(1)}, u32[]{:S(2)}) copy-start(bf16[3,3,3,128,128]{4,3,2,1,0:T(8,128)(2,1)S(1)} %squeeze.16) | copy-start | bytes 2654212
  115.0 1.5 copy-start.2
  117.6 19.9 %collective-permute-start.6 = (bf16[5,1,32,128]{3,2,1,0:T(8,128)(2,1)}, bf16[5,1,32,128]{3,2,1,0:T(8,128)(2,1)S(1)}, u32[]{:S(2)}, u32[]{:S(2)}) collective-permute-start(bf16[5,1,32,128]{3,2,1,0:T(8,128)(2,1)} %get-tuple-element.45), channel_id=1, source_target_pairs={{0,1},{1,2},{2,3},{3,4},{4,5},{5,6},{6,7},{8,9},{9,10},{10,11},{11... | collective-permute-start | bytes 122888 | tf_op jit(solution)/shard_map/ppermute | solution.py:14
  121.2 16.3 %collective-permute-start.7 = (bf16[5,1,32,128]{3,2,1,0:T(8,128)(2,1)S(1)}, bf16[5,1,32,128]{3,2,1,0:T(8,128)(2,1)}, u32[]{:S(2)}, u32[]{:S(2)}) collective-permute-start(bf16[5,1,32,128]{3,2,1,0:T(8,128)(2,1)S(1)} %get-tuple-element.46), channel_id=1, source_target_pairs={{1,0},{2,1},{3,2},{4,3},{5,4},{6,5},{7,6},{9,8},{10,9},{11,10},{12... | collective-permute-start | bytes 122888 | tf_op jit(solution)/shard_map/ppermute | solution.py:17
  131.8 6.9 %copy-start.3 = (bf16[3,3,3,128,128]{4,3,2,1,0:T(8,128)(2,1)S(1)}, bf16[3,3,3,128,128]{4,3,2,1,0:T(8,128)(2,1)}, u32[]{:S(2)}) copy-start(bf16[3,3,3,128,128]{4,3,2,1,0:T(8,128)(2,1)} %copy-done.2) | copy-start | bytes 2654212
  131.8 8.2 %collective-permute-start.2 = (bf16[5,1,32,128]{3,2,1,0:T(8,128)(2,1)S(1)}, bf16[5,1,32,128]{3,2,1,0:T(8,128)(2,1)S(1)}, u32[]{:S(2)}, u32[]{:S(2)}) collective-permute-start(bf16[5,1,32,128]{3,2,1,0:T(8,128)(2,1)S(1)} %get-tuple-element.51), channel_id=1, source_target_pairs={{0,1},{1,2},{2,3},{3,4},{4,5},{5,6},{6,7},{8,9},{9,10},{10,11},{11... | collective-permute-start | bytes 122888 | tf_op jit(solution)/shard_map/ppermute | solution.py:14
  135.6 5.3 %collective-permute-start.3 = (bf16[5,1,32,128]{3,2,1,0:T(8,128)(2,1)S(1)}, bf16[5,1,32,128]{3,2,1,0:T(8,128)(2,1)S(1)}, u32[]{:S(2)}, u32[]{:S(2)}) collective-permute-start(bf16[5,1,32,128]{3,2,1,0:T(8,128)(2,1)S(1)} %get-tuple-element.52), channel_id=1, source_target_pairs={{1,0},{2,1},{3,2},{4,3},{5,4},{6,5},{7,6},{9,8},{10,9},{11,10},{12... | collective-permute-start | bytes 122888 | tf_op jit(solution)/shard_map/ppermute | solution.py:17
  139.9 1.3 copy-start.1

commit v6 on v4

--- a/solution.py
+++ b/solution.py
@@ -1,8 +1,12 @@
+import functools
 import math
+
 
 import jax
 import jax.numpy as jnp
 from jax import lax
+from jax.experimental import pallas as pl
+from jax.experimental.pallas import tpu as pltpu
 from jax.sharding import PartitionSpec as P
 
 
@@ -42,6 +46,76 @@
     return full[0], full[1]
 
 
+def _wide_sum_kernel(count, x_ref, o_ref, recv, send_sems, recv_sems):
+    me = lax.axis_index("wide")
+    band = lax.axis_index("rows")
+    barrier = pltpu.get_barrier_semaphore()
+
+    def greet(k, carry):
+        peer = lax.rem(me + k, count)
+        pl.semaphore_signal(
+            barrier, 1, device_id=(peer, band), device_id_type=pl.DeviceIdType.MESH
+        )
+        return carry
+
+    lax.fori_loop(1, count, greet, 0)
+    pl.semaphore_wait(barrier, count - 1)
+
+    def send(k, carry):
+        peer = lax.rem(me + k, count)
+        pltpu.make_async_remote_copy(
+            src_ref=x_ref.at[peer],
+            dst_ref=recv.at[me],
+            send_sem=send_sems.at[peer],
+            recv_sem=recv_sems.at[me],
+            device_id=(peer, band),
+            device_id_type=pl.DeviceIdType.MESH,
+        ).start()
+        return carry
+
+    lax.fori_loop(1, count, send, 0)
+
+    def finish(k, total):
+        peer = lax.rem(me + k, count)
+        source = lax.rem(me + count - k, count)
+        pltpu.make_async_remote_copy(
+            src_ref=x_ref.at[peer],
+            dst_ref=recv.at[me],
+            send_sem=send_sems.at[peer],
+            recv_sem=recv_sems.at[me],
+            device_id=(peer, band),
+            device_id_type=pl.DeviceIdType.MESH,
+        ).wait_send()
+        pltpu.make_async_remote_copy(
+            src_ref=x_ref.at[source],
+            dst_ref=recv.at[source],
+            send_sem=send_sems.at[source],
+            recv_sem=recv_sems.at[source],
+            device_id=(source, band),
+            device_id_type=pl.DeviceIdType.MESH,
+        ).wait_recv()
+        return total + recv[source]
+
+    total = lax.fori_loop(1, count, finish, x_ref[me])
+    o_ref[...] = total
+
+
+def wide_sum(pieces):
+    count = pieces.shape[0]
+    return pl.pallas_call(
+        functools.partial(_wide_sum_kernel, count),
+        out_shape=jax.ShapeDtypeStruct(pieces.shape[1:], pieces.dtype),
+        in_specs=[pl.BlockSpec(memory_space=pltpu.VMEM)],
+        out_specs=pl.BlockSpec(memory_space=pltpu.VMEM),
+        scratch_shapes=[
+            pltpu.VMEM(pieces.shape, pieces.dtype),
+            pltpu.SemaphoreType.DMA((count,)),
+            pltpu.SemaphoreType.DMA((count,)),
+        ],
+        compiler_params=pltpu.CompilerParams(collective_id=0, has_side_effects=True),
+    )(pieces)
+
+
 def reduce_weight_grads(grad_t, band_count, wide_size):
     _, channels, total_rows = grad_t.shape
     part = channels // band_count
@@ -52,8 +126,11 @@
     band_sum = jnp.sum(band_parts.astype(jnp.float32), axis=0)
     band_sum = band_sum.reshape(2, part, wide_size, chunk)
     band_sum = jnp.transpose(band_sum, (2, 0, 1, 3)).reshape(wide_size, 2 * part * chunk)
-    wide_parts = lax.all_to_all(band_sum, "wide", 0, 0, tiled=True)
-    share = jnp.sum(wide_parts, axis=0, keepdims=True)
+    size = band_sum.shape[1]
+    lanes = 128
+    tall = -(-size // (8 * lanes)) * 8
+    padded = jnp.pad(band_sum, ((0, 0), (0, tall * lanes - size)))
+    share = wide_sum(padded.reshape(wide_size, tall, lanes)).reshape(1, tall * lanes)[:, :size]
     joined = lax.all_to_all(
         jnp.broadcast_to(share, (band_count,) + share.shape[1:]), "rows", 0, 0, tiled=True
     )

time: 205 us -> 206 us (level)
  blocking collectives: 59 us -> 37.2 us
  Pallas kernels: 0 us -> 21.7 us
  matrix products: 13.3 us -> 15.7 us
    pallas_call x0 -> x1, Pallas kernels: none -> 21.7 us  [wide_sum(): pl.pallas_call(functools.partial(_wide_sum_kernel, count), out_shape=jax....]
    all_to_all x1 -> x0, blocking collectives: 20.2 us -> none  [reduce_weight_grads(): wide_parts = lax.all_to_all(band_sum, 'wide', 0, 0, tiled=True)]
    unnamed x45 -> x37, local copies, waits for them, and re-layouts: 6.64 us -> 6.54 us
  transfers between devices with their start and end apart: 11 -> 11, of which waited for: 3 -> 3; matrix products, arithmetic and copies ran while one was open for 9% -> 8% of each run, Pallas kernels for 0% -> 0%
where the time goes in v6:
time: 206 us; the launch traced here: 205 us
  starting transfers between devices  49.8 us (24%)
  blocking collectives  37.2 us (18%)
  local copies, waits for them, and re-layouts  29.4 us (14%)
  waiting for transfers between devices  23 us (11%)
  Pallas kernels  21.7 us (11%)
  matrix products  15.7 us (8%)
  between operations  15.4 us (7%)
  other arithmetic  12.8 us (6%)
    all_to_all x1, blocking collectives, reduce_weight_grads(): band_parts = lax.all_to_all(blocks, 'rows', 0, 0, tiled=True)  27.7 us
    pallas_call x1, Pallas kernels, wide_sum(): pl.pallas_call(functools.partial(_wide_sum_kernel, count), out_shape=jax....  21.7 us
    ppermute x4, starting transfers between devices, with_halo(): lax.ppermute(lax.slice_in_dim(block, block.shape[dim] - width, None, axis...  18.2 us
    all_to_all x1, starting transfers between devices, body(): lax.all_to_all(jnp.broadcast_to(pieces[None], (wide_size, pieces.shape[0]...  17.1 us
    all_to_all x1, waiting for transfers between devices, body(): lax.all_to_all(jnp.broadcast_to(pieces[None], (wide_size, pieces.shape[0]...  11.9 us
    all_to_all x1, blocking collectives, reduce_weight_grads(): lax.all_to_all(jnp.broadcast_to(share, (band_count,) + share.shape[1:]),...  9.49 us
    ppermute x4, starting transfers between devices, with_halo(): lax.ppermute(lax.slice_in_dim(block, 0, width, axis=dim), axis, backward)  8.95 us
    all_to_all x1, waiting for transfers between devices, body(): lax.all_to_all(tagged, 'wide', split_axis=0, concat_axis=0, tiled=True)  7.9 us
  transfers between devices with their start and end apart: 11, of which 3 were waited for; matrix products, arithmetic and copies ran while one was open for 8% of the time, Pallas kernels for 0%

profile of v6, /device:TPU:1, one launch (start us, length us, event | category | flops | bytes accessed | tf_op | source)
XLA Modules:
  0.0 205.0 jit_solution(11628866639131471405)
XLA Ops:
  7.2 0.8 fusion.60
  8.2 0.2 broadcast_in_dim.70
  8.5 0.5 broadcast.169
  9.0 2.0 reduce.6
  11.0 0.9 reshape.262
  12.0 17.1 %all-to-all-start.1 = ((bf16[64,2,864]{2,1,0:T(2,128)(2,1)}), bf16[64,2,864]{2,1,0:T(2,128)(2,1)S(1)}, u32[]{:S(2)}, u32[]{:S(2)}) async-start(bf16[64,2,864]{2,1,0:T(2,128)(2,1)} %reshape.262), calls=%async_computation.1 | async-start | bytes 458752 | tf_op jit(solution)/shard_map/all_to_all | solution.py:199
  29.2 0.2 convert_reduce_fusion.2
  29.5 11.9 %all-to-all-done.1 = bf16[64,2,864]{2,1,0:T(2,128)(2,1)S(1)} async-done(((bf16[64,2,864]{2,1,0:T(2,128)(2,1)}), bf16[64,2,864]{2,1,0:T(2,128)(2,1)S(1)}, u32[]{:S(2)}, u32[]{:S(2)}) %all-to-all-start.1) | async-done | bytes 221216 | tf_op jit(solution)/shard_map/all_to_all | solution.py:199
  41.4 0.3 reshape.263
  41.7 1.4 reduce.1
  43.2 1.6 reshape.215
  44.7 0.2 copy.170
  45.0 1.3 reshape.216
  46.4 0.4 convolution_convert_fusion
  47.0 1.0 reduce.7
  48.0 1.2 reshape.260
  49.2 5.5 %all-to-all-start = ((bf16[64,2,2112]{2,1,0:T(2,128)(2,1)}), bf16[64,2,2112]{2,1,0:T(2,128)(2,1)S(1)}, u32[]{:S(2)}, u32[]{:S(2)}) async-start(bf16[64,2,2112]{2,1,0:T(2,128)(2,1)} %reshape.260), calls=%async_computation | async-start | bytes 1114112 | tf_op jit(solution)/shard_map/all_to_all | solution.py:206
  55.5 5.1 %collective-permute-start.4 = (bf16[5,1,32,128]{3,2,1,0:T(8,128)(2,1)S(1)}, bf16[5,1,32,128]{3,2,1,0:T(8,128)(2,1)S(1)}, u32[]{:S(2)}, u32[]{:S(2)}) collective-permute-start(bf16[5,1,32,128]{3,2,1,0:T(8,128)(2,1)S(1)} %get-tuple-element.39), channel_id=1, source_target_pairs={{0,1},{1,2},{2,3},{3,4},{4,5},{5,6},{6,7},{8,9},{9,10},{10,11},{11... | collective-permute-start | bytes 122888 | tf_op jit(solution)/shard_map/ppermute | solution.py:18
  60.6 1.9 collective-permute-start.5
  62.5 7.9 %all-to-all-done = bf16[64,2,2112]{2,1,0:T(2,128)(2,1)S(1)} async-done(((bf16[64,2,2112]{2,1,0:T(2,128)(2,1)}), bf16[64,2,2112]{2,1,0:T(2,128)(2,1)S(1)}, u32[]{:S(2)}, u32[]{:S(2)}) %all-to-all-start) | async-done | bytes 540704 | tf_op jit(solution)/shard_map/all_to_all | solution.py:206
  70.5 0.6 reshape.261
  71.2 0.2 fusion
  71.6 8.6 %collective-permute-start = (bf16[5,1,32,128]{3,2,1,0:T(8,128)(2,1)S(1)}, bf16[5,1,32,128]{3,2,1,0:T(8,128)(2,1)S(1)}, u32[]{:S(2)}, u32[]{:S(2)}) collective-permute-start(bf16[5,1,32,128]{3,2,1,0:T(8,128)(2,1)S(1)} %get-tuple-element.43), channel_id=1, source_target_pairs={{0,1},{1,2},{2,3},{3,4},{4,5},{5,6},{6,7},{8,9},{9,10},{10,11},{11... | collective-permute-start | bytes 122888 | tf_op jit(solution)/shard_map/ppermute | solution.py:18
  80.2 2.1 %collective-permute-start.1 = (bf16[5,1,32,128]{3,2,1,0:T(8,128)(2,1)S(1)}, bf16[5,1,32,128]{3,2,1,0:T(8,128)(2,1)S(1)}, u32[]{:S(2)}, u32[]{:S(2)}) collective-permute-start(bf16[5,1,32,128]{3,2,1,0:T(8,128)(2,1)S(1)} %get-tuple-element.44), channel_id=1, source_target_pairs={{1,0},{2,1},{3,2},{4,3},{5,4},{6,5},{7,6},{9,8},{10,9},{11,10},{12... | collective-permute-start | bytes 122888 | tf_op jit(solution)/shard_map/ppermute | solution.py:21
  82.3 3.1 %collective-permute-done.1 = bf16[5,1,32,128]{3,2,1,0:T(8,128)(2,1)S(1)} collective-permute-done((bf16[5,1,32,128]{3,2,1,0:T(8,128)(2,1)S(1)}, bf16[5,1,32,128]{3,2,1,0:T(8,128)(2,1)S(1)}, u32[]{:S(2)}, u32[]{:S(2)}) %collective-permute-start.1) | collective-permute-done | bytes 40992 | tf_op jit(solution)/shard_map/ppermute | solution.py:21
  85.5 0.7 maximum_bitcast_fusion.1
  86.2 1.6 fusion.72
  87.8 1.0 copy.177
  88.8 2.5 %fusion.5 = f32[1,7,2,32,128]{4,0,3,2,1:T(1,128)S(1)} fusion(bf16[128,3,3,3,128]{0,4,3,2,1:T(8,128)(2,1)S(1)} %bitcast.131, bf16[1,9,4,32,128]{4,3,2,1,0:T(8,128)(2,1)S(1)} %fusion.33), kind=kOutput, calls=%fused_computation.15 | convolution fusion | flops 388104192 | bytes 1409024 | tf_op jit(solution)/shard_map/conv_general_dilated | solution.py:166
  91.3 1.0 copy.171
  92.3 3.1 %fusion.25 = f32[1,5,2,32,128]{4,0,3,2,1:T(1,128)S(1)} fusion(bf16[128,3,3,3,128]{0,4,3,2,1:T(8,128)(2,1)S(1)} %bitcast.133, bf16[1,7,4,32,128]{4,3,2,1,0:T(8,128)(2,1)} %maximum_bitcast_fusion.1), kind=kOutput, calls=%fused_computation.36 | convolution fusion | flops 277217280 | bytes 1277952 | tf_op jit(solution)/shard_map/conv_general_dilated | solution.py:146
  95.6 0.6 copy-done.2
  96.2 0.6 fusion.75
  96.8 1.9 collective-permute-start.6
  98.8 3.0 %collective-permute-start.7 = (bf16[5,1,32,128]{3,2,1,0:T(8,128)(2,1)}, bf16[5,1,32,128]{3,2,1,0:T(8,128)(2,1)}, u32[]{:S(2)}, u32[]{:S(2)}) collective-permute-start(bf16[5,1,32,128]{3,2,1,0:T(8,128)(2,1)} %get-tuple-element.38), channel_id=1, source_target_pairs={{1,0},{2,1},{3,2},{4,3},{5,4},{6,5},{7,6},{9,8},{10,9},{11,10},{12... | collective-permute-start | bytes 122888 | tf_op jit(solution)/shard_map/ppermute | solution.py:21
  101.8 0.6 fusion.77
  102.4 2.5 %collective-permute-start.2 = (bf16[5,1,32,128]{3,2,1,0:T(8,128)(2,1)}, bf16[5,1,32,128]{3,2,1,0:T(8,128)(2,1)S(1)}, u32[]{:S(2)}, u32[]{:S(2)}) collective-permute-start(bf16[5,1,32,128]{3,2,1,0:T(8,128)(2,1)} %get-tuple-element.41), channel_id=1, source_target_pairs={{0,1},{1,2},{2,3},{3,4},{4,5},{5,6},{6,7},{8,9},{9,10},{10,11},{11... | collective-permute-start | bytes 122888 | tf_op jit(solution)/shard_map/ppermute | solution.py:18
  105.0 1.9 collective-permute-start.3
  107.0 3.7 %fusion.23 = f32[128,3,3,3,128]{0,4,3,2,1:T(8,128)} fusion(bf16[1,7,4,32,128]{4,3,2,1,0:T(8,128)(2,1)S(1)} %copy-done.5, bf16[1,5,2,32,128]{4,3,2,1,0:T(8,128)(2,1)S(1)} %fusion.53), kind=kOutput, calls=%fused_computation.34 | convolution fusion | flops 277217280 | bytes 2080768 | tf_op jit(solution)/shard_map/conv_general_dilated | solution.py:155
  110.7 2.8 %copy.194 = f32[128,3,3,3,128]{4,3,2,1,0:T(4,128)S(1)} copy(f32[128,3,3,3,128]{0,4,3,2,1:T(8,128)} %fusion.23) | data formatting | bytes 3538944 | tf_op jit(solution)/shard_map/conv_general_dilated | solution.py:155
  113.6 1.9 stack.19
  115.5 1.0 fusion.27
  116.5 0.2 copy.207
  117.0 1.2 convolution_select_fusion
  118.4 0.7 pad_maximum_fusion
  119.1 0.8 fusion.65
  120.2 0.9 convolution_select_fusion.1
  121.3 0.7 fusion.55
  122.0 3.7 %fusion.15 = f32[128,3,3,3,128]{0,4,3,2,1:T(8,128)} fusion(bf16[1,7,4,32,128]{4,3,2,1,0:T(8,128)(2,1)S(1)} %get-tuple-element.30, bf16[1,5,2,32,128]{4,3,2,1,0:T(8,128)(2,1)S(1)} %get-tuple-element.25), kind=kOutput, calls=%fused_computation.27 | convolution fusion | flops 277217280 | bytes 2080768 | tf_op jit(solution)/shard_map/conv_general_dilated | solution.py:155
  125.7 2.8 %copy.197 = f32[128,3,3,3,128]{4,3,2,1,0:T(4,128)S(1)} copy(f32[128,3,3,3,128]{0,4,3,2,1:T(8,128)} %fusion.15) | data formatting | bytes 3538944 | tf_op jit(solution)/shard_map/conv_general_dilated | solution.py:155
  128.6 1.9 stack.20
  130.5 2.3 %fusion.2 = bf16[8,2,16,3456]{3,2,0,1:T(8,128)(2,1)S(1)} fusion(f32[1,8,16,3456]{3,2,1,0:T(8,128)} %stack.20, f32[1,8,16,3456]{3,2,1,0:T(8,128)} %stack.19), kind=kLoop, calls=%fused_computation.6 | loop fusion | flops 2654208 | bytes 5308416 | tf_op jit(solution)/shard_map/transpose | solution.py:124
  132.9 27.7 %all_to_all.29 = bf16[8,2,16,3456]{3,2,1,0:T(8,128)(2,1)S(1)} all-to-all(bf16[8,2,16,3456]{3,2,1,0:T(8,128)(2,1)S(1)} %copy.198), channel_id=1, replica_groups=mesh['wide'=64,'rows'=8] {'rows'}, dimensions={0} | all-to-all | bytes 3538944 | tf_op jit(solution)/shard_map/all_to_all | solution.py:125
  160.6 0.2 convert_reduce_fusion
  160.9 1.4 reshape.217
  162.3 0.6 copy.199
  163.0 0.6 reshape.218
  163.5 0.9 copy.211
  164.4 21.7 %shard_map.102 = f32[16,128]{1,0:T(8,128)} custom-call(f32[64,16,128]{2,1,0:T(8,128)} %bitcast.125), custom_call_target="tpu_custom_call" | custom-call | tf_op jit(solution)/shard_map/pallas_call | solution.py:105
  186.2 0.7 slice_reduce_fusion
  186.9 9.5 %all_to_all.30 = f32[8,1,1728]{2,1,0:T(1,128)S(1)} all-to-all(f32[8,1,1728]{2,1,0:T(1,128)S(1)} %broadcast_in_dim.78), channel_id=1, replica_groups=mesh['wide'=64,'rows'=8] {'rows'}, dimensions={0} | all-to-all | bytes 110592 | tf_op jit(solution)/shard_map/all_to_all | solution.py:134
  196.5 0.2 reshape.221
  196.8 0.7 copy.201
  197.4 0.7 copy.200
  (77 shorter events, 2.4 us)
Async XLA Ops:
  7.2 22.0 %copy-start.7 = (s32[1,1,10]{2,1,0:T(1,128)S(1)}, s32[1,1,10]{2,1,0:T(1,128)}, u32[]{:S(2)}) copy-start(s32[1,1,10]{2,1,0:T(1,128)} %param.9) | copy-start | bytes 124
  7.2 22.0 %copy-start.8 = (s32[1,1,10]{2,1,0:T(1,128)S(1)}, s32[1,1,10]{2,1,0:T(1,128)}, u32[]{:S(2)}) copy-start(s32[1,1,10]{2,1,0:T(1,128)} %param.8) | copy-start | bytes 124
  12.0 29.4 %all-to-all-start.1 = ((bf16[64,2,864]{2,1,0:T(2,128)(2,1)}), bf16[64,2,864]{2,1,0:T(2,128)(2,1)S(1)}, u32[]{:S(2)}, u32[]{:S(2)}) async-start(bf16[64,2,864]{2,1,0:T(2,128)(2,1)} %reshape.262), calls=%async_computation.1 | async-start | bytes 458752 | tf_op jit(solution)/shard_map/all_to_all | solution.py:199
  29.1 57.1 %all-gather.2.cloned.1.call-start = ((), (), s32[]{:S(2)}) async-start(), calls=%async_computation.4 | async-start | bytes 1990656 | tf_op jit(solution)/shard_map/all_gather | solution.py:45
  41.7 4.6 %copy-start.6 = (bf16[1,1,10,32,128]{4,3,2,1,0:T(8,128)(2,1)S(1)}, bf16[1,1,10,32,128]{4,3,2,1,0:T(8,128)(2,1)}, u32[]{:S(2)}) copy-start(bf16[1,1,10,32,128]{4,3,2,1,0:T(8,128)(2,1)} %param.7) | copy-start | bytes 245764
  47.0 8.4 %copy-start.3 = (bf16[1,5,2,32,128]{4,3,2,1,0:T(8,128)(2,1)S(1)}, bf16[1,5,2,32,128]{4,3,2,1,0:T(8,128)(2,1)}, u32[]{:S(2)}) copy-start(bf16[1,5,2,32,128]{4,3,2,1,0:T(8,128)(2,1)} %param.11) | copy-start | bytes 245764
  49.2 21.3 %all-to-all-start = ((bf16[64,2,2112]{2,1,0:T(2,128)(2,1)}), bf16[64,2,2112]{2,1,0:T(2,128)(2,1)S(1)}, u32[]{:S(2)}, u32[]{:S(2)}) async-start(bf16[64,2,2112]{2,1,0:T(2,128)(2,1)} %reshape.260), calls=%async_computation | async-start | bytes 1114112 | tf_op jit(solution)/shard_map/all_to_all | solution.py:206
  55.5 26.8 %collective-permute-start.4 = (bf16[5,1,32,128]{3,2,1,0:T(8,128)(2,1)S(1)}, bf16[5,1,32,128]{3,2,1,0:T(8,128)(2,1)S(1)}, u32[]{:S(2)}, u32[]{:S(2)}) collective-permute-start(bf16[5,1,32,128]{3,2,1,0:T(8,128)(2,1)S(1)} %get-tuple-element.39), channel_id=1, source_target_pairs={{0,1},{1,2},{2,3},{3,4},{4,5},{5,6},{6,7},{8,9},{9,10},{10,11},{11... | collective-permute-start | bytes 122888 | tf_op jit(solution)/shard_map/ppermute | solution.py:18
  60.6 21.7 %collective-permute-start.5 = (bf16[5,1,32,128]{3,2,1,0:T(8,128)(2,1)S(1)}, bf16[5,1,32,128]{3,2,1,0:T(8,128)(2,1)S(1)}, u32[]{:S(2)}, u32[]{:S(2)}) collective-permute-start(bf16[5,1,32,128]{3,2,1,0:T(8,128)(2,1)S(1)} %get-tuple-element.40), channel_id=1, source_target_pairs={{1,0},{2,1},{3,2},{4,3},{5,4},{6,5},{7,6},{9,8},{10,9},{11,10},{12... | collective-permute-start | bytes 122888 | tf_op jit(solution)/shard_map/ppermute | solution.py:21
  71.6 10.7 %collective-permute-start = (bf16[5,1,32,128]{3,2,1,0:T(8,128)(2,1)S(1)}, bf16[5,1,32,128]{3,2,1,0:T(8,128)(2,1)S(1)}, u32[]{:S(2)}, u32[]{:S(2)}) collective-permute-start(bf16[5,1,32,128]{3,2,1,0:T(8,128)(2,1)S(1)} %get-tuple-element.43), channel_id=1, source_target_pairs={{0,1},{1,2},{2,3},{3,4},{4,5},{5,6},{6,7},{8,9},{9,10},{10,11},{11... | collective-permute-start | bytes 122888 | tf_op jit(solution)/shard_map/ppermute | solution.py:18
  80.2 5.3 %collective-permute-start.1 = (bf16[5,1,32,128]{3,2,1,0:T(8,128)(2,1)S(1)}, bf16[5,1,32,128]{3,2,1,0:T(8,128)(2,1)S(1)}, u32[]{:S(2)}, u32[]{:S(2)}) collective-permute-start(bf16[5,1,32,128]{3,2,1,0:T(8,128)(2,1)S(1)} %get-tuple-element.44), channel_id=1, source_target_pairs={{1,0},{2,1},{3,2},{4,3},{5,4},{6,5},{7,6},{9,8},{10,9},{11,10},{12... | collective-permute-start | bytes 122888 | tf_op jit(solution)/shard_map/ppermute | solution.py:21
  92.3 3.1 %copy-start = (bf16[1,128,3456]{1,2,0:T(8,128)(2,1)}, bf16[1,128,3456]{1,2,0:T(8,128)(2,1)S(1)}, u32[]{:S(2)}) copy-start(bf16[1,128,3456]{1,2,0:T(8,128)(2,1)S(1)} %copy.171) | copy-start | bytes 2654212
  92.3 14.7 %copy-start.5 = (bf16[1,7,4,32,128]{4,3,2,1,0:T(8,128)(2,1)S(1)}, bf16[1,7,4,32,128]{4,3,2,1,0:T(8,128)(2,1)}, u32[]{:S(2)}) copy-start(bf16[1,7,4,32,128]{4,3,2,1,0:T(8,128)(2,1)} %maximum_bitcast_fusion.1) | copy-start | bytes 688132
  95.6 0.6 copy-start.2
  96.8 18.7 %collective-permute-start.6 = (bf16[5,1,32,128]{3,2,1,0:T(8,128)(2,1)}, bf16[5,1,32,128]{3,2,1,0:T(8,128)(2,1)}, u32[]{:S(2)}, u32[]{:S(2)}) collective-permute-start(bf16[5,1,32,128]{3,2,1,0:T(8,128)(2,1)} %get-tuple-element.37), channel_id=1, source_target_pairs={{0,1},{1,2},{2,3},{3,4},{4,5},{5,6},{6,7},{8,9},{9,10},{10,11},{11... | collective-permute-start | bytes 122888 | tf_op jit(solution)/shard_map/ppermute | solution.py:18
  98.8 16.7 %collective-permute-start.7 = (bf16[5,1,32,128]{3,2,1,0:T(8,128)(2,1)}, bf16[5,1,32,128]{3,2,1,0:T(8,128)(2,1)}, u32[]{:S(2)}, u32[]{:S(2)}) collective-permute-start(bf16[5,1,32,128]{3,2,1,0:T(8,128)(2,1)} %get-tuple-element.38), channel_id=1, source_target_pairs={{1,0},{2,1},{3,2},{4,3},{5,4},{6,5},{7,6},{9,8},{10,9},{11,10},{12... | collective-permute-start | bytes 122888 | tf_op jit(solution)/shard_map/ppermute | solution.py:21
  102.4 15.9 %collective-permute-start.2 = (bf16[5,1,32,128]{3,2,1,0:T(8,128)(2,1)}, bf16[5,1,32,128]{3,2,1,0:T(8,128)(2,1)S(1)}, u32[]{:S(2)}, u32[]{:S(2)}) collective-permute-start(bf16[5,1,32,128]{3,2,1,0:T(8,128)(2,1)} %get-tuple-element.41), channel_id=1, source_target_pairs={{0,1},{1,2},{2,3},{3,4},{4,5},{5,6},{6,7},{8,9},{9,10},{10,11},{11... | collective-permute-start | bytes 122888 | tf_op jit(solution)/shard_map/ppermute | solution.py:18
  105.0 13.4 %collective-permute-start.3 = (bf16[5,1,32,128]{3,2,1,0:T(8,128)(2,1)}, bf16[5,1,32,128]{3,2,1,0:T(8,128)(2,1)}, u32[]{:S(2)}, u32[]{:S(2)}) collective-permute-start(bf16[5,1,32,128]{3,2,1,0:T(8,128)(2,1)} %get-tuple-element.42), channel_id=1, source_target_pairs={{1,0},{2,1},{3,2},{4,3},{5,4},{6,5},{7,6},{9,8},{10,9},{11,10},{12... | collective-permute-start | bytes 122888 | tf_op jit(solution)/shard_map/ppermute | solution.py:21
  115.5 1.4 copy-start.1
  115.5 1.5 copy-start.9
  120.2 1.0 copy-start.4
Sparse Core Ops, SparseCore 0:
  46.4 24.9 all-gather.1

commit v7 on v4

--- a/solution.py
+++ b/solution.py
@@ -1,8 +1,12 @@
+import functools
 import math
+
 
 import jax
 import jax.numpy as jnp
 from jax import lax
+from jax.experimental import pallas as pl
+from jax.experimental.pallas import tpu as pltpu
 from jax.sharding import PartitionSpec as P
 
 
@@ -42,6 +46,100 @@
     return full[0], full[1]
 
 
+def _wide_sum_kernel(outer, inner, x_ref, o_ref, recv1, part, recv2, send1, got1, send2, got2):
+    me = lax.axis_index("wide")
+    band = lax.axis_index("rows")
+    my_o = me // inner
+    my_i = lax.rem(me, inner)
+    mesh_id = pl.DeviceIdType.MESH
+    barrier = pltpu.get_barrier_semaphore()
+
+    def greet_inner(k, carry):
+        peer = my_o * inner + lax.rem(my_i + k, inner)
+        pl.semaphore_signal(barrier, 1, device_id=(peer, band), device_id_type=mesh_id)
+        return carry
+
+    def greet_outer(k, carry):
+        peer = lax.rem(my_o + k, outer) * inner + my_i
+        pl.semaphore_signal(barrier, 1, device_id=(peer, band), device_id_type=mesh_id)
+        return carry
+
+    lax.fori_loop(1, inner, greet_inner, 0)
+    lax.fori_loop(1, outer, greet_outer, 0)
+    pl.semaphore_wait(barrier, inner + outer - 2)
+
+    def first_copy(peer_i, slot):
+        return pltpu.make_async_remote_copy(
+            src_ref=x_ref.at[peer_i],
+            dst_ref=recv1.at[slot],
+            send_sem=send1.at[peer_i],
+            recv_sem=got1.at[slot],
+            device_id=(my_o * inner + peer_i, band),
+            device_id_type=mesh_id,
+        )
+
+    def send_first(k, carry):
+        first_copy(lax.rem(my_i + k, inner), my_i).start()
+        return carry
+
+    lax.fori_loop(1, inner, send_first, 0)
+
+    def finish_first(k, total):
+        first_copy(lax.rem(my_i + k, inner), my_i).wait_send()
+        source = lax.rem(my_i + inner - k, inner)
+        first_copy(source, source).wait_recv()
+        return total + recv1[source]
+
+    part[...] = lax.fori_loop(1, inner, finish_first, x_ref[my_i])
+
+    def second_copy(peer_o, slot):
+        return pltpu.make_async_remote_copy(
+            src_ref=part.at[peer_o],
+            dst_ref=recv2.at[slot],
+            send_sem=send2.at[peer_o],
+            recv_sem=got2.at[slot],
+            device_id=(peer_o * inner + my_i, band),
+            device_id_type=mesh_id,
+        )
+
+    def send_second(k, carry):
+        second_copy(lax.rem(my_o + k, outer), my_o).start()
+        return carry
+
+    lax.fori_loop(1, outer, send_second, 0)
+
+    def finish_second(k, total):
+        second_copy(lax.rem(my_o + k, outer), my_o).wait_send()
+        source = lax.rem(my_o + outer - k, outer)
+        second_copy(source, source).wait_recv()
+        return total + recv2[source]
+
+    o_ref[...] = lax.fori_loop(1, outer, finish_second, part[my_o])
+
+
+def wide_sum(pieces):
+    count, tall, lanes = pieces.shape
+    inner = 8 if count % 8 == 0 else 1
+    outer = count // inner
+    arranged = jnp.transpose(pieces.reshape(outer, inner, tall, lanes), (1, 0, 2, 3))
+    return pl.pallas_call(
+        functools.partial(_wide_sum_kernel, outer, inner),
+        out_shape=jax.ShapeDtypeStruct((tall, lanes), pieces.dtype),
+        in_specs=[pl.BlockSpec(memory_space=pltpu.VMEM)],
+        out_specs=pl.BlockSpec(memory_space=pltpu.VMEM),
+        scratch_shapes=[
+            pltpu.VMEM((inner, outer, tall, lanes), pieces.dtype),
+            pltpu.VMEM((outer, tall, lanes), pieces.dtype),
+            pltpu.VMEM((outer, tall, lanes), pieces.dtype),
+            pltpu.SemaphoreType.DMA((inner,)),
+            pltpu.SemaphoreType.DMA((inner,)),
+            pltpu.SemaphoreType.DMA((outer,)),
+            pltpu.SemaphoreType.DMA((outer,)),
+        ],
+        compiler_params=pltpu.CompilerParams(collective_id=0, has_side_effects=True),
+    )(arranged)
+
+
 def reduce_weight_grads(grad_t, band_count, wide_size):
     _, channels, total_rows = grad_t.shape
     part = channels // band_count
@@ -52,8 +150,11 @@
     band_sum = jnp.sum(band_parts.astype(jnp.float32), axis=0)
     band_sum = band_sum.reshape(2, part, wide_size, chunk)
     band_sum = jnp.transpose(band_sum, (2, 0, 1, 3)).reshape(wide_size, 2 * part * chunk)
-    wide_parts = lax.all_to_all(band_sum, "wide", 0, 0, tiled=True)
-    share = jnp.sum(wide_parts, axis=0, keepdims=True)
+    size = band_sum.shape[1]
+    lanes = 128
+    tall = -(-size // (8 * lanes)) * 8
+    padded = jnp.pad(band_sum, ((0, 0), (0, tall * lanes - size)))
+    share = wide_sum(padded.reshape(wide_size, tall, lanes)).reshape(1, tall * lanes)[:, :size]
     joined = lax.all_to_all(
         jnp.broadcast_to(share, (band_count,) + share.shape[1:]), "rows", 0, 0, tiled=True
     )

time: 205 us -> 207 us (level)
  Pallas kernels: 0 us -> 22.3 us
  blocking collectives: 59 us -> 37.3 us
  matrix products: 13.3 us -> 15.7 us
    pallas_call x0 -> x1, Pallas kernels: none -> 22.3 us  [wide_sum(): pl.pallas_call(functools.partial(_wide_sum_kernel, outer, inner), out_sha...]
    all_to_all x1 -> x0, blocking collectives: 20.2 us -> none  [reduce_weight_grads(): wide_parts = lax.all_to_all(band_sum, 'wide', 0, 0, tiled=True)]
    unnamed x45 -> x36, local copies, waits for them, and re-layouts: 6.64 us -> 5.64 us
  transfers between devices with their start and end apart: 11 -> 11, of which waited for: 3 -> 3; matrix products, arithmetic and copies ran while one was open for 9% -> 8% of each run, Pallas kernels for 0% -> 0%
where the time goes in v7:
time: 207 us; the launch traced here: 206 us
  starting transfers between devices  49.8 us (24%)
  blocking collectives  37.3 us (18%)
  local copies, waits for them, and re-layouts  29.4 us (14%)
  waiting for transfers between devices  23 us (11%)
  Pallas kernels  22.3 us (11%)
  matrix products  15.7 us (8%)
  between operations  15.4 us (7%)
  other arithmetic  12.8 us (6%)
    all_to_all x1, blocking collectives, reduce_weight_grads(): band_parts = lax.all_to_all(blocks, 'rows', 0, 0, tiled=True)  27.7 us
    pallas_call x1, Pallas kernels, wide_sum(): pl.pallas_call(functools.partial(_wide_sum_kernel, outer, inner), out_sha...  22.3 us
    ppermute x4, starting transfers between devices, with_halo(): lax.ppermute(lax.slice_in_dim(block, block.shape[dim] - width, None, axis...  18.2 us
    all_to_all x1, starting transfers between devices, body(): lax.all_to_all(jnp.broadcast_to(pieces[None], (wide_size, pieces.shape[0]...  17.1 us
    all_to_all x1, waiting for transfers between devices, body(): lax.all_to_all(jnp.broadcast_to(pieces[None], (wide_size, pieces.shape[0]...  11.9 us
    all_to_all x1, blocking collectives, reduce_weight_grads(): lax.all_to_all(jnp.broadcast_to(share, (band_count,) + share.shape[1:]),...  9.54 us
    ppermute x4, starting transfers between devices, with_halo(): lax.ppermute(lax.slice_in_dim(block, 0, width, axis=dim), axis, backward)  8.95 us
    all_to_all x1, waiting for transfers between devices, body(): lax.all_to_all(tagged, 'wide', split_axis=0, concat_axis=0, tiled=True)  7.9 us
  transfers between devices with their start and end apart: 11, of which 3 were waited for; matrix products, arithmetic and copies ran while one was open for 8% of the time, Pallas kernels for 0%

profile of v7, /device:TPU:1, one launch (start us, length us, event | category | flops | bytes accessed | tf_op | source)
XLA Modules:
  0.0 205.7 jit_solution(4808890177423122930)
XLA Ops:
  7.2 0.8 fusion.60
  8.2 0.2 broadcast_in_dim.70
  8.5 0.5 broadcast.169
  9.0 2.0 reduce.6
  11.0 0.9 reshape.258
  12.0 17.1 %all-to-all-start.1 = ((bf16[64,2,864]{2,1,0:T(2,128)(2,1)}), bf16[64,2,864]{2,1,0:T(2,128)(2,1)S(1)}, u32[]{:S(2)}, u32[]{:S(2)}) async-start(bf16[64,2,864]{2,1,0:T(2,128)(2,1)} %reshape.258), calls=%async_computation.1 | async-start | bytes 458752 | tf_op jit(solution)/shard_map/all_to_all | solution.py:223
  29.2 0.2 convert_reduce_fusion.2
  29.5 11.9 %all-to-all-done.1 = bf16[64,2,864]{2,1,0:T(2,128)(2,1)S(1)} async-done(((bf16[64,2,864]{2,1,0:T(2,128)(2,1)}), bf16[64,2,864]{2,1,0:T(2,128)(2,1)S(1)}, u32[]{:S(2)}, u32[]{:S(2)}) %all-to-all-start.1) | async-done | bytes 221216 | tf_op jit(solution)/shard_map/all_to_all | solution.py:223
  41.4 0.3 reshape.259
  41.7 1.4 reduce.1
  43.2 1.6 reshape.212
  44.7 0.2 copy.174
  45.0 1.3 reshape.213
  46.4 0.4 convolution_convert_fusion
  47.0 1.0 reduce.7
  48.0 1.2 reshape.256
  49.2 5.5 %all-to-all-start = ((bf16[64,2,2112]{2,1,0:T(2,128)(2,1)}), bf16[64,2,2112]{2,1,0:T(2,128)(2,1)S(1)}, u32[]{:S(2)}, u32[]{:S(2)}) async-start(bf16[64,2,2112]{2,1,0:T(2,128)(2,1)} %reshape.256), calls=%async_computation | async-start | bytes 1114112 | tf_op jit(solution)/shard_map/all_to_all | solution.py:230
  55.5 5.1 %collective-permute-start.4 = (bf16[5,1,32,128]{3,2,1,0:T(8,128)(2,1)S(1)}, bf16[5,1,32,128]{3,2,1,0:T(8,128)(2,1)S(1)}, u32[]{:S(2)}, u32[]{:S(2)}) collective-permute-start(bf16[5,1,32,128]{3,2,1,0:T(8,128)(2,1)S(1)} %get-tuple-element.39), channel_id=1, source_target_pairs={{0,1},{1,2},{2,3},{3,4},{4,5},{5,6},{6,7},{8,9},{9,10},{10,11},{11... | collective-permute-start | bytes 122888 | tf_op jit(solution)/shard_map/ppermute | solution.py:18
  60.6 1.9 collective-permute-start.5
  62.5 7.9 %all-to-all-done = bf16[64,2,2112]{2,1,0:T(2,128)(2,1)S(1)} async-done(((bf16[64,2,2112]{2,1,0:T(2,128)(2,1)}), bf16[64,2,2112]{2,1,0:T(2,128)(2,1)S(1)}, u32[]{:S(2)}, u32[]{:S(2)}) %all-to-all-start) | async-done | bytes 540704 | tf_op jit(solution)/shard_map/all_to_all | solution.py:230
  70.5 0.6 reshape.257
  71.2 0.2 fusion
  71.6 8.6 %collective-permute-start = (bf16[5,1,32,128]{3,2,1,0:T(8,128)(2,1)S(1)}, bf16[5,1,32,128]{3,2,1,0:T(8,128)(2,1)S(1)}, u32[]{:S(2)}, u32[]{:S(2)}) collective-permute-start(bf16[5,1,32,128]{3,2,1,0:T(8,128)(2,1)S(1)} %get-tuple-element.43), channel_id=1, source_target_pairs={{0,1},{1,2},{2,3},{3,4},{4,5},{5,6},{6,7},{8,9},{9,10},{10,11},{11... | collective-permute-start | bytes 122888 | tf_op jit(solution)/shard_map/ppermute | solution.py:18
  80.2 2.1 %collective-permute-start.1 = (bf16[5,1,32,128]{3,2,1,0:T(8,128)(2,1)S(1)}, bf16[5,1,32,128]{3,2,1,0:T(8,128)(2,1)S(1)}, u32[]{:S(2)}, u32[]{:S(2)}) collective-permute-start(bf16[5,1,32,128]{3,2,1,0:T(8,128)(2,1)S(1)} %get-tuple-element.44), channel_id=1, source_target_pairs={{1,0},{2,1},{3,2},{4,3},{5,4},{6,5},{7,6},{9,8},{10,9},{11,10},{12... | collective-permute-start | bytes 122888 | tf_op jit(solution)/shard_map/ppermute | solution.py:21
  82.3 3.1 %collective-permute-done.1 = bf16[5,1,32,128]{3,2,1,0:T(8,128)(2,1)S(1)} collective-permute-done((bf16[5,1,32,128]{3,2,1,0:T(8,128)(2,1)S(1)}, bf16[5,1,32,128]{3,2,1,0:T(8,128)(2,1)S(1)}, u32[]{:S(2)}, u32[]{:S(2)}) %collective-permute-start.1) | collective-permute-done | bytes 40992 | tf_op jit(solution)/shard_map/ppermute | solution.py:21
  85.5 0.7 maximum_bitcast_fusion.1
  86.2 1.6 fusion.72
  87.8 1.0 copy.181
  88.8 2.5 %fusion.5 = f32[1,7,2,32,128]{4,0,3,2,1:T(1,128)S(1)} fusion(bf16[128,3,3,3,128]{0,4,3,2,1:T(8,128)(2,1)S(1)} %bitcast.135, bf16[1,9,4,32,128]{4,3,2,1,0:T(8,128)(2,1)S(1)} %fusion.33), kind=kOutput, calls=%fused_computation.15 | convolution fusion | flops 388104192 | bytes 1409024 | tf_op jit(solution)/shard_map/conv_general_dilated | solution.py:190
  91.3 1.0 copy.175
  92.3 3.1 %fusion.25 = f32[1,5,2,32,128]{4,0,3,2,1:T(1,128)S(1)} fusion(bf16[128,3,3,3,128]{0,4,3,2,1:T(8,128)(2,1)S(1)} %bitcast.137, bf16[1,7,4,32,128]{4,3,2,1,0:T(8,128)(2,1)} %maximum_bitcast_fusion.1), kind=kOutput, calls=%fused_computation.38 | convolution fusion | flops 277217280 | bytes 1277952 | tf_op jit(solution)/shard_map/conv_general_dilated | solution.py:170
  95.6 0.6 copy-done.2
  96.2 0.6 fusion.75
  96.8 1.9 collective-permute-start.6
  98.8 3.0 %collective-permute-start.7 = (bf16[5,1,32,128]{3,2,1,0:T(8,128)(2,1)}, bf16[5,1,32,128]{3,2,1,0:T(8,128)(2,1)}, u32[]{:S(2)}, u32[]{:S(2)}) collective-permute-start(bf16[5,1,32,128]{3,2,1,0:T(8,128)(2,1)} %get-tuple-element.38), channel_id=1, source_target_pairs={{1,0},{2,1},{3,2},{4,3},{5,4},{6,5},{7,6},{9,8},{10,9},{11,10},{12... | collective-permute-start | bytes 122888 | tf_op jit(solution)/shard_map/ppermute | solution.py:21
  101.8 0.6 fusion.77
  102.4 2.5 %collective-permute-start.2 = (bf16[5,1,32,128]{3,2,1,0:T(8,128)(2,1)}, bf16[5,1,32,128]{3,2,1,0:T(8,128)(2,1)S(1)}, u32[]{:S(2)}, u32[]{:S(2)}) collective-permute-start(bf16[5,1,32,128]{3,2,1,0:T(8,128)(2,1)} %get-tuple-element.41), channel_id=1, source_target_pairs={{0,1},{1,2},{2,3},{3,4},{4,5},{5,6},{6,7},{8,9},{9,10},{10,11},{11... | collective-permute-start | bytes 122888 | tf_op jit(solution)/shard_map/ppermute | solution.py:18
  105.0 1.9 collective-permute-start.3
  107.0 3.7 %fusion.23 = f32[128,3,3,3,128]{0,4,3,2,1:T(8,128)} fusion(bf16[1,7,4,32,128]{4,3,2,1,0:T(8,128)(2,1)S(1)} %copy-done.5, bf16[1,5,2,32,128]{4,3,2,1,0:T(8,128)(2,1)S(1)} %fusion.53), kind=kOutput, calls=%fused_computation.36 | convolution fusion | flops 277217280 | bytes 2080768 | tf_op jit(solution)/shard_map/conv_general_dilated | solution.py:179
  110.7 2.8 %copy.198 = f32[128,3,3,3,128]{4,3,2,1,0:T(4,128)S(1)} copy(f32[128,3,3,3,128]{0,4,3,2,1:T(8,128)} %fusion.23) | data formatting | bytes 3538944 | tf_op jit(solution)/shard_map/conv_general_dilated | solution.py:179
  113.6 1.9 stack.19
  115.5 1.0 fusion.27
  116.5 0.2 copy.212
  117.0 1.2 convolution_select_fusion
  118.4 0.7 pad_maximum_fusion
  119.1 0.8 fusion.65
  120.2 0.9 convolution_select_fusion.1
  121.3 0.7 fusion.55
  122.0 3.7 %fusion.15 = f32[128,3,3,3,128]{0,4,3,2,1:T(8,128)} fusion(bf16[1,7,4,32,128]{4,3,2,1,0:T(8,128)(2,1)S(1)} %get-tuple-element.30, bf16[1,5,2,32,128]{4,3,2,1,0:T(8,128)(2,1)S(1)} %get-tuple-element.25), kind=kOutput, calls=%fused_computation.29 | convolution fusion | flops 277217280 | bytes 2080768 | tf_op jit(solution)/shard_map/conv_general_dilated | solution.py:179
  125.7 2.8 %copy.201 = f32[128,3,3,3,128]{4,3,2,1,0:T(4,128)S(1)} copy(f32[128,3,3,3,128]{0,4,3,2,1:T(8,128)} %fusion.15) | data formatting | bytes 3538944 | tf_op jit(solution)/shard_map/conv_general_dilated | solution.py:179
  128.6 1.9 stack.20
  130.5 2.3 %fusion.2 = bf16[8,2,16,3456]{3,2,0,1:T(8,128)(2,1)S(1)} fusion(f32[1,8,16,3456]{3,2,1,0:T(8,128)} %stack.20, f32[1,8,16,3456]{3,2,1,0:T(8,128)} %stack.19), kind=kLoop, calls=%fused_computation.6 | loop fusion | flops 2654208 | bytes 5308416 | tf_op jit(solution)/shard_map/transpose | solution.py:148
  132.9 27.7 %all_to_all.29 = bf16[8,2,16,3456]{3,2,1,0:T(8,128)(2,1)S(1)} all-to-all(bf16[8,2,16,3456]{3,2,1,0:T(8,128)(2,1)S(1)} %copy.202), channel_id=1, replica_groups=mesh['wide'=64,'rows'=8] {'rows'}, dimensions={0} | all-to-all | bytes 3538944 | tf_op jit(solution)/shard_map/all_to_all | solution.py:149
  160.6 0.2 convert_reduce_fusion
  160.9 1.4 reshape.214
  162.3 0.6 copy.203
  163.0 0.6 reshape.215
  163.5 0.9 copy_bitcast_fusion.2.x_ref
  164.4 22.3 %shard_map.102 = f32[16,128]{1,0:T(8,128)} custom-call(f32[8,8,16,128]{3,2,1,0:T(8,128)} %copy_bitcast_fusion.2.x_ref), custom_call_target="tpu_custom_call" | custom-call | tf_op jit(solution)/shard_map/pallas_call | solution.py:125
  186.8 0.7 slice_reduce_fusion
  187.6 9.5 %all_to_all.30 = f32[8,1,1728]{2,1,0:T(1,128)S(1)} all-to-all(f32[8,1,1728]{2,1,0:T(1,128)S(1)} %broadcast_in_dim.78), channel_id=1, replica_groups=mesh['wide'=64,'rows'=8] {'rows'}, dimensions={0} | all-to-all | bytes 110592 | tf_op jit(solution)/shard_map/all_to_all | solution.py:158
  197.2 0.2 reshape.217
  197.5 0.7 copy.206
  198.1 0.7 copy.205
  (77 shorter events, 2.4 us)
Async XLA Ops:
  7.2 22.0 %copy-start.7 = (s32[1,1,10]{2,1,0:T(1,128)S(1)}, s32[1,1,10]{2,1,0:T(1,128)}, u32[]{:S(2)}) copy-start(s32[1,1,10]{2,1,0:T(1,128)} %param.9) | copy-start | bytes 124
  7.2 22.0 %copy-start.8 = (s32[1,1,10]{2,1,0:T(1,128)S(1)}, s32[1,1,10]{2,1,0:T(1,128)}, u32[]{:S(2)}) copy-start(s32[1,1,10]{2,1,0:T(1,128)} %param.8) | copy-start | bytes 124
  12.0 29.4 %all-to-all-start.1 = ((bf16[64,2,864]{2,1,0:T(2,128)(2,1)}), bf16[64,2,864]{2,1,0:T(2,128)(2,1)S(1)}, u32[]{:S(2)}, u32[]{:S(2)}) async-start(bf16[64,2,864]{2,1,0:T(2,128)(2,1)} %reshape.258), calls=%async_computation.1 | async-start | bytes 458752 | tf_op jit(solution)/shard_map/all_to_all | solution.py:223
  29.1 57.1 %all-gather.2.cloned.1.call-start = ((), (), s32[]{:S(2)}) async-start(), calls=%async_computation.4 | async-start | bytes 1990656 | tf_op jit(solution)/shard_map/all_gather | solution.py:45
  41.7 4.6 %copy-start.6 = (bf16[1,1,10,32,128]{4,3,2,1,0:T(8,128)(2,1)S(1)}, bf16[1,1,10,32,128]{4,3,2,1,0:T(8,128)(2,1)}, u32[]{:S(2)}) copy-start(bf16[1,1,10,32,128]{4,3,2,1,0:T(8,128)(2,1)} %param.7) | copy-start | bytes 245764
  47.0 8.4 %copy-start.3 = (bf16[1,5,2,32,128]{4,3,2,1,0:T(8,128)(2,1)S(1)}, bf16[1,5,2,32,128]{4,3,2,1,0:T(8,128)(2,1)}, u32[]{:S(2)}) copy-start(bf16[1,5,2,32,128]{4,3,2,1,0:T(8,128)(2,1)} %param.11) | copy-start | bytes 245764
  49.2 21.3 %all-to-all-start = ((bf16[64,2,2112]{2,1,0:T(2,128)(2,1)}), bf16[64,2,2112]{2,1,0:T(2,128)(2,1)S(1)}, u32[]{:S(2)}, u32[]{:S(2)}) async-start(bf16[64,2,2112]{2,1,0:T(2,128)(2,1)} %reshape.256), calls=%async_computation | async-start | bytes 1114112 | tf_op jit(solution)/shard_map/all_to_all | solution.py:230
  55.5 26.8 %collective-permute-start.4 = (bf16[5,1,32,128]{3,2,1,0:T(8,128)(2,1)S(1)}, bf16[5,1,32,128]{3,2,1,0:T(8,128)(2,1)S(1)}, u32[]{:S(2)}, u32[]{:S(2)}) collective-permute-start(bf16[5,1,32,128]{3,2,1,0:T(8,128)(2,1)S(1)} %get-tuple-element.39), channel_id=1, source_target_pairs={{0,1},{1,2},{2,3},{3,4},{4,5},{5,6},{6,7},{8,9},{9,10},{10,11},{11... | collective-permute-start | bytes 122888 | tf_op jit(solution)/shard_map/ppermute | solution.py:18
  60.6 21.7 %collective-permute-start.5 = (bf16[5,1,32,128]{3,2,1,0:T(8,128)(2,1)S(1)}, bf16[5,1,32,128]{3,2,1,0:T(8,128)(2,1)S(1)}, u32[]{:S(2)}, u32[]{:S(2)}) collective-permute-start(bf16[5,1,32,128]{3,2,1,0:T(8,128)(2,1)S(1)} %get-tuple-element.40), channel_id=1, source_target_pairs={{1,0},{2,1},{3,2},{4,3},{5,4},{6,5},{7,6},{9,8},{10,9},{11,10},{12... | collective-permute-start | bytes 122888 | tf_op jit(solution)/shard_map/ppermute | solution.py:21
  71.6 10.7 %collective-permute-start = (bf16[5,1,32,128]{3,2,1,0:T(8,128)(2,1)S(1)}, bf16[5,1,32,128]{3,2,1,0:T(8,128)(2,1)S(1)}, u32[]{:S(2)}, u32[]{:S(2)}) collective-permute-start(bf16[5,1,32,128]{3,2,1,0:T(8,128)(2,1)S(1)} %get-tuple-element.43), channel_id=1, source_target_pairs={{0,1},{1,2},{2,3},{3,4},{4,5},{5,6},{6,7},{8,9},{9,10},{10,11},{11... | collective-permute-start | bytes 122888 | tf_op jit(solution)/shard_map/ppermute | solution.py:18
  80.2 5.3 %collective-permute-start.1 = (bf16[5,1,32,128]{3,2,1,0:T(8,128)(2,1)S(1)}, bf16[5,1,32,128]{3,2,1,0:T(8,128)(2,1)S(1)}, u32[]{:S(2)}, u32[]{:S(2)}) collective-permute-start(bf16[5,1,32,128]{3,2,1,0:T(8,128)(2,1)S(1)} %get-tuple-element.44), channel_id=1, source_target_pairs={{1,0},{2,1},{3,2},{4,3},{5,4},{6,5},{7,6},{9,8},{10,9},{11,10},{12... | collective-permute-start | bytes 122888 | tf_op jit(solution)/shard_map/ppermute | solution.py:21
  92.3 3.1 %copy-start = (bf16[1,128,3456]{1,2,0:T(8,128)(2,1)}, bf16[1,128,3456]{1,2,0:T(8,128)(2,1)S(1)}, u32[]{:S(2)}) copy-start(bf16[1,128,3456]{1,2,0:T(8,128)(2,1)S(1)} %copy.175) | copy-start | bytes 2654212
  92.3 14.7 %copy-start.5 = (bf16[1,7,4,32,128]{4,3,2,1,0:T(8,128)(2,1)S(1)}, bf16[1,7,4,32,128]{4,3,2,1,0:T(8,128)(2,1)}, u32[]{:S(2)}) copy-start(bf16[1,7,4,32,128]{4,3,2,1,0:T(8,128)(2,1)} %maximum_bitcast_fusion.1) | copy-start | bytes 688132
  95.6 0.6 copy-start.2
  96.8 18.7 %collective-permute-start.6 = (bf16[5,1,32,128]{3,2,1,0:T(8,128)(2,1)}, bf16[5,1,32,128]{3,2,1,0:T(8,128)(2,1)}, u32[]{:S(2)}, u32[]{:S(2)}) collective-permute-start(bf16[5,1,32,128]{3,2,1,0:T(8,128)(2,1)} %get-tuple-element.37), channel_id=1, source_target_pairs={{0,1},{1,2},{2,3},{3,4},{4,5},{5,6},{6,7},{8,9},{9,10},{10,11},{11... | collective-permute-start | bytes 122888 | tf_op jit(solution)/shard_map/ppermute | solution.py:18
  98.8 16.7 %collective-permute-start.7 = (bf16[5,1,32,128]{3,2,1,0:T(8,128)(2,1)}, bf16[5,1,32,128]{3,2,1,0:T(8,128)(2,1)}, u32[]{:S(2)}, u32[]{:S(2)}) collective-permute-start(bf16[5,1,32,128]{3,2,1,0:T(8,128)(2,1)} %get-tuple-element.38), channel_id=1, source_target_pairs={{1,0},{2,1},{3,2},{4,3},{5,4},{6,5},{7,6},{9,8},{10,9},{11,10},{12... | collective-permute-start | bytes 122888 | tf_op jit(solution)/shard_map/ppermute | solution.py:21
  102.4 15.9 %collective-permute-start.2 = (bf16[5,1,32,128]{3,2,1,0:T(8,128)(2,1)}, bf16[5,1,32,128]{3,2,1,0:T(8,128)(2,1)S(1)}, u32[]{:S(2)}, u32[]{:S(2)}) collective-permute-start(bf16[5,1,32,128]{3,2,1,0:T(8,128)(2,1)} %get-tuple-element.41), channel_id=1, source_target_pairs={{0,1},{1,2},{2,3},{3,4},{4,5},{5,6},{6,7},{8,9},{9,10},{10,11},{11... | collective-permute-start | bytes 122888 | tf_op jit(solution)/shard_map/ppermute | solution.py:18
  105.0 13.4 %collective-permute-start.3 = (bf16[5,1,32,128]{3,2,1,0:T(8,128)(2,1)}, bf16[5,1,32,128]{3,2,1,0:T(8,128)(2,1)}, u32[]{:S(2)}, u32[]{:S(2)}) collective-permute-start(bf16[5,1,32,128]{3,2,1,0:T(8,128)(2,1)} %get-tuple-element.42), channel_id=1, source_target_pairs={{1,0},{2,1},{3,2},{4,3},{5,4},{6,5},{7,6},{9,8},{10,9},{11,10},{12... | collective-permute-start | bytes 122888 | tf_op jit(solution)/shard_map/ppermute | solution.py:21
  115.5 1.4 copy-start.1
  115.5 1.5 copy-start.9
  120.2 1.0 copy-start.4
Sparse Core Ops, SparseCore 0:
  46.4 24.9 all-gather.1

commit v8 on v7

--- a/solution.py
+++ b/solution.py
@@ -140,14 +140,33 @@
     )(arranged)
 
 
+def rows_reduce(blocks, band_count):
+    me = lax.axis_index("rows")
+    core = lax.rem(me, 2)
+    chip = me // 2
+    chips = band_count // 2
+    pairs = blocks.reshape((chips, 2) + blocks.shape[1:])
+    keep = lax.dynamic_index_in_dim(pairs, core, axis=1, keepdims=False)
+    give = lax.dynamic_index_in_dim(pairs, 1 - core, axis=1, keepdims=False)
+    partner = [(r, r + 1 - 2 * (r % 2)) for r in range(band_count)]
+    got = lax.ppermute(give, "rows", partner)
+    mine = keep.astype(jnp.float32) + got.astype(jnp.float32)
+    outgoing = mine.astype(jnp.bfloat16)
+    total = lax.dynamic_index_in_dim(mine, chip, axis=0, keepdims=False)
+    for shift in range(1, chips):
+        route = [(r, ((r // 2 + shift) % chips) * 2 + r % 2) for r in range(band_count)]
+        piece = lax.dynamic_index_in_dim(outgoing, lax.rem(chip + shift, chips), axis=0, keepdims=False)
+        total = total + lax.ppermute(piece, "rows", route).astype(jnp.float32)
+    return total
+
+
 def reduce_weight_grads(grad_t, band_count, wide_size):
     _, channels, total_rows = grad_t.shape
     part = channels // band_count
     chunk = total_rows // wide_size
     blocks = grad_t.astype(jnp.bfloat16).reshape(2, band_count, part, total_rows)
     blocks = jnp.transpose(blocks, (1, 0, 2, 3))
-    band_parts = lax.all_to_all(blocks, "rows", 0, 0, tiled=True)
-    band_sum = jnp.sum(band_parts.astype(jnp.float32), axis=0)
+    band_sum = rows_reduce(blocks, band_count)
     band_sum = band_sum.reshape(2, part, wide_size, chunk)
     band_sum = jnp.transpose(band_sum, (2, 0, 1, 3)).reshape(wide_size, 2 * part * chunk)
     size = band_sum.shape[1]

time: 207 us -> 203 us (0.981)
  blocking collectives: 37.3 us -> 10.9 us
  starting transfers between devices: 49.8 us -> 63.3 us
  waiting for transfers between devices: 23 us -> 31.7 us
    all_to_all x1 -> x0, blocking collectives: 27.7 us -> none  [reduce_weight_grads(): band_parts = lax.all_to_all(blocks, 'rows', 0, 0, tiled=True)]
    ppermute x0 -> x4, starting transfers between devices: none -> 11.2 us  [the longest x3 9.26 us: rows_reduce(): total = total + lax.ppermute(piece, 'rows', route).astype(jnp.float32)]
    ppermute x0 -> x4, waiting for transfers between devices: none -> 11 us  [the longest x3 8.62 us: rows_reduce(): total = total + lax.ppermute(piece, 'rows', route).astype(jnp.float32)]
    ppermute x4, starting transfers between devices: 8.95 us -> 15.3 us  [with_halo(): lax.ppermute(lax.slice_in_dim(block, 0, width, axis=dim), axis, backward)]
    ppermute x4, starting transfers between devices: 18.2 us -> 14.1 us  [with_halo(): lax.ppermute(lax.slice_in_dim(block, block.shape[dim] - width, None, axis...]
    ppermute x4, waiting for transfers between devices: 3.15 us -> 0.01 us  [with_halo(): lax.ppermute(lax.slice_in_dim(block, 0, width, axis=dim), axis, backward)]
    convert_element_type x0 -> x1, other arithmetic: none -> 2.28 us  [reduce_weight_grads(): grad_t.astype(jnp.bfloat16).reshape(2, band_count, part, total_rows)]
    transpose x1 -> x0, other arithmetic: 2.28 us -> none  [reduce_weight_grads(): blocks = jnp.transpose(blocks, (1, 0, 2, 3))]
  transfers between devices with their start and end apart: 11 -> 15, of which waited for: 3 -> 6; matrix products, arithmetic and copies ran while one was open for 8% -> 8% of each run, Pallas kernels for 0% -> 0%
where the time goes in v8:
time: 203 us; the launch traced here: 202 us
  starting transfers between devices  63.3 us (31%)
  waiting for transfers between devices  31.7 us (16%)
  local copies, waits for them, and re-layouts  29.6 us (15%)
  Pallas kernels  22.3 us (11%)
  matrix products  15.7 us (8%)
  between operations  15.6 us (8%)
  other arithmetic  12.8 us (6%)
  blocking collectives  10.9 us (5%)
    pallas_call x1, Pallas kernels, wide_sum(): pl.pallas_call(functools.partial(_wide_sum_kernel, outer, inner), out_sha...  22.3 us
    all_to_all x1, starting transfers between devices, body(): lax.all_to_all(jnp.broadcast_to(pieces[None], (wide_size, pieces.shape[0]...  17.1 us
    ppermute x4, starting transfers between devices, with_halo(): lax.ppermute(lax.slice_in_dim(block, 0, width, axis=dim), axis, backward)  15.3 us
    ppermute x4, starting transfers between devices, with_halo(): lax.ppermute(lax.slice_in_dim(block, block.shape[dim] - width, None, axis...  14.1 us
    all_to_all x1, waiting for transfers between devices, body(): lax.all_to_all(jnp.broadcast_to(pieces[None], (wide_size, pieces.shape[0]...  11.9 us
    all_to_all x1, blocking collectives, reduce_weight_grads(): lax.all_to_all(jnp.broadcast_to(share, (band_count,) + share.shape[1:]),...  10.9 us
    ppermute x3, starting transfers between devices, rows_reduce(): total = total + lax.ppermute(piece, 'rows', route).astype(jnp.float32)  9.26 us
    ppermute x3, waiting for transfers between devices, rows_reduce(): total = total + lax.ppermute(piece, 'rows', route).astype(jnp.float32)  8.62 us
  transfers between devices with their start and end apart: 15, of which 6 were waited for; matrix products, arithmetic and copies ran while one was open for 8% of the time, Pallas kernels for 0%

profile of v8, /device:TPU:1, one launch (start us, length us, event | category | flops | bytes accessed | tf_op | source)
XLA Modules:
  0.0 201.8 jit_solution(8248566905996543127)
XLA Ops:
  7.2 0.8 fusion.61
  8.2 0.2 broadcast_in_dim.70
  8.5 0.5 broadcast.173
  9.0 2.0 %reduce.6 = bf16[64,1728]{1,0:T(8,128)(2,1)S(1)} reduce(bf16[64,1,1728]{2,1,0:T(2,128)(2,1)S(1)} %broadcast_in_dim.70, bf16[]{:T(256)} %broadcast.173), dimensions={1}, to_apply=%broadcast_in_dim.70.reduce_sub_computation | reduce | bytes 442370 | tf_op jit(solution)/shard_map/broadcast_in_dim | solution.py:243
  11.0 0.9 reshape.265
  12.0 17.1 %all-to-all-start.1 = ((bf16[64,2,864]{2,1,0:T(2,128)(2,1)}), bf16[64,2,864]{2,1,0:T(2,128)(2,1)S(1)}, u32[]{:S(2)}, u32[]{:S(2)}) async-start(bf16[64,2,864]{2,1,0:T(2,128)(2,1)} %reshape.265), calls=%async_computation.1 | async-start | bytes 458752 | tf_op jit(solution)/shard_map/all_to_all | solution.py:242
  29.5 11.9 %all-to-all-done.1 = bf16[64,2,864]{2,1,0:T(2,128)(2,1)S(1)} async-done(((bf16[64,2,864]{2,1,0:T(2,128)(2,1)}), bf16[64,2,864]{2,1,0:T(2,128)(2,1)S(1)}, u32[]{:S(2)}, u32[]{:S(2)}) %all-to-all-start.1) | async-done | bytes 221216 | tf_op jit(solution)/shard_map/all_to_all | solution.py:242
  41.4 0.3 reshape.266
  41.7 1.4 reduce.1
  43.2 1.6 reshape.217
  45.0 1.4 reshape.218
  46.4 0.4 convolution_convert_fusion
  47.0 1.0 reduce.7
  48.0 1.2 reshape.263
  49.2 5.5 %all-to-all-start = ((bf16[64,2,2112]{2,1,0:T(2,128)(2,1)}), bf16[64,2,2112]{2,1,0:T(2,128)(2,1)S(1)}, u32[]{:S(2)}, u32[]{:S(2)}) async-start(bf16[64,2,2112]{2,1,0:T(2,128)(2,1)} %reshape.263), calls=%async_computation | async-start | bytes 1114112 | tf_op jit(solution)/shard_map/all_to_all | solution.py:249
  55.5 4.0 %collective-permute-start.5 = (bf16[5,1,32,128]{3,2,1,0:T(8,128)(2,1)S(1)}, bf16[5,1,32,128]{3,2,1,0:T(8,128)(2,1)S(1)}, u32[]{:S(2)}, u32[]{:S(2)}) collective-permute-start(bf16[5,1,32,128]{3,2,1,0:T(8,128)(2,1)S(1)} %get-tuple-element.47), channel_id=1, source_target_pairs={{1,0},{2,1},{3,2},{4,3},{5,4},{6,5},{7,6},{9,8},{10,9},{11,10},{12... | collective-permute-start | bytes 122888 | tf_op jit(solution)/shard_map/ppermute | solution.py:21
  59.5 3.0 %collective-permute-start.4 = (bf16[5,1,32,128]{3,2,1,0:T(8,128)(2,1)S(1)}, bf16[5,1,32,128]{3,2,1,0:T(8,128)(2,1)S(1)}, u32[]{:S(2)}, u32[]{:S(2)}) collective-permute-start(bf16[5,1,32,128]{3,2,1,0:T(8,128)(2,1)S(1)} %get-tuple-element.46), channel_id=1, source_target_pairs={{0,1},{1,2},{2,3},{3,4},{4,5},{5,6},{6,7},{8,9},{9,10},{10,11},{11... | collective-permute-start | bytes 122888 | tf_op jit(solution)/shard_map/ppermute | solution.py:18
  62.6 7.9 %all-to-all-done = bf16[64,2,2112]{2,1,0:T(2,128)(2,1)S(1)} async-done(((bf16[64,2,2112]{2,1,0:T(2,128)(2,1)}), bf16[64,2,2112]{2,1,0:T(2,128)(2,1)S(1)}, u32[]{:S(2)}, u32[]{:S(2)}) %all-to-all-start) | async-done | bytes 540704 | tf_op jit(solution)/shard_map/all_to_all | solution.py:249
  70.5 0.6 reshape.264
  71.6 7.5 %collective-permute-start.1 = (bf16[5,1,32,128]{3,2,1,0:T(8,128)(2,1)S(1)}, bf16[5,1,32,128]{3,2,1,0:T(8,128)(2,1)S(1)}, u32[]{:S(2)}, u32[]{:S(2)}) collective-permute-start(bf16[5,1,32,128]{3,2,1,0:T(8,128)(2,1)S(1)} %get-tuple-element.51), channel_id=1, source_target_pairs={{1,0},{2,1},{3,2},{4,3},{5,4},{6,5},{7,6},{9,8},{10,9},{11,10},{12... | collective-permute-start | bytes 122888 | tf_op jit(solution)/shard_map/ppermute | solution.py:21
  79.1 3.2 %collective-permute-start = (bf16[5,1,32,128]{3,2,1,0:T(8,128)(2,1)S(1)}, bf16[5,1,32,128]{3,2,1,0:T(8,128)(2,1)S(1)}, u32[]{:S(2)}, u32[]{:S(2)}) collective-permute-start(bf16[5,1,32,128]{3,2,1,0:T(8,128)(2,1)S(1)} %get-tuple-element.50), channel_id=1, source_target_pairs={{0,1},{1,2},{2,3},{3,4},{4,5},{5,6},{6,7},{8,9},{9,10},{10,11},{11... | collective-permute-start | bytes 122888 | tf_op jit(solution)/shard_map/ppermute | solution.py:18
  82.3 0.8 collective-permute-done
  83.2 0.7 maximum_bitcast_fusion.1
  83.9 1.6 fusion.74
  85.5 1.0 copy.186
  86.5 2.5 %fusion.4 = f32[1,7,2,32,128]{4,0,3,2,1:T(1,128)S(1)} fusion(bf16[128,3,3,3,128]{0,4,3,2,1:T(8,128)(2,1)S(1)} %bitcast.159, bf16[1,9,4,32,128]{4,3,2,1,0:T(8,128)(2,1)S(1)} %fusion.34), kind=kOutput, calls=%fused_computation.16 | convolution fusion | flops 388104192 | bytes 1409024 | tf_op jit(solution)/shard_map/conv_general_dilated | solution.py:209
  89.0 1.0 copy.180
  90.0 3.1 %fusion.26 = f32[1,5,2,32,128]{4,0,3,2,1:T(1,128)S(1)} fusion(bf16[128,3,3,3,128]{0,4,3,2,1:T(8,128)(2,1)S(1)} %bitcast.162, bf16[1,7,4,32,128]{4,3,2,1,0:T(8,128)(2,1)} %maximum_bitcast_fusion.1), kind=kOutput, calls=%fused_computation.42 | convolution fusion | flops 277217280 | bytes 1277952 | tf_op jit(solution)/shard_map/conv_general_dilated | solution.py:189
  93.3 0.6 copy-done.2
  93.9 0.6 fusion.77
  94.5 1.9 collective-permute-start.7
  96.5 4.2 %collective-permute-start.6 = (bf16[5,1,32,128]{3,2,1,0:T(8,128)(2,1)}, bf16[5,1,32,128]{3,2,1,0:T(8,128)(2,1)}, u32[]{:S(2)}, u32[]{:S(2)}) collective-permute-start(bf16[5,1,32,128]{3,2,1,0:T(8,128)(2,1)} %get-tuple-element.44), channel_id=1, source_target_pairs={{0,1},{1,2},{2,3},{3,4},{4,5},{5,6},{6,7},{8,9},{9,10},{10,11},{11... | collective-permute-start | bytes 122888 | tf_op jit(solution)/shard_map/ppermute | solution.py:18
  100.7 0.6 fusion.79
  101.3 1.9 collective-permute-start.3
  103.3 3.6 %collective-permute-start.2 = (bf16[5,1,32,128]{3,2,1,0:T(8,128)(2,1)}, bf16[5,1,32,128]{3,2,1,0:T(8,128)(2,1)}, u32[]{:S(2)}, u32[]{:S(2)}) collective-permute-start(bf16[5,1,32,128]{3,2,1,0:T(8,128)(2,1)} %get-tuple-element.48), channel_id=1, source_target_pairs={{0,1},{1,2},{2,3},{3,4},{4,5},{5,6},{6,7},{8,9},{9,10},{10,11},{11... | collective-permute-start | bytes 122888 | tf_op jit(solution)/shard_map/ppermute | solution.py:18
  107.0 3.8 %fusion.24 = f32[128,3,3,3,128]{0,4,3,2,1:T(8,128)} fusion(bf16[1,7,4,32,128]{4,3,2,1,0:T(8,128)(2,1)S(1)} %copy-done.5, bf16[1,5,2,32,128]{4,3,2,1,0:T(8,128)(2,1)S(1)} %fusion.54), kind=kOutput, calls=%fused_computation.40 | convolution fusion | flops 277217280 | bytes 2080768 | tf_op jit(solution)/shard_map/conv_general_dilated | solution.py:198
  110.8 2.8 %copy.203 = f32[128,3,3,3,128]{4,3,2,1,0:T(4,128)S(1)} copy(f32[128,3,3,3,128]{0,4,3,2,1:T(8,128)} %fusion.24) | data formatting | bytes 3538944 | tf_op jit(solution)/shard_map/conv_general_dilated | solution.py:198
  113.6 2.0 stack.19
  115.6 1.0 fusion.28
  117.0 1.2 convolution_select_fusion
  118.4 0.7 pad_maximum_fusion
  119.2 0.8 fusion.66
  120.3 0.9 convolution_select_fusion.1
  121.3 0.7 fusion.56
  122.1 3.7 %fusion.14 = f32[128,3,3,3,128]{0,4,3,2,1:T(8,128)} fusion(bf16[1,7,4,32,128]{4,3,2,1,0:T(8,128)(2,1)S(1)} %get-tuple-element.37, bf16[1,5,2,32,128]{4,3,2,1,0:T(8,128)(2,1)S(1)} %get-tuple-element.25), kind=kOutput, calls=%fused_computation.30 | convolution fusion | flops 277217280 | bytes 2080768 | tf_op jit(solution)/shard_map/conv_general_dilated | solution.py:198
  125.8 2.8 %copy.206 = f32[128,3,3,3,128]{4,3,2,1,0:T(4,128)S(1)} copy(f32[128,3,3,3,128]{0,4,3,2,1:T(8,128)} %fusion.14) | data formatting | bytes 3538944 | tf_op jit(solution)/shard_map/conv_general_dilated | solution.py:198
  128.7 1.9 stack.20
  130.6 2.3 %fusion.1 = bf16[2,8,16,3456]{3,2,1,0:T(8,128)(2,1)S(1)} fusion(f32[1,8,16,3456]{3,2,1,0:T(8,128)} %stack.20, f32[1,8,16,3456]{3,2,1,0:T(8,128)} %stack.19), kind=kLoop, calls=%fused_computation.4 | loop fusion | flops 2654208 | bytes 5308416 | tf_op jit(solution)/shard_map/convert_element_type | solution.py:167
  133.1 1.9 collective-permute-start.8
  135.1 2.3 %collective-permute-done.8 = bf16[4,2,16,3456]{3,2,1,0:T(8,128)(2,1)S(1)} collective-permute-done((bf16[4,2,16,3456]{3,2,1,0:T(8,128)(2,1)S(1)}, bf16[4,2,16,3456]{3,2,1,0:T(8,128)(2,1)S(1)}, u32[]{:S(2)}, u32[]{:S(2)}) %collective-permute-start.8) | collective-permute-done | bytes 884768 | tf_op jit(solution)/shard_map/ppermute | solution.py:152
  137.7 2.9 %collective-permute-start.11 = (bf16[2,16,3456]{2,1,0:T(8,128)(2,1)S(1)}, bf16[2,16,3456]{2,1,0:T(8,128)(2,1)S(1)}, u32[]{:S(2)}, u32[]{:S(2)}) collective-permute-start(bf16[2,16,3456]{2,1,0:T(8,128)(2,1)S(1)} %get-tuple-element.33), channel_id=1, source_target_pairs={{0,6},{1,7},{2,0},{3,1},{4,2},{5,3},{6,4},{7,5},{8,14},{9,15},{10,... | collective-permute-start | bytes 663560 | tf_op jit(solution)/shard_map/ppermute | solution.py:159
  140.6 3.9 %collective-permute-start.10 = (bf16[2,16,3456]{2,1,0:T(8,128)(2,1)S(1)}, bf16[2,16,3456]{2,1,0:T(8,128)(2,1)S(1)}, u32[]{:S(2)}, u32[]{:S(2)}) collective-permute-start(bf16[2,16,3456]{2,1,0:T(8,128)(2,1)S(1)} %get-tuple-element.34), channel_id=1, source_target_pairs={{0,4},{1,5},{2,6},{3,7},{4,0},{5,1},{6,2},{7,3},{8,12},{9,13},{10,... | collective-permute-start | bytes 663560 | tf_op jit(solution)/shard_map/ppermute | solution.py:159
  144.5 2.4 %collective-permute-start.9 = (bf16[2,16,3456]{2,1,0:T(8,128)(2,1)S(1)}, bf16[2,16,3456]{2,1,0:T(8,128)(2,1)S(1)}, u32[]{:S(2)}, u32[]{:S(2)}) collective-permute-start(bf16[2,16,3456]{2,1,0:T(8,128)(2,1)S(1)} %get-tuple-element.32), channel_id=1, source_target_pairs={{0,2},{1,3},{2,4},{3,5},{4,6},{5,7},{6,0},{7,1},{8,10},{9,11},{10,... | collective-permute-start | bytes 663560 | tf_op jit(solution)/shard_map/ppermute | solution.py:159
  147.0 3.4 %collective-permute-done.10 = bf16[2,16,3456]{2,1,0:T(8,128)(2,1)S(1)} collective-permute-done((bf16[2,16,3456]{2,1,0:T(8,128)(2,1)S(1)}, bf16[2,16,3456]{2,1,0:T(8,128)(2,1)S(1)}, u32[]{:S(2)}, u32[]{:S(2)}) %collective-permute-start.10) | collective-permute-done | bytes 221216 | tf_op jit(solution)/shard_map/ppermute | solution.py:159
  150.3 5.3 %collective-permute-done.9 = bf16[2,16,3456]{2,1,0:T(8,128)(2,1)S(1)} collective-permute-done((bf16[2,16,3456]{2,1,0:T(8,128)(2,1)S(1)}, bf16[2,16,3456]{2,1,0:T(8,128)(2,1)S(1)}, u32[]{:S(2)}, u32[]{:S(2)}) %collective-permute-start.9) | collective-permute-done | bytes 221216 | tf_op jit(solution)/shard_map/ppermute | solution.py:159
  155.7 1.4 reshape.220
  157.2 0.6 copy.209
  157.8 0.6 reshape.221
  158.4 0.9 copy_bitcast_fusion.4.x_ref
  159.3 22.3 %shard_map.102 = f32[16,128]{1,0:T(8,128)} custom-call(f32[8,8,16,128]{3,2,1,0:T(8,128)} %copy_bitcast_fusion.4.x_ref), custom_call_target="tpu_custom_call" | custom-call | tf_op jit(solution)/shard_map/pallas_call | solution.py:125
  181.6 0.7 slice_reduce_fusion
  182.4 10.9 %all_to_all.24 = f32[8,1,1728]{2,1,0:T(1,128)S(1)} all-to-all(f32[8,1,1728]{2,1,0:T(1,128)S(1)} %broadcast_in_dim.78), channel_id=1, replica_groups=mesh['wide'=64,'rows'=8] {'rows'}, dimensions={0} | all-to-all | bytes 110592 | tf_op jit(solution)/shard_map/all_to_all | solution.py:177
  193.6 0.7 copy.211
  194.3 0.7 copy.212
  (87 shorter events, 3.8 us)
Async XLA Ops:
  7.2 22.0 %copy-start.7 = (s32[1,1,10]{2,1,0:T(1,128)S(1)}, s32[1,1,10]{2,1,0:T(1,128)}, u32[]{:S(2)}) copy-start(s32[1,1,10]{2,1,0:T(1,128)} %param.9) | copy-start | bytes 124
  7.2 22.0 %copy-start.8 = (s32[1,1,10]{2,1,0:T(1,128)S(1)}, s32[1,1,10]{2,1,0:T(1,128)}, u32[]{:S(2)}) copy-start(s32[1,1,10]{2,1,0:T(1,128)} %param.8) | copy-start | bytes 124
  12.0 29.4 %all-to-all-start.1 = ((bf16[64,2,864]{2,1,0:T(2,128)(2,1)}), bf16[64,2,864]{2,1,0:T(2,128)(2,1)S(1)}, u32[]{:S(2)}, u32[]{:S(2)}) async-start(bf16[64,2,864]{2,1,0:T(2,128)(2,1)} %reshape.265), calls=%async_computation.1 | async-start | bytes 458752 | tf_op jit(solution)/shard_map/all_to_all | solution.py:242
  29.1 54.8 %all-gather.2.cloned.1.call-start = ((), (), s32[]{:S(2)}) async-start(), calls=%async_computation.3 | async-start | bytes 1990656 | tf_op jit(solution)/shard_map/all_gather | solution.py:45
  41.7 4.6 %copy-start.6 = (bf16[1,1,10,32,128]{4,3,2,1,0:T(8,128)(2,1)S(1)}, bf16[1,1,10,32,128]{4,3,2,1,0:T(8,128)(2,1)}, u32[]{:S(2)}) copy-start(bf16[1,1,10,32,128]{4,3,2,1,0:T(8,128)(2,1)} %param.7) | copy-start | bytes 245764
  47.0 8.4 %copy-start.3 = (bf16[1,5,2,32,128]{4,3,2,1,0:T(8,128)(2,1)S(1)}, bf16[1,5,2,32,128]{4,3,2,1,0:T(8,128)(2,1)}, u32[]{:S(2)}) copy-start(bf16[1,5,2,32,128]{4,3,2,1,0:T(8,128)(2,1)} %param.11) | copy-start | bytes 245764
  49.2 21.3 %all-to-all-start = ((bf16[64,2,2112]{2,1,0:T(2,128)(2,1)}), bf16[64,2,2112]{2,1,0:T(2,128)(2,1)S(1)}, u32[]{:S(2)}, u32[]{:S(2)}) async-start(bf16[64,2,2112]{2,1,0:T(2,128)(2,1)} %reshape.263), calls=%async_computation | async-start | bytes 1114112 | tf_op jit(solution)/shard_map/all_to_all | solution.py:249
  55.5 26.8 %collective-permute-start.5 = (bf16[5,1,32,128]{3,2,1,0:T(8,128)(2,1)S(1)}, bf16[5,1,32,128]{3,2,1,0:T(8,128)(2,1)S(1)}, u32[]{:S(2)}, u32[]{:S(2)}) collective-permute-start(bf16[5,1,32,128]{3,2,1,0:T(8,128)(2,1)S(1)} %get-tuple-element.47), channel_id=1, source_target_pairs={{1,0},{2,1},{3,2},{4,3},{5,4},{6,5},{7,6},{9,8},{10,9},{11,10},{12... | collective-permute-start | bytes 122888 | tf_op jit(solution)/shard_map/ppermute | solution.py:21
  59.5 22.8 %collective-permute-start.4 = (bf16[5,1,32,128]{3,2,1,0:T(8,128)(2,1)S(1)}, bf16[5,1,32,128]{3,2,1,0:T(8,128)(2,1)S(1)}, u32[]{:S(2)}, u32[]{:S(2)}) collective-permute-start(bf16[5,1,32,128]{3,2,1,0:T(8,128)(2,1)S(1)} %get-tuple-element.46), channel_id=1, source_target_pairs={{0,1},{1,2},{2,3},{3,4},{4,5},{5,6},{6,7},{8,9},{9,10},{10,11},{11... | collective-permute-start | bytes 122888 | tf_op jit(solution)/shard_map/ppermute | solution.py:18
  71.6 10.7 %collective-permute-start.1 = (bf16[5,1,32,128]{3,2,1,0:T(8,128)(2,1)S(1)}, bf16[5,1,32,128]{3,2,1,0:T(8,128)(2,1)S(1)}, u32[]{:S(2)}, u32[]{:S(2)}) collective-permute-start(bf16[5,1,32,128]{3,2,1,0:T(8,128)(2,1)S(1)} %get-tuple-element.51), channel_id=1, source_target_pairs={{1,0},{2,1},{3,2},{4,3},{5,4},{6,5},{7,6},{9,8},{10,9},{11,10},{12... | collective-permute-start | bytes 122888 | tf_op jit(solution)/shard_map/ppermute | solution.py:21
  79.1 4.1 %collective-permute-start = (bf16[5,1,32,128]{3,2,1,0:T(8,128)(2,1)S(1)}, bf16[5,1,32,128]{3,2,1,0:T(8,128)(2,1)S(1)}, u32[]{:S(2)}, u32[]{:S(2)}) collective-permute-start(bf16[5,1,32,128]{3,2,1,0:T(8,128)(2,1)S(1)} %get-tuple-element.50), channel_id=1, source_target_pairs={{0,1},{1,2},{2,3},{3,4},{4,5},{5,6},{6,7},{8,9},{9,10},{10,11},{11... | collective-permute-start | bytes 122888 | tf_op jit(solution)/shard_map/ppermute | solution.py:18
  90.0 3.1 %copy-start = (bf16[1,128,3456]{1,2,0:T(8,128)(2,1)}, bf16[1,128,3456]{1,2,0:T(8,128)(2,1)S(1)}, u32[]{:S(2)}) copy-start(bf16[1,128,3456]{1,2,0:T(8,128)(2,1)S(1)} %copy.180) | copy-start | bytes 2654212
  90.0 17.0 %copy-start.5 = (bf16[1,7,4,32,128]{4,3,2,1,0:T(8,128)(2,1)S(1)}, bf16[1,7,4,32,128]{4,3,2,1,0:T(8,128)(2,1)}, u32[]{:S(2)}) copy-start(bf16[1,7,4,32,128]{4,3,2,1,0:T(8,128)(2,1)} %maximum_bitcast_fusion.1) | copy-start | bytes 688132
  93.3 0.6 copy-start.2
  94.5 21.0 %collective-permute-start.7 = (bf16[5,1,32,128]{3,2,1,0:T(8,128)(2,1)}, bf16[5,1,32,128]{3,2,1,0:T(8,128)(2,1)}, u32[]{:S(2)}, u32[]{:S(2)}) collective-permute-start(bf16[5,1,32,128]{3,2,1,0:T(8,128)(2,1)} %get-tuple-element.45), channel_id=1, source_target_pairs={{1,0},{2,1},{3,2},{4,3},{5,4},{6,5},{7,6},{9,8},{10,9},{11,10},{12... | collective-permute-start | bytes 122888 | tf_op jit(solution)/shard_map/ppermute | solution.py:21
  96.5 19.1 %collective-permute-start.6 = (bf16[5,1,32,128]{3,2,1,0:T(8,128)(2,1)}, bf16[5,1,32,128]{3,2,1,0:T(8,128)(2,1)}, u32[]{:S(2)}, u32[]{:S(2)}) collective-permute-start(bf16[5,1,32,128]{3,2,1,0:T(8,128)(2,1)} %get-tuple-element.44), channel_id=1, source_target_pairs={{0,1},{1,2},{2,3},{3,4},{4,5},{5,6},{6,7},{8,9},{9,10},{10,11},{11... | collective-permute-start | bytes 122888 | tf_op jit(solution)/shard_map/ppermute | solution.py:18
  101.3 17.1 %collective-permute-start.3 = (bf16[5,1,32,128]{3,2,1,0:T(8,128)(2,1)}, bf16[5,1,32,128]{3,2,1,0:T(8,128)(2,1)S(1)}, u32[]{:S(2)}, u32[]{:S(2)}) collective-permute-start(bf16[5,1,32,128]{3,2,1,0:T(8,128)(2,1)} %get-tuple-element.49), channel_id=1, source_target_pairs={{1,0},{2,1},{3,2},{4,3},{5,4},{6,5},{7,6},{9,8},{10,9},{11,10},{12... | collective-permute-start | bytes 122888 | tf_op jit(solution)/shard_map/ppermute | solution.py:21
  103.3 15.2 %collective-permute-start.2 = (bf16[5,1,32,128]{3,2,1,0:T(8,128)(2,1)}, bf16[5,1,32,128]{3,2,1,0:T(8,128)(2,1)}, u32[]{:S(2)}, u32[]{:S(2)}) collective-permute-start(bf16[5,1,32,128]{3,2,1,0:T(8,128)(2,1)} %get-tuple-element.48), channel_id=1, source_target_pairs={{0,1},{1,2},{2,3},{3,4},{4,5},{5,6},{6,7},{8,9},{9,10},{10,11},{11... | collective-permute-start | bytes 122888 | tf_op jit(solution)/shard_map/ppermute | solution.py:18
  115.6 1.4 copy-start.1
  115.6 1.5 copy-start.9
  120.3 1.0 copy-start.4
  133.1 4.3 %collective-permute-start.8 = (bf16[4,2,16,3456]{3,2,1,0:T(8,128)(2,1)S(1)}, bf16[4,2,16,3456]{3,2,1,0:T(8,128)(2,1)S(1)}, u32[]{:S(2)}, u32[]{:S(2)}) collective-permute-start(bf16[4,2,16,3456]{3,2,1,0:T(8,128)(2,1)S(1)} %bitcast.161), channel_id=1, source_target_pairs={{0,1},{1,0},{2,3},{3,2},{4,5},{5,4},{6,7},{7,6},{8,9},{9,8},{10,11... | collective-permute-start | bytes 2654216 | tf_op jit(solution)/shard_map/ppermute | solution.py:152
  137.7 9.3 %collective-permute-start.11 = (bf16[2,16,3456]{2,1,0:T(8,128)(2,1)S(1)}, bf16[2,16,3456]{2,1,0:T(8,128)(2,1)S(1)}, u32[]{:S(2)}, u32[]{:S(2)}) collective-permute-start(bf16[2,16,3456]{2,1,0:T(8,128)(2,1)S(1)} %get-tuple-element.33), channel_id=1, source_target_pairs={{0,6},{1,7},{2,0},{3,1},{4,2},{5,3},{6,4},{7,5},{8,14},{9,15},{10,... | collective-permute-start | bytes 663560 | tf_op jit(solution)/shard_map/ppermute | solution.py:159
  140.6 9.7 %collective-permute-start.10 = (bf16[2,16,3456]{2,1,0:T(8,128)(2,1)S(1)}, bf16[2,16,3456]{2,1,0:T(8,128)(2,1)S(1)}, u32[]{:S(2)}, u32[]{:S(2)}) collective-permute-start(bf16[2,16,3456]{2,1,0:T(8,128)(2,1)S(1)} %get-tuple-element.34), channel_id=1, source_target_pairs={{0,4},{1,5},{2,6},{3,7},{4,0},{5,1},{6,2},{7,3},{8,12},{9,13},{10,... | collective-permute-start | bytes 663560 | tf_op jit(solution)/shard_map/ppermute | solution.py:159
  144.5 11.1 %collective-permute-start.9 = (bf16[2,16,3456]{2,1,0:T(8,128)(2,1)S(1)}, bf16[2,16,3456]{2,1,0:T(8,128)(2,1)S(1)}, u32[]{:S(2)}, u32[]{:S(2)}) collective-permute-start(bf16[2,16,3456]{2,1,0:T(8,128)(2,1)S(1)} %get-tuple-element.32), channel_id=1, source_target_pairs={{0,2},{1,3},{2,4},{3,5},{4,6},{5,7},{6,0},{7,1},{8,10},{9,11},{10,... | collective-permute-start | bytes 663560 | tf_op jit(solution)/shard_map/ppermute | solution.py:159
Sparse Core Ops, SparseCore 0:
  46.5 24.9 all-gather.1

commit v9 on v8

--- a/solution.py
+++ b/solution.py
@@ -42,8 +42,26 @@
     part = channels // band_count
     block = pieces.reshape(count, 2, part, rows_local)
     block = jnp.transpose(block, (1, 2, 0, 3)).reshape(2, part, count * rows_local)
-    full = lax.all_gather(block, "rows", axis=1, tiled=True)
+    full = rows_gather(block, band_count)
+    full = jnp.transpose(full, (1, 0, 2, 3)).reshape(2, channels, count * rows_local)
     return full[0], full[1]
+
+
+def rows_gather(block, band_count):
+    me = lax.axis_index("rows")
+    core = lax.rem(me, 2)
+    chip = me // 2
+    chips = band_count // 2
+    partner = [(r, r + 1 - 2 * (r % 2)) for r in range(band_count)]
+    got = lax.ppermute(block, "rows", partner)
+    pair = jnp.where(core == 0, jnp.stack([block, got]), jnp.stack([got, block]))
+    held = [pair]
+    for shift in range(1, chips):
+        route = [(r, ((r // 2 + shift) % chips) * 2 + r % 2) for r in range(band_count)]
+        held.append(lax.ppermute(pair, "rows", route))
+    order = lax.rem(chip - jnp.arange(chips, dtype=jnp.int32) + chips, chips)
+    full = jnp.take(jnp.stack(held), order, axis=0)
+    return full.reshape((band_count,) + block.shape)
 
 
 def _wide_sum_kernel(outer, inner, x_ref, o_ref, recv1, part, recv2, send1, got1, send2, got2):
@@ -239,18 +257,22 @@
     labels = labels.reshape(wide_size, capacity).astype(jnp.bfloat16)
     label_block = 128
     pieces = weight_pieces(w_first, w_second, band_count)
-    pieces = lax.all_to_all(
-        jnp.broadcast_to(pieces[None], (wide_size, pieces.shape[0])), "wide", 0, 0, tiled=True
-    )
-    kernel_first, kernel_second = assemble_weights(pieces, band_count, rows_local, channels)
     tagged = jnp.concatenate(
-        [outgoing, jnp.repeat(labels, label_block // capacity, axis=1)], axis=1
+        [
+            outgoing,
+            jnp.repeat(labels, label_block // capacity, axis=1),
+            jnp.broadcast_to(pieces[None], (wide_size, pieces.shape[0])),
+        ],
+        axis=1,
     )
     tagged = lax.all_to_all(tagged, "wide", split_axis=0, concat_axis=0, tiled=True)
     payload = capacity * columns * channels
     arrived = tagged[:, :payload].reshape(slot_count, columns * channels)
     arrived_places = tagged[:, payload : payload + label_block : label_block // capacity]
     arrived_places = arrived_places.astype(jnp.int32).reshape(slot_count)
+    kernel_first, kernel_second = assemble_weights(
+        tagged[:, payload + label_block :], band_count, rows_local, channels
+    )
     settle = arrived_places[None, :] == jnp.arange(slab_count, dtype=jnp.int32)[:, None]
     tile = jnp.dot(settle.astype(jnp.bfloat16), arrived, preferred_element_type=jnp.float32)
     tile = tile.astype(jnp.bfloat16).reshape(frames, band_rows, columns, channels)

time: 203 us -> 202 us (level)
  waiting for transfers between devices: 31.7 us -> 46 us
  between operations: 15.6 us -> 2.16 us
  other arithmetic: 12.8 us -> 10.7 us
    ppermute x0 -> x4, waiting for transfers between devices: none -> 19.7 us  [the longest x3 19.1 us: rows_gather(): held.append(lax.ppermute(pair, 'rows', route))]
    all_to_all x1 -> x0, starting transfers between devices: 17.1 us -> none  [body(): lax.all_to_all(jnp.broadcast_to(pieces[None], (wide_size, pieces.shape[0]...]
    all_to_all x1 -> x0, waiting for transfers between devices: 11.9 us -> none  [body(): lax.all_to_all(jnp.broadcast_to(pieces[None], (wide_size, pieces.shape[0]...]
    all_to_all x1, starting transfers between devices: 5.5 us -> 17.1 us  [body(): lax.all_to_all(tagged, 'wide', split_axis=0, concat_axis=0, tiled=True)]
    ppermute x0 -> x4, starting transfers between devices: none -> 11.1 us  [the longest x3 9.22 us: rows_gather(): held.append(lax.ppermute(pair, 'rows', route))]
    all_to_all x1, waiting for transfers between devices: 7.89 us -> 15 us  [body(): lax.all_to_all(tagged, 'wide', split_axis=0, concat_axis=0, tiled=True)]
    unnamed x37, local copies, waits for them, and re-layouts: 5.7 us -> 9.18 us
    slice x3 -> x1, local copies, waits for them, and re-layouts: 3.56 us -> 0.12 us  [assemble_weights(): return (full[0], full[1])]
  transfers between devices with their start and end apart: 15 -> 17, of which waited for: 6 -> 9; matrix products, arithmetic and copies ran while one was open for 8% -> 9% of each run, Pallas kernels for 0% -> 0%
where the time goes in v9:
time: 202 us; the launch traced here: 201 us
  starting transfers between devices  64 us (32%)
  waiting for transfers between devices  46 us (23%)
  local copies, waits for them, and re-layouts  30.3 us (15%)
  Pallas kernels  22.9 us (11%)
  matrix products  14.3 us (7%)
  other arithmetic  10.7 us (5%)
  blocking collectives  10.4 us (5%)
  between operations  2.16 us (1%)
    pallas_call x1, Pallas kernels, wide_sum(): pl.pallas_call(functools.partial(_wide_sum_kernel, outer, inner), out_sha...  22.9 us
    ppermute x3, waiting for transfers between devices, rows_gather(): held.append(lax.ppermute(pair, 'rows', route))  19.1 us
    all_to_all x1, starting transfers between devices, body(): lax.all_to_all(tagged, 'wide', split_axis=0, concat_axis=0, tiled=True)  17.1 us
    all_to_all x1, waiting for transfers between devices, body(): lax.all_to_all(tagged, 'wide', split_axis=0, concat_axis=0, tiled=True)  15 us
    ppermute x4, starting transfers between devices, with_halo(): lax.ppermute(lax.slice_in_dim(block, block.shape[dim] - width, None, axis...  13.1 us
    ppermute x4, starting transfers between devices, with_halo(): lax.ppermute(lax.slice_in_dim(block, 0, width, axis=dim), axis, backward)  12.4 us
    all_to_all x1, blocking collectives, reduce_weight_grads(): lax.all_to_all(jnp.broadcast_to(share, (band_count,) + share.shape[1:]),...  10.4 us
    ppermute x3, starting transfers between devices, rows_gather(): held.append(lax.ppermute(pair, 'rows', route))  9.22 us
  transfers between devices with their start and end apart: 17, of which 9 were waited for; matrix products, arithmetic and copies ran while one was open for 9% of the time, Pallas kernels for 0%

profile of v9, /device:TPU:1, one launch (start us, length us, event | category | flops | bytes accessed | tf_op | source)
XLA Modules:
  0.0 200.7 jit_solution(12338263656887825493)
XLA Ops:
  0.6 0.7 add_bitcast_fusion
  1.3 0.9 convert_reduce_fusion.1
  2.2 0.7 bitcast_add_fusion.1
  3.0 0.9 pad.84
  4.4 0.8 fusion.66
  6.1 1.1 reduce.5
  7.2 1.7 reshape.372
  9.0 17.1 %all-to-all-start = ((bf16[64,2,2976]{2,1,0:T(2,128)(2,1)}), bf16[64,2,2976]{2,1,0:T(2,128)(2,1)S(1)}, u32[]{:S(2)}, u32[]{:S(2)}) async-start(bf16[64,2,2976]{2,1,0:T(2,128)(2,1)} %reshape.372), calls=%async_computation | async-start | bytes 1572864 | tf_op jit(solution)/shard_map/all_to_all | solution.py:268
  26.9 2.9 %collective-permute-start.9 = (bf16[5,1,32,128]{3,2,1,0:T(8,128)(2,1)S(1)}, bf16[5,1,32,128]{3,2,1,0:T(8,128)(2,1)S(1)}, u32[]{:S(2)}, u32[]{:S(2)}) collective-permute-start(bf16[5,1,32,128]{3,2,1,0:T(8,128)(2,1)S(1)} %get-tuple-element.47), channel_id=1, source_target_pairs={{1,0},{2,1},{3,2},{4,3},{5,4},{6,5},{7,6},{9,8},{10,9},{11,10},{12... | collective-permute-start | bytes 122888 | tf_op jit(solution)/shard_map/ppermute | solution.py:21
  29.8 3.0 %collective-permute-start.8 = (bf16[5,1,32,128]{3,2,1,0:T(8,128)(2,1)S(1)}, bf16[5,1,32,128]{3,2,1,0:T(8,128)(2,1)S(1)}, u32[]{:S(2)}, u32[]{:S(2)}) collective-permute-start(bf16[5,1,32,128]{3,2,1,0:T(8,128)(2,1)S(1)} %get-tuple-element.46), channel_id=1, source_target_pairs={{0,1},{1,2},{2,3},{3,4},{4,5},{5,6},{6,7},{8,9},{9,10},{10,11},{11... | collective-permute-start | bytes 122888 | tf_op jit(solution)/shard_map/ppermute | solution.py:18
  33.0 15.0 %all-to-all-done = bf16[64,2,2976]{2,1,0:T(2,128)(2,1)S(1)} async-done(((bf16[64,2,2976]{2,1,0:T(2,128)(2,1)}), bf16[64,2,2976]{2,1,0:T(2,128)(2,1)S(1)}, u32[]{:S(2)}, u32[]{:S(2)}) %all-to-all-start) | async-done | bytes 761888 | tf_op jit(solution)/shard_map/all_to_all | solution.py:268
  48.0 1.0 reshape.373
  49.5 0.7 copy-done
  50.2 5.2 %collective-permute-start.1 = (bf16[5,1,32,128]{3,2,1,0:T(8,128)(2,1)S(1)}, bf16[5,1,32,128]{3,2,1,0:T(8,128)(2,1)S(1)}, u32[]{:S(2)}, u32[]{:S(2)}) collective-permute-start(bf16[5,1,32,128]{3,2,1,0:T(8,128)(2,1)S(1)} %get-tuple-element.51), channel_id=1, source_target_pairs={{1,0},{2,1},{3,2},{4,3},{5,4},{6,5},{7,6},{9,8},{10,9},{11,10},{12... | collective-permute-start | bytes 122888 | tf_op jit(solution)/shard_map/ppermute | solution.py:21
  55.5 3.0 %collective-permute-start = (bf16[5,1,32,128]{3,2,1,0:T(8,128)(2,1)S(1)}, bf16[5,1,32,128]{3,2,1,0:T(8,128)(2,1)S(1)}, u32[]{:S(2)}, u32[]{:S(2)}) collective-permute-start(bf16[5,1,32,128]{3,2,1,0:T(8,128)(2,1)S(1)} %get-tuple-element.50), channel_id=1, source_target_pairs={{0,1},{1,2},{2,3},{3,4},{4,5},{5,6},{6,7},{8,9},{9,10},{10,11},{11... | collective-permute-start | bytes 122888 | tf_op jit(solution)/shard_map/ppermute | solution.py:18
  58.5 0.7 fusion.39
  59.3 1.6 reshape.318
  61.1 0.7 reshape.319
  61.7 0.7 stack_reshape.2
  62.4 0.7 stack.50
  63.1 1.9 collective-permute-start.2
  65.0 0.7 maximum_bitcast_fusion.1
  65.7 0.7 collective-permute-done.2
  66.5 3.4 %collective-permute-start.5 = (bf16[2,2,16,3456]{3,2,1,0:T(8,128)(2,1)S(1)}, bf16[2,2,16,3456]{3,2,1,0:T(8,128)(2,1)S(1)}, u32[]{:S(2)}, u32[]{:S(2)}) collective-permute-start(bf16[2,2,16,3456]{3,2,1,0:T(8,128)(2,1)S(1)} %maximum_select_fusion.1), channel_id=1, source_target_pairs={{0,6},{1,7},{2,0},{3,1},{4,2},{5,3},{6,4},{7,5},{8,14},{9,15},{10,... | collective-permute-start | bytes 1327112 | tf_op jit(solution)/shard_map/ppermute | solution.py:61
  69.9 3.4 %collective-permute-start.4 = (bf16[2,2,16,3456]{3,2,1,0:T(8,128)(2,1)S(1)}, bf16[2,2,16,3456]{3,2,1,0:T(8,128)(2,1)S(1)}, u32[]{:S(2)}, u32[]{:S(2)}) collective-permute-start(bf16[2,2,16,3456]{3,2,1,0:T(8,128)(2,1)S(1)} %maximum_select_fusion.1), channel_id=1, source_target_pairs={{0,4},{1,5},{2,6},{3,7},{4,0},{5,1},{6,2},{7,3},{8,12},{9,13},{10,... | collective-permute-start | bytes 1327112 | tf_op jit(solution)/shard_map/ppermute | solution.py:61
  73.3 2.4 %collective-permute-start.3 = (bf16[2,2,16,3456]{3,2,1,0:T(8,128)(2,1)S(1)}, bf16[2,2,16,3456]{3,2,1,0:T(8,128)(2,1)S(1)}, u32[]{:S(2)}, u32[]{:S(2)}) collective-permute-start(bf16[2,2,16,3456]{3,2,1,0:T(8,128)(2,1)S(1)} %maximum_select_fusion.1), channel_id=1, source_target_pairs={{0,2},{1,3},{2,4},{3,5},{4,6},{5,7},{6,0},{7,1},{8,10},{9,11},{10,... | collective-permute-start | bytes 1327112 | tf_op jit(solution)/shard_map/ppermute | solution.py:61
  75.8 4.2 %collective-permute-done.5 = bf16[2,2,16,3456]{3,2,1,0:T(8,128)(2,1)S(1)} collective-permute-done((bf16[2,2,16,3456]{3,2,1,0:T(8,128)(2,1)S(1)}, bf16[2,2,16,3456]{3,2,1,0:T(8,128)(2,1)S(1)}, u32[]{:S(2)}, u32[]{:S(2)}) %collective-permute-start.5) | collective-permute-done | bytes 442400 | tf_op jit(solution)/shard_map/ppermute | solution.py:61
  80.0 4.4 %collective-permute-done.4 = bf16[2,2,16,3456]{3,2,1,0:T(8,128)(2,1)S(1)} collective-permute-done((bf16[2,2,16,3456]{3,2,1,0:T(8,128)(2,1)S(1)}, bf16[2,2,16,3456]{3,2,1,0:T(8,128)(2,1)S(1)}, u32[]{:S(2)}, u32[]{:S(2)}) %collective-permute-start.4) | collective-permute-done | bytes 442400 | tf_op jit(solution)/shard_map/ppermute | solution.py:61
  84.4 10.5 %collective-permute-done.3 = bf16[2,2,16,3456]{3,2,1,0:T(8,128)(2,1)S(1)} collective-permute-done((bf16[2,2,16,3456]{3,2,1,0:T(8,128)(2,1)S(1)}, bf16[2,2,16,3456]{3,2,1,0:T(8,128)(2,1)S(1)}, u32[]{:S(2)}, u32[]{:S(2)}) %collective-permute-start.3) | collective-permute-done | bytes 442400 | tf_op jit(solution)/shard_map/ppermute | solution.py:61
  95.2 0.8 gather_fusion
  96.8 0.7 copy-done.8
  97.5 2.4 %fusion.8 = f32[1,7,2,32,128]{4,0,3,2,1:T(1,128)S(1)} fusion(bf16[128,3,3,3,128]{4,3,2,1,0:T(4,128)(2,1)S(1)} %reshape_squeeze.13, bf16[1,9,4,32,128]{4,3,2,1,0:T(8,128)(2,1)S(1)} %copy-done.8), kind=kOutput, calls=%fused_computation.25 | convolution fusion | flops 388104192 | bytes 1409024 | tf_op jit(solution)/shard_map/conv_general_dilated | solution.py:227
  100.9 1.8 fusion.6
  102.8 2.4 %collective-permute-start.11 = (bf16[5,1,32,128]{3,2,1,0:T(8,128)(2,1)S(1)}, bf16[5,1,32,128]{3,2,1,0:T(8,128)(2,1)S(1)}, u32[]{:S(2)}, u32[]{:S(2)}) collective-permute-start(bf16[5,1,32,128]{3,2,1,0:T(8,128)(2,1)S(1)} %get-tuple-element.45), channel_id=1, source_target_pairs={{1,0},{2,1},{3,2},{4,3},{5,4},{6,5},{7,6},{9,8},{10,9},{11,10},{12... | collective-permute-start | bytes 122888 | tf_op jit(solution)/shard_map/ppermute | solution.py:21
  105.2 3.2 %collective-permute-start.10 = (bf16[5,1,32,128]{3,2,1,0:T(8,128)(2,1)S(1)}, bf16[5,1,32,128]{3,2,1,0:T(8,128)(2,1)S(1)}, u32[]{:S(2)}, u32[]{:S(2)}) collective-permute-start(bf16[5,1,32,128]{3,2,1,0:T(8,128)(2,1)S(1)} %get-tuple-element.44), channel_id=1, source_target_pairs={{0,1},{1,2},{2,3},{3,4},{4,5},{5,6},{6,7},{8,9},{9,10},{10,11},{11... | collective-permute-start | bytes 122888 | tf_op jit(solution)/shard_map/ppermute | solution.py:18
  108.4 1.9 collective-permute-start.7
  110.3 3.9 %collective-permute-start.6 = (bf16[5,1,32,128]{3,2,1,0:T(8,128)(2,1)S(1)}, bf16[5,1,32,128]{3,2,1,0:T(8,128)(2,1)S(1)}, u32[]{:S(2)}, u32[]{:S(2)}) collective-permute-start(bf16[5,1,32,128]{3,2,1,0:T(8,128)(2,1)S(1)} %get-tuple-element.48), channel_id=1, source_target_pairs={{0,1},{1,2},{2,3},{3,4},{4,5},{5,6},{6,7},{8,9},{9,10},{10,11},{11... | collective-permute-start | bytes 122888 | tf_op jit(solution)/shard_map/ppermute | solution.py:18
  114.3 3.7 %fusion.30 = f32[128,3,3,3,128]{0,4,3,2,1:T(8,128)} fusion(bf16[1,7,4,32,128]{4,3,2,1,0:T(8,128)(2,1)S(1)} %copy-done.9, bf16[1,5,2,32,128]{4,3,2,1,0:T(8,128)(2,1)S(1)} %fusion.59), kind=kOutput, calls=%fused_computation.51 | convolution fusion | flops 277217280 | bytes 2080768 | tf_op jit(solution)/shard_map/conv_general_dilated | solution.py:216
  117.9 2.8 %copy.228 = f32[128,3,3,3,128]{4,3,2,1,0:T(4,128)S(1)} copy(f32[128,3,3,3,128]{0,4,3,2,1:T(8,128)} %fusion.30) | data formatting | bytes 3538944 | tf_op jit(solution)/shard_map/conv_general_dilated | solution.py:216
  120.8 1.9 stack.61
  123.2 0.8 copy-done.5
  124.0 1.2 convolution_select_fusion
  125.8 0.8 copy-done.3
  126.6 0.9 convolution_select_fusion.1
  127.6 0.7 fusion.61
  128.4 3.7 %fusion.20 = f32[128,3,3,3,128]{0,4,3,2,1:T(8,128)} fusion(bf16[1,7,4,32,128]{4,3,2,1,0:T(8,128)(2,1)S(1)} %get-tuple-element.37, bf16[1,5,2,32,128]{4,3,2,1,0:T(8,128)(2,1)S(1)} %get-tuple-element.25), kind=kOutput, calls=%fused_computation.39 | convolution fusion | flops 277217280 | bytes 2080768 | tf_op jit(solution)/shard_map/conv_general_dilated | solution.py:216
  132.1 2.8 %copy.231 = f32[128,3,3,3,128]{4,3,2,1,0:T(4,128)S(1)} copy(f32[128,3,3,3,128]{0,4,3,2,1:T(8,128)} %fusion.20) | data formatting | bytes 3538944 | tf_op jit(solution)/shard_map/conv_general_dilated | solution.py:216
  134.9 1.9 stack.62
  136.9 2.3 %fusion.1 = bf16[2,8,16,3456]{3,2,1,0:T(8,128)(2,1)S(1)} fusion(f32[1,8,16,3456]{3,2,1,0:T(8,128)} %stack.62, f32[1,8,16,3456]{3,2,1,0:T(8,128)} %stack.61), kind=kLoop, calls=%fused_computation.5 | loop fusion | flops 2654208 | bytes 5308416 | tf_op jit(solution)/shard_map/convert_element_type | solution.py:185
  139.4 1.9 collective-permute-start.12
  141.3 2.4 %collective-permute-done.12 = bf16[4,2,16,3456]{3,2,1,0:T(8,128)(2,1)S(1)} collective-permute-done((bf16[4,2,16,3456]{3,2,1,0:T(8,128)(2,1)S(1)}, bf16[4,2,16,3456]{3,2,1,0:T(8,128)(2,1)S(1)}, u32[]{:S(2)}, u32[]{:S(2)}) %collective-permute-start.12) | collective-permute-done | bytes 884768 | tf_op jit(solution)/shard_map/ppermute | solution.py:170
  144.0 1.9 collective-permute-start.15
  145.9 3.5 %collective-permute-start.14 = (bf16[2,16,3456]{2,1,0:T(8,128)(2,1)S(1)}, bf16[2,16,3456]{2,1,0:T(8,128)(2,1)S(1)}, u32[]{:S(2)}, u32[]{:S(2)}) collective-permute-start(bf16[2,16,3456]{2,1,0:T(8,128)(2,1)S(1)} %get-tuple-element.34), channel_id=1, source_target_pairs={{0,4},{1,5},{2,6},{3,7},{4,0},{5,1},{6,2},{7,3},{8,12},{9,13},{10,... | collective-permute-start | bytes 663560 | tf_op jit(solution)/shard_map/ppermute | solution.py:177
  149.4 2.9 %collective-permute-start.13 = (bf16[2,16,3456]{2,1,0:T(8,128)(2,1)S(1)}, bf16[2,16,3456]{2,1,0:T(8,128)(2,1)S(1)}, u32[]{:S(2)}, u32[]{:S(2)}) collective-permute-start(bf16[2,16,3456]{2,1,0:T(8,128)(2,1)S(1)} %get-tuple-element.32), channel_id=1, source_target_pairs={{0,2},{1,3},{2,4},{3,5},{4,6},{5,7},{6,0},{7,1},{8,10},{9,11},{10,... | collective-permute-start | bytes 663560 | tf_op jit(solution)/shard_map/ppermute | solution.py:177
  152.7 2.9 %collective-permute-done.14 = bf16[2,16,3456]{2,1,0:T(8,128)(2,1)S(1)} collective-permute-done((bf16[2,16,3456]{2,1,0:T(8,128)(2,1)S(1)}, bf16[2,16,3456]{2,1,0:T(8,128)(2,1)S(1)}, u32[]{:S(2)}, u32[]{:S(2)}) %collective-permute-start.14) | collective-permute-done | bytes 221216 | tf_op jit(solution)/shard_map/ppermute | solution.py:177
  155.6 5.6 %collective-permute-done.13 = bf16[2,16,3456]{2,1,0:T(8,128)(2,1)S(1)} collective-permute-done((bf16[2,16,3456]{2,1,0:T(8,128)(2,1)S(1)}, bf16[2,16,3456]{2,1,0:T(8,128)(2,1)S(1)}, u32[]{:S(2)}, u32[]{:S(2)}) %collective-permute-start.13) | collective-permute-done | bytes 221216 | tf_op jit(solution)/shard_map/ppermute | solution.py:177
  161.4 1.4 reshape.321
  162.8 0.6 copy.234
  164.0 0.9 copy_bitcast_fusion.4.x_ref
  164.9 22.9 %shard_map.102 = f32[16,128]{1,0:T(8,128)} custom-call(f32[8,8,16,128]{3,2,1,0:T(8,128)} %copy_bitcast_fusion.4.x_ref), custom_call_target="tpu_custom_call" | custom-call | tf_op jit(solution)/shard_map/pallas_call | solution.py:143
  187.8 0.7 slice_reduce_fusion
  188.6 10.4 %all_to_all.18 = f32[8,1,1728]{2,1,0:T(1,128)S(1)} all-to-all(f32[8,1,1728]{2,1,0:T(1,128)S(1)} %broadcast_in_dim.96), channel_id=1, replica_groups=mesh['wide'=64,'rows'=8] {'rows'}, dimensions={0} | all-to-all | bytes 110592 | tf_op jit(solution)/shard_map/all_to_all | solution.py:195
  199.3 0.7 copy.236
  200.0 0.7 copy.237
  (101 shorter events, 7.9 us)
Async XLA Ops:
  7.2 19.5 %copy-start.6 = (bf16[1,5,2,32,128]{4,3,2,1,0:T(8,128)(2,1)S(1)}, bf16[1,5,2,32,128]{4,3,2,1,0:T(8,128)(2,1)}, u32[]{:S(2)}) copy-start(bf16[1,5,2,32,128]{4,3,2,1,0:T(8,128)(2,1)} %param.11) | copy-start | bytes 245764
  9.0 39.0 %all-to-all-start = ((bf16[64,2,2976]{2,1,0:T(2,128)(2,1)}), bf16[64,2,2976]{2,1,0:T(2,128)(2,1)S(1)}, u32[]{:S(2)}, u32[]{:S(2)}) async-start(bf16[64,2,2976]{2,1,0:T(2,128)(2,1)} %reshape.372), calls=%async_computation | async-start | bytes 1572864 | tf_op jit(solution)/shard_map/all_to_all | solution.py:268
  26.9 31.6 %collective-permute-start.9 = (bf16[5,1,32,128]{3,2,1,0:T(8,128)(2,1)S(1)}, bf16[5,1,32,128]{3,2,1,0:T(8,128)(2,1)S(1)}, u32[]{:S(2)}, u32[]{:S(2)}) collective-permute-start(bf16[5,1,32,128]{3,2,1,0:T(8,128)(2,1)S(1)} %get-tuple-element.47), channel_id=1, source_target_pairs={{1,0},{2,1},{3,2},{4,3},{5,4},{6,5},{7,6},{9,8},{10,9},{11,10},{12... | collective-permute-start | bytes 122888 | tf_op jit(solution)/shard_map/ppermute | solution.py:21
  29.8 28.7 %collective-permute-start.8 = (bf16[5,1,32,128]{3,2,1,0:T(8,128)(2,1)S(1)}, bf16[5,1,32,128]{3,2,1,0:T(8,128)(2,1)S(1)}, u32[]{:S(2)}, u32[]{:S(2)}) collective-permute-start(bf16[5,1,32,128]{3,2,1,0:T(8,128)(2,1)S(1)} %get-tuple-element.46), channel_id=1, source_target_pairs={{0,1},{1,2},{2,3},{3,4},{4,5},{5,6},{6,7},{8,9},{9,10},{10,11},{11... | collective-permute-start | bytes 122888 | tf_op jit(solution)/shard_map/ppermute | solution.py:18
  49.5 0.7 copy-start
  50.2 14.8 %collective-permute-start.1 = (bf16[5,1,32,128]{3,2,1,0:T(8,128)(2,1)S(1)}, bf16[5,1,32,128]{3,2,1,0:T(8,128)(2,1)S(1)}, u32[]{:S(2)}, u32[]{:S(2)}) collective-permute-start(bf16[5,1,32,128]{3,2,1,0:T(8,128)(2,1)S(1)} %get-tuple-element.51), channel_id=1, source_target_pairs={{1,0},{2,1},{3,2},{4,3},{5,4},{6,5},{7,6},{9,8},{10,9},{11,10},{12... | collective-permute-start | bytes 122888 | tf_op jit(solution)/shard_map/ppermute | solution.py:21
  55.5 9.6 %collective-permute-start = (bf16[5,1,32,128]{3,2,1,0:T(8,128)(2,1)S(1)}, bf16[5,1,32,128]{3,2,1,0:T(8,128)(2,1)S(1)}, u32[]{:S(2)}, u32[]{:S(2)}) collective-permute-start(bf16[5,1,32,128]{3,2,1,0:T(8,128)(2,1)S(1)} %get-tuple-element.50), channel_id=1, source_target_pairs={{0,1},{1,2},{2,3},{3,4},{4,5},{5,6},{6,7},{8,9},{9,10},{10,11},{11... | collective-permute-start | bytes 122888 | tf_op jit(solution)/shard_map/ppermute | solution.py:18
  63.1 3.4 %collective-permute-start.2 = (bf16[2,16,3456]{2,1,0:T(8,128)(2,1)S(1)}, bf16[2,16,3456]{2,1,0:T(8,128)(2,1)S(1)}, u32[]{:S(2)}, u32[]{:S(2)}) collective-permute-start(bf16[2,16,3456]{2,1,0:T(8,128)(2,1)S(1)} %reshape.319), channel_id=1, source_target_pairs={{0,1},{1,0},{2,3},{3,2},{4,5},{5,4},{6,7},{7,6},{8,9},{9,8},{10,11... | collective-permute-start | bytes 663560 | tf_op jit(solution)/shard_map/ppermute | solution.py:56
  66.5 13.5 %collective-permute-start.5 = (bf16[2,2,16,3456]{3,2,1,0:T(8,128)(2,1)S(1)}, bf16[2,2,16,3456]{3,2,1,0:T(8,128)(2,1)S(1)}, u32[]{:S(2)}, u32[]{:S(2)}) collective-permute-start(bf16[2,2,16,3456]{3,2,1,0:T(8,128)(2,1)S(1)} %maximum_select_fusion.1), channel_id=1, source_target_pairs={{0,6},{1,7},{2,0},{3,1},{4,2},{5,3},{6,4},{7,5},{8,14},{9,15},{10,... | collective-permute-start | bytes 1327112 | tf_op jit(solution)/shard_map/ppermute | solution.py:61
  69.9 14.5 %collective-permute-start.4 = (bf16[2,2,16,3456]{3,2,1,0:T(8,128)(2,1)S(1)}, bf16[2,2,16,3456]{3,2,1,0:T(8,128)(2,1)S(1)}, u32[]{:S(2)}, u32[]{:S(2)}) collective-permute-start(bf16[2,2,16,3456]{3,2,1,0:T(8,128)(2,1)S(1)} %maximum_select_fusion.1), channel_id=1, source_target_pairs={{0,4},{1,5},{2,6},{3,7},{4,0},{5,1},{6,2},{7,3},{8,12},{9,13},{10,... | collective-permute-start | bytes 1327112 | tf_op jit(solution)/shard_map/ppermute | solution.py:61
  73.3 21.6 %collective-permute-start.3 = (bf16[2,2,16,3456]{3,2,1,0:T(8,128)(2,1)S(1)}, bf16[2,2,16,3456]{3,2,1,0:T(8,128)(2,1)S(1)}, u32[]{:S(2)}, u32[]{:S(2)}) collective-permute-start(bf16[2,2,16,3456]{3,2,1,0:T(8,128)(2,1)S(1)} %maximum_select_fusion.1), channel_id=1, source_target_pairs={{0,2},{1,3},{2,4},{3,5},{4,6},{5,7},{6,0},{7,1},{8,10},{9,11},{10,... | collective-permute-start | bytes 1327112 | tf_op jit(solution)/shard_map/ppermute | solution.py:61
  96.5 1.0 copy-start.8
  97.5 2.4 %copy-start.2 = (bf16[128,3,3,3,128]{4,3,2,1,0:T(4,128)(2,1)}, bf16[128,3,3,3,128]{4,3,2,1,0:T(4,128)(2,1)S(1)}, u32[]{:S(2)}) copy-start(bf16[128,3,3,3,128]{4,3,2,1,0:T(4,128)(2,1)S(1)} %reshape_squeeze.13) | copy-start | bytes 2654212
  99.9 0.9 copy-start.9
  100.9 1.8 copy-start.4
  102.8 19.9 %collective-permute-start.11 = (bf16[5,1,32,128]{3,2,1,0:T(8,128)(2,1)S(1)}, bf16[5,1,32,128]{3,2,1,0:T(8,128)(2,1)S(1)}, u32[]{:S(2)}, u32[]{:S(2)}) collective-permute-start(bf16[5,1,32,128]{3,2,1,0:T(8,128)(2,1)S(1)} %get-tuple-element.45), channel_id=1, source_target_pairs={{1,0},{2,1},{3,2},{4,3},{5,4},{6,5},{7,6},{9,8},{10,9},{11,10},{12... | collective-permute-start | bytes 122888 | tf_op jit(solution)/shard_map/ppermute | solution.py:21
  105.2 17.5 %collective-permute-start.10 = (bf16[5,1,32,128]{3,2,1,0:T(8,128)(2,1)S(1)}, bf16[5,1,32,128]{3,2,1,0:T(8,128)(2,1)S(1)}, u32[]{:S(2)}, u32[]{:S(2)}) collective-permute-start(bf16[5,1,32,128]{3,2,1,0:T(8,128)(2,1)S(1)} %get-tuple-element.44), channel_id=1, source_target_pairs={{0,1},{1,2},{2,3},{3,4},{4,5},{5,6},{6,7},{8,9},{9,10},{10,11},{11... | collective-permute-start | bytes 122888 | tf_op jit(solution)/shard_map/ppermute | solution.py:18
  108.4 17.0 %collective-permute-start.7 = (bf16[5,1,32,128]{3,2,1,0:T(8,128)(2,1)S(1)}, bf16[5,1,32,128]{3,2,1,0:T(8,128)(2,1)S(1)}, u32[]{:S(2)}, u32[]{:S(2)}) collective-permute-start(bf16[5,1,32,128]{3,2,1,0:T(8,128)(2,1)S(1)} %get-tuple-element.49), channel_id=1, source_target_pairs={{1,0},{2,1},{3,2},{4,3},{5,4},{6,5},{7,6},{9,8},{10,9},{11,10},{12... | collective-permute-start | bytes 122888 | tf_op jit(solution)/shard_map/ppermute | solution.py:21
  110.3 15.1 %collective-permute-start.6 = (bf16[5,1,32,128]{3,2,1,0:T(8,128)(2,1)S(1)}, bf16[5,1,32,128]{3,2,1,0:T(8,128)(2,1)S(1)}, u32[]{:S(2)}, u32[]{:S(2)}) collective-permute-start(bf16[5,1,32,128]{3,2,1,0:T(8,128)(2,1)S(1)} %get-tuple-element.48), channel_id=1, source_target_pairs={{0,1},{1,2},{2,3},{3,4},{4,5},{5,6},{6,7},{8,9},{9,10},{10,11},{11... | collective-permute-start | bytes 122888 | tf_op jit(solution)/shard_map/ppermute | solution.py:18
  122.7 1.3 copy-start.5
  122.7 1.3 copy-start.10
  125.3 1.3 copy-start.3
  126.6 1.1 copy-start.1
  126.6 1.1 copy-start.7
  139.4 4.3 %collective-permute-start.12 = (bf16[4,2,16,3456]{3,2,1,0:T(8,128)(2,1)S(1)}, bf16[4,2,16,3456]{3,2,1,0:T(8,128)(2,1)S(1)}, u32[]{:S(2)}, u32[]{:S(2)}) collective-permute-start(bf16[4,2,16,3456]{3,2,1,0:T(8,128)(2,1)S(1)} %bitcast.174), channel_id=1, source_target_pairs={{0,1},{1,0},{2,3},{3,2},{4,5},{5,4},{6,7},{7,6},{8,9},{9,8},{10,11... | collective-permute-start | bytes 2654216 | tf_op jit(solution)/shard_map/ppermute | solution.py:170
  144.0 8.8 %collective-permute-start.15 = (bf16[2,16,3456]{2,1,0:T(8,128)(2,1)S(1)}, bf16[2,16,3456]{2,1,0:T(8,128)(2,1)S(1)}, u32[]{:S(2)}, u32[]{:S(2)}) collective-permute-start(bf16[2,16,3456]{2,1,0:T(8,128)(2,1)S(1)} %get-tuple-element.33), channel_id=1, source_target_pairs={{0,6},{1,7},{2,0},{3,1},{4,2},{5,3},{6,4},{7,5},{8,14},{9,15},{10,... | collective-permute-start | bytes 663560 | tf_op jit(solution)/shard_map/ppermute | solution.py:177
  145.9 9.7 %collective-permute-start.14 = (bf16[2,16,3456]{2,1,0:T(8,128)(2,1)S(1)}, bf16[2,16,3456]{2,1,0:T(8,128)(2,1)S(1)}, u32[]{:S(2)}, u32[]{:S(2)}) collective-permute-start(bf16[2,16,3456]{2,1,0:T(8,128)(2,1)S(1)} %get-tuple-element.34), channel_id=1, source_target_pairs={{0,4},{1,5},{2,6},{3,7},{4,0},{5,1},{6,2},{7,3},{8,12},{9,13},{10,... | collective-permute-start | bytes 663560 | tf_op jit(solution)/shard_map/ppermute | solution.py:177
  149.4 11.9 %collective-permute-start.13 = (bf16[2,16,3456]{2,1,0:T(8,128)(2,1)S(1)}, bf16[2,16,3456]{2,1,0:T(8,128)(2,1)S(1)}, u32[]{:S(2)}, u32[]{:S(2)}) collective-permute-start(bf16[2,16,3456]{2,1,0:T(8,128)(2,1)S(1)} %get-tuple-element.32), channel_id=1, source_target_pairs={{0,2},{1,3},{2,4},{3,5},{4,6},{5,7},{6,0},{7,1},{8,10},{9,11},{10,... | collective-permute-start | bytes 663560 | tf_op jit(solution)/shard_map/ppermute | solution.py:177

commit v10 on v9

--- a/solution.py
+++ b/solution.py
@@ -182,7 +182,7 @@
     _, channels, total_rows = grad_t.shape
     part = channels // band_count
     chunk = total_rows // wide_size
-    blocks = grad_t.astype(jnp.bfloat16).reshape(2, band_count, part, total_rows)
+    blocks = grad_t.reshape(2, band_count, part, total_rows)
     blocks = jnp.transpose(blocks, (1, 0, 2, 3))
     band_sum = rows_reduce(blocks, band_count)
     band_sum = band_sum.reshape(2, part, wide_size, chunk)
@@ -192,9 +192,7 @@
     tall = -(-size // (8 * lanes)) * 8
     padded = jnp.pad(band_sum, ((0, 0), (0, tall * lanes - size)))
     share = wide_sum(padded.reshape(wide_size, tall, lanes)).reshape(1, tall * lanes)[:, :size]
-    joined = lax.all_to_all(
-        jnp.broadcast_to(share, (band_count,) + share.shape[1:]), "rows", 0, 0, tiled=True
-    )
+    joined = rows_gather(share[0], band_count)
     joined = joined.reshape(band_count, 2, part, chunk)
     joined = jnp.transpose(joined, (1, 3, 0, 2)).reshape(2, chunk, channels)
     return joined[0], joined[1]
@@ -296,7 +294,9 @@
         jnp.bfloat16
     )
     scale = 1.0 / math.sqrt(frames * band_rows * columns * band_count * wide_size)
-    grads = jnp.stack([weight_first, weight_second]) * scale
+    grads = jnp.stack(
+        [(weight_first * scale).astype(jnp.bfloat16), (weight_second * scale).astype(jnp.bfloat16)]
+    )
     share_first, share_second = reduce_weight_grads(grads, band_count, wide_size)
     return (block_out[None], grad_input[None], share_first, share_second)
 

time: 202 us -> 203 us (level)
  starting transfers between devices: 64 us -> 76.7 us
  blocking collectives: 10.4 us -> 0 us
  local copies, waits for them, and re-layouts: 30.3 us -> 24.8 us
  waiting for transfers between devices: 46 us -> 49.7 us
    all_to_all x1 -> x0, blocking collectives: 10.4 us -> none  [reduce_weight_grads(): lax.all_to_all(jnp.broadcast_to(share, (band_count,) + share.shape[1:]),...]
    ppermute x3 -> x6, starting transfers between devices: 9.22 us -> 17.3 us  [rows_gather(): held.append(lax.ppermute(pair, 'rows', route))]
    conv_general_dilated x2 -> x0, local copies, waits for them, and re-layouts: 5.66 us -> none  [conv_weight_grad_t(): lax.conv_general_dilated(padded[None], upstream[None], (1, 1, 1), ((0, 0)...]
    ppermute x1 -> x2, starting transfers between devices: 1.91 us -> 6.52 us  [rows_gather(): got = lax.ppermute(block, 'rows', partner)]
    another operation x2 -> x0, local copies, waits for them, and re-layouts: 3.82 us -> none  [body(): grads = jnp.stack([weight_first, weight_second]) * scale]
    convert_element_type x0 -> x4, local copies, waits for them, and re-layouts: none -> 3.5 us  [the longest x2 1.75 us: body(): (weight_first * scale).astype(jnp.bfloat16)]
    ppermute x3 -> x6, waiting for transfers between devices: 19.1 us -> 21.9 us  [rows_gather(): held.append(lax.ppermute(pair, 'rows', route))]
    convert_element_type x1 -> x0, other arithmetic: 2.28 us -> none  [reduce_weight_grads(): grad_t.astype(jnp.bfloat16).reshape(2, band_count, part, total_rows)]
  transfers between devices with their start and end apart: 17 -> 21, of which waited for: 9 -> 11; matrix products, arithmetic and copies ran while one was open for 9% -> 7% of each run, Pallas kernels for 0% -> 0%
where the time goes in v10:
time: 203 us; the launch traced here: 202 us
  starting transfers between devices  76.7 us (38%)
  waiting for transfers between devices  49.7 us (24%)
  local copies, waits for them, and re-layouts  24.8 us (12%)
  Pallas kernels  22.9 us (11%)
  matrix products  13.5 us (7%)
  other arithmetic  12.3 us (6%)
  between operations  2.35 us (1%)
    pallas_call x1, Pallas kernels, wide_sum(): pl.pallas_call(functools.partial(_wide_sum_kernel, outer, inner), out_sha...  22.9 us
    ppermute x6, waiting for transfers between devices, rows_gather(): held.append(lax.ppermute(pair, 'rows', route))  21.9 us
    ppermute x6, starting transfers between devices, rows_gather(): held.append(lax.ppermute(pair, 'rows', route))  17.3 us
    all_to_all x1, starting transfers between devices, body(): lax.all_to_all(tagged, 'wide', split_axis=0, concat_axis=0, tiled=True)  17.1 us
    all_to_all x1, waiting for transfers between devices, body(): lax.all_to_all(tagged, 'wide', split_axis=0, concat_axis=0, tiled=True)  15 us
    ppermute x4, starting transfers between devices, with_halo(): lax.ppermute(lax.slice_in_dim(block, block.shape[dim] - width, None, axis...  13.1 us
    ppermute x4, starting transfers between devices, with_halo(): lax.ppermute(lax.slice_in_dim(block, 0, width, axis=dim), axis, backward)  12.4 us
    ppermute x3, waiting for transfers between devices, rows_reduce(): total = total + lax.ppermute(piece, 'rows', route).astype(jnp.float32)  8.93 us
  transfers between devices with their start and end apart: 21, of which 11 were waited for; matrix products, arithmetic and copies ran while one was open for 7% of the time, Pallas kernels for 0%

profile of v10, /device:TPU:1, one launch (start us, length us, event | category | flops | bytes accessed | tf_op | source)
XLA Modules:
  0.0 202.1 jit_solution(8467467505188304209)
XLA Ops:
  1.3 0.9 convert_reduce_fusion.1
  3.0 0.9 pad.97
  4.4 0.8 fusion.63
  6.1 1.1 reduce.4
  7.2 1.7 reshape.461
  9.0 17.1 %all-to-all-start = ((bf16[64,2,2976]{2,1,0:T(2,128)(2,1)}), bf16[64,2,2976]{2,1,0:T(2,128)(2,1)S(1)}, u32[]{:S(2)}, u32[]{:S(2)}) async-start(bf16[64,2,2976]{2,1,0:T(2,128)(2,1)} %reshape.461), calls=%async_computation | async-start | bytes 1572864 | tf_op jit(solution)/shard_map/all_to_all | solution.py:266
  26.9 2.9 %collective-permute-start.9 = (bf16[5,1,32,128]{3,2,1,0:T(8,128)(2,1)S(1)}, bf16[5,1,32,128]{3,2,1,0:T(8,128)(2,1)S(1)}, u32[]{:S(2)}, u32[]{:S(2)}) collective-permute-start(bf16[5,1,32,128]{3,2,1,0:T(8,128)(2,1)S(1)} %get-tuple-element.51), channel_id=1, source_target_pairs={{1,0},{2,1},{3,2},{4,3},{5,4},{6,5},{7,6},{9,8},{10,9},{11,10},{12... | collective-permute-start | bytes 122888 | tf_op jit(solution)/shard_map/ppermute | solution.py:21
  29.8 3.0 %collective-permute-start.8 = (bf16[5,1,32,128]{3,2,1,0:T(8,128)(2,1)S(1)}, bf16[5,1,32,128]{3,2,1,0:T(8,128)(2,1)S(1)}, u32[]{:S(2)}, u32[]{:S(2)}) collective-permute-start(bf16[5,1,32,128]{3,2,1,0:T(8,128)(2,1)S(1)} %get-tuple-element.50), channel_id=1, source_target_pairs={{0,1},{1,2},{2,3},{3,4},{4,5},{5,6},{6,7},{8,9},{9,10},{10,11},{11... | collective-permute-start | bytes 122888 | tf_op jit(solution)/shard_map/ppermute | solution.py:18
  33.0 15.0 %all-to-all-done = bf16[64,2,2976]{2,1,0:T(2,128)(2,1)S(1)} async-done(((bf16[64,2,2976]{2,1,0:T(2,128)(2,1)}), bf16[64,2,2976]{2,1,0:T(2,128)(2,1)S(1)}, u32[]{:S(2)}, u32[]{:S(2)}) %all-to-all-start) | async-done | bytes 761888 | tf_op jit(solution)/shard_map/all_to_all | solution.py:266
  48.0 1.0 reshape.462
  50.2 5.2 %collective-permute-start.1 = (bf16[5,1,32,128]{3,2,1,0:T(8,128)(2,1)S(1)}, bf16[5,1,32,128]{3,2,1,0:T(8,128)(2,1)S(1)}, u32[]{:S(2)}, u32[]{:S(2)}) collective-permute-start(bf16[5,1,32,128]{3,2,1,0:T(8,128)(2,1)S(1)} %get-tuple-element.55), channel_id=1, source_target_pairs={{1,0},{2,1},{3,2},{4,3},{5,4},{6,5},{7,6},{9,8},{10,9},{11,10},{12... | collective-permute-start | bytes 122888 | tf_op jit(solution)/shard_map/ppermute | solution.py:21
  55.5 3.0 %collective-permute-start = (bf16[5,1,32,128]{3,2,1,0:T(8,128)(2,1)S(1)}, bf16[5,1,32,128]{3,2,1,0:T(8,128)(2,1)S(1)}, u32[]{:S(2)}, u32[]{:S(2)}) collective-permute-start(bf16[5,1,32,128]{3,2,1,0:T(8,128)(2,1)S(1)} %get-tuple-element.54), channel_id=1, source_target_pairs={{0,1},{1,2},{2,3},{3,4},{4,5},{5,6},{6,7},{8,9},{9,10},{10,11},{11... | collective-permute-start | bytes 122888 | tf_op jit(solution)/shard_map/ppermute | solution.py:18
  58.5 0.8 fusion.36
  59.3 1.6 reshape.401
  63.1 1.9 collective-permute-start.2
  65.1 0.7 maximum_bitcast_fusion.1
  65.8 0.7 collective-permute-done.2
  66.5 3.4 %collective-permute-start.5 = (bf16[2,2,16,3456]{3,2,1,0:T(8,128)(2,1)S(1)}, bf16[2,2,16,3456]{3,2,1,0:T(8,128)(2,1)S(1)}, u32[]{:S(2)}, u32[]{:S(2)}) collective-permute-start(bf16[2,2,16,3456]{3,2,1,0:T(8,128)(2,1)S(1)} %maximum_select_fusion.1), channel_id=1, source_target_pairs={{0,6},{1,7},{2,0},{3,1},{4,2},{5,3},{6,4},{7,5},{8,14},{9,15},{10,... | collective-permute-start | bytes 1327112 | tf_op jit(solution)/shard_map/ppermute | solution.py:61
  70.0 3.4 %collective-permute-start.4 = (bf16[2,2,16,3456]{3,2,1,0:T(8,128)(2,1)S(1)}, bf16[2,2,16,3456]{3,2,1,0:T(8,128)(2,1)S(1)}, u32[]{:S(2)}, u32[]{:S(2)}) collective-permute-start(bf16[2,2,16,3456]{3,2,1,0:T(8,128)(2,1)S(1)} %maximum_select_fusion.1), channel_id=1, source_target_pairs={{0,4},{1,5},{2,6},{3,7},{4,0},{5,1},{6,2},{7,3},{8,12},{9,13},{10,... | collective-permute-start | bytes 1327112 | tf_op jit(solution)/shard_map/ppermute | solution.py:61
  73.4 2.4 %collective-permute-start.3 = (bf16[2,2,16,3456]{3,2,1,0:T(8,128)(2,1)S(1)}, bf16[2,2,16,3456]{3,2,1,0:T(8,128)(2,1)S(1)}, u32[]{:S(2)}, u32[]{:S(2)}) collective-permute-start(bf16[2,2,16,3456]{3,2,1,0:T(8,128)(2,1)S(1)} %maximum_select_fusion.1), channel_id=1, source_target_pairs={{0,2},{1,3},{2,4},{3,5},{4,6},{5,7},{6,0},{7,1},{8,10},{9,11},{10,... | collective-permute-start | bytes 1327112 | tf_op jit(solution)/shard_map/ppermute | solution.py:61
  75.9 4.2 %collective-permute-done.5 = bf16[2,2,16,3456]{3,2,1,0:T(8,128)(2,1)S(1)} collective-permute-done((bf16[2,2,16,3456]{3,2,1,0:T(8,128)(2,1)S(1)}, bf16[2,2,16,3456]{3,2,1,0:T(8,128)(2,1)S(1)}, u32[]{:S(2)}, u32[]{:S(2)}) %collective-permute-start.5) | collective-permute-done | bytes 442400 | tf_op jit(solution)/shard_map/ppermute | solution.py:61
  80.1 4.4 %collective-permute-done.4 = bf16[2,2,16,3456]{3,2,1,0:T(8,128)(2,1)S(1)} collective-permute-done((bf16[2,2,16,3456]{3,2,1,0:T(8,128)(2,1)S(1)}, bf16[2,2,16,3456]{3,2,1,0:T(8,128)(2,1)S(1)}, u32[]{:S(2)}, u32[]{:S(2)}) %collective-permute-start.4) | collective-permute-done | bytes 442400 | tf_op jit(solution)/shard_map/ppermute | solution.py:61
  84.5 10.5 %collective-permute-done.3 = bf16[2,2,16,3456]{3,2,1,0:T(8,128)(2,1)S(1)} collective-permute-done((bf16[2,2,16,3456]{3,2,1,0:T(8,128)(2,1)S(1)}, bf16[2,2,16,3456]{3,2,1,0:T(8,128)(2,1)S(1)}, u32[]{:S(2)}, u32[]{:S(2)}) %collective-permute-start.3) | collective-permute-done | bytes 442400 | tf_op jit(solution)/shard_map/ppermute | solution.py:61
  95.2 0.8 gather_fusion
  96.9 0.7 copy-done.7
  97.5 2.4 %fusion.7 = f32[1,7,2,32,128]{4,0,3,2,1:T(1,128)S(1)} fusion(bf16[128,3,3,3,128]{4,3,2,1,0:T(4,128)(2,1)S(1)} %reshape_squeeze.13, bf16[1,9,4,32,128]{4,3,2,1,0:T(8,128)(2,1)S(1)} %copy-done.7), kind=kOutput, calls=%fused_computation.27 | convolution fusion | flops 388104192 | bytes 1409024 | tf_op jit(solution)/shard_map/conv_general_dilated | solution.py:225
  100.0 0.7 fusion.80
  102.2 3.2 %fusion.5 = f32[1,5,2,32,128]{4,0,3,2,1:T(1,128)S(1)} fusion(bf16[128,3,3,3,128]{4,3,2,1,0:T(4,128)(2,1)S(1)} %reshape_squeeze.12, bf16[1,7,4,32,128]{4,3,2,1,0:T(8,128)(2,1)} %maximum_bitcast_fusion.1), kind=kOutput, calls=%fused_computation.25 | convolution fusion | flops 277217280 | bytes 1277952 | tf_op jit(solution)/shard_map/conv_general_dilated | solution.py:205
  106.2 2.4 %collective-permute-start.11 = (bf16[5,1,32,128]{3,2,1,0:T(8,128)(2,1)}, bf16[5,1,32,128]{3,2,1,0:T(8,128)(2,1)}, u32[]{:S(2)}, u32[]{:S(2)}) collective-permute-start(bf16[5,1,32,128]{3,2,1,0:T(8,128)(2,1)} %get-tuple-element.49), channel_id=1, source_target_pairs={{1,0},{2,1},{3,2},{4,3},{5,4},{6,5},{7,6},{9,8},{10,9},{11,10},{12... | collective-permute-start | bytes 122888 | tf_op jit(solution)/shard_map/ppermute | solution.py:21
  108.6 3.2 %collective-permute-start.10 = (bf16[5,1,32,128]{3,2,1,0:T(8,128)(2,1)}, bf16[5,1,32,128]{3,2,1,0:T(8,128)(2,1)}, u32[]{:S(2)}, u32[]{:S(2)}) collective-permute-start(bf16[5,1,32,128]{3,2,1,0:T(8,128)(2,1)} %get-tuple-element.48), channel_id=1, source_target_pairs={{0,1},{1,2},{2,3},{3,4},{4,5},{5,6},{6,7},{8,9},{9,10},{10,11},{11... | collective-permute-start | bytes 122888 | tf_op jit(solution)/shard_map/ppermute | solution.py:18
  112.4 1.9 collective-permute-start.7
  114.3 3.9 %collective-permute-start.6 = (bf16[5,1,32,128]{3,2,1,0:T(8,128)(2,1)}, bf16[5,1,32,128]{3,2,1,0:T(8,128)(2,1)}, u32[]{:S(2)}, u32[]{:S(2)}) collective-permute-start(bf16[5,1,32,128]{3,2,1,0:T(8,128)(2,1)} %get-tuple-element.52), channel_id=1, source_target_pairs={{0,1},{1,2},{2,3},{3,4},{4,5},{5,6},{6,7},{8,9},{9,10},{10,11},{11... | collective-permute-start | bytes 122888 | tf_op jit(solution)/shard_map/ppermute | solution.py:18
  118.3 2.6 %multiply_convert_fusion.1 = bf16[128,3,3,3,128]{0,4,3,2,1:T(8,128)(2,1)S(1)} fusion(bf16[1,7,4,32,128]{4,3,2,1,0:T(8,128)(2,1)S(1)} %copy-done.8, bf16[1,5,2,32,128]{4,3,2,1,0:T(8,128)(2,1)S(1)} %fusion.56), kind=kOutput, calls=%fused_computation.11 | convolution fusion | flops 278102016 | bytes 1196032 | tf_op jit(solution)/shard_map/conv_general_dilated | solution.py:214
  120.8 1.0 copy.271
  121.8 0.8 convert_element_type.153
  122.7 0.9 fusion.30
  124.0 1.2 convolution_select_fusion
  125.4 0.7 pad_maximum_fusion.3
  126.2 0.8 fusion.68
  127.3 0.9 convolution_select_fusion.1
  128.4 0.7 fusion.58
  129.2 2.6 %multiply_convert_fusion = bf16[128,3,3,3,128]{0,4,3,2,1:T(8,128)(2,1)S(1)} fusion(bf16[1,7,4,32,128]{4,3,2,1,0:T(8,128)(2,1)S(1)} %get-tuple-element.41, bf16[1,5,2,32,128]{4,3,2,1,0:T(8,128)(2,1)S(1)} %get-tuple-element.29), kind=kOutput, calls=%fused_computation.10 | convolution fusion | flops 278102016 | bytes 1196032 | tf_op jit(solution)/shard_map/conv_general_dilated | solution.py:214
  131.7 1.0 copy.274
  132.7 0.8 convert_element_type.155
  133.9 1.9 collective-permute-start.12
  135.9 2.4 %collective-permute-done.12 = bf16[4,2,16,3456]{3,2,1,0:T(8,128)(2,1)S(1)} collective-permute-done((bf16[4,2,16,3456]{3,2,1,0:T(8,128)(2,1)S(1)}, bf16[4,2,16,3456]{3,2,1,0:T(8,128)(2,1)S(1)}, u32[]{:S(2)}, u32[]{:S(2)}) %collective-permute-start.12) | collective-permute-done | bytes 884768 | tf_op jit(solution)/shard_map/ppermute | solution.py:170
  138.5 1.9 collective-permute-start.15
  140.5 3.5 %collective-permute-start.14 = (bf16[2,16,3456]{2,1,0:T(8,128)(2,1)S(1)}, bf16[2,16,3456]{2,1,0:T(8,128)(2,1)S(1)}, u32[]{:S(2)}, u32[]{:S(2)}) collective-permute-start(bf16[2,16,3456]{2,1,0:T(8,128)(2,1)S(1)} %get-tuple-element.38), channel_id=1, source_target_pairs={{0,4},{1,5},{2,6},{3,7},{4,0},{5,1},{6,2},{7,3},{8,12},{9,13},{10,... | collective-permute-start | bytes 663560 | tf_op jit(solution)/shard_map/ppermute | solution.py:177
  143.9 2.9 %collective-permute-start.13 = (bf16[2,16,3456]{2,1,0:T(8,128)(2,1)S(1)}, bf16[2,16,3456]{2,1,0:T(8,128)(2,1)S(1)}, u32[]{:S(2)}, u32[]{:S(2)}) collective-permute-start(bf16[2,16,3456]{2,1,0:T(8,128)(2,1)S(1)} %get-tuple-element.36), channel_id=1, source_target_pairs={{0,2},{1,3},{2,4},{3,5},{4,6},{5,7},{6,0},{7,1},{8,10},{9,11},{10,... | collective-permute-start | bytes 663560 | tf_op jit(solution)/shard_map/ppermute | solution.py:177
  147.3 2.9 %collective-permute-done.14 = bf16[2,16,3456]{2,1,0:T(8,128)(2,1)S(1)} collective-permute-done((bf16[2,16,3456]{2,1,0:T(8,128)(2,1)S(1)}, bf16[2,16,3456]{2,1,0:T(8,128)(2,1)S(1)}, u32[]{:S(2)}, u32[]{:S(2)}) %collective-permute-start.14) | collective-permute-done | bytes 221216 | tf_op jit(solution)/shard_map/ppermute | solution.py:177
  150.2 5.6 %collective-permute-done.13 = bf16[2,16,3456]{2,1,0:T(8,128)(2,1)S(1)} collective-permute-done((bf16[2,16,3456]{2,1,0:T(8,128)(2,1)S(1)}, bf16[2,16,3456]{2,1,0:T(8,128)(2,1)S(1)}, u32[]{:S(2)}, u32[]{:S(2)}) %collective-permute-start.13) | collective-permute-done | bytes 221216 | tf_op jit(solution)/shard_map/ppermute | solution.py:177
  155.9 1.4 reshape.404
  158.6 0.9 copy_bitcast_fusion.4.x_ref
  159.5 22.9 %shard_map.102 = f32[16,128]{1,0:T(8,128)} custom-call(f32[8,8,16,128]{3,2,1,0:T(8,128)} %copy_bitcast_fusion.4.x_ref), custom_call_target="tpu_custom_call" | custom-call | tf_op jit(solution)/shard_map/pallas_call | solution.py:143
  182.4 0.7 slice_bitcast_fusion
  183.1 4.6 %collective-permute-start.16 = (f32[1728]{0:T(1024)S(1)}, f32[1728]{0:T(1024)S(1)}, u32[]{:S(2)}, u32[]{:S(2)}) collective-permute-start(f32[1728]{0:T(1024)S(1)} %get-tuple-element.57), channel_id=1, source_target_pairs={{0,1},{1,0},{2,3},{3,2},{4,5},{5,4},{6,7},{7,6},{8,9},{9,8},{10,11... | collective-permute-start | bytes 20744 | tf_op jit(solution)/shard_map/ppermute | solution.py:56
  187.7 0.8 collective-permute-done.16
  188.6 1.9 collective-permute-start.19
  190.5 3.4 %collective-permute-start.18 = (f32[2,1728]{1,0:T(2,128)S(1)}, f32[2,1728]{1,0:T(2,128)S(1)}, u32[]{:S(2)}, u32[]{:S(2)}) collective-permute-start(f32[2,1728]{1,0:T(2,128)S(1)} %maximum_select_fusion.3), channel_id=1, source_target_pairs={{0,4},{1,5},{2,6},{3,7},{4,0},{5,1},{6,2},{7,3},{8,12},{9,13},{10,... | collective-permute-start | bytes 41480 | tf_op jit(solution)/shard_map/ppermute | solution.py:61
  193.9 2.8 %collective-permute-start.17 = (f32[2,1728]{1,0:T(2,128)S(1)}, f32[2,1728]{1,0:T(2,128)S(1)}, u32[]{:S(2)}, u32[]{:S(2)}) collective-permute-start(f32[2,1728]{1,0:T(2,128)S(1)} %maximum_select_fusion.3), channel_id=1, source_target_pairs={{0,2},{1,3},{2,4},{3,5},{4,6},{5,7},{6,0},{7,1},{8,10},{9,11},{10,... | collective-permute-start | bytes 41480 | tf_op jit(solution)/shard_map/ppermute | solution.py:61
  196.8 2.8 %collective-permute-done.17 = f32[2,1728]{1,0:T(2,128)S(1)} collective-permute-done((f32[2,1728]{1,0:T(2,128)S(1)}, f32[2,1728]{1,0:T(2,128)S(1)}, u32[]{:S(2)}, u32[]{:S(2)}) %collective-permute-start.17) | collective-permute-done | bytes 13856 | tf_op jit(solution)/shard_map/ppermute | solution.py:61
  199.6 0.7 gather_fusion.1
  200.7 0.7 copy.279
  201.4 0.7 copy.280
  (121 shorter events, 14.5 us)
Async XLA Ops:
  7.2 19.6 %copy-start.5 = (bf16[1,5,2,32,128]{4,3,2,1,0:T(8,128)(2,1)S(1)}, bf16[1,5,2,32,128]{4,3,2,1,0:T(8,128)(2,1)}, u32[]{:S(2)}) copy-start(bf16[1,5,2,32,128]{4,3,2,1,0:T(8,128)(2,1)} %param.11) | copy-start | bytes 245764
  9.0 39.0 %all-to-all-start = ((bf16[64,2,2976]{2,1,0:T(2,128)(2,1)}), bf16[64,2,2976]{2,1,0:T(2,128)(2,1)S(1)}, u32[]{:S(2)}, u32[]{:S(2)}) async-start(bf16[64,2,2976]{2,1,0:T(2,128)(2,1)} %reshape.461), calls=%async_computation | async-start | bytes 1572864 | tf_op jit(solution)/shard_map/all_to_all | solution.py:266
  26.9 31.6 %collective-permute-start.9 = (bf16[5,1,32,128]{3,2,1,0:T(8,128)(2,1)S(1)}, bf16[5,1,32,128]{3,2,1,0:T(8,128)(2,1)S(1)}, u32[]{:S(2)}, u32[]{:S(2)}) collective-permute-start(bf16[5,1,32,128]{3,2,1,0:T(8,128)(2,1)S(1)} %get-tuple-element.51), channel_id=1, source_target_pairs={{1,0},{2,1},{3,2},{4,3},{5,4},{6,5},{7,6},{9,8},{10,9},{11,10},{12... | collective-permute-start | bytes 122888 | tf_op jit(solution)/shard_map/ppermute | solution.py:21
  29.8 28.7 %collective-permute-start.8 = (bf16[5,1,32,128]{3,2,1,0:T(8,128)(2,1)S(1)}, bf16[5,1,32,128]{3,2,1,0:T(8,128)(2,1)S(1)}, u32[]{:S(2)}, u32[]{:S(2)}) collective-permute-start(bf16[5,1,32,128]{3,2,1,0:T(8,128)(2,1)S(1)} %get-tuple-element.50), channel_id=1, source_target_pairs={{0,1},{1,2},{2,3},{3,4},{4,5},{5,6},{6,7},{8,9},{9,10},{10,11},{11... | collective-permute-start | bytes 122888 | tf_op jit(solution)/shard_map/ppermute | solution.py:18
  33.0 63.0 %copy-start.12 = (pred[8]{0:T(512)(128)(4,1)}, pred[8]{0:T(512)(128)(4,1)S(1)}, u32[]{:S(2)}) copy-start(pred[8]{0:T(512)(128)(4,1)S(1)} %broadcast_in_dim.91) | copy-start | bytes 28
  33.0 62.2 %copy-start.11 = (s32[1024]{0:T(1024)}, s32[1024]{0:T(1024)S(1)}, u32[]{:S(2)}) copy-start(s32[1024]{0:T(1024)S(1)} %pad_clamp_fusion) | copy-start | bytes 12292
  49.5 0.7 copy-start
  50.2 14.8 %collective-permute-start.1 = (bf16[5,1,32,128]{3,2,1,0:T(8,128)(2,1)S(1)}, bf16[5,1,32,128]{3,2,1,0:T(8,128)(2,1)S(1)}, u32[]{:S(2)}, u32[]{:S(2)}) collective-permute-start(bf16[5,1,32,128]{3,2,1,0:T(8,128)(2,1)S(1)} %get-tuple-element.55), channel_id=1, source_target_pairs={{1,0},{2,1},{3,2},{4,3},{5,4},{6,5},{7,6},{9,8},{10,9},{11,10},{12... | collective-permute-start | bytes 122888 | tf_op jit(solution)/shard_map/ppermute | solution.py:21
  55.5 9.6 %collective-permute-start = (bf16[5,1,32,128]{3,2,1,0:T(8,128)(2,1)S(1)}, bf16[5,1,32,128]{3,2,1,0:T(8,128)(2,1)S(1)}, u32[]{:S(2)}, u32[]{:S(2)}) collective-permute-start(bf16[5,1,32,128]{3,2,1,0:T(8,128)(2,1)S(1)} %get-tuple-element.54), channel_id=1, source_target_pairs={{0,1},{1,2},{2,3},{3,4},{4,5},{5,6},{6,7},{8,9},{9,10},{10,11},{11... | collective-permute-start | bytes 122888 | tf_op jit(solution)/shard_map/ppermute | solution.py:18
  63.1 3.4 %collective-permute-start.2 = (bf16[2,16,3456]{2,1,0:T(8,128)(2,1)S(1)}, bf16[2,16,3456]{2,1,0:T(8,128)(2,1)S(1)}, u32[]{:S(2)}, u32[]{:S(2)}) collective-permute-start(bf16[2,16,3456]{2,1,0:T(8,128)(2,1)S(1)} %reshape.402), channel_id=1, source_target_pairs={{0,1},{1,0},{2,3},{3,2},{4,5},{5,4},{6,7},{7,6},{8,9},{9,8},{10,11... | collective-permute-start | bytes 663560 | tf_op jit(solution)/shard_map/ppermute | solution.py:56
  66.5 13.5 %collective-permute-start.5 = (bf16[2,2,16,3456]{3,2,1,0:T(8,128)(2,1)S(1)}, bf16[2,2,16,3456]{3,2,1,0:T(8,128)(2,1)S(1)}, u32[]{:S(2)}, u32[]{:S(2)}) collective-permute-start(bf16[2,2,16,3456]{3,2,1,0:T(8,128)(2,1)S(1)} %maximum_select_fusion.1), channel_id=1, source_target_pairs={{0,6},{1,7},{2,0},{3,1},{4,2},{5,3},{6,4},{7,5},{8,14},{9,15},{10,... | collective-permute-start | bytes 1327112 | tf_op jit(solution)/shard_map/ppermute | solution.py:61
  70.0 14.5 %collective-permute-start.4 = (bf16[2,2,16,3456]{3,2,1,0:T(8,128)(2,1)S(1)}, bf16[2,2,16,3456]{3,2,1,0:T(8,128)(2,1)S(1)}, u32[]{:S(2)}, u32[]{:S(2)}) collective-permute-start(bf16[2,2,16,3456]{3,2,1,0:T(8,128)(2,1)S(1)} %maximum_select_fusion.1), channel_id=1, source_target_pairs={{0,4},{1,5},{2,6},{3,7},{4,0},{5,1},{6,2},{7,3},{8,12},{9,13},{10,... | collective-permute-start | bytes 1327112 | tf_op jit(solution)/shard_map/ppermute | solution.py:61
  73.4 21.6 %collective-permute-start.3 = (bf16[2,2,16,3456]{3,2,1,0:T(8,128)(2,1)S(1)}, bf16[2,2,16,3456]{3,2,1,0:T(8,128)(2,1)S(1)}, u32[]{:S(2)}, u32[]{:S(2)}) collective-permute-start(bf16[2,2,16,3456]{3,2,1,0:T(8,128)(2,1)S(1)} %maximum_select_fusion.1), channel_id=1, source_target_pairs={{0,2},{1,3},{2,4},{3,5},{4,6},{5,7},{6,0},{7,1},{8,10},{9,11},{10,... | collective-permute-start | bytes 1327112 | tf_op jit(solution)/shard_map/ppermute | solution.py:61
  96.6 1.0 copy-start.7
  102.1 3.3 %copy-start.2 = (bf16[128,3,3,3,128]{4,3,2,1,0:T(4,128)(2,1)}, bf16[128,3,3,3,128]{4,3,2,1,0:T(4,128)(2,1)S(1)}, u32[]{:S(2)}) copy-start(bf16[128,3,3,3,128]{4,3,2,1,0:T(4,128)(2,1)S(1)} %reshape_squeeze.12) | copy-start | bytes 2654212
  102.1 3.3 %copy-start.4 = (f32[4,2,32,128]{3,2,1,0:T(8,128)S(1)}, f32[4,2,32,128]{3,2,1,0:T(8,128)}, u32[]{:S(2)}) copy-start(f32[4,2,32,128]{3,2,1,0:T(8,128)} %get-tuple-element.40) | copy-start | bytes 393220
  102.2 3.3 %copy-start.10 = (f32[1,2,32,128]{3,2,1,0:T(8,128)S(1)}, f32[1,2,32,128]{3,2,1,0:T(8,128)}, u32[]{:S(2)}) copy-start(f32[1,2,32,128]{3,2,1,0:T(8,128)} %fusion.87) | copy-start | bytes 98308
  102.2 16.0 %copy-start.9 = (f32[1,1,2,32,128]{4,3,2,1,0:T(8,128)S(1)}, f32[1,1,2,32,128]{4,3,2,1,0:T(8,128)}, u32[]{:S(2)}) copy-start(f32[1,1,2,32,128]{4,3,2,1,0:T(8,128)} %slice_add_fusion.2) | copy-start | bytes 98308
  102.2 16.1 %copy-start.8 = (bf16[1,7,4,32,128]{4,3,2,1,0:T(8,128)(2,1)S(1)}, bf16[1,7,4,32,128]{4,3,2,1,0:T(8,128)(2,1)}, u32[]{:S(2)}) copy-start(bf16[1,7,4,32,128]{4,3,2,1,0:T(8,128)(2,1)} %maximum_bitcast_fusion.1) | copy-start | bytes 688132
  106.2 16.5 %collective-permute-start.11 = (bf16[5,1,32,128]{3,2,1,0:T(8,128)(2,1)}, bf16[5,1,32,128]{3,2,1,0:T(8,128)(2,1)}, u32[]{:S(2)}, u32[]{:S(2)}) collective-permute-start(bf16[5,1,32,128]{3,2,1,0:T(8,128)(2,1)} %get-tuple-element.49), channel_id=1, source_target_pairs={{1,0},{2,1},{3,2},{4,3},{5,4},{6,5},{7,6},{9,8},{10,9},{11,10},{12... | collective-permute-start | bytes 122888 | tf_op jit(solution)/shard_map/ppermute | solution.py:21
  108.6 14.1 %collective-permute-start.10 = (bf16[5,1,32,128]{3,2,1,0:T(8,128)(2,1)}, bf16[5,1,32,128]{3,2,1,0:T(8,128)(2,1)}, u32[]{:S(2)}, u32[]{:S(2)}) collective-permute-start(bf16[5,1,32,128]{3,2,1,0:T(8,128)(2,1)} %get-tuple-element.48), channel_id=1, source_target_pairs={{0,1},{1,2},{2,3},{3,4},{4,5},{5,6},{6,7},{8,9},{9,10},{10,11},{11... | collective-permute-start | bytes 122888 | tf_op jit(solution)/shard_map/ppermute | solution.py:18
  112.4 13.0 %collective-permute-start.7 = (bf16[5,1,32,128]{3,2,1,0:T(8,128)(2,1)}, bf16[5,1,32,128]{3,2,1,0:T(8,128)(2,1)}, u32[]{:S(2)}, u32[]{:S(2)}) collective-permute-start(bf16[5,1,32,128]{3,2,1,0:T(8,128)(2,1)} %get-tuple-element.53), channel_id=1, source_target_pairs={{1,0},{2,1},{3,2},{4,3},{5,4},{6,5},{7,6},{9,8},{10,9},{11,10},{12... | collective-permute-start | bytes 122888 | tf_op jit(solution)/shard_map/ppermute | solution.py:21
  114.3 11.1 %collective-permute-start.6 = (bf16[5,1,32,128]{3,2,1,0:T(8,128)(2,1)}, bf16[5,1,32,128]{3,2,1,0:T(8,128)(2,1)}, u32[]{:S(2)}, u32[]{:S(2)}) collective-permute-start(bf16[5,1,32,128]{3,2,1,0:T(8,128)(2,1)} %get-tuple-element.52), channel_id=1, source_target_pairs={{0,1},{1,2},{2,3},{3,4},{4,5},{5,6},{6,7},{8,9},{9,10},{10,11},{11... | collective-permute-start | bytes 122888 | tf_op jit(solution)/shard_map/ppermute | solution.py:18
  122.6 1.4 copy-start.3
  122.6 1.4 copy-start.14
  127.3 1.1 copy-start.1
  127.3 1.1 copy-start.6
  133.9 4.3 %collective-permute-start.12 = (bf16[4,2,16,3456]{3,2,1,0:T(8,128)(2,1)S(1)}, bf16[4,2,16,3456]{3,2,1,0:T(8,128)(2,1)S(1)}, u32[]{:S(2)}, u32[]{:S(2)}) collective-permute-start(bf16[4,2,16,3456]{3,2,1,0:T(8,128)(2,1)S(1)} %bitcast.180), channel_id=1, source_target_pairs={{0,1},{1,0},{2,3},{3,2},{4,5},{5,4},{6,7},{7,6},{8,9},{9,8},{10,11... | collective-permute-start | bytes 2654216 | tf_op jit(solution)/shard_map/ppermute | solution.py:170
  138.5 8.8 %collective-permute-start.15 = (bf16[2,16,3456]{2,1,0:T(8,128)(2,1)S(1)}, bf16[2,16,3456]{2,1,0:T(8,128)(2,1)S(1)}, u32[]{:S(2)}, u32[]{:S(2)}) collective-permute-start(bf16[2,16,3456]{2,1,0:T(8,128)(2,1)S(1)} %get-tuple-element.37), channel_id=1, source_target_pairs={{0,6},{1,7},{2,0},{3,1},{4,2},{5,3},{6,4},{7,5},{8,14},{9,15},{10,... | collective-permute-start | bytes 663560 | tf_op jit(solution)/shard_map/ppermute | solution.py:177
  140.5 9.7 %collective-permute-start.14 = (bf16[2,16,3456]{2,1,0:T(8,128)(2,1)S(1)}, bf16[2,16,3456]{2,1,0:T(8,128)(2,1)S(1)}, u32[]{:S(2)}, u32[]{:S(2)}) collective-permute-start(bf16[2,16,3456]{2,1,0:T(8,128)(2,1)S(1)} %get-tuple-element.38), channel_id=1, source_target_pairs={{0,4},{1,5},{2,6},{3,7},{4,0},{5,1},{6,2},{7,3},{8,12},{9,13},{10,... | collective-permute-start | bytes 663560 | tf_op jit(solution)/shard_map/ppermute | solution.py:177
  143.9 11.9 %collective-permute-start.13 = (bf16[2,16,3456]{2,1,0:T(8,128)(2,1)S(1)}, bf16[2,16,3456]{2,1,0:T(8,128)(2,1)S(1)}, u32[]{:S(2)}, u32[]{:S(2)}) collective-permute-start(bf16[2,16,3456]{2,1,0:T(8,128)(2,1)S(1)} %get-tuple-element.36), channel_id=1, source_target_pairs={{0,2},{1,3},{2,4},{3,5},{4,6},{5,7},{6,0},{7,1},{8,10},{9,11},{10,... | collective-permute-start | bytes 663560 | tf_op jit(solution)/shard_map/ppermute | solution.py:177
  158.5 42.0 %copy-start.13 = (pred[8]{0:T(512)(128)(4,1)S(1)}, pred[8]{0:T(512)(128)(4,1)}, u32[]{:S(2)}) copy-start(pred[8]{0:T(512)(128)(4,1)} %copy-done.12) | copy-start | bytes 28
  183.1 5.4 %collective-permute-start.16 = (f32[1728]{0:T(1024)S(1)}, f32[1728]{0:T(1024)S(1)}, u32[]{:S(2)}, u32[]{:S(2)}) collective-permute-start(f32[1728]{0:T(1024)S(1)} %get-tuple-element.57), channel_id=1, source_target_pairs={{0,1},{1,0},{2,3},{3,2},{4,5},{5,4},{6,7},{7,6},{8,9},{9,8},{10,11... | collective-permute-start | bytes 20744 | tf_op jit(solution)/shard_map/ppermute | solution.py:56
  188.6 8.2 %collective-permute-start.19 = (f32[2,1728]{1,0:T(2,128)S(1)}, f32[2,1728]{1,0:T(2,128)S(1)}, u32[]{:S(2)}, u32[]{:S(2)}) collective-permute-start(f32[2,1728]{1,0:T(2,128)S(1)} %maximum_select_fusion.3), channel_id=1, source_target_pairs={{0,6},{1,7},{2,0},{3,1},{4,2},{5,3},{6,4},{7,5},{8,14},{9,15},{10,... | collective-permute-start | bytes 41480 | tf_op jit(solution)/shard_map/ppermute | solution.py:61
  190.5 6.3 %collective-permute-start.18 = (f32[2,1728]{1,0:T(2,128)S(1)}, f32[2,1728]{1,0:T(2,128)S(1)}, u32[]{:S(2)}, u32[]{:S(2)}) collective-permute-start(f32[2,1728]{1,0:T(2,128)S(1)} %maximum_select_fusion.3), channel_id=1, source_target_pairs={{0,4},{1,5},{2,6},{3,7},{4,0},{5,1},{6,2},{7,3},{8,12},{9,13},{10,... | collective-permute-start | bytes 41480 | tf_op jit(solution)/shard_map/ppermute | solution.py:61
  193.9 5.7 %collective-permute-start.17 = (f32[2,1728]{1,0:T(2,128)S(1)}, f32[2,1728]{1,0:T(2,128)S(1)}, u32[]{:S(2)}, u32[]{:S(2)}) collective-permute-start(f32[2,1728]{1,0:T(2,128)S(1)} %maximum_select_fusion.3), channel_id=1, source_target_pairs={{0,2},{1,3},{2,4},{3,5},{4,6},{5,7},{6,0},{7,1},{8,10},{9,11},{10,... | collective-permute-start | bytes 41480 | tf_op jit(solution)/shard_map/ppermute | solution.py:61

commit v11 on v9

--- a/solution.py
+++ b/solution.py
@@ -52,15 +52,15 @@
     core = lax.rem(me, 2)
     chip = me // 2
     chips = band_count // 2
-    partner = [(r, r + 1 - 2 * (r % 2)) for r in range(band_count)]
-    got = lax.ppermute(block, "rows", partner)
-    pair = jnp.where(core == 0, jnp.stack([block, got]), jnp.stack([got, block]))
-    held = [pair]
+    held = [block]
     for shift in range(1, chips):
         route = [(r, ((r // 2 + shift) % chips) * 2 + r % 2) for r in range(band_count)]
-        held.append(lax.ppermute(pair, "rows", route))
+        held.append(lax.ppermute(block, "rows", route))
     order = lax.rem(chip - jnp.arange(chips, dtype=jnp.int32) + chips, chips)
-    full = jnp.take(jnp.stack(held), order, axis=0)
+    column = jnp.take(jnp.stack(held), order, axis=0)
+    partner = [(r, r + 1 - 2 * (r % 2)) for r in range(band_count)]
+    got = lax.ppermute(column, "rows", partner)
+    full = jnp.where(core == 0, jnp.stack([column, got], axis=1), jnp.stack([got, column], axis=1))
     return full.reshape((band_count,) + block.shape)
 
 

time: 202 us -> 193 us (0.955)
  waiting for transfers between devices: 46 us -> 36.4 us
    ppermute x4, waiting for transfers between devices: 19.7 us -> 10.2 us  [the longest x3 8.53 us: rows_gather(): held.append(lax.ppermute(block, 'rows', route))]
    unnamed x37 -> x27, local copies, waits for them, and re-layouts: 9.18 us -> 7.91 us
  transfers between devices with their start and end apart: 17 -> 17, of which waited for: 9 -> 7; matrix products, arithmetic and copies ran while one was open for 9% -> 8% of each run, Pallas kernels for 0% -> 0%
where the time goes in v11:
time: 193 us; the launch traced here: 192 us
  starting transfers between devices  65 us (34%)
  waiting for transfers between devices  36.4 us (19%)
  local copies, waits for them, and re-layouts  29.1 us (15%)
  Pallas kernels  22.8 us (12%)
  matrix products  15.6 us (8%)
  blocking collectives  10.8 us (6%)
  other arithmetic  10.2 us (5%)
  between operations  2.15 us (1%)
    pallas_call x1, Pallas kernels, wide_sum(): pl.pallas_call(functools.partial(_wide_sum_kernel, outer, inner), out_sha...  22.8 us
    all_to_all x1, starting transfers between devices, body(): lax.all_to_all(tagged, 'wide', split_axis=0, concat_axis=0, tiled=True)  17.1 us
    all_to_all x1, waiting for transfers between devices, body(): lax.all_to_all(tagged, 'wide', split_axis=0, concat_axis=0, tiled=True)  15.1 us
    ppermute x4, starting transfers between devices, with_halo(): lax.ppermute(lax.slice_in_dim(block, block.shape[dim] - width, None, axis...  13.2 us
    ppermute x4, starting transfers between devices, with_halo(): lax.ppermute(lax.slice_in_dim(block, 0, width, axis=dim), axis, backward)  12.3 us
    all_to_all x1, blocking collectives, reduce_weight_grads(): lax.all_to_all(jnp.broadcast_to(share, (band_count,) + share.shape[1:]),...  10.8 us
    ppermute x3, starting transfers between devices, rows_gather(): held.append(lax.ppermute(block, 'rows', route))  9.03 us
    ppermute x3, starting transfers between devices, rows_reduce(): total = total + lax.ppermute(piece, 'rows', route).astype(jnp.float32)  8.8 us
  transfers between devices with their start and end apart: 17, of which 7 were waited for; matrix products, arithmetic and copies ran while one was open for 8% of the time, Pallas kernels for 0%

profile of v11, /device:TPU:1, one launch (start us, length us, event | category | flops | bytes accessed | tf_op | source)
XLA Modules:
  0.0 192.1 jit_solution(9785010214705935330)
XLA Ops:
  0.6 0.7 add_bitcast_fusion
  1.3 0.9 convert_reduce_fusion.1
  2.2 0.7 bitcast_add_fusion.1
  3.0 0.9 pad.80
  3.9 0.4 convolution_convert_fusion
  4.4 0.8 fusion.65
  5.6 0.5 broadcast.279
  6.1 1.1 reduce.5
  7.2 1.7 reshape.322
  9.0 17.1 %all-to-all-start = ((bf16[64,2,2976]{2,1,0:T(2,128)(2,1)}), bf16[64,2,2976]{2,1,0:T(2,128)(2,1)S(1)}, u32[]{:S(2)}, u32[]{:S(2)}) async-start(bf16[64,2,2976]{2,1,0:T(2,128)(2,1)} %reshape.322), calls=%async_computation | async-start | bytes 1572864 | tf_op jit(solution)/shard_map/all_to_all | solution.py:268
  26.9 2.9 %collective-permute-start.9 = (bf16[5,1,32,128]{3,2,1,0:T(8,128)(2,1)S(1)}, bf16[5,1,32,128]{3,2,1,0:T(8,128)(2,1)S(1)}, u32[]{:S(2)}, u32[]{:S(2)}) collective-permute-start(bf16[5,1,32,128]{3,2,1,0:T(8,128)(2,1)S(1)} %get-tuple-element.51), channel_id=1, source_target_pairs={{1,0},{2,1},{3,2},{4,3},{5,4},{6,5},{7,6},{9,8},{10,9},{11,10},{12... | collective-permute-start | bytes 122888 | tf_op jit(solution)/shard_map/ppermute | solution.py:21
  29.8 3.0 %collective-permute-start.8 = (bf16[5,1,32,128]{3,2,1,0:T(8,128)(2,1)S(1)}, bf16[5,1,32,128]{3,2,1,0:T(8,128)(2,1)S(1)}, u32[]{:S(2)}, u32[]{:S(2)}) collective-permute-start(bf16[5,1,32,128]{3,2,1,0:T(8,128)(2,1)S(1)} %get-tuple-element.50), channel_id=1, source_target_pairs={{0,1},{1,2},{2,3},{3,4},{4,5},{5,6},{6,7},{8,9},{9,10},{10,11},{11... | collective-permute-start | bytes 122888 | tf_op jit(solution)/shard_map/ppermute | solution.py:18
  32.9 15.1 %all-to-all-done = bf16[64,2,2976]{2,1,0:T(2,128)(2,1)S(1)} async-done(((bf16[64,2,2976]{2,1,0:T(2,128)(2,1)}), bf16[64,2,2976]{2,1,0:T(2,128)(2,1)S(1)}, u32[]{:S(2)}, u32[]{:S(2)}) %all-to-all-start) | async-done | bytes 761888 | tf_op jit(solution)/shard_map/all_to_all | solution.py:268
  48.0 1.0 reshape.323
  49.6 5.2 %collective-permute-start.1 = (bf16[5,1,32,128]{3,2,1,0:T(8,128)(2,1)S(1)}, bf16[5,1,32,128]{3,2,1,0:T(8,128)(2,1)S(1)}, u32[]{:S(2)}, u32[]{:S(2)}) collective-permute-start(bf16[5,1,32,128]{3,2,1,0:T(8,128)(2,1)S(1)} %get-tuple-element.55), channel_id=1, source_target_pairs={{1,0},{2,1},{3,2},{4,3},{5,4},{6,5},{7,6},{9,8},{10,9},{11,10},{12... | collective-permute-start | bytes 122888 | tf_op jit(solution)/shard_map/ppermute | solution.py:21
  54.8 3.0 %collective-permute-start = (bf16[5,1,32,128]{3,2,1,0:T(8,128)(2,1)S(1)}, bf16[5,1,32,128]{3,2,1,0:T(8,128)(2,1)S(1)}, u32[]{:S(2)}, u32[]{:S(2)}) collective-permute-start(bf16[5,1,32,128]{3,2,1,0:T(8,128)(2,1)S(1)} %get-tuple-element.54), channel_id=1, source_target_pairs={{0,1},{1,2},{2,3},{3,4},{4,5},{5,6},{6,7},{8,9},{9,10},{10,11},{11... | collective-permute-start | bytes 122888 | tf_op jit(solution)/shard_map/ppermute | solution.py:18
  57.9 1.6 reshape.268
  59.7 0.7 reshape.269
  60.4 2.7 %collective-permute-start.4 = (bf16[2,16,3456]{2,1,0:T(8,128)(2,1)S(1)}, bf16[2,16,3456]{2,1,0:T(8,128)(2,1)S(1)}, u32[]{:S(2)}, u32[]{:S(2)}) collective-permute-start(bf16[2,16,3456]{2,1,0:T(8,128)(2,1)S(1)} %reshape.269), channel_id=1, source_target_pairs={{0,6},{1,7},{2,0},{3,1},{4,2},{5,3},{6,4},{7,5},{8,14},{9,15},{10,... | collective-permute-start | bytes 663560 | tf_op jit(solution)/shard_map/ppermute | solution.py:58
  63.0 4.2 %collective-permute-start.3 = (bf16[2,16,3456]{2,1,0:T(8,128)(2,1)S(1)}, bf16[2,16,3456]{2,1,0:T(8,128)(2,1)S(1)}, u32[]{:S(2)}, u32[]{:S(2)}) collective-permute-start(bf16[2,16,3456]{2,1,0:T(8,128)(2,1)S(1)} %reshape.269), channel_id=1, source_target_pairs={{0,4},{1,5},{2,6},{3,7},{4,0},{5,1},{6,2},{7,3},{8,12},{9,13},{10,... | collective-permute-start | bytes 663560 | tf_op jit(solution)/shard_map/ppermute | solution.py:58
  67.2 2.2 %collective-permute-start.2 = (bf16[2,16,3456]{2,1,0:T(8,128)(2,1)S(1)}, bf16[2,16,3456]{2,1,0:T(8,128)(2,1)S(1)}, u32[]{:S(2)}, u32[]{:S(2)}) collective-permute-start(bf16[2,16,3456]{2,1,0:T(8,128)(2,1)S(1)} %reshape.269), channel_id=1, source_target_pairs={{0,2},{1,3},{2,4},{3,5},{4,6},{5,7},{6,0},{7,1},{8,10},{9,11},{10,... | collective-permute-start | bytes 663560 | tf_op jit(solution)/shard_map/ppermute | solution.py:58
  69.4 0.7 stack_reshape.2
  70.2 2.2 %collective-permute-done.3 = bf16[2,16,3456]{2,1,0:T(8,128)(2,1)S(1)} collective-permute-done((bf16[2,16,3456]{2,1,0:T(8,128)(2,1)S(1)}, bf16[2,16,3456]{2,1,0:T(8,128)(2,1)S(1)}, u32[]{:S(2)}, u32[]{:S(2)}) %collective-permute-start.3) | collective-permute-done | bytes 221216 | tf_op jit(solution)/shard_map/ppermute | solution.py:58
  72.3 6.4 %collective-permute-done.2 = bf16[2,16,3456]{2,1,0:T(8,128)(2,1)S(1)} collective-permute-done((bf16[2,16,3456]{2,1,0:T(8,128)(2,1)S(1)}, bf16[2,16,3456]{2,1,0:T(8,128)(2,1)S(1)}, u32[]{:S(2)}, u32[]{:S(2)}) %collective-permute-start.2) | collective-permute-done | bytes 221216 | tf_op jit(solution)/shard_map/ppermute | solution.py:58
  78.7 0.7 copy-done.4
  79.4 1.1 pad_maximum_fusion
  80.4 0.7 gather_fusion
  81.3 2.7 %collective-permute-start.5 = (bf16[4,2,16,3456]{3,2,1,0:T(8,128)(2,1)S(1)}, bf16[4,2,16,3456]{3,2,1,0:T(8,128)(2,1)S(1)}, u32[]{:S(2)}, u32[]{:S(2)}) collective-permute-start(bf16[4,2,16,3456]{3,2,1,0:T(8,128)(2,1)S(1)} %broadcast_select_fusion), channel_id=1, source_target_pairs={{0,1},{1,0},{2,3},{3,2},{4,5},{5,4},{6,7},{7,6},{8,9},{9,8},{10,11... | collective-permute-start | bytes 2654216 | tf_op jit(solution)/shard_map/ppermute | solution.py:62
  84.1 1.7 collective-permute-done.5
  86.4 1.2 reshape_squeeze.13
  87.6 3.7 %fusion.7 = f32[1,7,2,32,128]{4,0,3,2,1:T(1,128)S(1)} fusion(bf16[128,3,3,3,128]{4,3,2,1,0:T(4,128)(2,1)} %reshape_squeeze.13, bf16[1,9,4,32,128]{4,3,2,1,0:T(8,128)(2,1)S(1)} %fusion.38), kind=kOutput, calls=%fused_computation.26 | convolution fusion | flops 388104192 | bytes 1409024 | tf_op jit(solution)/shard_map/conv_general_dilated | solution.py:227
  91.6 1.8 fusion.5
  93.5 2.3 %collective-permute-start.11 = (bf16[5,1,32,128]{3,2,1,0:T(8,128)(2,1)S(1)}, bf16[5,1,32,128]{3,2,1,0:T(8,128)(2,1)S(1)}, u32[]{:S(2)}, u32[]{:S(2)}) collective-permute-start(bf16[5,1,32,128]{3,2,1,0:T(8,128)(2,1)S(1)} %get-tuple-element.49), channel_id=1, source_target_pairs={{1,0},{2,1},{3,2},{4,3},{5,4},{6,5},{7,6},{9,8},{10,9},{11,10},{12... | collective-permute-start | bytes 122888 | tf_op jit(solution)/shard_map/ppermute | solution.py:21
  95.8 3.3 %collective-permute-start.10 = (bf16[5,1,32,128]{3,2,1,0:T(8,128)(2,1)S(1)}, bf16[5,1,32,128]{3,2,1,0:T(8,128)(2,1)S(1)}, u32[]{:S(2)}, u32[]{:S(2)}) collective-permute-start(bf16[5,1,32,128]{3,2,1,0:T(8,128)(2,1)S(1)} %get-tuple-element.48), channel_id=1, source_target_pairs={{0,1},{1,2},{2,3},{3,4},{4,5},{5,6},{6,7},{8,9},{9,10},{10,11},{11... | collective-permute-start | bytes 122888 | tf_op jit(solution)/shard_map/ppermute | solution.py:18
  99.1 1.9 collective-permute-start.7
  101.1 3.9 %collective-permute-start.6 = (bf16[5,1,32,128]{3,2,1,0:T(8,128)(2,1)S(1)}, bf16[5,1,32,128]{3,2,1,0:T(8,128)(2,1)S(1)}, u32[]{:S(2)}, u32[]{:S(2)}) collective-permute-start(bf16[5,1,32,128]{3,2,1,0:T(8,128)(2,1)S(1)} %get-tuple-element.52), channel_id=1, source_target_pairs={{0,1},{1,2},{2,3},{3,4},{4,5},{5,6},{6,7},{8,9},{9,10},{10,11},{11... | collective-permute-start | bytes 122888 | tf_op jit(solution)/shard_map/ppermute | solution.py:18
  105.0 3.7 %fusion.29 = f32[128,3,3,3,128]{0,4,3,2,1:T(8,128)} fusion(bf16[1,7,4,32,128]{4,3,2,1,0:T(8,128)(2,1)S(1)} %maximum_bitcast_fusion.1, bf16[1,5,2,32,128]{4,3,2,1,0:T(8,128)(2,1)S(1)} %fusion.58), kind=kOutput, calls=%fused_computation.50 | convolution fusion | flops 277217280 | bytes 2080768 | tf_op jit(solution)/shard_map/conv_general_dilated | solution.py:216
  108.7 2.8 %copy.264 = f32[128,3,3,3,128]{4,3,2,1,0:T(4,128)S(1)} copy(f32[128,3,3,3,128]{0,4,3,2,1:T(8,128)} %fusion.29) | data formatting | bytes 3538944 | tf_op jit(solution)/shard_map/conv_general_dilated | solution.py:216
  111.6 2.0 %stack.50 = f32[1,8,16,3456]{3,2,1,0:T(8,128)} reshape(f32[128,3,3,3,128]{4,3,2,1,0:T(4,128)S(1)} %copy.264) | data formatting | bytes 3538944 | tf_op jit(solution)/shard_map/stack | solution.py:299
  114.0 0.8 copy-done.2
  114.8 1.2 convolution_select_fusion
  116.6 0.8 copy-done
  117.4 0.9 convolution_select_fusion.1
  118.4 0.7 fusion.60
  119.2 3.7 %fusion.19 = f32[128,3,3,3,128]{0,4,3,2,1:T(8,128)} fusion(bf16[1,7,4,32,128]{4,3,2,1,0:T(8,128)(2,1)S(1)} %get-tuple-element.41, bf16[1,5,2,32,128]{4,3,2,1,0:T(8,128)(2,1)S(1)} %get-tuple-element.29), kind=kOutput, calls=%fused_computation.40 | convolution fusion | flops 277217280 | bytes 2080768 | tf_op jit(solution)/shard_map/conv_general_dilated | solution.py:216
  122.9 2.8 %copy.267 = f32[128,3,3,3,128]{4,3,2,1,0:T(4,128)S(1)} copy(f32[128,3,3,3,128]{0,4,3,2,1:T(8,128)} %fusion.19) | data formatting | bytes 3538944 | tf_op jit(solution)/shard_map/conv_general_dilated | solution.py:216
  125.7 1.9 stack.51
  127.6 2.3 %fusion.1 = bf16[2,8,16,3456]{3,2,1,0:T(8,128)(2,1)S(1)} fusion(f32[1,8,16,3456]{3,2,1,0:T(8,128)} %stack.51, f32[1,8,16,3456]{3,2,1,0:T(8,128)} %stack.50), kind=kLoop, calls=%fused_computation.5 | loop fusion | flops 2654208 | bytes 5308416 | tf_op jit(solution)/shard_map/convert_element_type | solution.py:185
  130.2 1.9 collective-permute-start.12
  132.1 2.4 %collective-permute-done.12 = bf16[4,2,16,3456]{3,2,1,0:T(8,128)(2,1)S(1)} collective-permute-done((bf16[4,2,16,3456]{3,2,1,0:T(8,128)(2,1)S(1)}, bf16[4,2,16,3456]{3,2,1,0:T(8,128)(2,1)S(1)}, u32[]{:S(2)}, u32[]{:S(2)}) %collective-permute-start.12) | collective-permute-done | bytes 884768 | tf_op jit(solution)/shard_map/ppermute | solution.py:170
  134.8 2.4 %collective-permute-start.15 = (bf16[2,16,3456]{2,1,0:T(8,128)(2,1)S(1)}, bf16[2,16,3456]{2,1,0:T(8,128)(2,1)S(1)}, u32[]{:S(2)}, u32[]{:S(2)}) collective-permute-start(bf16[2,16,3456]{2,1,0:T(8,128)(2,1)S(1)} %get-tuple-element.37), channel_id=1, source_target_pairs={{0,6},{1,7},{2,0},{3,1},{4,2},{5,3},{6,4},{7,5},{8,14},{9,15},{10,... | collective-permute-start | bytes 663560 | tf_op jit(solution)/shard_map/ppermute | solution.py:177
  137.2 3.7 %collective-permute-start.14 = (bf16[2,16,3456]{2,1,0:T(8,128)(2,1)S(1)}, bf16[2,16,3456]{2,1,0:T(8,128)(2,1)S(1)}, u32[]{:S(2)}, u32[]{:S(2)}) collective-permute-start(bf16[2,16,3456]{2,1,0:T(8,128)(2,1)S(1)} %get-tuple-element.38), channel_id=1, source_target_pairs={{0,4},{1,5},{2,6},{3,7},{4,0},{5,1},{6,2},{7,3},{8,12},{9,13},{10,... | collective-permute-start | bytes 663560 | tf_op jit(solution)/shard_map/ppermute | solution.py:177
  140.9 2.7 %collective-permute-start.13 = (bf16[2,16,3456]{2,1,0:T(8,128)(2,1)S(1)}, bf16[2,16,3456]{2,1,0:T(8,128)(2,1)S(1)}, u32[]{:S(2)}, u32[]{:S(2)}) collective-permute-start(bf16[2,16,3456]{2,1,0:T(8,128)(2,1)S(1)} %get-tuple-element.36), channel_id=1, source_target_pairs={{0,2},{1,3},{2,4},{3,5},{4,6},{5,7},{6,0},{7,1},{8,10},{9,11},{10,... | collective-permute-start | bytes 663560 | tf_op jit(solution)/shard_map/ppermute | solution.py:177
  143.6 3.3 %collective-permute-done.14 = bf16[2,16,3456]{2,1,0:T(8,128)(2,1)S(1)} collective-permute-done((bf16[2,16,3456]{2,1,0:T(8,128)(2,1)S(1)}, bf16[2,16,3456]{2,1,0:T(8,128)(2,1)S(1)}, u32[]{:S(2)}, u32[]{:S(2)}) %collective-permute-start.14) | collective-permute-done | bytes 221216 | tf_op jit(solution)/shard_map/ppermute | solution.py:177
  146.9 5.4 %collective-permute-done.13 = bf16[2,16,3456]{2,1,0:T(8,128)(2,1)S(1)} collective-permute-done((bf16[2,16,3456]{2,1,0:T(8,128)(2,1)S(1)}, bf16[2,16,3456]{2,1,0:T(8,128)(2,1)S(1)}, u32[]{:S(2)}, u32[]{:S(2)}) %collective-permute-start.13) | collective-permute-done | bytes 221216 | tf_op jit(solution)/shard_map/ppermute | solution.py:177
  152.4 1.4 reshape.271
  153.9 0.6 copy.270
  154.5 0.6 reshape.272
  155.1 0.9 copy_bitcast_fusion.4.x_ref
  156.0 22.8 %shard_map.102 = f32[16,128]{1,0:T(8,128)} custom-call(f32[8,8,16,128]{3,2,1,0:T(8,128)} %copy_bitcast_fusion.4.x_ref), custom_call_target="tpu_custom_call" | custom-call | tf_op jit(solution)/shard_map/pallas_call | solution.py:143
  178.8 0.7 slice_reduce_fusion
  179.6 10.8 %all_to_all.18 = f32[8,1,1728]{2,1,0:T(1,128)S(1)} all-to-all(f32[8,1,1728]{2,1,0:T(1,128)S(1)} %broadcast_in_dim.96), channel_id=1, replica_groups=mesh['wide'=64,'rows'=8] {'rows'}, dimensions={0} | all-to-all | bytes 110592 | tf_op jit(solution)/shard_map/all_to_all | solution.py:195
  190.7 0.7 copy.272
  191.4 0.7 copy.273
  (89 shorter events, 4.9 us)
Async XLA Ops:
  7.2 19.6 %copy-start.3 = (bf16[1,5,2,32,128]{4,3,2,1,0:T(8,128)(2,1)S(1)}, bf16[1,5,2,32,128]{4,3,2,1,0:T(8,128)(2,1)}, u32[]{:S(2)}) copy-start(bf16[1,5,2,32,128]{4,3,2,1,0:T(8,128)(2,1)} %param.11) | copy-start | bytes 245764
  9.0 39.0 %all-to-all-start = ((bf16[64,2,2976]{2,1,0:T(2,128)(2,1)}), bf16[64,2,2976]{2,1,0:T(2,128)(2,1)S(1)}, u32[]{:S(2)}, u32[]{:S(2)}) async-start(bf16[64,2,2976]{2,1,0:T(2,128)(2,1)} %reshape.322), calls=%async_computation | async-start | bytes 1572864 | tf_op jit(solution)/shard_map/all_to_all | solution.py:268
  26.9 30.9 %collective-permute-start.9 = (bf16[5,1,32,128]{3,2,1,0:T(8,128)(2,1)S(1)}, bf16[5,1,32,128]{3,2,1,0:T(8,128)(2,1)S(1)}, u32[]{:S(2)}, u32[]{:S(2)}) collective-permute-start(bf16[5,1,32,128]{3,2,1,0:T(8,128)(2,1)S(1)} %get-tuple-element.51), channel_id=1, source_target_pairs={{1,0},{2,1},{3,2},{4,3},{5,4},{6,5},{7,6},{9,8},{10,9},{11,10},{12... | collective-permute-start | bytes 122888 | tf_op jit(solution)/shard_map/ppermute | solution.py:21
  29.8 28.1 %collective-permute-start.8 = (bf16[5,1,32,128]{3,2,1,0:T(8,128)(2,1)S(1)}, bf16[5,1,32,128]{3,2,1,0:T(8,128)(2,1)S(1)}, u32[]{:S(2)}, u32[]{:S(2)}) collective-permute-start(bf16[5,1,32,128]{3,2,1,0:T(8,128)(2,1)S(1)} %get-tuple-element.50), channel_id=1, source_target_pairs={{0,1},{1,2},{2,3},{3,4},{4,5},{5,6},{6,7},{8,9},{9,10},{10,11},{11... | collective-permute-start | bytes 122888 | tf_op jit(solution)/shard_map/ppermute | solution.py:18
  49.6 20.5 %collective-permute-start.1 = (bf16[5,1,32,128]{3,2,1,0:T(8,128)(2,1)S(1)}, bf16[5,1,32,128]{3,2,1,0:T(8,128)(2,1)S(1)}, u32[]{:S(2)}, u32[]{:S(2)}) collective-permute-start(bf16[5,1,32,128]{3,2,1,0:T(8,128)(2,1)S(1)} %get-tuple-element.55), channel_id=1, source_target_pairs={{1,0},{2,1},{3,2},{4,3},{5,4},{6,5},{7,6},{9,8},{10,9},{11,10},{12... | collective-permute-start | bytes 122888 | tf_op jit(solution)/shard_map/ppermute | solution.py:21
  54.8 15.3 %collective-permute-start = (bf16[5,1,32,128]{3,2,1,0:T(8,128)(2,1)S(1)}, bf16[5,1,32,128]{3,2,1,0:T(8,128)(2,1)S(1)}, u32[]{:S(2)}, u32[]{:S(2)}) collective-permute-start(bf16[5,1,32,128]{3,2,1,0:T(8,128)(2,1)S(1)} %get-tuple-element.54), channel_id=1, source_target_pairs={{0,1},{1,2},{2,3},{3,4},{4,5},{5,6},{6,7},{8,9},{9,10},{10,11},{11... | collective-permute-start | bytes 122888 | tf_op jit(solution)/shard_map/ppermute | solution.py:18
  60.4 9.8 %collective-permute-start.4 = (bf16[2,16,3456]{2,1,0:T(8,128)(2,1)S(1)}, bf16[2,16,3456]{2,1,0:T(8,128)(2,1)S(1)}, u32[]{:S(2)}, u32[]{:S(2)}) collective-permute-start(bf16[2,16,3456]{2,1,0:T(8,128)(2,1)S(1)} %reshape.269), channel_id=1, source_target_pairs={{0,6},{1,7},{2,0},{3,1},{4,2},{5,3},{6,4},{7,5},{8,14},{9,15},{10,... | collective-permute-start | bytes 663560 | tf_op jit(solution)/shard_map/ppermute | solution.py:58
  63.0 9.3 %collective-permute-start.3 = (bf16[2,16,3456]{2,1,0:T(8,128)(2,1)S(1)}, bf16[2,16,3456]{2,1,0:T(8,128)(2,1)S(1)}, u32[]{:S(2)}, u32[]{:S(2)}) collective-permute-start(bf16[2,16,3456]{2,1,0:T(8,128)(2,1)S(1)} %reshape.269), channel_id=1, source_target_pairs={{0,4},{1,5},{2,6},{3,7},{4,0},{5,1},{6,2},{7,3},{8,12},{9,13},{10,... | collective-permute-start | bytes 663560 | tf_op jit(solution)/shard_map/ppermute | solution.py:58
  67.2 11.5 %collective-permute-start.2 = (bf16[2,16,3456]{2,1,0:T(8,128)(2,1)S(1)}, bf16[2,16,3456]{2,1,0:T(8,128)(2,1)S(1)}, u32[]{:S(2)}, u32[]{:S(2)}) collective-permute-start(bf16[2,16,3456]{2,1,0:T(8,128)(2,1)S(1)} %reshape.269), channel_id=1, source_target_pairs={{0,2},{1,3},{2,4},{3,5},{4,6},{5,7},{6,0},{7,1},{8,10},{9,11},{10,... | collective-permute-start | bytes 663560 | tf_op jit(solution)/shard_map/ppermute | solution.py:58
  78.7 0.7 copy-start.4
  81.3 4.6 %collective-permute-start.5 = (bf16[4,2,16,3456]{3,2,1,0:T(8,128)(2,1)S(1)}, bf16[4,2,16,3456]{3,2,1,0:T(8,128)(2,1)S(1)}, u32[]{:S(2)}, u32[]{:S(2)}) collective-permute-start(bf16[4,2,16,3456]{3,2,1,0:T(8,128)(2,1)S(1)} %broadcast_select_fusion), channel_id=1, source_target_pairs={{0,1},{1,0},{2,3},{3,2},{4,5},{5,4},{6,7},{7,6},{8,9},{9,8},{10,11... | collective-permute-start | bytes 2654216 | tf_op jit(solution)/shard_map/ppermute | solution.py:62
  91.6 1.8 copy-start.1
  93.5 20.0 %collective-permute-start.11 = (bf16[5,1,32,128]{3,2,1,0:T(8,128)(2,1)S(1)}, bf16[5,1,32,128]{3,2,1,0:T(8,128)(2,1)S(1)}, u32[]{:S(2)}, u32[]{:S(2)}) collective-permute-start(bf16[5,1,32,128]{3,2,1,0:T(8,128)(2,1)S(1)} %get-tuple-element.49), channel_id=1, source_target_pairs={{1,0},{2,1},{3,2},{4,3},{5,4},{6,5},{7,6},{9,8},{10,9},{11,10},{12... | collective-permute-start | bytes 122888 | tf_op jit(solution)/shard_map/ppermute | solution.py:21
  95.8 17.7 %collective-permute-start.10 = (bf16[5,1,32,128]{3,2,1,0:T(8,128)(2,1)S(1)}, bf16[5,1,32,128]{3,2,1,0:T(8,128)(2,1)S(1)}, u32[]{:S(2)}, u32[]{:S(2)}) collective-permute-start(bf16[5,1,32,128]{3,2,1,0:T(8,128)(2,1)S(1)} %get-tuple-element.48), channel_id=1, source_target_pairs={{0,1},{1,2},{2,3},{3,4},{4,5},{5,6},{6,7},{8,9},{9,10},{10,11},{11... | collective-permute-start | bytes 122888 | tf_op jit(solution)/shard_map/ppermute | solution.py:18
  99.1 17.1 %collective-permute-start.7 = (bf16[5,1,32,128]{3,2,1,0:T(8,128)(2,1)S(1)}, bf16[5,1,32,128]{3,2,1,0:T(8,128)(2,1)S(1)}, u32[]{:S(2)}, u32[]{:S(2)}) collective-permute-start(bf16[5,1,32,128]{3,2,1,0:T(8,128)(2,1)S(1)} %get-tuple-element.53), channel_id=1, source_target_pairs={{1,0},{2,1},{3,2},{4,3},{5,4},{6,5},{7,6},{9,8},{10,9},{11,10},{12... | collective-permute-start | bytes 122888 | tf_op jit(solution)/shard_map/ppermute | solution.py:21
  101.1 15.2 %collective-permute-start.6 = (bf16[5,1,32,128]{3,2,1,0:T(8,128)(2,1)S(1)}, bf16[5,1,32,128]{3,2,1,0:T(8,128)(2,1)S(1)}, u32[]{:S(2)}, u32[]{:S(2)}) collective-permute-start(bf16[5,1,32,128]{3,2,1,0:T(8,128)(2,1)S(1)} %get-tuple-element.52), channel_id=1, source_target_pairs={{0,1},{1,2},{2,3},{3,4},{4,5},{5,6},{6,7},{8,9},{9,10},{10,11},{11... | collective-permute-start | bytes 122888 | tf_op jit(solution)/shard_map/ppermute | solution.py:18
  113.5 1.3 copy-start.2
  113.5 1.3 copy-start.5
  116.1 1.3 copy-start
  130.2 4.3 %collective-permute-start.12 = (bf16[4,2,16,3456]{3,2,1,0:T(8,128)(2,1)S(1)}, bf16[4,2,16,3456]{3,2,1,0:T(8,128)(2,1)S(1)}, u32[]{:S(2)}, u32[]{:S(2)}) collective-permute-start(bf16[4,2,16,3456]{3,2,1,0:T(8,128)(2,1)S(1)} %bitcast.176), channel_id=1, source_target_pairs={{0,1},{1,0},{2,3},{3,2},{4,5},{5,4},{6,7},{7,6},{8,9},{9,8},{10,11... | collective-permute-start | bytes 2654216 | tf_op jit(solution)/shard_map/ppermute | solution.py:170
  134.8 8.8 %collective-permute-start.15 = (bf16[2,16,3456]{2,1,0:T(8,128)(2,1)S(1)}, bf16[2,16,3456]{2,1,0:T(8,128)(2,1)S(1)}, u32[]{:S(2)}, u32[]{:S(2)}) collective-permute-start(bf16[2,16,3456]{2,1,0:T(8,128)(2,1)S(1)} %get-tuple-element.37), channel_id=1, source_target_pairs={{0,6},{1,7},{2,0},{3,1},{4,2},{5,3},{6,4},{7,5},{8,14},{9,15},{10,... | collective-permute-start | bytes 663560 | tf_op jit(solution)/shard_map/ppermute | solution.py:177
  137.2 9.7 %collective-permute-start.14 = (bf16[2,16,3456]{2,1,0:T(8,128)(2,1)S(1)}, bf16[2,16,3456]{2,1,0:T(8,128)(2,1)S(1)}, u32[]{:S(2)}, u32[]{:S(2)}) collective-permute-start(bf16[2,16,3456]{2,1,0:T(8,128)(2,1)S(1)} %get-tuple-element.38), channel_id=1, source_target_pairs={{0,4},{1,5},{2,6},{3,7},{4,0},{5,1},{6,2},{7,3},{8,12},{9,13},{10,... | collective-permute-start | bytes 663560 | tf_op jit(solution)/shard_map/ppermute | solution.py:177
  140.9 11.4 %collective-permute-start.13 = (bf16[2,16,3456]{2,1,0:T(8,128)(2,1)S(1)}, bf16[2,16,3456]{2,1,0:T(8,128)(2,1)S(1)}, u32[]{:S(2)}, u32[]{:S(2)}) collective-permute-start(bf16[2,16,3456]{2,1,0:T(8,128)(2,1)S(1)} %get-tuple-element.36), channel_id=1, source_target_pairs={{0,2},{1,3},{2,4},{3,5},{4,6},{5,7},{6,0},{7,1},{8,10},{9,11},{10,... | collective-permute-start | bytes 663560 | tf_op jit(solution)/shard_map/ppermute | solution.py:177

commit v12 on v11

--- a/solution.py
+++ b/solution.py
@@ -192,9 +192,7 @@
     tall = -(-size // (8 * lanes)) * 8
     padded = jnp.pad(band_sum, ((0, 0), (0, tall * lanes - size)))
     share = wide_sum(padded.reshape(wide_size, tall, lanes)).reshape(1, tall * lanes)[:, :size]
-    joined = lax.all_to_all(
-        jnp.broadcast_to(share, (band_count,) + share.shape[1:]), "rows", 0, 0, tiled=True
-    )
+    joined = rows_gather(share[0], band_count)
     joined = joined.reshape(band_count, 2, part, chunk)
     joined = jnp.transpose(joined, (1, 3, 0, 2)).reshape(2, chunk, channels)
     return joined[0], joined[1]

time: 193 us -> 202 us (1.047)
  starting transfers between devices: 65 us -> 79.8 us
  blocking collectives: 10.8 us -> 0 us
  waiting for transfers between devices: 36.4 us -> 39.9 us
    all_to_all x1 -> x0, blocking collectives: 10.8 us -> none  [reduce_weight_grads(): lax.all_to_all(jnp.broadcast_to(share, (band_count,) + share.shape[1:]),...]
    ppermute x3 -> x6, starting transfers between devices: 9.03 us -> 17.8 us  [rows_gather(): held.append(lax.ppermute(block, 'rows', route))]
    ppermute x1 -> x2, starting transfers between devices: 2.7 us -> 8.64 us  [rows_gather(): got = lax.ppermute(column, 'rows', partner)]
    ppermute x3 -> x6, waiting for transfers between devices: 8.53 us -> 11.3 us  [rows_gather(): held.append(lax.ppermute(block, 'rows', route))]
    unnamed x27 -> x33, local copies, waits for them, and re-layouts: 7.91 us -> 7.95 us
  transfers between devices with their start and end apart: 17 -> 21, of which waited for: 7 -> 9; matrix products, arithmetic and copies ran while one was open for 8% -> 8% of each run, Pallas kernels for 0% -> 0%
where the time goes in v12:
time: 202 us; the launch traced here: 200 us
  starting transfers between devices  79.8 us (40%)
  waiting for transfers between devices  39.9 us (20%)
  local copies, waits for them, and re-layouts  29.8 us (15%)
  Pallas kernels  22.8 us (11%)
  matrix products  15.6 us (8%)
  other arithmetic  10.2 us (5%)
  between operations  2.27 us (1%)
    pallas_call x1, Pallas kernels, wide_sum(): pl.pallas_call(functools.partial(_wide_sum_kernel, outer, inner), out_sha...  22.8 us
    ppermute x6, starting transfers between devices, rows_gather(): held.append(lax.ppermute(block, 'rows', route))  17.8 us
    all_to_all x1, starting transfers between devices, body(): lax.all_to_all(tagged, 'wide', split_axis=0, concat_axis=0, tiled=True)  17.1 us
    all_to_all x1, waiting for transfers between devices, body(): lax.all_to_all(tagged, 'wide', split_axis=0, concat_axis=0, tiled=True)  15.1 us
    ppermute x4, starting transfers between devices, with_halo(): lax.ppermute(lax.slice_in_dim(block, block.shape[dim] - width, None, axis...  13.2 us
    ppermute x4, starting transfers between devices, with_halo(): lax.ppermute(lax.slice_in_dim(block, 0, width, axis=dim), axis, backward)  12.3 us
    ppermute x6, waiting for transfers between devices, rows_gather(): held.append(lax.ppermute(block, 'rows', route))  11.3 us
    ppermute x3, starting transfers between devices, rows_reduce(): total = total + lax.ppermute(piece, 'rows', route).astype(jnp.float32)  8.8 us
  transfers between devices with their start and end apart: 21, of which 9 were waited for; matrix products, arithmetic and copies ran while one was open for 8% of the time, Pallas kernels for 0%

profile of v12, /device:TPU:1, one launch (start us, length us, event | category | flops | bytes accessed | tf_op | source)
XLA Modules:
  0.0 200.4 jit_solution(2143091383749636156)
XLA Ops:
  1.3 0.9 convert_reduce_fusion.1
  3.0 0.9 pad.89
  4.4 0.8 fusion.65
  6.1 1.1 reduce.4
  7.2 1.8 reshape.345
  9.0 17.1 %all-to-all-start = ((bf16[64,2,2976]{2,1,0:T(2,128)(2,1)}), bf16[64,2,2976]{2,1,0:T(2,128)(2,1)S(1)}, u32[]{:S(2)}, u32[]{:S(2)}) async-start(bf16[64,2,2976]{2,1,0:T(2,128)(2,1)} %reshape.345), calls=%async_computation | async-start | bytes 1572864 | tf_op jit(solution)/shard_map/all_to_all | solution.py:266
  26.9 2.9 %collective-permute-start.9 = (bf16[5,1,32,128]{3,2,1,0:T(8,128)(2,1)S(1)}, bf16[5,1,32,128]{3,2,1,0:T(8,128)(2,1)S(1)}, u32[]{:S(2)}, u32[]{:S(2)}) collective-permute-start(bf16[5,1,32,128]{3,2,1,0:T(8,128)(2,1)S(1)} %get-tuple-element.51), channel_id=1, source_target_pairs={{1,0},{2,1},{3,2},{4,3},{5,4},{6,5},{7,6},{9,8},{10,9},{11,10},{12... | collective-permute-start | bytes 122888 | tf_op jit(solution)/shard_map/ppermute | solution.py:21
  29.8 3.0 %collective-permute-start.8 = (bf16[5,1,32,128]{3,2,1,0:T(8,128)(2,1)S(1)}, bf16[5,1,32,128]{3,2,1,0:T(8,128)(2,1)S(1)}, u32[]{:S(2)}, u32[]{:S(2)}) collective-permute-start(bf16[5,1,32,128]{3,2,1,0:T(8,128)(2,1)S(1)} %get-tuple-element.50), channel_id=1, source_target_pairs={{0,1},{1,2},{2,3},{3,4},{4,5},{5,6},{6,7},{8,9},{9,10},{10,11},{11... | collective-permute-start | bytes 122888 | tf_op jit(solution)/shard_map/ppermute | solution.py:18
  32.9 15.1 %all-to-all-done = bf16[64,2,2976]{2,1,0:T(2,128)(2,1)S(1)} async-done(((bf16[64,2,2976]{2,1,0:T(2,128)(2,1)}), bf16[64,2,2976]{2,1,0:T(2,128)(2,1)S(1)}, u32[]{:S(2)}, u32[]{:S(2)}) %all-to-all-start) | async-done | bytes 761888 | tf_op jit(solution)/shard_map/all_to_all | solution.py:266
  48.0 1.0 reshape.346
  49.6 5.2 %collective-permute-start.1 = (bf16[5,1,32,128]{3,2,1,0:T(8,128)(2,1)S(1)}, bf16[5,1,32,128]{3,2,1,0:T(8,128)(2,1)S(1)}, u32[]{:S(2)}, u32[]{:S(2)}) collective-permute-start(bf16[5,1,32,128]{3,2,1,0:T(8,128)(2,1)S(1)} %get-tuple-element.55), channel_id=1, source_target_pairs={{1,0},{2,1},{3,2},{4,3},{5,4},{6,5},{7,6},{9,8},{10,9},{11,10},{12... | collective-permute-start | bytes 122888 | tf_op jit(solution)/shard_map/ppermute | solution.py:21
  54.8 3.0 %collective-permute-start = (bf16[5,1,32,128]{3,2,1,0:T(8,128)(2,1)S(1)}, bf16[5,1,32,128]{3,2,1,0:T(8,128)(2,1)S(1)}, u32[]{:S(2)}, u32[]{:S(2)}) collective-permute-start(bf16[5,1,32,128]{3,2,1,0:T(8,128)(2,1)S(1)} %get-tuple-element.54), channel_id=1, source_target_pairs={{0,1},{1,2},{2,3},{3,4},{4,5},{5,6},{6,7},{8,9},{9,10},{10,11},{11... | collective-permute-start | bytes 122888 | tf_op jit(solution)/shard_map/ppermute | solution.py:18
  57.9 1.6 reshape.285
  59.7 0.7 reshape.286
  60.4 2.7 %collective-permute-start.4 = (bf16[2,16,3456]{2,1,0:T(8,128)(2,1)S(1)}, bf16[2,16,3456]{2,1,0:T(8,128)(2,1)S(1)}, u32[]{:S(2)}, u32[]{:S(2)}) collective-permute-start(bf16[2,16,3456]{2,1,0:T(8,128)(2,1)S(1)} %reshape.286), channel_id=1, source_target_pairs={{0,6},{1,7},{2,0},{3,1},{4,2},{5,3},{6,4},{7,5},{8,14},{9,15},{10,... | collective-permute-start | bytes 663560 | tf_op jit(solution)/shard_map/ppermute | solution.py:58
  63.0 4.2 %collective-permute-start.3 = (bf16[2,16,3456]{2,1,0:T(8,128)(2,1)S(1)}, bf16[2,16,3456]{2,1,0:T(8,128)(2,1)S(1)}, u32[]{:S(2)}, u32[]{:S(2)}) collective-permute-start(bf16[2,16,3456]{2,1,0:T(8,128)(2,1)S(1)} %reshape.286), channel_id=1, source_target_pairs={{0,4},{1,5},{2,6},{3,7},{4,0},{5,1},{6,2},{7,3},{8,12},{9,13},{10,... | collective-permute-start | bytes 663560 | tf_op jit(solution)/shard_map/ppermute | solution.py:58
  67.2 2.2 %collective-permute-start.2 = (bf16[2,16,3456]{2,1,0:T(8,128)(2,1)S(1)}, bf16[2,16,3456]{2,1,0:T(8,128)(2,1)S(1)}, u32[]{:S(2)}, u32[]{:S(2)}) collective-permute-start(bf16[2,16,3456]{2,1,0:T(8,128)(2,1)S(1)} %reshape.286), channel_id=1, source_target_pairs={{0,2},{1,3},{2,4},{3,5},{4,6},{5,7},{6,0},{7,1},{8,10},{9,11},{10,... | collective-permute-start | bytes 663560 | tf_op jit(solution)/shard_map/ppermute | solution.py:58
  69.4 0.7 stack_reshape.2
  70.2 2.2 %collective-permute-done.3 = bf16[2,16,3456]{2,1,0:T(8,128)(2,1)S(1)} collective-permute-done((bf16[2,16,3456]{2,1,0:T(8,128)(2,1)S(1)}, bf16[2,16,3456]{2,1,0:T(8,128)(2,1)S(1)}, u32[]{:S(2)}, u32[]{:S(2)}) %collective-permute-start.3) | collective-permute-done | bytes 221216 | tf_op jit(solution)/shard_map/ppermute | solution.py:58
  72.3 6.4 %collective-permute-done.2 = bf16[2,16,3456]{2,1,0:T(8,128)(2,1)S(1)} collective-permute-done((bf16[2,16,3456]{2,1,0:T(8,128)(2,1)S(1)}, bf16[2,16,3456]{2,1,0:T(8,128)(2,1)S(1)}, u32[]{:S(2)}, u32[]{:S(2)}) %collective-permute-start.2) | collective-permute-done | bytes 221216 | tf_op jit(solution)/shard_map/ppermute | solution.py:58
  78.7 0.7 copy-done.4
  79.4 1.1 pad_maximum_fusion
  80.5 0.7 gather_fusion
  81.3 2.7 %collective-permute-start.5 = (bf16[4,2,16,3456]{3,2,1,0:T(8,128)(2,1)S(1)}, bf16[4,2,16,3456]{3,2,1,0:T(8,128)(2,1)S(1)}, u32[]{:S(2)}, u32[]{:S(2)}) collective-permute-start(bf16[4,2,16,3456]{3,2,1,0:T(8,128)(2,1)S(1)} %broadcast_select_fusion), channel_id=1, source_target_pairs={{0,1},{1,0},{2,3},{3,2},{4,5},{5,4},{6,7},{7,6},{8,9},{9,8},{10,11... | collective-permute-start | bytes 2654216 | tf_op jit(solution)/shard_map/ppermute | solution.py:62
  84.2 1.7 collective-permute-done.5
  86.4 1.1 reshape_squeeze.13
  87.6 3.7 %fusion.7 = f32[1,7,2,32,128]{4,0,3,2,1:T(1,128)S(1)} fusion(bf16[128,3,3,3,128]{4,3,2,1,0:T(4,128)(2,1)} %reshape_squeeze.13, bf16[1,9,4,32,128]{4,3,2,1,0:T(8,128)(2,1)S(1)} %fusion.38), kind=kOutput, calls=%fused_computation.27 | convolution fusion | flops 388104192 | bytes 1409024 | tf_op jit(solution)/shard_map/conv_general_dilated | solution.py:225
  91.6 1.8 fusion.5
  93.5 2.3 %collective-permute-start.11 = (bf16[5,1,32,128]{3,2,1,0:T(8,128)(2,1)S(1)}, bf16[5,1,32,128]{3,2,1,0:T(8,128)(2,1)S(1)}, u32[]{:S(2)}, u32[]{:S(2)}) collective-permute-start(bf16[5,1,32,128]{3,2,1,0:T(8,128)(2,1)S(1)} %get-tuple-element.49), channel_id=1, source_target_pairs={{1,0},{2,1},{3,2},{4,3},{5,4},{6,5},{7,6},{9,8},{10,9},{11,10},{12... | collective-permute-start | bytes 122888 | tf_op jit(solution)/shard_map/ppermute | solution.py:21
  95.8 3.3 %collective-permute-start.10 = (bf16[5,1,32,128]{3,2,1,0:T(8,128)(2,1)S(1)}, bf16[5,1,32,128]{3,2,1,0:T(8,128)(2,1)S(1)}, u32[]{:S(2)}, u32[]{:S(2)}) collective-permute-start(bf16[5,1,32,128]{3,2,1,0:T(8,128)(2,1)S(1)} %get-tuple-element.48), channel_id=1, source_target_pairs={{0,1},{1,2},{2,3},{3,4},{4,5},{5,6},{6,7},{8,9},{9,10},{10,11},{11... | collective-permute-start | bytes 122888 | tf_op jit(solution)/shard_map/ppermute | solution.py:18
  99.1 1.9 collective-permute-start.7
  101.1 3.9 %collective-permute-start.6 = (bf16[5,1,32,128]{3,2,1,0:T(8,128)(2,1)S(1)}, bf16[5,1,32,128]{3,2,1,0:T(8,128)(2,1)S(1)}, u32[]{:S(2)}, u32[]{:S(2)}) collective-permute-start(bf16[5,1,32,128]{3,2,1,0:T(8,128)(2,1)S(1)} %get-tuple-element.52), channel_id=1, source_target_pairs={{0,1},{1,2},{2,3},{3,4},{4,5},{5,6},{6,7},{8,9},{9,10},{10,11},{11... | collective-permute-start | bytes 122888 | tf_op jit(solution)/shard_map/ppermute | solution.py:18
  105.0 3.7 %fusion.29 = f32[128,3,3,3,128]{0,4,3,2,1:T(8,128)} fusion(bf16[1,7,4,32,128]{4,3,2,1,0:T(8,128)(2,1)S(1)} %maximum_bitcast_fusion.1, bf16[1,5,2,32,128]{4,3,2,1,0:T(8,128)(2,1)S(1)} %fusion.58), kind=kOutput, calls=%fused_computation.51 | convolution fusion | flops 277217280 | bytes 2080768 | tf_op jit(solution)/shard_map/conv_general_dilated | solution.py:214
  108.7 2.8 %copy.269 = f32[128,3,3,3,128]{4,3,2,1,0:T(4,128)S(1)} copy(f32[128,3,3,3,128]{0,4,3,2,1:T(8,128)} %fusion.29) | data formatting | bytes 3538944 | tf_op jit(solution)/shard_map/conv_general_dilated | solution.py:214
  111.6 1.9 stack.74
  113.9 0.8 copy-done.2
  114.7 1.2 convolution_select_fusion
  116.6 0.8 copy-done
  117.3 0.9 convolution_select_fusion.1
  118.4 0.7 fusion.60
  119.1 3.7 %fusion.19 = f32[128,3,3,3,128]{0,4,3,2,1:T(8,128)} fusion(bf16[1,7,4,32,128]{4,3,2,1,0:T(8,128)(2,1)S(1)} %get-tuple-element.41, bf16[1,5,2,32,128]{4,3,2,1,0:T(8,128)(2,1)S(1)} %get-tuple-element.29), kind=kOutput, calls=%fused_computation.41 | convolution fusion | flops 277217280 | bytes 2080768 | tf_op jit(solution)/shard_map/conv_general_dilated | solution.py:214
  122.8 2.8 %copy.272 = f32[128,3,3,3,128]{4,3,2,1,0:T(4,128)S(1)} copy(f32[128,3,3,3,128]{0,4,3,2,1:T(8,128)} %fusion.19) | data formatting | bytes 3538944 | tf_op jit(solution)/shard_map/conv_general_dilated | solution.py:214
  125.7 1.9 stack.75
  127.6 2.3 %fusion.1 = bf16[2,8,16,3456]{3,2,1,0:T(8,128)(2,1)S(1)} fusion(f32[1,8,16,3456]{3,2,1,0:T(8,128)} %stack.75, f32[1,8,16,3456]{3,2,1,0:T(8,128)} %stack.74), kind=kLoop, calls=%fused_computation.6 | loop fusion | flops 2654208 | bytes 5308416 | tf_op jit(solution)/shard_map/convert_element_type | solution.py:185
  130.1 1.9 collective-permute-start.12
  132.0 2.4 %collective-permute-done.12 = bf16[4,2,16,3456]{3,2,1,0:T(8,128)(2,1)S(1)} collective-permute-done((bf16[4,2,16,3456]{3,2,1,0:T(8,128)(2,1)S(1)}, bf16[4,2,16,3456]{3,2,1,0:T(8,128)(2,1)S(1)}, u32[]{:S(2)}, u32[]{:S(2)}) %collective-permute-start.12) | collective-permute-done | bytes 884768 | tf_op jit(solution)/shard_map/ppermute | solution.py:170
  134.7 2.4 %collective-permute-start.15 = (bf16[2,16,3456]{2,1,0:T(8,128)(2,1)S(1)}, bf16[2,16,3456]{2,1,0:T(8,128)(2,1)S(1)}, u32[]{:S(2)}, u32[]{:S(2)}) collective-permute-start(bf16[2,16,3456]{2,1,0:T(8,128)(2,1)S(1)} %get-tuple-element.37), channel_id=1, source_target_pairs={{0,6},{1,7},{2,0},{3,1},{4,2},{5,3},{6,4},{7,5},{8,14},{9,15},{10,... | collective-permute-start | bytes 663560 | tf_op jit(solution)/shard_map/ppermute | solution.py:177
  137.1 3.7 %collective-permute-start.14 = (bf16[2,16,3456]{2,1,0:T(8,128)(2,1)S(1)}, bf16[2,16,3456]{2,1,0:T(8,128)(2,1)S(1)}, u32[]{:S(2)}, u32[]{:S(2)}) collective-permute-start(bf16[2,16,3456]{2,1,0:T(8,128)(2,1)S(1)} %get-tuple-element.38), channel_id=1, source_target_pairs={{0,4},{1,5},{2,6},{3,7},{4,0},{5,1},{6,2},{7,3},{8,12},{9,13},{10,... | collective-permute-start | bytes 663560 | tf_op jit(solution)/shard_map/ppermute | solution.py:177
  140.8 2.7 %collective-permute-start.13 = (bf16[2,16,3456]{2,1,0:T(8,128)(2,1)S(1)}, bf16[2,16,3456]{2,1,0:T(8,128)(2,1)S(1)}, u32[]{:S(2)}, u32[]{:S(2)}) collective-permute-start(bf16[2,16,3456]{2,1,0:T(8,128)(2,1)S(1)} %get-tuple-element.36), channel_id=1, source_target_pairs={{0,2},{1,3},{2,4},{3,5},{4,6},{5,7},{6,0},{7,1},{8,10},{9,11},{10,... | collective-permute-start | bytes 663560 | tf_op jit(solution)/shard_map/ppermute | solution.py:177
  143.5 3.3 %collective-permute-done.14 = bf16[2,16,3456]{2,1,0:T(8,128)(2,1)S(1)} collective-permute-done((bf16[2,16,3456]{2,1,0:T(8,128)(2,1)S(1)}, bf16[2,16,3456]{2,1,0:T(8,128)(2,1)S(1)}, u32[]{:S(2)}, u32[]{:S(2)}) %collective-permute-start.14) | collective-permute-done | bytes 221216 | tf_op jit(solution)/shard_map/ppermute | solution.py:177
  146.8 5.4 %collective-permute-done.13 = bf16[2,16,3456]{2,1,0:T(8,128)(2,1)S(1)} collective-permute-done((bf16[2,16,3456]{2,1,0:T(8,128)(2,1)S(1)}, bf16[2,16,3456]{2,1,0:T(8,128)(2,1)S(1)}, u32[]{:S(2)}, u32[]{:S(2)}) %collective-permute-start.13) | collective-permute-done | bytes 221216 | tf_op jit(solution)/shard_map/ppermute | solution.py:177
  152.3 1.4 reshape.288
  155.0 0.9 copy_bitcast_fusion.4.x_ref
  155.9 22.8 %shard_map.102 = f32[16,128]{1,0:T(8,128)} custom-call(f32[8,8,16,128]{3,2,1,0:T(8,128)} %copy_bitcast_fusion.4.x_ref), custom_call_target="tpu_custom_call" | custom-call | tf_op jit(solution)/shard_map/pallas_call | solution.py:143
  178.7 0.7 fusion.88
  179.4 1.9 collective-permute-start.18
  181.4 4.1 %collective-permute-start.17 = (f32[1728]{0:T(1024)S(1)}, f32[1728]{0:T(1024)S(1)}, u32[]{:S(2)}, u32[]{:S(2)}) collective-permute-start(f32[1728]{0:T(1024)S(1)} %get-tuple-element.57), channel_id=1, source_target_pairs={{0,4},{1,5},{2,6},{3,7},{4,0},{5,1},{6,2},{7,3},{8,12},{9,13},{10,... | collective-permute-start | bytes 20744 | tf_op jit(solution)/shard_map/ppermute | solution.py:58
  185.5 2.8 %collective-permute-start.16 = (f32[1728]{0:T(1024)S(1)}, f32[1728]{0:T(1024)S(1)}, u32[]{:S(2)}, u32[]{:S(2)}) collective-permute-start(f32[1728]{0:T(1024)S(1)} %get-tuple-element.57), channel_id=1, source_target_pairs={{0,2},{1,3},{2,4},{3,5},{4,6},{5,7},{6,0},{7,1},{8,10},{9,11},{10,... | collective-permute-start | bytes 20744 | tf_op jit(solution)/shard_map/ppermute | solution.py:58
  188.3 2.8 %collective-permute-done.16 = f32[1728]{0:T(1024)S(1)} collective-permute-done((f32[1728]{0:T(1024)S(1)}, f32[1728]{0:T(1024)S(1)}, u32[]{:S(2)}, u32[]{:S(2)}) %collective-permute-start.16) | collective-permute-done | bytes 6944 | tf_op jit(solution)/shard_map/ppermute | solution.py:58
  191.2 0.7 gather_fusion.1
  191.9 5.9 %collective-permute-start.19 = (f32[4,1728]{1,0:T(4,128)S(1)}, f32[4,1728]{1,0:T(4,128)S(1)}, u32[]{:S(2)}, u32[]{:S(2)}) collective-permute-start(f32[4,1728]{1,0:T(4,128)S(1)} %broadcast_select_fusion.2), channel_id=1, source_target_pairs={{0,1},{1,0},{2,3},{3,2},{4,5},{5,4},{6,7},{7,6},{8,9},{9,8},{10,11... | collective-permute-start | bytes 82952 | tf_op jit(solution)/shard_map/ppermute | solution.py:62
  198.0 0.8 collective-permute-done.19
  199.0 0.7 copy.278
  199.7 0.7 copy.279
  (109 shorter events, 8.5 us)
Async XLA Ops:
  7.2 19.6 %copy-start.3 = (bf16[1,5,2,32,128]{4,3,2,1,0:T(8,128)(2,1)S(1)}, bf16[1,5,2,32,128]{4,3,2,1,0:T(8,128)(2,1)}, u32[]{:S(2)}) copy-start(bf16[1,5,2,32,128]{4,3,2,1,0:T(8,128)(2,1)} %param.11) | copy-start | bytes 245764
  9.0 39.0 %all-to-all-start = ((bf16[64,2,2976]{2,1,0:T(2,128)(2,1)}), bf16[64,2,2976]{2,1,0:T(2,128)(2,1)S(1)}, u32[]{:S(2)}, u32[]{:S(2)}) async-start(bf16[64,2,2976]{2,1,0:T(2,128)(2,1)} %reshape.345), calls=%async_computation | async-start | bytes 1572864 | tf_op jit(solution)/shard_map/all_to_all | solution.py:266
  26.9 30.9 %collective-permute-start.9 = (bf16[5,1,32,128]{3,2,1,0:T(8,128)(2,1)S(1)}, bf16[5,1,32,128]{3,2,1,0:T(8,128)(2,1)S(1)}, u32[]{:S(2)}, u32[]{:S(2)}) collective-permute-start(bf16[5,1,32,128]{3,2,1,0:T(8,128)(2,1)S(1)} %get-tuple-element.51), channel_id=1, source_target_pairs={{1,0},{2,1},{3,2},{4,3},{5,4},{6,5},{7,6},{9,8},{10,9},{11,10},{12... | collective-permute-start | bytes 122888 | tf_op jit(solution)/shard_map/ppermute | solution.py:21
  29.8 28.1 %collective-permute-start.8 = (bf16[5,1,32,128]{3,2,1,0:T(8,128)(2,1)S(1)}, bf16[5,1,32,128]{3,2,1,0:T(8,128)(2,1)S(1)}, u32[]{:S(2)}, u32[]{:S(2)}) collective-permute-start(bf16[5,1,32,128]{3,2,1,0:T(8,128)(2,1)S(1)} %get-tuple-element.50), channel_id=1, source_target_pairs={{0,1},{1,2},{2,3},{3,4},{4,5},{5,6},{6,7},{8,9},{9,10},{10,11},{11... | collective-permute-start | bytes 122888 | tf_op jit(solution)/shard_map/ppermute | solution.py:18
  32.9 51.2 %copy-start.5 = (pred[4]{0:T(512)(128)(4,1)}, pred[4]{0:T(512)(128)(4,1)S(1)}, u32[]{:S(2)}) copy-start(pred[4]{0:T(512)(128)(4,1)S(1)} %compare_and_fusion) | copy-start | bytes 16
  32.9 47.6 %copy-start.7 = (s32[1024]{0:T(1024)}, s32[1024]{0:T(1024)S(1)}, u32[]{:S(2)}) copy-start(s32[1024]{0:T(1024)S(1)} %pad_clamp_fusion) | copy-start | bytes 12292
  49.6 20.5 %collective-permute-start.1 = (bf16[5,1,32,128]{3,2,1,0:T(8,128)(2,1)S(1)}, bf16[5,1,32,128]{3,2,1,0:T(8,128)(2,1)S(1)}, u32[]{:S(2)}, u32[]{:S(2)}) collective-permute-start(bf16[5,1,32,128]{3,2,1,0:T(8,128)(2,1)S(1)} %get-tuple-element.55), channel_id=1, source_target_pairs={{1,0},{2,1},{3,2},{4,3},{5,4},{6,5},{7,6},{9,8},{10,9},{11,10},{12... | collective-permute-start | bytes 122888 | tf_op jit(solution)/shard_map/ppermute | solution.py:21
  54.8 15.3 %collective-permute-start = (bf16[5,1,32,128]{3,2,1,0:T(8,128)(2,1)S(1)}, bf16[5,1,32,128]{3,2,1,0:T(8,128)(2,1)S(1)}, u32[]{:S(2)}, u32[]{:S(2)}) collective-permute-start(bf16[5,1,32,128]{3,2,1,0:T(8,128)(2,1)S(1)} %get-tuple-element.54), channel_id=1, source_target_pairs={{0,1},{1,2},{2,3},{3,4},{4,5},{5,6},{6,7},{8,9},{9,10},{10,11},{11... | collective-permute-start | bytes 122888 | tf_op jit(solution)/shard_map/ppermute | solution.py:18
  60.4 9.8 %collective-permute-start.4 = (bf16[2,16,3456]{2,1,0:T(8,128)(2,1)S(1)}, bf16[2,16,3456]{2,1,0:T(8,128)(2,1)S(1)}, u32[]{:S(2)}, u32[]{:S(2)}) collective-permute-start(bf16[2,16,3456]{2,1,0:T(8,128)(2,1)S(1)} %reshape.286), channel_id=1, source_target_pairs={{0,6},{1,7},{2,0},{3,1},{4,2},{5,3},{6,4},{7,5},{8,14},{9,15},{10,... | collective-permute-start | bytes 663560 | tf_op jit(solution)/shard_map/ppermute | solution.py:58
  63.0 9.3 %collective-permute-start.3 = (bf16[2,16,3456]{2,1,0:T(8,128)(2,1)S(1)}, bf16[2,16,3456]{2,1,0:T(8,128)(2,1)S(1)}, u32[]{:S(2)}, u32[]{:S(2)}) collective-permute-start(bf16[2,16,3456]{2,1,0:T(8,128)(2,1)S(1)} %reshape.286), channel_id=1, source_target_pairs={{0,4},{1,5},{2,6},{3,7},{4,0},{5,1},{6,2},{7,3},{8,12},{9,13},{10,... | collective-permute-start | bytes 663560 | tf_op jit(solution)/shard_map/ppermute | solution.py:58
  67.2 11.5 %collective-permute-start.2 = (bf16[2,16,3456]{2,1,0:T(8,128)(2,1)S(1)}, bf16[2,16,3456]{2,1,0:T(8,128)(2,1)S(1)}, u32[]{:S(2)}, u32[]{:S(2)}) collective-permute-start(bf16[2,16,3456]{2,1,0:T(8,128)(2,1)S(1)} %reshape.286), channel_id=1, source_target_pairs={{0,2},{1,3},{2,4},{3,5},{4,6},{5,7},{6,0},{7,1},{8,10},{9,11},{10,... | collective-permute-start | bytes 663560 | tf_op jit(solution)/shard_map/ppermute | solution.py:58
  78.7 0.7 copy-start.4
  81.3 4.6 %collective-permute-start.5 = (bf16[4,2,16,3456]{3,2,1,0:T(8,128)(2,1)S(1)}, bf16[4,2,16,3456]{3,2,1,0:T(8,128)(2,1)S(1)}, u32[]{:S(2)}, u32[]{:S(2)}) collective-permute-start(bf16[4,2,16,3456]{3,2,1,0:T(8,128)(2,1)S(1)} %broadcast_select_fusion), channel_id=1, source_target_pairs={{0,1},{1,0},{2,3},{3,2},{4,5},{5,4},{6,7},{7,6},{8,9},{9,8},{10,11... | collective-permute-start | bytes 2654216 | tf_op jit(solution)/shard_map/ppermute | solution.py:62
  91.6 1.8 copy-start.1
  93.5 19.9 %collective-permute-start.11 = (bf16[5,1,32,128]{3,2,1,0:T(8,128)(2,1)S(1)}, bf16[5,1,32,128]{3,2,1,0:T(8,128)(2,1)S(1)}, u32[]{:S(2)}, u32[]{:S(2)}) collective-permute-start(bf16[5,1,32,128]{3,2,1,0:T(8,128)(2,1)S(1)} %get-tuple-element.49), channel_id=1, source_target_pairs={{1,0},{2,1},{3,2},{4,3},{5,4},{6,5},{7,6},{9,8},{10,9},{11,10},{12... | collective-permute-start | bytes 122888 | tf_op jit(solution)/shard_map/ppermute | solution.py:21
  95.8 17.6 %collective-permute-start.10 = (bf16[5,1,32,128]{3,2,1,0:T(8,128)(2,1)S(1)}, bf16[5,1,32,128]{3,2,1,0:T(8,128)(2,1)S(1)}, u32[]{:S(2)}, u32[]{:S(2)}) collective-permute-start(bf16[5,1,32,128]{3,2,1,0:T(8,128)(2,1)S(1)} %get-tuple-element.48), channel_id=1, source_target_pairs={{0,1},{1,2},{2,3},{3,4},{4,5},{5,6},{6,7},{8,9},{9,10},{10,11},{11... | collective-permute-start | bytes 122888 | tf_op jit(solution)/shard_map/ppermute | solution.py:18
  99.1 17.0 %collective-permute-start.7 = (bf16[5,1,32,128]{3,2,1,0:T(8,128)(2,1)S(1)}, bf16[5,1,32,128]{3,2,1,0:T(8,128)(2,1)S(1)}, u32[]{:S(2)}, u32[]{:S(2)}) collective-permute-start(bf16[5,1,32,128]{3,2,1,0:T(8,128)(2,1)S(1)} %get-tuple-element.53), channel_id=1, source_target_pairs={{1,0},{2,1},{3,2},{4,3},{5,4},{6,5},{7,6},{9,8},{10,9},{11,10},{12... | collective-permute-start | bytes 122888 | tf_op jit(solution)/shard_map/ppermute | solution.py:21
  101.1 15.1 %collective-permute-start.6 = (bf16[5,1,32,128]{3,2,1,0:T(8,128)(2,1)S(1)}, bf16[5,1,32,128]{3,2,1,0:T(8,128)(2,1)S(1)}, u32[]{:S(2)}, u32[]{:S(2)}) collective-permute-start(bf16[5,1,32,128]{3,2,1,0:T(8,128)(2,1)S(1)} %get-tuple-element.52), channel_id=1, source_target_pairs={{0,1},{1,2},{2,3},{3,4},{4,5},{5,6},{6,7},{8,9},{9,10},{10,11},{11... | collective-permute-start | bytes 122888 | tf_op jit(solution)/shard_map/ppermute | solution.py:18
  113.5 1.3 copy-start.2
  113.5 1.3 copy-start.8
  116.1 1.3 copy-start
  130.1 4.3 %collective-permute-start.12 = (bf16[4,2,16,3456]{3,2,1,0:T(8,128)(2,1)S(1)}, bf16[4,2,16,3456]{3,2,1,0:T(8,128)(2,1)S(1)}, u32[]{:S(2)}, u32[]{:S(2)}) collective-permute-start(bf16[4,2,16,3456]{3,2,1,0:T(8,128)(2,1)S(1)} %bitcast.179), channel_id=1, source_target_pairs={{0,1},{1,0},{2,3},{3,2},{4,5},{5,4},{6,7},{7,6},{8,9},{9,8},{10,11... | collective-permute-start | bytes 2654216 | tf_op jit(solution)/shard_map/ppermute | solution.py:170
  134.7 8.8 %collective-permute-start.15 = (bf16[2,16,3456]{2,1,0:T(8,128)(2,1)S(1)}, bf16[2,16,3456]{2,1,0:T(8,128)(2,1)S(1)}, u32[]{:S(2)}, u32[]{:S(2)}) collective-permute-start(bf16[2,16,3456]{2,1,0:T(8,128)(2,1)S(1)} %get-tuple-element.37), channel_id=1, source_target_pairs={{0,6},{1,7},{2,0},{3,1},{4,2},{5,3},{6,4},{7,5},{8,14},{9,15},{10,... | collective-permute-start | bytes 663560 | tf_op jit(solution)/shard_map/ppermute | solution.py:177
  137.1 9.7 %collective-permute-start.14 = (bf16[2,16,3456]{2,1,0:T(8,128)(2,1)S(1)}, bf16[2,16,3456]{2,1,0:T(8,128)(2,1)S(1)}, u32[]{:S(2)}, u32[]{:S(2)}) collective-permute-start(bf16[2,16,3456]{2,1,0:T(8,128)(2,1)S(1)} %get-tuple-element.38), channel_id=1, source_target_pairs={{0,4},{1,5},{2,6},{3,7},{4,0},{5,1},{6,2},{7,3},{8,12},{9,13},{10,... | collective-permute-start | bytes 663560 | tf_op jit(solution)/shard_map/ppermute | solution.py:177
  140.8 11.4 %collective-permute-start.13 = (bf16[2,16,3456]{2,1,0:T(8,128)(2,1)S(1)}, bf16[2,16,3456]{2,1,0:T(8,128)(2,1)S(1)}, u32[]{:S(2)}, u32[]{:S(2)}) collective-permute-start(bf16[2,16,3456]{2,1,0:T(8,128)(2,1)S(1)} %get-tuple-element.36), channel_id=1, source_target_pairs={{0,2},{1,3},{2,4},{3,5},{4,6},{5,7},{6,0},{7,1},{8,10},{9,11},{10,... | collective-permute-start | bytes 663560 | tf_op jit(solution)/shard_map/ppermute | solution.py:177
  154.9 36.9 %copy-start.6 = (pred[4]{0:T(512)(128)(4,1)S(1)}, pred[4]{0:T(512)(128)(4,1)}, u32[]{:S(2)}) copy-start(pred[4]{0:T(512)(128)(4,1)} %copy-done.5) | copy-start | bytes 16
  179.4 8.8 %collective-permute-start.18 = (f32[1728]{0:T(1024)S(1)}, f32[1728]{0:T(1024)S(1)}, u32[]{:S(2)}, u32[]{:S(2)}) collective-permute-start(f32[1728]{0:T(1024)S(1)} %get-tuple-element.57), channel_id=1, source_target_pairs={{0,6},{1,7},{2,0},{3,1},{4,2},{5,3},{6,4},{7,5},{8,14},{9,15},{10,... | collective-permute-start | bytes 20744 | tf_op jit(solution)/shard_map/ppermute | solution.py:58
  181.4 6.9 %collective-permute-start.17 = (f32[1728]{0:T(1024)S(1)}, f32[1728]{0:T(1024)S(1)}, u32[]{:S(2)}, u32[]{:S(2)}) collective-permute-start(f32[1728]{0:T(1024)S(1)} %get-tuple-element.57), channel_id=1, source_target_pairs={{0,4},{1,5},{2,6},{3,7},{4,0},{5,1},{6,2},{7,3},{8,12},{9,13},{10,... | collective-permute-start | bytes 20744 | tf_op jit(solution)/shard_map/ppermute | solution.py:58
  185.5 5.6 %collective-permute-start.16 = (f32[1728]{0:T(1024)S(1)}, f32[1728]{0:T(1024)S(1)}, u32[]{:S(2)}, u32[]{:S(2)}) collective-permute-start(f32[1728]{0:T(1024)S(1)} %get-tuple-element.57), channel_id=1, source_target_pairs={{0,2},{1,3},{2,4},{3,5},{4,6},{5,7},{6,0},{7,1},{8,10},{9,11},{10,... | collective-permute-start | bytes 20744 | tf_op jit(solution)/shard_map/ppermute | solution.py:58
  191.9 6.8 %collective-permute-start.19 = (f32[4,1728]{1,0:T(4,128)S(1)}, f32[4,1728]{1,0:T(4,128)S(1)}, u32[]{:S(2)}, u32[]{:S(2)}) collective-permute-start(f32[4,1728]{1,0:T(4,128)S(1)} %broadcast_select_fusion.2), channel_id=1, source_target_pairs={{0,1},{1,0},{2,3},{3,2},{4,5},{5,4},{6,7},{7,6},{8,9},{9,8},{10,11... | collective-permute-start | bytes 82952 | tf_op jit(solution)/shard_map/ppermute | solution.py:62

commit v13 on v11

--- a/solution.py
+++ b/solution.py
@@ -182,7 +182,7 @@
     _, channels, total_rows = grad_t.shape
     part = channels // band_count
     chunk = total_rows // wide_size
-    blocks = grad_t.astype(jnp.bfloat16).reshape(2, band_count, part, total_rows)
+    blocks = grad_t.reshape(2, band_count, part, total_rows)
     blocks = jnp.transpose(blocks, (1, 0, 2, 3))
     band_sum = rows_reduce(blocks, band_count)
     band_sum = band_sum.reshape(2, part, wide_size, chunk)
@@ -296,7 +296,9 @@
         jnp.bfloat16
     )
     scale = 1.0 / math.sqrt(frames * band_rows * columns * band_count * wide_size)
-    grads = jnp.stack([weight_first, weight_second]) * scale
+    grads = jnp.stack(
+        [(weight_first * scale).astype(jnp.bfloat16), (weight_second * scale).astype(jnp.bfloat16)]
+    )
     share_first, share_second = reduce_weight_grads(grads, band_count, wide_size)
     return (block_out[None], grad_input[None], share_first, share_second)
 

time: 193 us -> 185 us (0.959)
  local copies, waits for them, and re-layouts: 29.1 us -> 22.6 us
  matrix products: 15.6 us -> 13.4 us
    conv_general_dilated x2 -> x0, local copies, waits for them, and re-layouts: 5.66 us -> none  [conv_weight_grad_t(): lax.conv_general_dilated(padded[None], upstream[None], (1, 1, 1), ((0, 0)...]
    another operation x2 -> x0, local copies, waits for them, and re-layouts: 3.87 us -> none  [body(): grads = jnp.stack([weight_first, weight_second]) * scale]
    convert_element_type x0 -> x4, local copies, waits for them, and re-layouts: none -> 3.5 us  [the longest x2 1.75 us: body(): (weight_first * scale).astype(jnp.bfloat16)]
    conv_general_dilated x2, matrix products: 7.43 us -> 5.12 us  [conv_weight_grad_t(): lax.conv_general_dilated(padded[None], upstream[None], (1, 1, 1), ((0, 0)...]
    convert_element_type x1 -> x0, other arithmetic: 2.28 us -> none  [reduce_weight_grads(): grad_t.astype(jnp.bfloat16).reshape(2, band_count, part, total_rows)]
    unnamed x27 -> x37, local copies, waits for them, and re-layouts: 7.91 us -> 6.36 us
where the time goes in v13:
time: 185 us; the launch traced here: 184 us
  starting transfers between devices  65 us (35%)
  waiting for transfers between devices  35.7 us (19%)
  Pallas kernels  22.9 us (12%)
  local copies, waits for them, and re-layouts  22.6 us (12%)
  matrix products  13.4 us (7%)
  other arithmetic  11.6 us (6%)
  blocking collectives  10.9 us (6%)
  between operations  2.25 us (1%)
    pallas_call x1, Pallas kernels, wide_sum(): pl.pallas_call(functools.partial(_wide_sum_kernel, outer, inner), out_sha...  22.9 us
    all_to_all x1, starting transfers between devices, body(): lax.all_to_all(tagged, 'wide', split_axis=0, concat_axis=0, tiled=True)  17.1 us
    all_to_all x1, waiting for transfers between devices, body(): lax.all_to_all(tagged, 'wide', split_axis=0, concat_axis=0, tiled=True)  15.1 us
    ppermute x4, starting transfers between devices, with_halo(): lax.ppermute(lax.slice_in_dim(block, block.shape[dim] - width, None, axis...  13.2 us
    ppermute x4, starting transfers between devices, with_halo(): lax.ppermute(lax.slice_in_dim(block, 0, width, axis=dim), axis, backward)  12.3 us
    all_to_all x1, blocking collectives, reduce_weight_grads(): lax.all_to_all(jnp.broadcast_to(share, (band_count,) + share.shape[1:]),...  10.9 us
    ppermute x3, starting transfers between devices, rows_gather(): held.append(lax.ppermute(block, 'rows', route))  9.03 us
    ppermute x3, starting transfers between devices, rows_reduce(): total = total + lax.ppermute(piece, 'rows', route).astype(jnp.float32)  8.81 us
  transfers between devices with their start and end apart: 17, of which 7 were waited for; matrix products, arithmetic and copies ran while one was open for 8% of the time, Pallas kernels for 0%

profile of v13, /device:TPU:1, one launch (start us, length us, event | category | flops | bytes accessed | tf_op | source)
XLA Modules:
  0.0 184.4 jit_solution(7507506339218032454)
XLA Ops:
  0.6 0.7 add_bitcast_fusion
  1.3 0.9 convert_reduce_fusion.1
  2.2 0.7 bitcast_add_fusion.1
  3.0 0.9 pad.80
  4.4 0.8 fusion.62
  6.1 1.1 reduce.5
  7.2 1.7 reshape.356
  9.0 17.1 %all-to-all-start = ((bf16[64,2,2976]{2,1,0:T(2,128)(2,1)}), bf16[64,2,2976]{2,1,0:T(2,128)(2,1)S(1)}, u32[]{:S(2)}, u32[]{:S(2)}) async-start(bf16[64,2,2976]{2,1,0:T(2,128)(2,1)} %reshape.356), calls=%async_computation | async-start | bytes 1572864 | tf_op jit(solution)/shard_map/all_to_all | solution.py:268
  26.9 2.9 %collective-permute-start.9 = (bf16[5,1,32,128]{3,2,1,0:T(8,128)(2,1)S(1)}, bf16[5,1,32,128]{3,2,1,0:T(8,128)(2,1)S(1)}, u32[]{:S(2)}, u32[]{:S(2)}) collective-permute-start(bf16[5,1,32,128]{3,2,1,0:T(8,128)(2,1)S(1)} %get-tuple-element.51), channel_id=1, source_target_pairs={{1,0},{2,1},{3,2},{4,3},{5,4},{6,5},{7,6},{9,8},{10,9},{11,10},{12... | collective-permute-start | bytes 122888 | tf_op jit(solution)/shard_map/ppermute | solution.py:21
  29.8 3.0 %collective-permute-start.8 = (bf16[5,1,32,128]{3,2,1,0:T(8,128)(2,1)S(1)}, bf16[5,1,32,128]{3,2,1,0:T(8,128)(2,1)S(1)}, u32[]{:S(2)}, u32[]{:S(2)}) collective-permute-start(bf16[5,1,32,128]{3,2,1,0:T(8,128)(2,1)S(1)} %get-tuple-element.50), channel_id=1, source_target_pairs={{0,1},{1,2},{2,3},{3,4},{4,5},{5,6},{6,7},{8,9},{9,10},{10,11},{11... | collective-permute-start | bytes 122888 | tf_op jit(solution)/shard_map/ppermute | solution.py:18
  32.8 15.1 %all-to-all-done = bf16[64,2,2976]{2,1,0:T(2,128)(2,1)S(1)} async-done(((bf16[64,2,2976]{2,1,0:T(2,128)(2,1)}), bf16[64,2,2976]{2,1,0:T(2,128)(2,1)S(1)}, u32[]{:S(2)}, u32[]{:S(2)}) %all-to-all-start) | async-done | bytes 761888 | tf_op jit(solution)/shard_map/all_to_all | solution.py:268
  48.0 1.0 reshape.357
  49.6 5.2 %collective-permute-start.1 = (bf16[5,1,32,128]{3,2,1,0:T(8,128)(2,1)S(1)}, bf16[5,1,32,128]{3,2,1,0:T(8,128)(2,1)S(1)}, u32[]{:S(2)}, u32[]{:S(2)}) collective-permute-start(bf16[5,1,32,128]{3,2,1,0:T(8,128)(2,1)S(1)} %get-tuple-element.55), channel_id=1, source_target_pairs={{1,0},{2,1},{3,2},{4,3},{5,4},{6,5},{7,6},{9,8},{10,9},{11,10},{12... | collective-permute-start | bytes 122888 | tf_op jit(solution)/shard_map/ppermute | solution.py:21
  54.8 3.0 %collective-permute-start = (bf16[5,1,32,128]{3,2,1,0:T(8,128)(2,1)S(1)}, bf16[5,1,32,128]{3,2,1,0:T(8,128)(2,1)S(1)}, u32[]{:S(2)}, u32[]{:S(2)}) collective-permute-start(bf16[5,1,32,128]{3,2,1,0:T(8,128)(2,1)S(1)} %get-tuple-element.54), channel_id=1, source_target_pairs={{0,1},{1,2},{2,3},{3,4},{4,5},{5,6},{6,7},{8,9},{9,10},{10,11},{11... | collective-permute-start | bytes 122888 | tf_op jit(solution)/shard_map/ppermute | solution.py:18
  57.8 0.8 fusion.35
  58.6 1.6 reshape.302
  60.4 0.7 reshape.303
  61.1 2.7 %collective-permute-start.4 = (bf16[2,16,3456]{2,1,0:T(8,128)(2,1)S(1)}, bf16[2,16,3456]{2,1,0:T(8,128)(2,1)S(1)}, u32[]{:S(2)}, u32[]{:S(2)}) collective-permute-start(bf16[2,16,3456]{2,1,0:T(8,128)(2,1)S(1)} %reshape.303), channel_id=1, source_target_pairs={{0,6},{1,7},{2,0},{3,1},{4,2},{5,3},{6,4},{7,5},{8,14},{9,15},{10,... | collective-permute-start | bytes 663560 | tf_op jit(solution)/shard_map/ppermute | solution.py:58
  63.7 4.2 %collective-permute-start.3 = (bf16[2,16,3456]{2,1,0:T(8,128)(2,1)S(1)}, bf16[2,16,3456]{2,1,0:T(8,128)(2,1)S(1)}, u32[]{:S(2)}, u32[]{:S(2)}) collective-permute-start(bf16[2,16,3456]{2,1,0:T(8,128)(2,1)S(1)} %reshape.303), channel_id=1, source_target_pairs={{0,4},{1,5},{2,6},{3,7},{4,0},{5,1},{6,2},{7,3},{8,12},{9,13},{10,... | collective-permute-start | bytes 663560 | tf_op jit(solution)/shard_map/ppermute | solution.py:58
  67.9 2.2 %collective-permute-start.2 = (bf16[2,16,3456]{2,1,0:T(8,128)(2,1)S(1)}, bf16[2,16,3456]{2,1,0:T(8,128)(2,1)S(1)}, u32[]{:S(2)}, u32[]{:S(2)}) collective-permute-start(bf16[2,16,3456]{2,1,0:T(8,128)(2,1)S(1)} %reshape.303), channel_id=1, source_target_pairs={{0,2},{1,3},{2,4},{3,5},{4,6},{5,7},{6,0},{7,1},{8,10},{9,11},{10,... | collective-permute-start | bytes 663560 | tf_op jit(solution)/shard_map/ppermute | solution.py:58
  70.1 0.7 stack_reshape.3
  70.8 0.7 maximum_bitcast_fusion.1
  71.5 1.5 collective-permute-done.3
  73.0 6.4 %collective-permute-done.2 = bf16[2,16,3456]{2,1,0:T(8,128)(2,1)S(1)} collective-permute-done((bf16[2,16,3456]{2,1,0:T(8,128)(2,1)S(1)}, bf16[2,16,3456]{2,1,0:T(8,128)(2,1)S(1)}, u32[]{:S(2)}, u32[]{:S(2)}) %collective-permute-start.2) | collective-permute-done | bytes 221216 | tf_op jit(solution)/shard_map/ppermute | solution.py:58
  79.5 0.7 gather_fusion
  80.4 2.7 %collective-permute-start.5 = (bf16[4,2,16,3456]{3,2,1,0:T(8,128)(2,1)S(1)}, bf16[4,2,16,3456]{3,2,1,0:T(8,128)(2,1)S(1)}, u32[]{:S(2)}, u32[]{:S(2)}) collective-permute-start(bf16[4,2,16,3456]{3,2,1,0:T(8,128)(2,1)S(1)} %broadcast_select_fusion), channel_id=1, source_target_pairs={{0,1},{1,0},{2,3},{3,2},{4,5},{5,4},{6,7},{7,6},{8,9},{9,8},{10,11... | collective-permute-start | bytes 2654216 | tf_op jit(solution)/shard_map/ppermute | solution.py:62
  83.2 1.7 collective-permute-done.5
  85.8 0.7 copy-done.7
  86.4 2.4 %fusion.6 = f32[1,7,2,32,128]{4,0,3,2,1:T(1,128)S(1)} fusion(bf16[128,3,3,3,128]{4,3,2,1,0:T(4,128)(2,1)S(1)} %reshape_squeeze.13, bf16[1,9,4,32,128]{4,3,2,1,0:T(8,128)(2,1)S(1)} %copy-done.7), kind=kOutput, calls=%fused_computation.27 | convolution fusion | flops 388104192 | bytes 1409024 | tf_op jit(solution)/shard_map/conv_general_dilated | solution.py:227
  88.9 0.7 fusion.79
  90.6 3.2 %fusion.4 = f32[1,5,2,32,128]{4,0,3,2,1:T(1,128)S(1)} fusion(bf16[128,3,3,3,128]{4,3,2,1,0:T(4,128)(2,1)S(1)} %reshape_squeeze.12, bf16[1,7,4,32,128]{4,3,2,1,0:T(8,128)(2,1)} %maximum_bitcast_fusion.1), kind=kOutput, calls=%fused_computation.25 | convolution fusion | flops 277217280 | bytes 1277952 | tf_op jit(solution)/shard_map/conv_general_dilated | solution.py:207
  93.9 0.7 fusion.81
  94.6 2.3 %collective-permute-start.11 = (bf16[5,1,32,128]{3,2,1,0:T(8,128)(2,1)}, bf16[5,1,32,128]{3,2,1,0:T(8,128)(2,1)}, u32[]{:S(2)}, u32[]{:S(2)}) collective-permute-start(bf16[5,1,32,128]{3,2,1,0:T(8,128)(2,1)} %get-tuple-element.49), channel_id=1, source_target_pairs={{1,0},{2,1},{3,2},{4,3},{5,4},{6,5},{7,6},{9,8},{10,9},{11,10},{12... | collective-permute-start | bytes 122888 | tf_op jit(solution)/shard_map/ppermute | solution.py:21
  96.8 3.3 %collective-permute-start.10 = (bf16[5,1,32,128]{3,2,1,0:T(8,128)(2,1)}, bf16[5,1,32,128]{3,2,1,0:T(8,128)(2,1)}, u32[]{:S(2)}, u32[]{:S(2)}) collective-permute-start(bf16[5,1,32,128]{3,2,1,0:T(8,128)(2,1)} %get-tuple-element.48), channel_id=1, source_target_pairs={{0,1},{1,2},{2,3},{3,4},{4,5},{5,6},{6,7},{8,9},{9,10},{10,11},{11... | collective-permute-start | bytes 122888 | tf_op jit(solution)/shard_map/ppermute | solution.py:18
  100.1 0.7 fusion.83
  100.8 1.9 %collective-permute-start.7 = (bf16[5,1,32,128]{3,2,1,0:T(8,128)(2,1)}, bf16[5,1,32,128]{3,2,1,0:T(8,128)(2,1)S(1)}, u32[]{:S(2)}, u32[]{:S(2)}) collective-permute-start(bf16[5,1,32,128]{3,2,1,0:T(8,128)(2,1)} %get-tuple-element.53), channel_id=1, source_target_pairs={{1,0},{2,1},{3,2},{4,3},{5,4},{6,5},{7,6},{9,8},{10,9},{11,10},{12... | collective-permute-start | bytes 122888 | tf_op jit(solution)/shard_map/ppermute | solution.py:21
  102.7 3.9 %collective-permute-start.6 = (bf16[5,1,32,128]{3,2,1,0:T(8,128)(2,1)}, bf16[5,1,32,128]{3,2,1,0:T(8,128)(2,1)}, u32[]{:S(2)}, u32[]{:S(2)}) collective-permute-start(bf16[5,1,32,128]{3,2,1,0:T(8,128)(2,1)} %get-tuple-element.52), channel_id=1, source_target_pairs={{0,1},{1,2},{2,3},{3,4},{4,5},{5,6},{6,7},{8,9},{9,10},{10,11},{11... | collective-permute-start | bytes 122888 | tf_op jit(solution)/shard_map/ppermute | solution.py:18
  106.7 2.6 %multiply_convert_fusion.1 = bf16[128,3,3,3,128]{0,4,3,2,1:T(8,128)(2,1)S(1)} fusion(bf16[1,7,4,32,128]{4,3,2,1,0:T(8,128)(2,1)S(1)} %copy-done.8, bf16[1,5,2,32,128]{4,3,2,1,0:T(8,128)(2,1)S(1)} %fusion.55), kind=kOutput, calls=%fused_computation.8 | convolution fusion | flops 278102016 | bytes 1196032 | tf_op jit(solution)/shard_map/conv_general_dilated | solution.py:216
  109.3 1.0 copy.264
  110.2 0.8 convert_element_type.153
  111.1 1.0 fusion.29
  112.5 1.2 convolution_select_fusion
  114.0 0.7 pad_maximum_fusion.2
  114.7 0.8 fusion.67
  115.8 0.9 convolution_select_fusion.1
  116.9 0.7 fusion.57
  117.6 2.6 %multiply_convert_fusion = bf16[128,3,3,3,128]{0,4,3,2,1:T(8,128)(2,1)S(1)} fusion(bf16[1,7,4,32,128]{4,3,2,1,0:T(8,128)(2,1)S(1)} %get-tuple-element.41, bf16[1,5,2,32,128]{4,3,2,1,0:T(8,128)(2,1)S(1)} %get-tuple-element.29), kind=kOutput, calls=%fused_computation.7 | convolution fusion | flops 278102016 | bytes 1196032 | tf_op jit(solution)/shard_map/conv_general_dilated | solution.py:216
  120.2 1.0 copy.267
  121.2 0.8 convert_element_type.155
  122.4 1.9 %collective-permute-start.12 = (bf16[4,2,16,3456]{3,2,1,0:T(8,128)(2,1)S(1)}, bf16[4,2,16,3456]{3,2,1,0:T(8,128)(2,1)S(1)}, u32[]{:S(2)}, u32[]{:S(2)}) collective-permute-start(bf16[4,2,16,3456]{3,2,1,0:T(8,128)(2,1)S(1)} %bitcast.176), channel_id=1, source_target_pairs={{0,1},{1,0},{2,3},{3,2},{4,5},{5,4},{6,7},{7,6},{8,9},{9,8},{10,11... | collective-permute-start | bytes 2654216 | tf_op jit(solution)/shard_map/ppermute | solution.py:170
  124.3 2.4 %collective-permute-done.12 = bf16[4,2,16,3456]{3,2,1,0:T(8,128)(2,1)S(1)} collective-permute-done((bf16[4,2,16,3456]{3,2,1,0:T(8,128)(2,1)S(1)}, bf16[4,2,16,3456]{3,2,1,0:T(8,128)(2,1)S(1)}, u32[]{:S(2)}, u32[]{:S(2)}) %collective-permute-start.12) | collective-permute-done | bytes 884768 | tf_op jit(solution)/shard_map/ppermute | solution.py:170
  127.0 2.4 %collective-permute-start.15 = (bf16[2,16,3456]{2,1,0:T(8,128)(2,1)S(1)}, bf16[2,16,3456]{2,1,0:T(8,128)(2,1)S(1)}, u32[]{:S(2)}, u32[]{:S(2)}) collective-permute-start(bf16[2,16,3456]{2,1,0:T(8,128)(2,1)S(1)} %get-tuple-element.37), channel_id=1, source_target_pairs={{0,6},{1,7},{2,0},{3,1},{4,2},{5,3},{6,4},{7,5},{8,14},{9,15},{10,... | collective-permute-start | bytes 663560 | tf_op jit(solution)/shard_map/ppermute | solution.py:177
  129.4 3.7 %collective-permute-start.14 = (bf16[2,16,3456]{2,1,0:T(8,128)(2,1)S(1)}, bf16[2,16,3456]{2,1,0:T(8,128)(2,1)S(1)}, u32[]{:S(2)}, u32[]{:S(2)}) collective-permute-start(bf16[2,16,3456]{2,1,0:T(8,128)(2,1)S(1)} %get-tuple-element.38), channel_id=1, source_target_pairs={{0,4},{1,5},{2,6},{3,7},{4,0},{5,1},{6,2},{7,3},{8,12},{9,13},{10,... | collective-permute-start | bytes 663560 | tf_op jit(solution)/shard_map/ppermute | solution.py:177
  133.1 2.7 %collective-permute-start.13 = (bf16[2,16,3456]{2,1,0:T(8,128)(2,1)S(1)}, bf16[2,16,3456]{2,1,0:T(8,128)(2,1)S(1)}, u32[]{:S(2)}, u32[]{:S(2)}) collective-permute-start(bf16[2,16,3456]{2,1,0:T(8,128)(2,1)S(1)} %get-tuple-element.36), channel_id=1, source_target_pairs={{0,2},{1,3},{2,4},{3,5},{4,6},{5,7},{6,0},{7,1},{8,10},{9,11},{10,... | collective-permute-start | bytes 663560 | tf_op jit(solution)/shard_map/ppermute | solution.py:177
  135.8 3.3 %collective-permute-done.14 = bf16[2,16,3456]{2,1,0:T(8,128)(2,1)S(1)} collective-permute-done((bf16[2,16,3456]{2,1,0:T(8,128)(2,1)S(1)}, bf16[2,16,3456]{2,1,0:T(8,128)(2,1)S(1)}, u32[]{:S(2)}, u32[]{:S(2)}) %collective-permute-start.14) | collective-permute-done | bytes 221216 | tf_op jit(solution)/shard_map/ppermute | solution.py:177
  139.1 5.4 %collective-permute-done.13 = bf16[2,16,3456]{2,1,0:T(8,128)(2,1)S(1)} collective-permute-done((bf16[2,16,3456]{2,1,0:T(8,128)(2,1)S(1)}, bf16[2,16,3456]{2,1,0:T(8,128)(2,1)S(1)}, u32[]{:S(2)}, u32[]{:S(2)}) %collective-permute-start.13) | collective-permute-done | bytes 221216 | tf_op jit(solution)/shard_map/ppermute | solution.py:177
  144.6 1.4 reshape.305
  146.1 0.6 copy.270
  147.3 0.9 copy_bitcast_fusion.4.x_ref
  148.2 22.9 %shard_map.102 = f32[16,128]{1,0:T(8,128)} custom-call(f32[8,8,16,128]{3,2,1,0:T(8,128)} %copy_bitcast_fusion.4.x_ref), custom_call_target="tpu_custom_call" | custom-call | tf_op jit(solution)/shard_map/pallas_call | solution.py:143
  171.0 0.7 slice_reduce_fusion
  171.8 10.9 %all_to_all.18 = f32[8,1,1728]{2,1,0:T(1,128)S(1)} all-to-all(f32[8,1,1728]{2,1,0:T(1,128)S(1)} %broadcast_in_dim.96), channel_id=1, replica_groups=mesh['wide'=64,'rows'=8] {'rows'}, dimensions={0} | all-to-all | bytes 110592 | tf_op jit(solution)/shard_map/all_to_all | solution.py:195
  183.0 0.7 copy.272
  183.7 0.7 copy.273
  (99 shorter events, 7.4 us)
Async XLA Ops:
  7.2 19.5 %copy-start.5 = (bf16[1,5,2,32,128]{4,3,2,1,0:T(8,128)(2,1)S(1)}, bf16[1,5,2,32,128]{4,3,2,1,0:T(8,128)(2,1)}, u32[]{:S(2)}) copy-start(bf16[1,5,2,32,128]{4,3,2,1,0:T(8,128)(2,1)} %param.11) | copy-start | bytes 245764
  9.0 39.0 %all-to-all-start = ((bf16[64,2,2976]{2,1,0:T(2,128)(2,1)}), bf16[64,2,2976]{2,1,0:T(2,128)(2,1)S(1)}, u32[]{:S(2)}, u32[]{:S(2)}) async-start(bf16[64,2,2976]{2,1,0:T(2,128)(2,1)} %reshape.356), calls=%async_computation | async-start | bytes 1572864 | tf_op jit(solution)/shard_map/all_to_all | solution.py:268
  26.9 30.9 %collective-permute-start.9 = (bf16[5,1,32,128]{3,2,1,0:T(8,128)(2,1)S(1)}, bf16[5,1,32,128]{3,2,1,0:T(8,128)(2,1)S(1)}, u32[]{:S(2)}, u32[]{:S(2)}) collective-permute-start(bf16[5,1,32,128]{3,2,1,0:T(8,128)(2,1)S(1)} %get-tuple-element.51), channel_id=1, source_target_pairs={{1,0},{2,1},{3,2},{4,3},{5,4},{6,5},{7,6},{9,8},{10,9},{11,10},{12... | collective-permute-start | bytes 122888 | tf_op jit(solution)/shard_map/ppermute | solution.py:21
  29.8 28.1 %collective-permute-start.8 = (bf16[5,1,32,128]{3,2,1,0:T(8,128)(2,1)S(1)}, bf16[5,1,32,128]{3,2,1,0:T(8,128)(2,1)S(1)}, u32[]{:S(2)}, u32[]{:S(2)}) collective-permute-start(bf16[5,1,32,128]{3,2,1,0:T(8,128)(2,1)S(1)} %get-tuple-element.50), channel_id=1, source_target_pairs={{0,1},{1,2},{2,3},{3,4},{4,5},{5,6},{6,7},{8,9},{9,10},{10,11},{11... | collective-permute-start | bytes 122888 | tf_op jit(solution)/shard_map/ppermute | solution.py:18
  49.6 21.2 %collective-permute-start.1 = (bf16[5,1,32,128]{3,2,1,0:T(8,128)(2,1)S(1)}, bf16[5,1,32,128]{3,2,1,0:T(8,128)(2,1)S(1)}, u32[]{:S(2)}, u32[]{:S(2)}) collective-permute-start(bf16[5,1,32,128]{3,2,1,0:T(8,128)(2,1)S(1)} %get-tuple-element.55), channel_id=1, source_target_pairs={{1,0},{2,1},{3,2},{4,3},{5,4},{6,5},{7,6},{9,8},{10,9},{11,10},{12... | collective-permute-start | bytes 122888 | tf_op jit(solution)/shard_map/ppermute | solution.py:21
  54.8 16.0 %collective-permute-start = (bf16[5,1,32,128]{3,2,1,0:T(8,128)(2,1)S(1)}, bf16[5,1,32,128]{3,2,1,0:T(8,128)(2,1)S(1)}, u32[]{:S(2)}, u32[]{:S(2)}) collective-permute-start(bf16[5,1,32,128]{3,2,1,0:T(8,128)(2,1)S(1)} %get-tuple-element.54), channel_id=1, source_target_pairs={{0,1},{1,2},{2,3},{3,4},{4,5},{5,6},{6,7},{8,9},{9,10},{10,11},{11... | collective-permute-start | bytes 122888 | tf_op jit(solution)/shard_map/ppermute | solution.py:18
  61.1 10.5 %collective-permute-start.4 = (bf16[2,16,3456]{2,1,0:T(8,128)(2,1)S(1)}, bf16[2,16,3456]{2,1,0:T(8,128)(2,1)S(1)}, u32[]{:S(2)}, u32[]{:S(2)}) collective-permute-start(bf16[2,16,3456]{2,1,0:T(8,128)(2,1)S(1)} %reshape.303), channel_id=1, source_target_pairs={{0,6},{1,7},{2,0},{3,1},{4,2},{5,3},{6,4},{7,5},{8,14},{9,15},{10,... | collective-permute-start | bytes 663560 | tf_op jit(solution)/shard_map/ppermute | solution.py:58
  63.7 9.3 %collective-permute-start.3 = (bf16[2,16,3456]{2,1,0:T(8,128)(2,1)S(1)}, bf16[2,16,3456]{2,1,0:T(8,128)(2,1)S(1)}, u32[]{:S(2)}, u32[]{:S(2)}) collective-permute-start(bf16[2,16,3456]{2,1,0:T(8,128)(2,1)S(1)} %reshape.303), channel_id=1, source_target_pairs={{0,4},{1,5},{2,6},{3,7},{4,0},{5,1},{6,2},{7,3},{8,12},{9,13},{10,... | collective-permute-start | bytes 663560 | tf_op jit(solution)/shard_map/ppermute | solution.py:58
  67.9 11.5 %collective-permute-start.2 = (bf16[2,16,3456]{2,1,0:T(8,128)(2,1)S(1)}, bf16[2,16,3456]{2,1,0:T(8,128)(2,1)S(1)}, u32[]{:S(2)}, u32[]{:S(2)}) collective-permute-start(bf16[2,16,3456]{2,1,0:T(8,128)(2,1)S(1)} %reshape.303), channel_id=1, source_target_pairs={{0,2},{1,3},{2,4},{3,5},{4,6},{5,7},{6,0},{7,1},{8,10},{9,11},{10,... | collective-permute-start | bytes 663560 | tf_op jit(solution)/shard_map/ppermute | solution.py:58
  80.4 4.6 %collective-permute-start.5 = (bf16[4,2,16,3456]{3,2,1,0:T(8,128)(2,1)S(1)}, bf16[4,2,16,3456]{3,2,1,0:T(8,128)(2,1)S(1)}, u32[]{:S(2)}, u32[]{:S(2)}) collective-permute-start(bf16[4,2,16,3456]{3,2,1,0:T(8,128)(2,1)S(1)} %broadcast_select_fusion), channel_id=1, source_target_pairs={{0,1},{1,0},{2,3},{3,2},{4,5},{5,4},{6,7},{7,6},{8,9},{9,8},{10,11... | collective-permute-start | bytes 2654216 | tf_op jit(solution)/shard_map/ppermute | solution.py:62
  85.5 1.0 copy-start.7
  90.5 3.3 %copy-start = (bf16[128,3,3,3,128]{4,3,2,1,0:T(4,128)(2,1)}, bf16[128,3,3,3,128]{4,3,2,1,0:T(4,128)(2,1)S(1)}, u32[]{:S(2)}) copy-start(bf16[128,3,3,3,128]{4,3,2,1,0:T(4,128)(2,1)S(1)} %reshape_squeeze.12) | copy-start | bytes 2654212
  90.5 3.3 %copy-start.4 = (f32[4,2,32,128]{3,2,1,0:T(8,128)S(1)}, f32[4,2,32,128]{3,2,1,0:T(8,128)}, u32[]{:S(2)}) copy-start(f32[4,2,32,128]{3,2,1,0:T(8,128)} %get-tuple-element.40) | copy-start | bytes 393220
  90.5 16.1 %copy-start.3 = (f32[1,4,2,32,128]{4,3,2,1,0:T(8,128)S(1)}, f32[1,4,2,32,128]{4,3,2,1,0:T(8,128)}, u32[]{:S(2)}) copy-start(f32[1,4,2,32,128]{4,3,2,1,0:T(8,128)} %get-tuple-element.39) | copy-start | bytes 393220
  90.5 16.1 %copy-start.9 = (f32[1,1,2,32,128]{4,3,2,1,0:T(8,128)S(1)}, f32[1,1,2,32,128]{4,3,2,1,0:T(8,128)}, u32[]{:S(2)}) copy-start(f32[1,1,2,32,128]{4,3,2,1,0:T(8,128)} %slice_add_fusion.2) | copy-start | bytes 98308
  90.5 16.1 %copy-start.8 = (bf16[1,7,4,32,128]{4,3,2,1,0:T(8,128)(2,1)S(1)}, bf16[1,7,4,32,128]{4,3,2,1,0:T(8,128)(2,1)}, u32[]{:S(2)}) copy-start(bf16[1,7,4,32,128]{4,3,2,1,0:T(8,128)(2,1)} %maximum_bitcast_fusion.1) | copy-start | bytes 688132
  93.9 12.7 %copy-start.2 = (bf16[5,2,32,128]{3,2,1,0:T(8,128)(2,1)}, bf16[5,2,32,128]{3,2,1,0:T(8,128)(2,1)S(1)}, u32[]{:S(2)}) copy-start(bf16[5,2,32,128]{3,2,1,0:T(8,128)(2,1)S(1)} %get-tuple-element.44) | copy-start | bytes 245764
  94.6 16.5 %collective-permute-start.11 = (bf16[5,1,32,128]{3,2,1,0:T(8,128)(2,1)}, bf16[5,1,32,128]{3,2,1,0:T(8,128)(2,1)}, u32[]{:S(2)}, u32[]{:S(2)}) collective-permute-start(bf16[5,1,32,128]{3,2,1,0:T(8,128)(2,1)} %get-tuple-element.49), channel_id=1, source_target_pairs={{1,0},{2,1},{3,2},{4,3},{5,4},{6,5},{7,6},{9,8},{10,9},{11,10},{12... | collective-permute-start | bytes 122888 | tf_op jit(solution)/shard_map/ppermute | solution.py:21
  96.8 14.2 %collective-permute-start.10 = (bf16[5,1,32,128]{3,2,1,0:T(8,128)(2,1)}, bf16[5,1,32,128]{3,2,1,0:T(8,128)(2,1)}, u32[]{:S(2)}, u32[]{:S(2)}) collective-permute-start(bf16[5,1,32,128]{3,2,1,0:T(8,128)(2,1)} %get-tuple-element.48), channel_id=1, source_target_pairs={{0,1},{1,2},{2,3},{3,4},{4,5},{5,6},{6,7},{8,9},{9,10},{10,11},{11... | collective-permute-start | bytes 122888 | tf_op jit(solution)/shard_map/ppermute | solution.py:18
  100.8 13.2 %collective-permute-start.7 = (bf16[5,1,32,128]{3,2,1,0:T(8,128)(2,1)}, bf16[5,1,32,128]{3,2,1,0:T(8,128)(2,1)S(1)}, u32[]{:S(2)}, u32[]{:S(2)}) collective-permute-start(bf16[5,1,32,128]{3,2,1,0:T(8,128)(2,1)} %get-tuple-element.53), channel_id=1, source_target_pairs={{1,0},{2,1},{3,2},{4,3},{5,4},{6,5},{7,6},{9,8},{10,9},{11,10},{12... | collective-permute-start | bytes 122888 | tf_op jit(solution)/shard_map/ppermute | solution.py:21
  102.7 11.2 %collective-permute-start.6 = (bf16[5,1,32,128]{3,2,1,0:T(8,128)(2,1)}, bf16[5,1,32,128]{3,2,1,0:T(8,128)(2,1)}, u32[]{:S(2)}, u32[]{:S(2)}) collective-permute-start(bf16[5,1,32,128]{3,2,1,0:T(8,128)(2,1)} %get-tuple-element.52), channel_id=1, source_target_pairs={{0,1},{1,2},{2,3},{3,4},{4,5},{5,6},{6,7},{8,9},{9,10},{10,11},{11... | collective-permute-start | bytes 122888 | tf_op jit(solution)/shard_map/ppermute | solution.py:18
  111.0 1.5 copy-start.1
  111.0 1.5 copy-start.10
  115.8 1.1 copy-start.6
  122.4 4.3 %collective-permute-start.12 = (bf16[4,2,16,3456]{3,2,1,0:T(8,128)(2,1)S(1)}, bf16[4,2,16,3456]{3,2,1,0:T(8,128)(2,1)S(1)}, u32[]{:S(2)}, u32[]{:S(2)}) collective-permute-start(bf16[4,2,16,3456]{3,2,1,0:T(8,128)(2,1)S(1)} %bitcast.176), channel_id=1, source_target_pairs={{0,1},{1,0},{2,3},{3,2},{4,5},{5,4},{6,7},{7,6},{8,9},{9,8},{10,11... | collective-permute-start | bytes 2654216 | tf_op jit(solution)/shard_map/ppermute | solution.py:170
  127.0 8.8 %collective-permute-start.15 = (bf16[2,16,3456]{2,1,0:T(8,128)(2,1)S(1)}, bf16[2,16,3456]{2,1,0:T(8,128)(2,1)S(1)}, u32[]{:S(2)}, u32[]{:S(2)}) collective-permute-start(bf16[2,16,3456]{2,1,0:T(8,128)(2,1)S(1)} %get-tuple-element.37), channel_id=1, source_target_pairs={{0,6},{1,7},{2,0},{3,1},{4,2},{5,3},{6,4},{7,5},{8,14},{9,15},{10,... | collective-permute-start | bytes 663560 | tf_op jit(solution)/shard_map/ppermute | solution.py:177
  129.4 9.7 %collective-permute-start.14 = (bf16[2,16,3456]{2,1,0:T(8,128)(2,1)S(1)}, bf16[2,16,3456]{2,1,0:T(8,128)(2,1)S(1)}, u32[]{:S(2)}, u32[]{:S(2)}) collective-permute-start(bf16[2,16,3456]{2,1,0:T(8,128)(2,1)S(1)} %get-tuple-element.38), channel_id=1, source_target_pairs={{0,4},{1,5},{2,6},{3,7},{4,0},{5,1},{6,2},{7,3},{8,12},{9,13},{10,... | collective-permute-start | bytes 663560 | tf_op jit(solution)/shard_map/ppermute | solution.py:177
  133.1 11.4 %collective-permute-start.13 = (bf16[2,16,3456]{2,1,0:T(8,128)(2,1)S(1)}, bf16[2,16,3456]{2,1,0:T(8,128)(2,1)S(1)}, u32[]{:S(2)}, u32[]{:S(2)}) collective-permute-start(bf16[2,16,3456]{2,1,0:T(8,128)(2,1)S(1)} %get-tuple-element.36), channel_id=1, source_target_pairs={{0,2},{1,3},{2,4},{3,5},{4,6},{5,7},{6,0},{7,1},{8,10},{9,11},{10,... | collective-permute-start | bytes 663560 | tf_op jit(solution)/shard_map/ppermute | solution.py:177

commit v14 on v13

--- a/solution.py
+++ b/solution.py
@@ -106,9 +106,9 @@
         first_copy(lax.rem(my_i + k, inner), my_i).wait_send()
         source = lax.rem(my_i + inner - k, inner)
         first_copy(source, source).wait_recv()
-        return total + recv1[source]
-
-    part[...] = lax.fori_loop(1, inner, finish_first, x_ref[my_i])
+        return total + recv1[source].astype(jnp.float32)
+
+    part[...] = lax.fori_loop(1, inner, finish_first, x_ref[my_i].astype(jnp.float32))
 
     def second_copy(peer_o, slot):
         return pltpu.make_async_remote_copy(
@@ -142,13 +142,13 @@
     arranged = jnp.transpose(pieces.reshape(outer, inner, tall, lanes), (1, 0, 2, 3))
     return pl.pallas_call(
         functools.partial(_wide_sum_kernel, outer, inner),
-        out_shape=jax.ShapeDtypeStruct((tall, lanes), pieces.dtype),
+        out_shape=jax.ShapeDtypeStruct((tall, lanes), jnp.float32),
         in_specs=[pl.BlockSpec(memory_space=pltpu.VMEM)],
         out_specs=pl.BlockSpec(memory_space=pltpu.VMEM),
         scratch_shapes=[
             pltpu.VMEM((inner, outer, tall, lanes), pieces.dtype),
-            pltpu.VMEM((outer, tall, lanes), pieces.dtype),
-            pltpu.VMEM((outer, tall, lanes), pieces.dtype),
+            pltpu.VMEM((outer, tall, lanes), jnp.float32),
+            pltpu.VMEM((outer, tall, lanes), jnp.float32),
             pltpu.SemaphoreType.DMA((inner,)),
             pltpu.SemaphoreType.DMA((inner,)),
             pltpu.SemaphoreType.DMA((outer,)),
@@ -191,7 +191,7 @@
     lanes = 128
     tall = -(-size // (8 * lanes)) * 8
     padded = jnp.pad(band_sum, ((0, 0), (0, tall * lanes - size)))
-    share = wide_sum(padded.reshape(wide_size, tall, lanes)).reshape(1, tall * lanes)[:, :size]
+    share = wide_sum(padded.reshape(wide_size, tall, lanes).astype(jnp.bfloat16)).reshape(1, tall * lanes)[:, :size]
     joined = lax.all_to_all(
         jnp.broadcast_to(share, (band_count,) + share.shape[1:]), "rows", 0, 0, tiled=True
     )

time: 185 us -> 180 us (0.973)
  Pallas kernels: 22.9 us -> 17.6 us
    pallas_call x1, Pallas kernels: 22.9 us -> 17.6 us  [wide_sum(): pl.pallas_call(functools.partial(_wide_sum_kernel, outer, inner), out_sha...]
where the time goes in v14:
time: 180 us; the launch traced here: 179 us
  starting transfers between devices  65 us (36%)
  waiting for transfers between devices  35.7 us (20%)
  local copies, waits for them, and re-layouts  22.5 us (12%)
  Pallas kernels  17.6 us (10%)
  matrix products  13.4 us (7%)
  other arithmetic  11.6 us (6%)
  blocking collectives  10.4 us (6%)
  between operations  2.26 us (1%)
    pallas_call x1, Pallas kernels, wide_sum(): pl.pallas_call(functools.partial(_wide_sum_kernel, outer, inner), out_sha...  17.6 us
    all_to_all x1, starting transfers between devices, body(): lax.all_to_all(tagged, 'wide', split_axis=0, concat_axis=0, tiled=True)  17.1 us
    all_to_all x1, waiting for transfers between devices, body(): lax.all_to_all(tagged, 'wide', split_axis=0, concat_axis=0, tiled=True)  15.1 us
    ppermute x4, starting transfers between devices, with_halo(): lax.ppermute(lax.slice_in_dim(block, block.shape[dim] - width, None, axis...  13.2 us
    ppermute x4, starting transfers between devices, with_halo(): lax.ppermute(lax.slice_in_dim(block, 0, width, axis=dim), axis, backward)  12.3 us
    all_to_all x1, blocking collectives, reduce_weight_grads(): lax.all_to_all(jnp.broadcast_to(share, (band_count,) + share.shape[1:]),...  10.4 us
    ppermute x3, starting transfers between devices, rows_gather(): held.append(lax.ppermute(block, 'rows', route))  9.03 us
    ppermute x3, starting transfers between devices, rows_reduce(): total = total + lax.ppermute(piece, 'rows', route).astype(jnp.float32)  8.81 us
  transfers between devices with their start and end apart: 17, of which 7 were waited for; matrix products, arithmetic and copies ran while one was open for 8% of the time, Pallas kernels for 0%

profile of v14, /device:TPU:1, one launch (start us, length us, event | category | flops | bytes accessed | tf_op | source)
XLA Modules:
  0.0 178.6 jit_solution(3380632156448905203)
XLA Ops:
  0.6 0.7 add_bitcast_fusion
  1.3 0.9 convert_reduce_fusion.1
  2.2 0.7 bitcast_add_fusion.1
  3.0 0.9 pad.81
  4.4 0.8 fusion.63
  6.1 1.1 reduce.5
  7.2 1.7 reshape.362
  9.0 17.1 %all-to-all-start = ((bf16[64,2,2976]{2,1,0:T(2,128)(2,1)}), bf16[64,2,2976]{2,1,0:T(2,128)(2,1)S(1)}, u32[]{:S(2)}, u32[]{:S(2)}) async-start(bf16[64,2,2976]{2,1,0:T(2,128)(2,1)} %reshape.362), calls=%async_computation | async-start | bytes 1572864 | tf_op jit(solution)/shard_map/all_to_all | solution.py:268
  26.9 2.9 %collective-permute-start.9 = (bf16[5,1,32,128]{3,2,1,0:T(8,128)(2,1)S(1)}, bf16[5,1,32,128]{3,2,1,0:T(8,128)(2,1)S(1)}, u32[]{:S(2)}, u32[]{:S(2)}) collective-permute-start(bf16[5,1,32,128]{3,2,1,0:T(8,128)(2,1)S(1)} %get-tuple-element.51), channel_id=1, source_target_pairs={{1,0},{2,1},{3,2},{4,3},{5,4},{6,5},{7,6},{9,8},{10,9},{11,10},{12... | collective-permute-start | bytes 122888 | tf_op jit(solution)/shard_map/ppermute | solution.py:21
  29.8 3.0 %collective-permute-start.8 = (bf16[5,1,32,128]{3,2,1,0:T(8,128)(2,1)S(1)}, bf16[5,1,32,128]{3,2,1,0:T(8,128)(2,1)S(1)}, u32[]{:S(2)}, u32[]{:S(2)}) collective-permute-start(bf16[5,1,32,128]{3,2,1,0:T(8,128)(2,1)S(1)} %get-tuple-element.50), channel_id=1, source_target_pairs={{0,1},{1,2},{2,3},{3,4},{4,5},{5,6},{6,7},{8,9},{9,10},{10,11},{11... | collective-permute-start | bytes 122888 | tf_op jit(solution)/shard_map/ppermute | solution.py:18
  32.8 15.1 %all-to-all-done = bf16[64,2,2976]{2,1,0:T(2,128)(2,1)S(1)} async-done(((bf16[64,2,2976]{2,1,0:T(2,128)(2,1)}), bf16[64,2,2976]{2,1,0:T(2,128)(2,1)S(1)}, u32[]{:S(2)}, u32[]{:S(2)}) %all-to-all-start) | async-done | bytes 761888 | tf_op jit(solution)/shard_map/all_to_all | solution.py:268
  48.0 1.0 reshape.363
  49.6 5.2 %collective-permute-start.1 = (bf16[5,1,32,128]{3,2,1,0:T(8,128)(2,1)S(1)}, bf16[5,1,32,128]{3,2,1,0:T(8,128)(2,1)S(1)}, u32[]{:S(2)}, u32[]{:S(2)}) collective-permute-start(bf16[5,1,32,128]{3,2,1,0:T(8,128)(2,1)S(1)} %get-tuple-element.55), channel_id=1, source_target_pairs={{1,0},{2,1},{3,2},{4,3},{5,4},{6,5},{7,6},{9,8},{10,9},{11,10},{12... | collective-permute-start | bytes 122888 | tf_op jit(solution)/shard_map/ppermute | solution.py:21
  54.8 3.0 %collective-permute-start = (bf16[5,1,32,128]{3,2,1,0:T(8,128)(2,1)S(1)}, bf16[5,1,32,128]{3,2,1,0:T(8,128)(2,1)S(1)}, u32[]{:S(2)}, u32[]{:S(2)}) collective-permute-start(bf16[5,1,32,128]{3,2,1,0:T(8,128)(2,1)S(1)} %get-tuple-element.54), channel_id=1, source_target_pairs={{0,1},{1,2},{2,3},{3,4},{4,5},{5,6},{6,7},{8,9},{9,10},{10,11},{11... | collective-permute-start | bytes 122888 | tf_op jit(solution)/shard_map/ppermute | solution.py:18
  57.8 0.8 fusion.36
  58.6 1.6 reshape.308
  60.4 0.7 reshape.309
  61.1 2.7 %collective-permute-start.4 = (bf16[2,16,3456]{2,1,0:T(8,128)(2,1)S(1)}, bf16[2,16,3456]{2,1,0:T(8,128)(2,1)S(1)}, u32[]{:S(2)}, u32[]{:S(2)}) collective-permute-start(bf16[2,16,3456]{2,1,0:T(8,128)(2,1)S(1)} %reshape.309), channel_id=1, source_target_pairs={{0,6},{1,7},{2,0},{3,1},{4,2},{5,3},{6,4},{7,5},{8,14},{9,15},{10,... | collective-permute-start | bytes 663560 | tf_op jit(solution)/shard_map/ppermute | solution.py:58
  63.7 4.2 %collective-permute-start.3 = (bf16[2,16,3456]{2,1,0:T(8,128)(2,1)S(1)}, bf16[2,16,3456]{2,1,0:T(8,128)(2,1)S(1)}, u32[]{:S(2)}, u32[]{:S(2)}) collective-permute-start(bf16[2,16,3456]{2,1,0:T(8,128)(2,1)S(1)} %reshape.309), channel_id=1, source_target_pairs={{0,4},{1,5},{2,6},{3,7},{4,0},{5,1},{6,2},{7,3},{8,12},{9,13},{10,... | collective-permute-start | bytes 663560 | tf_op jit(solution)/shard_map/ppermute | solution.py:58
  67.9 2.2 %collective-permute-start.2 = (bf16[2,16,3456]{2,1,0:T(8,128)(2,1)S(1)}, bf16[2,16,3456]{2,1,0:T(8,128)(2,1)S(1)}, u32[]{:S(2)}, u32[]{:S(2)}) collective-permute-start(bf16[2,16,3456]{2,1,0:T(8,128)(2,1)S(1)} %reshape.309), channel_id=1, source_target_pairs={{0,2},{1,3},{2,4},{3,5},{4,6},{5,7},{6,0},{7,1},{8,10},{9,11},{10,... | collective-permute-start | bytes 663560 | tf_op jit(solution)/shard_map/ppermute | solution.py:58
  70.1 0.7 stack_reshape.3
  70.8 0.7 maximum_bitcast_fusion.1
  71.5 1.5 collective-permute-done.3
  73.0 6.4 %collective-permute-done.2 = bf16[2,16,3456]{2,1,0:T(8,128)(2,1)S(1)} collective-permute-done((bf16[2,16,3456]{2,1,0:T(8,128)(2,1)S(1)}, bf16[2,16,3456]{2,1,0:T(8,128)(2,1)S(1)}, u32[]{:S(2)}, u32[]{:S(2)}) %collective-permute-start.2) | collective-permute-done | bytes 221216 | tf_op jit(solution)/shard_map/ppermute | solution.py:58
  79.5 0.7 gather_fusion
  80.4 2.7 %collective-permute-start.5 = (bf16[4,2,16,3456]{3,2,1,0:T(8,128)(2,1)S(1)}, bf16[4,2,16,3456]{3,2,1,0:T(8,128)(2,1)S(1)}, u32[]{:S(2)}, u32[]{:S(2)}) collective-permute-start(bf16[4,2,16,3456]{3,2,1,0:T(8,128)(2,1)S(1)} %broadcast_select_fusion), channel_id=1, source_target_pairs={{0,1},{1,0},{2,3},{3,2},{4,5},{5,4},{6,7},{7,6},{8,9},{9,8},{10,11... | collective-permute-start | bytes 2654216 | tf_op jit(solution)/shard_map/ppermute | solution.py:62
  83.2 1.7 collective-permute-done.5
  85.8 0.7 copy-done.7
  86.4 2.4 %fusion.6 = f32[1,7,2,32,128]{4,0,3,2,1:T(1,128)S(1)} fusion(bf16[128,3,3,3,128]{4,3,2,1,0:T(4,128)(2,1)S(1)} %reshape_squeeze.13, bf16[1,9,4,32,128]{4,3,2,1,0:T(8,128)(2,1)S(1)} %copy-done.7), kind=kOutput, calls=%fused_computation.27 | convolution fusion | flops 388104192 | bytes 1409024 | tf_op jit(solution)/shard_map/conv_general_dilated | solution.py:227
  88.9 0.7 fusion.80
  90.6 3.2 %fusion.4 = f32[1,5,2,32,128]{4,0,3,2,1:T(1,128)S(1)} fusion(bf16[128,3,3,3,128]{4,3,2,1,0:T(4,128)(2,1)S(1)} %reshape_squeeze.12, bf16[1,7,4,32,128]{4,3,2,1,0:T(8,128)(2,1)} %maximum_bitcast_fusion.1), kind=kOutput, calls=%fused_computation.25 | convolution fusion | flops 277217280 | bytes 1277952 | tf_op jit(solution)/shard_map/conv_general_dilated | solution.py:207
  93.9 0.7 fusion.82
  94.6 2.3 %collective-permute-start.11 = (bf16[5,1,32,128]{3,2,1,0:T(8,128)(2,1)}, bf16[5,1,32,128]{3,2,1,0:T(8,128)(2,1)}, u32[]{:S(2)}, u32[]{:S(2)}) collective-permute-start(bf16[5,1,32,128]{3,2,1,0:T(8,128)(2,1)} %get-tuple-element.49), channel_id=1, source_target_pairs={{1,0},{2,1},{3,2},{4,3},{5,4},{6,5},{7,6},{9,8},{10,9},{11,10},{12... | collective-permute-start | bytes 122888 | tf_op jit(solution)/shard_map/ppermute | solution.py:21
  96.8 3.3 %collective-permute-start.10 = (bf16[5,1,32,128]{3,2,1,0:T(8,128)(2,1)}, bf16[5,1,32,128]{3,2,1,0:T(8,128)(2,1)}, u32[]{:S(2)}, u32[]{:S(2)}) collective-permute-start(bf16[5,1,32,128]{3,2,1,0:T(8,128)(2,1)} %get-tuple-element.48), channel_id=1, source_target_pairs={{0,1},{1,2},{2,3},{3,4},{4,5},{5,6},{6,7},{8,9},{9,10},{10,11},{11... | collective-permute-start | bytes 122888 | tf_op jit(solution)/shard_map/ppermute | solution.py:18
  100.1 0.7 fusion.84
  100.8 1.9 %collective-permute-start.7 = (bf16[5,1,32,128]{3,2,1,0:T(8,128)(2,1)}, bf16[5,1,32,128]{3,2,1,0:T(8,128)(2,1)S(1)}, u32[]{:S(2)}, u32[]{:S(2)}) collective-permute-start(bf16[5,1,32,128]{3,2,1,0:T(8,128)(2,1)} %get-tuple-element.53), channel_id=1, source_target_pairs={{1,0},{2,1},{3,2},{4,3},{5,4},{6,5},{7,6},{9,8},{10,9},{11,10},{12... | collective-permute-start | bytes 122888 | tf_op jit(solution)/shard_map/ppermute | solution.py:21
  102.7 3.9 %collective-permute-start.6 = (bf16[5,1,32,128]{3,2,1,0:T(8,128)(2,1)}, bf16[5,1,32,128]{3,2,1,0:T(8,128)(2,1)}, u32[]{:S(2)}, u32[]{:S(2)}) collective-permute-start(bf16[5,1,32,128]{3,2,1,0:T(8,128)(2,1)} %get-tuple-element.52), channel_id=1, source_target_pairs={{0,1},{1,2},{2,3},{3,4},{4,5},{5,6},{6,7},{8,9},{9,10},{10,11},{11... | collective-permute-start | bytes 122888 | tf_op jit(solution)/shard_map/ppermute | solution.py:18
  106.7 2.6 %multiply_convert_fusion.1 = bf16[128,3,3,3,128]{0,4,3,2,1:T(8,128)(2,1)S(1)} fusion(bf16[1,7,4,32,128]{4,3,2,1,0:T(8,128)(2,1)S(1)} %copy-done.8, bf16[1,5,2,32,128]{4,3,2,1,0:T(8,128)(2,1)S(1)} %fusion.56), kind=kOutput, calls=%fused_computation.8 | convolution fusion | flops 278102016 | bytes 1196032 | tf_op jit(solution)/shard_map/conv_general_dilated | solution.py:216
  109.3 1.0 copy.264
  110.2 0.8 convert_element_type.158
  111.1 1.0 fusion.30
  112.5 1.2 convolution_select_fusion
  114.0 0.7 pad_maximum_fusion.2
  114.7 0.8 fusion.68
  115.8 0.9 convolution_select_fusion.1
  116.9 0.7 fusion.58
  117.6 2.6 %multiply_convert_fusion = bf16[128,3,3,3,128]{0,4,3,2,1:T(8,128)(2,1)S(1)} fusion(bf16[1,7,4,32,128]{4,3,2,1,0:T(8,128)(2,1)S(1)} %get-tuple-element.41, bf16[1,5,2,32,128]{4,3,2,1,0:T(8,128)(2,1)S(1)} %get-tuple-element.29), kind=kOutput, calls=%fused_computation.7 | convolution fusion | flops 278102016 | bytes 1196032 | tf_op jit(solution)/shard_map/conv_general_dilated | solution.py:216
  120.2 1.0 copy.267
  121.2 0.8 convert_element_type.160
  122.4 1.9 %collective-permute-start.12 = (bf16[4,2,16,3456]{3,2,1,0:T(8,128)(2,1)S(1)}, bf16[4,2,16,3456]{3,2,1,0:T(8,128)(2,1)S(1)}, u32[]{:S(2)}, u32[]{:S(2)}) collective-permute-start(bf16[4,2,16,3456]{3,2,1,0:T(8,128)(2,1)S(1)} %bitcast.178), channel_id=1, source_target_pairs={{0,1},{1,0},{2,3},{3,2},{4,5},{5,4},{6,7},{7,6},{8,9},{9,8},{10,11... | collective-permute-start | bytes 2654216 | tf_op jit(solution)/shard_map/ppermute | solution.py:170
  124.3 2.4 %collective-permute-done.12 = bf16[4,2,16,3456]{3,2,1,0:T(8,128)(2,1)S(1)} collective-permute-done((bf16[4,2,16,3456]{3,2,1,0:T(8,128)(2,1)S(1)}, bf16[4,2,16,3456]{3,2,1,0:T(8,128)(2,1)S(1)}, u32[]{:S(2)}, u32[]{:S(2)}) %collective-permute-start.12) | collective-permute-done | bytes 884768 | tf_op jit(solution)/shard_map/ppermute | solution.py:170
  127.0 2.4 %collective-permute-start.15 = (bf16[2,16,3456]{2,1,0:T(8,128)(2,1)S(1)}, bf16[2,16,3456]{2,1,0:T(8,128)(2,1)S(1)}, u32[]{:S(2)}, u32[]{:S(2)}) collective-permute-start(bf16[2,16,3456]{2,1,0:T(8,128)(2,1)S(1)} %get-tuple-element.37), channel_id=1, source_target_pairs={{0,6},{1,7},{2,0},{3,1},{4,2},{5,3},{6,4},{7,5},{8,14},{9,15},{10,... | collective-permute-start | bytes 663560 | tf_op jit(solution)/shard_map/ppermute | solution.py:177
  129.4 3.7 %collective-permute-start.14 = (bf16[2,16,3456]{2,1,0:T(8,128)(2,1)S(1)}, bf16[2,16,3456]{2,1,0:T(8,128)(2,1)S(1)}, u32[]{:S(2)}, u32[]{:S(2)}) collective-permute-start(bf16[2,16,3456]{2,1,0:T(8,128)(2,1)S(1)} %get-tuple-element.38), channel_id=1, source_target_pairs={{0,4},{1,5},{2,6},{3,7},{4,0},{5,1},{6,2},{7,3},{8,12},{9,13},{10,... | collective-permute-start | bytes 663560 | tf_op jit(solution)/shard_map/ppermute | solution.py:177
  133.1 2.7 %collective-permute-start.13 = (bf16[2,16,3456]{2,1,0:T(8,128)(2,1)S(1)}, bf16[2,16,3456]{2,1,0:T(8,128)(2,1)S(1)}, u32[]{:S(2)}, u32[]{:S(2)}) collective-permute-start(bf16[2,16,3456]{2,1,0:T(8,128)(2,1)S(1)} %get-tuple-element.36), channel_id=1, source_target_pairs={{0,2},{1,3},{2,4},{3,5},{4,6},{5,7},{6,0},{7,1},{8,10},{9,11},{10,... | collective-permute-start | bytes 663560 | tf_op jit(solution)/shard_map/ppermute | solution.py:177
  135.8 3.3 %collective-permute-done.14 = bf16[2,16,3456]{2,1,0:T(8,128)(2,1)S(1)} collective-permute-done((bf16[2,16,3456]{2,1,0:T(8,128)(2,1)S(1)}, bf16[2,16,3456]{2,1,0:T(8,128)(2,1)S(1)}, u32[]{:S(2)}, u32[]{:S(2)}) %collective-permute-start.14) | collective-permute-done | bytes 221216 | tf_op jit(solution)/shard_map/ppermute | solution.py:177
  139.1 5.4 %collective-permute-done.13 = bf16[2,16,3456]{2,1,0:T(8,128)(2,1)S(1)} collective-permute-done((bf16[2,16,3456]{2,1,0:T(8,128)(2,1)S(1)}, bf16[2,16,3456]{2,1,0:T(8,128)(2,1)S(1)}, u32[]{:S(2)}, u32[]{:S(2)}) %collective-permute-start.13) | collective-permute-done | bytes 221216 | tf_op jit(solution)/shard_map/ppermute | solution.py:177
  144.6 1.5 reshape.311
  146.5 0.8 reshape.312
  147.3 0.8 copy_bitcast_fusion.4.x_ref
  148.1 17.6 %shard_map.102 = f32[16,128]{1,0:T(8,128)} custom-call(bf16[8,8,16,128]{3,2,1,0:T(8,128)(2,1)} %copy_bitcast_fusion.4.x_ref), custom_call_target="tpu_custom_call" | custom-call | tf_op jit(solution)/shard_map/pallas_call | solution.py:143
  165.7 0.7 slice_reduce_fusion
  166.4 10.4 %all_to_all.18 = f32[8,1,1728]{2,1,0:T(1,128)S(1)} all-to-all(f32[8,1,1728]{2,1,0:T(1,128)S(1)} %broadcast_in_dim.96), channel_id=1, replica_groups=mesh['wide'=64,'rows'=8] {'rows'}, dimensions={0} | all-to-all | bytes 110592 | tf_op jit(solution)/shard_map/all_to_all | solution.py:195
  177.2 0.7 copy.272
  177.9 0.7 copy.273
  (99 shorter events, 7.2 us)
Async XLA Ops:
  7.2 19.5 %copy-start.5 = (bf16[1,5,2,32,128]{4,3,2,1,0:T(8,128)(2,1)S(1)}, bf16[1,5,2,32,128]{4,3,2,1,0:T(8,128)(2,1)}, u32[]{:S(2)}) copy-start(bf16[1,5,2,32,128]{4,3,2,1,0:T(8,128)(2,1)} %param.11) | copy-start | bytes 245764
  9.0 39.0 %all-to-all-start = ((bf16[64,2,2976]{2,1,0:T(2,128)(2,1)}), bf16[64,2,2976]{2,1,0:T(2,128)(2,1)S(1)}, u32[]{:S(2)}, u32[]{:S(2)}) async-start(bf16[64,2,2976]{2,1,0:T(2,128)(2,1)} %reshape.362), calls=%async_computation | async-start | bytes 1572864 | tf_op jit(solution)/shard_map/all_to_all | solution.py:268
  26.9 30.9 %collective-permute-start.9 = (bf16[5,1,32,128]{3,2,1,0:T(8,128)(2,1)S(1)}, bf16[5,1,32,128]{3,2,1,0:T(8,128)(2,1)S(1)}, u32[]{:S(2)}, u32[]{:S(2)}) collective-permute-start(bf16[5,1,32,128]{3,2,1,0:T(8,128)(2,1)S(1)} %get-tuple-element.51), channel_id=1, source_target_pairs={{1,0},{2,1},{3,2},{4,3},{5,4},{6,5},{7,6},{9,8},{10,9},{11,10},{12... | collective-permute-start | bytes 122888 | tf_op jit(solution)/shard_map/ppermute | solution.py:21
  29.8 28.1 %collective-permute-start.8 = (bf16[5,1,32,128]{3,2,1,0:T(8,128)(2,1)S(1)}, bf16[5,1,32,128]{3,2,1,0:T(8,128)(2,1)S(1)}, u32[]{:S(2)}, u32[]{:S(2)}) collective-permute-start(bf16[5,1,32,128]{3,2,1,0:T(8,128)(2,1)S(1)} %get-tuple-element.50), channel_id=1, source_target_pairs={{0,1},{1,2},{2,3},{3,4},{4,5},{5,6},{6,7},{8,9},{9,10},{10,11},{11... | collective-permute-start | bytes 122888 | tf_op jit(solution)/shard_map/ppermute | solution.py:18
  49.6 21.2 %collective-permute-start.1 = (bf16[5,1,32,128]{3,2,1,0:T(8,128)(2,1)S(1)}, bf16[5,1,32,128]{3,2,1,0:T(8,128)(2,1)S(1)}, u32[]{:S(2)}, u32[]{:S(2)}) collective-permute-start(bf16[5,1,32,128]{3,2,1,0:T(8,128)(2,1)S(1)} %get-tuple-element.55), channel_id=1, source_target_pairs={{1,0},{2,1},{3,2},{4,3},{5,4},{6,5},{7,6},{9,8},{10,9},{11,10},{12... | collective-permute-start | bytes 122888 | tf_op jit(solution)/shard_map/ppermute | solution.py:21
  54.8 16.0 %collective-permute-start = (bf16[5,1,32,128]{3,2,1,0:T(8,128)(2,1)S(1)}, bf16[5,1,32,128]{3,2,1,0:T(8,128)(2,1)S(1)}, u32[]{:S(2)}, u32[]{:S(2)}) collective-permute-start(bf16[5,1,32,128]{3,2,1,0:T(8,128)(2,1)S(1)} %get-tuple-element.54), channel_id=1, source_target_pairs={{0,1},{1,2},{2,3},{3,4},{4,5},{5,6},{6,7},{8,9},{9,10},{10,11},{11... | collective-permute-start | bytes 122888 | tf_op jit(solution)/shard_map/ppermute | solution.py:18
  61.1 10.5 %collective-permute-start.4 = (bf16[2,16,3456]{2,1,0:T(8,128)(2,1)S(1)}, bf16[2,16,3456]{2,1,0:T(8,128)(2,1)S(1)}, u32[]{:S(2)}, u32[]{:S(2)}) collective-permute-start(bf16[2,16,3456]{2,1,0:T(8,128)(2,1)S(1)} %reshape.309), channel_id=1, source_target_pairs={{0,6},{1,7},{2,0},{3,1},{4,2},{5,3},{6,4},{7,5},{8,14},{9,15},{10,... | collective-permute-start | bytes 663560 | tf_op jit(solution)/shard_map/ppermute | solution.py:58
  63.7 9.3 %collective-permute-start.3 = (bf16[2,16,3456]{2,1,0:T(8,128)(2,1)S(1)}, bf16[2,16,3456]{2,1,0:T(8,128)(2,1)S(1)}, u32[]{:S(2)}, u32[]{:S(2)}) collective-permute-start(bf16[2,16,3456]{2,1,0:T(8,128)(2,1)S(1)} %reshape.309), channel_id=1, source_target_pairs={{0,4},{1,5},{2,6},{3,7},{4,0},{5,1},{6,2},{7,3},{8,12},{9,13},{10,... | collective-permute-start | bytes 663560 | tf_op jit(solution)/shard_map/ppermute | solution.py:58
  67.9 11.5 %collective-permute-start.2 = (bf16[2,16,3456]{2,1,0:T(8,128)(2,1)S(1)}, bf16[2,16,3456]{2,1,0:T(8,128)(2,1)S(1)}, u32[]{:S(2)}, u32[]{:S(2)}) collective-permute-start(bf16[2,16,3456]{2,1,0:T(8,128)(2,1)S(1)} %reshape.309), channel_id=1, source_target_pairs={{0,2},{1,3},{2,4},{3,5},{4,6},{5,7},{6,0},{7,1},{8,10},{9,11},{10,... | collective-permute-start | bytes 663560 | tf_op jit(solution)/shard_map/ppermute | solution.py:58
  80.4 4.6 %collective-permute-start.5 = (bf16[4,2,16,3456]{3,2,1,0:T(8,128)(2,1)S(1)}, bf16[4,2,16,3456]{3,2,1,0:T(8,128)(2,1)S(1)}, u32[]{:S(2)}, u32[]{:S(2)}) collective-permute-start(bf16[4,2,16,3456]{3,2,1,0:T(8,128)(2,1)S(1)} %broadcast_select_fusion), channel_id=1, source_target_pairs={{0,1},{1,0},{2,3},{3,2},{4,5},{5,4},{6,7},{7,6},{8,9},{9,8},{10,11... | collective-permute-start | bytes 2654216 | tf_op jit(solution)/shard_map/ppermute | solution.py:62
  85.5 1.0 copy-start.7
  90.5 3.3 %copy-start = (bf16[128,3,3,3,128]{4,3,2,1,0:T(4,128)(2,1)}, bf16[128,3,3,3,128]{4,3,2,1,0:T(4,128)(2,1)S(1)}, u32[]{:S(2)}) copy-start(bf16[128,3,3,3,128]{4,3,2,1,0:T(4,128)(2,1)S(1)} %reshape_squeeze.12) | copy-start | bytes 2654212
  90.5 3.3 %copy-start.4 = (f32[4,2,32,128]{3,2,1,0:T(8,128)S(1)}, f32[4,2,32,128]{3,2,1,0:T(8,128)}, u32[]{:S(2)}) copy-start(f32[4,2,32,128]{3,2,1,0:T(8,128)} %get-tuple-element.40) | copy-start | bytes 393220
  90.5 16.1 %copy-start.3 = (f32[1,4,2,32,128]{4,3,2,1,0:T(8,128)S(1)}, f32[1,4,2,32,128]{4,3,2,1,0:T(8,128)}, u32[]{:S(2)}) copy-start(f32[1,4,2,32,128]{4,3,2,1,0:T(8,128)} %get-tuple-element.39) | copy-start | bytes 393220
  90.5 16.1 %copy-start.9 = (f32[1,1,2,32,128]{4,3,2,1,0:T(8,128)S(1)}, f32[1,1,2,32,128]{4,3,2,1,0:T(8,128)}, u32[]{:S(2)}) copy-start(f32[1,1,2,32,128]{4,3,2,1,0:T(8,128)} %slice_add_fusion.2) | copy-start | bytes 98308
  90.5 16.1 %copy-start.8 = (bf16[1,7,4,32,128]{4,3,2,1,0:T(8,128)(2,1)S(1)}, bf16[1,7,4,32,128]{4,3,2,1,0:T(8,128)(2,1)}, u32[]{:S(2)}) copy-start(bf16[1,7,4,32,128]{4,3,2,1,0:T(8,128)(2,1)} %maximum_bitcast_fusion.1) | copy-start | bytes 688132
  93.9 12.7 %copy-start.2 = (bf16[5,2,32,128]{3,2,1,0:T(8,128)(2,1)}, bf16[5,2,32,128]{3,2,1,0:T(8,128)(2,1)S(1)}, u32[]{:S(2)}) copy-start(bf16[5,2,32,128]{3,2,1,0:T(8,128)(2,1)S(1)} %get-tuple-element.44) | copy-start | bytes 245764
  94.6 16.5 %collective-permute-start.11 = (bf16[5,1,32,128]{3,2,1,0:T(8,128)(2,1)}, bf16[5,1,32,128]{3,2,1,0:T(8,128)(2,1)}, u32[]{:S(2)}, u32[]{:S(2)}) collective-permute-start(bf16[5,1,32,128]{3,2,1,0:T(8,128)(2,1)} %get-tuple-element.49), channel_id=1, source_target_pairs={{1,0},{2,1},{3,2},{4,3},{5,4},{6,5},{7,6},{9,8},{10,9},{11,10},{12... | collective-permute-start | bytes 122888 | tf_op jit(solution)/shard_map/ppermute | solution.py:21
  96.8 14.2 %collective-permute-start.10 = (bf16[5,1,32,128]{3,2,1,0:T(8,128)(2,1)}, bf16[5,1,32,128]{3,2,1,0:T(8,128)(2,1)}, u32[]{:S(2)}, u32[]{:S(2)}) collective-permute-start(bf16[5,1,32,128]{3,2,1,0:T(8,128)(2,1)} %get-tuple-element.48), channel_id=1, source_target_pairs={{0,1},{1,2},{2,3},{3,4},{4,5},{5,6},{6,7},{8,9},{9,10},{10,11},{11... | collective-permute-start | bytes 122888 | tf_op jit(solution)/shard_map/ppermute | solution.py:18
  100.8 13.2 %collective-permute-start.7 = (bf16[5,1,32,128]{3,2,1,0:T(8,128)(2,1)}, bf16[5,1,32,128]{3,2,1,0:T(8,128)(2,1)S(1)}, u32[]{:S(2)}, u32[]{:S(2)}) collective-permute-start(bf16[5,1,32,128]{3,2,1,0:T(8,128)(2,1)} %get-tuple-element.53), channel_id=1, source_target_pairs={{1,0},{2,1},{3,2},{4,3},{5,4},{6,5},{7,6},{9,8},{10,9},{11,10},{12... | collective-permute-start | bytes 122888 | tf_op jit(solution)/shard_map/ppermute | solution.py:21
  102.7 11.2 %collective-permute-start.6 = (bf16[5,1,32,128]{3,2,1,0:T(8,128)(2,1)}, bf16[5,1,32,128]{3,2,1,0:T(8,128)(2,1)}, u32[]{:S(2)}, u32[]{:S(2)}) collective-permute-start(bf16[5,1,32,128]{3,2,1,0:T(8,128)(2,1)} %get-tuple-element.52), channel_id=1, source_target_pairs={{0,1},{1,2},{2,3},{3,4},{4,5},{5,6},{6,7},{8,9},{9,10},{10,11},{11... | collective-permute-start | bytes 122888 | tf_op jit(solution)/shard_map/ppermute | solution.py:18
  111.0 1.5 copy-start.1
  111.0 1.5 copy-start.10
  115.8 1.1 copy-start.6
  122.4 4.3 %collective-permute-start.12 = (bf16[4,2,16,3456]{3,2,1,0:T(8,128)(2,1)S(1)}, bf16[4,2,16,3456]{3,2,1,0:T(8,128)(2,1)S(1)}, u32[]{:S(2)}, u32[]{:S(2)}) collective-permute-start(bf16[4,2,16,3456]{3,2,1,0:T(8,128)(2,1)S(1)} %bitcast.178), channel_id=1, source_target_pairs={{0,1},{1,0},{2,3},{3,2},{4,5},{5,4},{6,7},{7,6},{8,9},{9,8},{10,11... | collective-permute-start | bytes 2654216 | tf_op jit(solution)/shard_map/ppermute | solution.py:170
  127.0 8.8 %collective-permute-start.15 = (bf16[2,16,3456]{2,1,0:T(8,128)(2,1)S(1)}, bf16[2,16,3456]{2,1,0:T(8,128)(2,1)S(1)}, u32[]{:S(2)}, u32[]{:S(2)}) collective-permute-start(bf16[2,16,3456]{2,1,0:T(8,128)(2,1)S(1)} %get-tuple-element.37), channel_id=1, source_target_pairs={{0,6},{1,7},{2,0},{3,1},{4,2},{5,3},{6,4},{7,5},{8,14},{9,15},{10,... | collective-permute-start | bytes 663560 | tf_op jit(solution)/shard_map/ppermute | solution.py:177
  129.4 9.7 %collective-permute-start.14 = (bf16[2,16,3456]{2,1,0:T(8,128)(2,1)S(1)}, bf16[2,16,3456]{2,1,0:T(8,128)(2,1)S(1)}, u32[]{:S(2)}, u32[]{:S(2)}) collective-permute-start(bf16[2,16,3456]{2,1,0:T(8,128)(2,1)S(1)} %get-tuple-element.38), channel_id=1, source_target_pairs={{0,4},{1,5},{2,6},{3,7},{4,0},{5,1},{6,2},{7,3},{8,12},{9,13},{10,... | collective-permute-start | bytes 663560 | tf_op jit(solution)/shard_map/ppermute | solution.py:177
  133.1 11.4 %collective-permute-start.13 = (bf16[2,16,3456]{2,1,0:T(8,128)(2,1)S(1)}, bf16[2,16,3456]{2,1,0:T(8,128)(2,1)S(1)}, u32[]{:S(2)}, u32[]{:S(2)}) collective-permute-start(bf16[2,16,3456]{2,1,0:T(8,128)(2,1)S(1)} %get-tuple-element.36), channel_id=1, source_target_pairs={{0,2},{1,3},{2,4},{3,5},{4,6},{5,7},{6,0},{7,1},{8,10},{9,11},{10,... | collective-permute-start | bytes 663560 | tf_op jit(solution)/shard_map/ppermute | solution.py:177
